TPU v7x, 32 devices: a whole 2x2x4 slice. The times are simulated.
32 devices in a mesh: dp: 8 (over y, x, core), mp: 4 (over z).
Axes of the slice: x: 2, y: 2, z: 4, core: 2. Of those that a mesh axis runs over, the one named last changes fastest.
Arguments:
- inputs: bfloat16 [2, 16384, 1024], P(None, ('dp', 'mp')), may hold values from -6 to 6
- segments: int32 [2, 8, 2048], P(None, 'dp'), may hold values from 0 to 3, as said below
- w_query: bfloat16 [1024, 1024], P('dp', 'mp'), may hold values from -0.1875 to 0.1875
- w_key: bfloat16 [1024, 1024], P('dp', 'mp'), may hold values from -0.1875 to 0.1875
- w_value: bfloat16 [1024, 1024], P('dp', 'mp'), may hold values from -0.1875 to 0.1875
- w_output: bfloat16 [1024, 1024], P('mp', 'dp'), may hold values from -0.75 to 0.75
- w_gate: bfloat16 [1024, 2816], P('dp', 'mp'), may hold values from -0.1875 to 0.1875
- w_up: bfloat16 [1024, 2816], P('dp', 'mp'), may hold values from -0.1875 to 0.1875
- w_down: bfloat16 [2816, 1024], P('mp', 'dp'), may hold values from -0.109375 to 0.109375
- gain_attn: float32 [1024], P('dp'), may hold values from 0.25 to 1.75
- gain_ffn: float32 [1024], P('dp'), may hold values from 0.25 to 1.75
- cotangent: bfloat16 [2, 16384, 1024], P(None, ('dp', 'mp')), may hold values from -6 to 6
Outputs:
- result: bfloat16 [2, 16384, 1024], P(None, ('dp', 'mp'))
- grad_inputs: bfloat16 [2, 16384, 1024], P(None, ('dp', 'mp'))
- grad_query: float32 [1024, 1024], P('dp', 'mp')
- grad_key: float32 [1024, 1024], P('dp', 'mp')
- grad_value: float32 [1024, 1024], P('dp', 'mp')
- grad_output: float32 [1024, 1024], P('mp', 'dp')
- grad_gate: float32 [1024, 2816], P('dp', 'mp')
- grad_up: float32 [1024, 2816], P('dp', 'mp')
- grad_down: float32 [2816, 1024], P('mp', 'dp')
- grad_norm_attn: float32 [1024], P(('dp', 'mp'))
- grad_norm_ffn: float32 [1024], P(('dp', 'mp'))
Inputs may be any that keep to these rules, and one draw needn't show every extreme that they name: `segments`: within each packed row the segment numbers never fall and each number names one run of consecutive patches; every row holds four documents, one of exactly 1024 patches and three of 204 patches or more.
All inputs are finite; a program needn't handle non-finite values.
Results may differ from a plain program's by a relative error of at most 0.035.
Values may be sent and summed in bfloat16 or wider, within the bound.
A program may use at most 320 MiB of HBM per device.

v0:
```python
import functools
import math

import jax
import jax.numpy as jnp
from jax import lax
from jax.experimental import pallas as pl
from jax.experimental.pallas import tpu as pltpu
from jax.sharding import PartitionSpec as P


HD = 64
BQ = 512
BK = 256
HPS = 2


def attn_fwd_kernel(lo_ref, q_ref, k_ref, v_ref, start_ref, o_ref, lse_ref, k_scr, *, bq, bk, heads):
    length = q_ref.shape[1]
    k_scr[...] = k_ref[...].T

    def q_step(qi, carry):
        q0 = pl.multiple_of(qi * bq, bq)
        qcols = pl.ds(q0, bq)
        q_blk = q_ref[:, qcols]
        start = start_ref[:, qcols]
        q_idx = q0 + lax.broadcasted_iota(jnp.int32, (1, bq), 1)

        def k_step(kb, state):
            k0 = pl.multiple_of(kb * bk, bk)
            k_idx = k0 + lax.broadcasted_iota(jnp.int32, (bk, bq), 0)
            allowed = (k_idx >= start) & (k_idx <= q_idx)
            out = []
            for h in range(heads):
                peak, total, acc = state[h]
                s = jnp.dot(k_scr[pl.ds(k0, bk), h * HD:(h + 1) * HD], q_blk[h * HD:(h + 1) * HD], preferred_element_type=jnp.float32)
                s = jnp.where(allowed, s, -1e30)
                new_peak = jnp.maximum(peak, jnp.max(s, axis=0, keepdims=True))
                p = jnp.exp(s - new_peak)
                fade = jnp.exp(peak - new_peak)
                total = total * fade + jnp.sum(p, axis=0, keepdims=True)
                acc = acc * fade + jnp.dot(v_ref[h * HD:(h + 1) * HD, pl.ds(k0, bk)], p.astype(jnp.bfloat16), preferred_element_type=jnp.float32)
                out.append((new_peak, total, acc))
            return tuple(out)

        init = tuple((jnp.full((1, bq), -1e30, jnp.float32), jnp.zeros((1, bq), jnp.float32), jnp.zeros((HD, bq), jnp.float32)) for _ in range(heads))
        hi = (q0 + bq - 1) // bk
        state = lax.fori_loop(lo_ref[qi], hi + 1, k_step, init)
        for h in range(heads):
            peak, total, acc = state[h]
            o_ref[h * HD:(h + 1) * HD, qcols] = (acc / total).astype(jnp.bfloat16)
            lse_ref[h, :, qcols] = peak + jnp.log(total)
        return carry

    lax.fori_loop(0, length // bq, q_step, 0)


def attn_bwd_kernel(lo_ref, q_ref, k_ref, v_ref, do_ref, o_ref, lse_ref, start_ref, cos_ref, sin_ref, out_ref, k_scr, v_scr, dk_scr, dv_scr, *, bq, bk, heads):
    length = q_ref.shape[1]
    k_scr[...] = k_ref[...].T
    v_scr[...] = v_ref[...].T
    dk_scr[...] = jnp.zeros_like(dk_scr)
    dv_scr[...] = jnp.zeros_like(dv_scr)
    half = HD // 2

    def unrotate(g, cos, sin):
        a, b = g[:half], g[half:]
        return jnp.concatenate([a * cos + b * sin, b * cos - a * sin], axis=0).astype(jnp.bfloat16)

    def q_step(qi, carry):
        q0 = pl.multiple_of(qi * bq, bq)
        qcols = pl.ds(q0, bq)
        q_blk = q_ref[:, qcols]
        do_blk = do_ref[:, qcols]
        q_t = q_blk.T
        do_t = do_blk.T
        prod = do_blk.astype(jnp.float32) * o_ref[:, qcols].astype(jnp.float32)
        start = start_ref[:, qcols]
        q_idx = q0 + lax.broadcasted_iota(jnp.int32, (1, bq), 1)
        deltas = [jnp.sum(prod[h * HD:(h + 1) * HD], axis=0, keepdims=True) for h in range(heads)]
        lses = [lse_ref[h, :, qcols] for h in range(heads)]

        def k_step(kb, state):
            k0 = pl.multiple_of(kb * bk, bk)
            rows = pl.ds(k0, bk)
            k_idx = k0 + lax.broadcasted_iota(jnp.int32, (bk, bq), 0)
            allowed = (k_idx >= start) & (k_idx <= q_idx)
            out = []
            for h in range(heads):
                hs = slice(h * HD, (h + 1) * HD)
                s = jnp.dot(k_scr[rows, hs], q_blk[hs], preferred_element_type=jnp.float32)
                p = jnp.exp(jnp.where(allowed, s - lses[h], -1e30))
                dp = jnp.dot(v_scr[rows, hs], do_blk[hs], preferred_element_type=jnp.float32)
                ds = (p * (dp - deltas[h])).astype(jnp.bfloat16)
                dv_scr[h, rows, :] += jnp.dot(p.astype(jnp.bfloat16), do_t[:, hs], preferred_element_type=jnp.float32)
                dk_scr[h, rows, :] += jnp.dot(ds, q_t[:, hs], preferred_element_type=jnp.float32)
                out.append(state[h] + jnp.dot(k_ref[hs, rows], ds, preferred_element_type=jnp.float32))
            return tuple(out)

        init = tuple(jnp.zeros((HD, bq), jnp.float32) for _ in range(heads))
        hi = (q0 + bq - 1) // bk
        state = lax.fori_loop(lo_ref[qi], hi + 1, k_step, init)
        cos, sin = cos_ref[:, qcols], sin_ref[:, qcols]
        for h in range(heads):
            out_ref[0, h * HD:(h + 1) * HD, qcols] = unrotate(state[h] * HD ** -0.5, cos, sin)
        return carry

    lax.fori_loop(0, length // bq, q_step, 0)
    for h in range(heads):
        out_ref[1, h * HD:(h + 1) * HD, :] = unrotate(dk_scr[h].T, cos_ref[...], sin_ref[...])
        out_ref[2, h * HD:(h + 1) * HD, :] = dv_scr[h].T.astype(jnp.bfloat16)


def attn_fwd(qkv_t, start, lo, bq=BQ, bk=BK, hps=HPS):
    cols3, length = qkv_t.shape
    cols = cols3 // 3
    steps = cols // (HD * hps)
    blk = (HD * hps, length)
    area = cols * length * length // 4
    return pl.pallas_call(
        functools.partial(attn_fwd_kernel, bq=bq, bk=bk, heads=hps),
        out_shape=(jax.ShapeDtypeStruct((cols, length), jnp.bfloat16), jax.ShapeDtypeStruct((cols // HD, 1, length), jnp.float32)),
        grid_spec=pltpu.PrefetchScalarGridSpec(
            num_scalar_prefetch=1, grid=(steps,),
            in_specs=[pl.BlockSpec(blk, lambda i, lo: (i, 0)), pl.BlockSpec(blk, lambda i, lo: (i + steps, 0)), pl.BlockSpec(blk, lambda i, lo: (i + 2 * steps, 0)),
                      pl.BlockSpec((1, length), lambda i, lo: (0, 0))],
            out_specs=[pl.BlockSpec(blk, lambda i, lo: (i, 0)), pl.BlockSpec((hps, 1, length), lambda i, lo: (i, 0, 0))],
            scratch_shapes=[pltpu.VMEM((length, HD * hps), jnp.bfloat16)]),
        cost_estimate=pl.CostEstimate(flops=16 * area, bytes_accessed=cols * length * 8, transcendentals=area // HD),
        name="attn_fwd",
    )(lo, qkv_t, qkv_t, qkv_t, start)


def attn_bwd(qkv_t, do_t, o_t, lse, start, lo, cos, sin, bq=BQ, bk=BK, hps=HPS):
    cols3, length = qkv_t.shape
    cols = cols3 // 3
    steps = cols // (HD * hps)
    blk = (HD * hps, length)
    area = cols * length * length // 4
    return pl.pallas_call(
        functools.partial(attn_bwd_kernel, bq=bq, bk=bk, heads=hps),
        out_shape=jax.ShapeDtypeStruct((3, cols, length), jnp.bfloat16),
        grid_spec=pltpu.PrefetchScalarGridSpec(
            num_scalar_prefetch=1, grid=(steps,),
            in_specs=[pl.BlockSpec(blk, lambda i, lo: (i, 0)), pl.BlockSpec(blk, lambda i, lo: (i + steps, 0)), pl.BlockSpec(blk, lambda i, lo: (i + 2 * steps, 0)),
                      pl.BlockSpec(blk, lambda i, lo: (i, 0)), pl.BlockSpec(blk, lambda i, lo: (i, 0)),
                      pl.BlockSpec((hps, 1, length), lambda i, lo: (i, 0, 0)),
                      pl.BlockSpec((1, length), lambda i, lo: (0, 0)),
                      pl.BlockSpec((HD // 2, length), lambda i, lo: (0, 0)), pl.BlockSpec((HD // 2, length), lambda i, lo: (0, 0))],
            out_specs=pl.BlockSpec((3,) + blk, lambda i, lo: (0, i, 0)),
            scratch_shapes=[pltpu.VMEM((length, HD * hps), jnp.bfloat16)] * 2 + [pltpu.VMEM((hps, length, HD), jnp.float32)] * 2),
        cost_estimate=pl.CostEstimate(flops=40 * area, bytes_accessed=cols * length * 20, transcendentals=area // HD),
        name="attn_bwd",
    )(lo, qkv_t, qkv_t, qkv_t, do_t, o_t, lse, start, cos, sin)


eps_norm = 1e-05


def dot_dims(left, right, left_dim, right_dim):
    return lax.dot_general(
        left, right, (((left_dim,), (right_dim,)), ((), ())), preferred_element_type=jnp.float32
    )


def row_starts(seg_row):
    ones = [jnp.sum((seg_row < s).astype(jnp.int32)) for s in (1, 2, 3)]
    start = jnp.zeros_like(seg_row)
    before = 0
    for s, count in zip((1, 2, 3), ones):
        start = start + jnp.where(seg_row >= s, count - before, 0)
        before = count
    return start


def rope_tables(start):
    half_dim = HD // 2
    offsets = (jnp.arange(start.shape[0], dtype=jnp.int32) - start).astype(jnp.float32)
    frequency = jnp.exp(jnp.arange(half_dim, dtype=jnp.float32) * (-math.log(10000.0) / half_dim))
    angles = frequency[:, None] * offsets[None, :]
    return jnp.cos(angles), jnp.sin(angles)


def rotate(rows, cos_table, sin_table):
    count, length = rows.shape
    parts = rows.reshape(count // HD, 2, HD // 2, length)
    low, high = parts[:, 0], parts[:, 1]
    turned = jnp.stack(
        [low * cos_table - high * sin_table, high * cos_table + low * sin_table], axis=1
    )
    return turned.reshape(count, length)


def rms_factor(values):
    return lax.rsqrt(jnp.mean(values * values, axis=-1, keepdims=True) + eps_norm)


def rms_back(values_in, factor, gain, grad_normed):
    scaled = grad_normed * gain
    gain_part = jnp.sum(grad_normed * values_in * factor, axis=0)
    inner = jnp.mean(scaled * values_in, axis=-1, keepdims=True)
    return factor * scaled - values_in * (factor * factor * factor) * inner, gain_part


def scatter(partial_sum, axis, dim):
    return lax.psum_scatter(partial_sum, axis, scatter_dimension=dim, tiled=True)


def line_steps(count):
    near_right = [(i, i + 1) for i in range(count - 1)]
    near_left = [(i, i - 1) for i in range(1, count)]
    return near_right, near_left


def line_gather(piece, axis, hold=lambda *arrays: arrays):
    count, me = lax.axis_size(axis), lax.axis_index(axis)
    assert count == 4
    near_right, near_left = line_steps(count)
    one_left = lax.ppermute(piece, axis, near_right)
    one_right = lax.ppermute(piece, axis, near_left)
    one_left, one_right = hold(one_left, one_right)
    two_left = lax.ppermute(one_left, axis, [(1, 2), (2, 3)])
    two_right = lax.ppermute(one_right, axis, [(1, 0), (2, 1)])
    three_left = lax.ppermute(one_left, axis, [(1, 3)])
    three_right = lax.ppermute(one_right, axis, [(2, 0)])
    slots = jnp.concatenate(
        [three_left, two_left, one_left, piece, one_right, two_right, three_right], axis=0
    )
    rows = piece.shape[0]
    return lax.dynamic_slice_in_dim(slots, (count - 1 - me) * rows, count * rows, axis=0)


def line_scatter(partial_sum, axis):
    count, me = lax.axis_size(axis), lax.axis_index(axis)
    assert count == 4
    rows = partial_sum.shape[0] // count
    near_right, near_left = line_steps(count)

    def block(offset):
        first = jnp.clip(me + offset, 0, count - 1) * rows
        return lax.dynamic_slice_in_dim(partial_sum, first, rows, axis=0)

    two_right = lax.ppermute(block(2), axis, [(0, 1), (1, 2)])
    two_left = lax.ppermute(block(-2), axis, [(3, 2), (2, 1)])
    three_right = lax.ppermute(block(3), axis, [(0, 2)])
    three_left = lax.ppermute(block(-3), axis, [(3, 1)])

    def total(*parts):
        return sum(part.astype(jnp.float32) for part in parts)

    right = lax.ppermute(
        total(block(1), two_right, three_right).astype(jnp.bfloat16), axis, near_right
    )
    left = lax.ppermute(
        total(block(-1), two_left, three_left).astype(jnp.bfloat16), axis, near_left
    )
    return total(block(0), right, left)


def exchange_sum(partial_sum, axis):
    count = lax.axis_size(axis)
    parts = partial_sum.reshape((count, partial_sum.shape[0] // count) + partial_sum.shape[1:])
    swapped = lax.all_to_all(parts, axis, split_axis=0, concat_axis=0, tiled=True)
    return jnp.sum(swapped.astype(jnp.float32), axis=0)


def local(
    inputs, segments, w_query, w_key, w_value, w_output, w_gate, w_up, w_down,
    gain_attn, gain_ffn, cotangent,
):
    low = jnp.bfloat16
    n_dp, n_mp = lax.axis_size("dp"), lax.axis_size("mp")
    batches, tokens, width = inputs.shape
    cols = w_query.shape[1]
    depth = w_query.shape[0]

    def split16(gain):
        high = gain.astype(low)
        return high, (gain - high.astype(jnp.float32)).astype(low)

    pieces = split16(gain_attn) + split16(gain_ffn)
    gain_row = jnp.concatenate(pieces + (jnp.zeros((3 * cols - 4 * depth,), low),))
    qkv_piece = jnp.concatenate(
        [
            jnp.concatenate([w_query, w_key, w_value], axis=1),
            jnp.pad(gain_row[None], ((0, 15), (0, 0))),
        ],
        axis=0,
    )
    qkv_all = lax.all_gather(qkv_piece, "dp", axis=0, tiled=False)
    w_qkv = qkv_all[:, :depth].reshape(width, 3 * cols)
    gains = qkv_all[:, depth, : 4 * depth].astype(jnp.float32).reshape(n_dp, 4, depth)
    gain_one = (gains[:, 0] + gains[:, 1]).reshape(width)
    gain_two = (gains[:, 2] + gains[:, 3]).reshape(width)

    first_rows = line_gather(inputs[0], "mp")
    first_rows, second_piece, w_output, gate_t, up_t, w_down = lax.optimization_barrier(
        (first_rows, inputs[1], w_output, w_gate.T, w_up.T, w_down)
    )
    rows_all = [first_rows, None]

    def whole(piece):
        every = lax.all_gather(piece, ("dp", "mp"), axis=0, tiled=False)
        every = every.reshape((n_dp, n_mp) + piece.shape)
        return every.transpose(1, 2, 0, 3).reshape(n_mp * piece.shape[0], width)

    output_full, gate_full, up_full, down_full = (
        whole(piece) for piece in (w_output, gate_t, up_t, w_down)
    )

    normed, factors, qkv, tables, starts, lows, mixed, logs = [], [], [], [], [], [], [], []
    for m in range(batches):
        start = row_starts(segments[m, 0])
        cos_table, sin_table = rope_tables(start)
        tables.append((cos_table, sin_table))
        starts.append(start[None])
        lows.append(start[::BQ] // BK)
        if m == 1:
            def after_first(left, right):
                left, right, mixed[0] = lax.optimization_barrier((left, right, mixed[0]))
                return left, right

            rows_all[1] = line_gather(second_piece, "mp", after_first)
        rows = rows_all[m].astype(jnp.float32)
        factors.append(rms_factor(rows))
        normed.append((rows * factors[m] * gain_one).astype(low))
        pre = dot_dims(w_qkv, normed[m], 0, 1)
        turned_q = rotate(pre[:cols], cos_table, sin_table) * HD ** -0.5
        turned_k = rotate(pre[cols : 2 * cols], cos_table, sin_table)
        qkv.append(jnp.concatenate([turned_q, turned_k, pre[2 * cols :]], axis=0).astype(low))
        out, log = attn_fwd(qkv[m], starts[m], lows[m])
        mixed.append(out)
        logs.append(log)
    mixed_own = [
        lax.all_to_all(mixed[m], "mp", split_axis=1, concat_axis=0, tiled=True)
        for m in range(batches)
    ]
    in_float = inputs.astype(jnp.float32).reshape(batches * tokens, width)
    mixed_both = jnp.concatenate(mixed_own, axis=1)
    hidden_in = in_float + dot_dims(mixed_both, output_full, 0, 0)
    factor_ffn = rms_factor(hidden_in)
    normed_ffn = (hidden_in * factor_ffn * gain_two).astype(low)
    gate_pre = dot_dims(normed_ffn, gate_full, 1, 1)
    up_pre = dot_dims(normed_ffn, up_full, 1, 1)
    sig_gate = jax.nn.sigmoid(gate_pre)
    silu_gate = gate_pre * sig_gate
    hidden = (silu_gate * up_pre).astype(low)
    result = (hidden_in + dot_dims(hidden, down_full, 1, 0)).astype(low)

    grad_top = cotangent.reshape(batches * tokens, width)
    grad_down = dot_dims(grad_top, hidden, 0, 0).astype(low)
    grad_hidden = dot_dims(grad_top, down_full, 1, 1)
    grad_gate_pre = (
        grad_hidden * up_pre * sig_gate * (1.0 + gate_pre * (1.0 - sig_gate))
    ).astype(low)
    grad_up_pre = (grad_hidden * silu_gate).astype(low)
    grad_gate = dot_dims(normed_ffn, grad_gate_pre, 0, 0).astype(low)
    grad_up = dot_dims(normed_ffn, grad_up_pre, 0, 0).astype(low)
    grad_normed_ffn = dot_dims(grad_gate_pre, gate_full, 1, 0) + dot_dims(
        grad_up_pre, up_full, 1, 0
    )
    grad_middle, gain_ffn_part = rms_back(hidden_in, factor_ffn, gain_two, grad_normed_ffn)
    grad_hidden_in = grad_top.astype(jnp.float32) + grad_middle
    grad_branch = grad_hidden_in.astype(low)
    grad_mixed = dot_dims(output_full, grad_branch, 1, 1).astype(low)
    grad_mixed_rows = []
    for m in range(batches):
        grad_mixed_rows.append(
            lax.all_to_all(
                grad_mixed[:, m * tokens : (m + 1) * tokens], "mp", split_axis=0,
                concat_axis=1, tiled=True,
            )
        )
    grad_output = dot_dims(grad_branch, mixed_both, 0, 1).astype(low)
    grad_mixed_rows[0], grad_down, grad_gate, grad_up, grad_output = lax.optimization_barrier(
        (grad_mixed_rows[0], grad_down, grad_gate, grad_up, grad_output)
    )

    mine = [scatter(g, "dp", 0) for g in (grad_down, grad_gate, grad_up, grad_output)]


    grad_qkv, grad_normed = [], []
    gain_attn_part = jnp.zeros((width,), jnp.float32)
    for m in range(batches):
        cos_table, sin_table = tables[m]
        back = attn_bwd(
            qkv[m], grad_mixed_rows[m], mixed[m], logs[m], starts[m], lows[m], cos_table,
            sin_table,
        ).reshape(3 * cols, n_mp * tokens)
        grad_qkv.append(back)
        spread = dot_dims(back, w_qkv, 0, 1).astype(low)
        if m == 0:
            spread, grad_mixed_rows[1] = lax.optimization_barrier((spread, grad_mixed_rows[1]))
        grad_normed.append(line_scatter(spread, "mp"))
        gain_attn_part = gain_attn_part + jnp.sum(
            spread.astype(jnp.float32) * rows_all[m].astype(jnp.float32) * factors[m], axis=0
        )
    grad_w = sum(dot_dims(normed[m], grad_qkv[m], 0, 1) for m in range(batches))

    def owned(part):
        parts = part.reshape(depth, n_mp, -1).transpose(1, 0, 2)
        return scatter(parts, "mp", 0)[0].astype(jnp.float32)

    own_down, own_gate, own_up, own_output = (owned(part) for part in mine)
    own_qkv = exchange_sum(grad_w.astype(low), "dp")

    grad_normed_attn = jnp.concatenate(grad_normed, axis=0)
    grad_lower, _ = rms_back(in_float, rms_factor(in_float), gain_one, grad_normed_attn)
    grad_inputs = (grad_hidden_in + grad_lower).astype(low)
    grad_norms = exchange_sum(jnp.stack([gain_attn_part, gain_ffn_part], axis=1), ("dp", "mp")).T
    return (
        result.reshape(inputs.shape),
        grad_inputs.reshape(inputs.shape),
        own_qkv[:, :cols],
        own_qkv[:, cols : 2 * cols],
        own_qkv[:, 2 * cols :],
        own_output.T,
        own_gate,
        own_up,
        own_down.T,
        grad_norms[0],
        grad_norms[1],
    )


def solution(mesh):
    row_spec = P(None, ("dp", "mp"), None)
    first, second = P("dp", "mp"), P("mp", "dp")
    both = P(("dp", "mp"))

    return jax.shard_map(
        local,
        mesh=mesh,
        in_specs=(
            row_spec, P(None, "dp", None), first, first, first, second, first, first, second,
            P("dp"), P("dp"), row_spec,
        ),
        out_specs=(
            row_spec, row_spec, first, first, first, second, first, first, second, both, both,
        ),
        check_vma=False,
    )
```

profile of v0, /device:TPU:0, one launch (start us, length us, event | category | flops | bytes accessed | tf_op | source)
XLA Modules:
  0.0 875.7 jit_solution(17454221769546377524)
XLA Ops:
  10.0 6.1 collective-permute-start
  19.2 18.6 %collective-permute-done = bf16[512,1024]{1,0:T(8,128)(2,1)} collective-permute-done((bf16[512,1024]{1,0:T(8,128)(2,1)}, bf16[512,1024]{1,0:T(8,128)(2,1)}, u32[]{:S(2)}, u32[]{:S(2)}) %collective-permute-start) | collective-permute-done | bytes 1048608 | tf_op jit(solution)/shard_map/ppermute | solution.py:219
  52.6 20.7 %collective-permute-done.4 = bf16[512,1024]{1,0:T(8,128)(2,1)} collective-permute-done((bf16[512,1024]{1,0:T(8,128)(2,1)}, bf16[512,1024]{1,0:T(8,128)(2,1)}, u32[]{:S(2)}, u32[]{:S(2)}) %collective-permute-start.4) | collective-permute-done | bytes 1048608 | tf_op jit(solution)/shard_map/ppermute | solution.py:223
  74.7 21.3 %collective-permute-done.5 = bf16[512,1024]{1,0:T(8,128)(2,1)} collective-permute-done((bf16[512,1024]{1,0:T(8,128)(2,1)}, bf16[512,1024]{1,0:T(8,128)(2,1)}, u32[]{:S(2)}, u32[]{:S(2)}) %collective-permute-start.5) | collective-permute-done | bytes 1048608 | tf_op jit(solution)/shard_map/ppermute | solution.py:225
  120.9 6.2 fusion.59
  131.0 22.4 %attn_fwd.2 = (bf16[256,2048]{1,0:T(8,128)(2,1)}, f32[4,1,2048]{2,1,0:T(1,128)}) custom-call(s32[4]{0:T(128)} %get-tuple-element.123.lo_ref, bf16[768,2048]{1,0:T(8,128)(2,1)} %pad_maximum_fusion.1.q_ref.k_ref.v_ref, bf16[768,2048]{1,0:T(8,128)(2,1)} %pad_maximum_fusion.1.q_ref.k_ref.v_ref, bf16[768,2048]{1,0:T(8,128)(2,1)} %pad_maximum_fusion.1.q_ref.k_ref.v_ref, ...), custom_call_target="tpu_custom_call" | custom-call | flops 4294967296 | bytes 4194304 | tf_op jit(solution)/shard_map/attn_fwd/pallas_call | solution.py:120
  161.7 12.6 %all-to-all-start = ((bf16[256,4,512]{2,0,1:T(8,128)(2,1)}), bf16[256,4,512]{2,0,1:T(8,128)(2,1)}, u32[]{:S(2)}, u32[]{:S(2)}) async-start(bf16[256,4,512]{2,0,1:T(8,128)(2,1)} %bitcast.188), calls=%async_computation | async-start | bytes 2097152 | tf_op jit(solution)/shard_map/all_to_all | solution.py:335
  179.6 19.8 %collective-permute-done.10 = bf16[512,1024]{1,0:T(8,128)(2,1)} collective-permute-done((bf16[512,1024]{1,0:T(8,128)(2,1)}, bf16[512,1024]{1,0:T(8,128)(2,1)}, u32[]{:S(2)}, u32[]{:S(2)}) %collective-permute-start.10) | collective-permute-done | bytes 1048608 | tf_op jit(solution)/shard_map/ppermute | solution.py:223
  200.7 51.6 %collective-permute-done.11 = bf16[512,1024]{1,0:T(8,128)(2,1)} collective-permute-done((bf16[512,1024]{1,0:T(8,128)(2,1)}, bf16[512,1024]{1,0:T(8,128)(2,1)}, u32[]{:S(2)}, u32[]{:S(2)}) %collective-permute-start.11) | collective-permute-done | bytes 1048608 | tf_op jit(solution)/shard_map/ppermute | solution.py:225
  264.7 22.6 %attn_fwd.3 = (bf16[256,2048]{1,0:T(8,128)(2,1)}, f32[4,1,2048]{2,1,0:T(1,128)}) custom-call(s32[4]{0:T(128)} %get-tuple-element.122.lo_ref, bf16[768,2048]{1,0:T(8,128)(2,1)} %pad_maximum_fusion.2.q_ref.k_ref.v_ref, bf16[768,2048]{1,0:T(8,128)(2,1)} %pad_maximum_fusion.2.q_ref.k_ref.v_ref, bf16[768,2048]{1,0:T(8,128)(2,1)} %pad_maximum_fusion.2.q_ref.k_ref.v_ref, ...), custom_call_target="tpu_custom_call" | custom-call | flops 4294967296 | bytes 4194304 | tf_op jit(solution)/shard_map/attn_fwd/pallas_call | solution.py:120
  297.8 33.4 %all-to-all-done.1 = bf16[256,4,512]{2,0,1:T(8,128)(2,1)S(1)} async-done(((bf16[256,4,512]{2,0,1:T(8,128)(2,1)}), bf16[256,4,512]{2,0,1:T(8,128)(2,1)S(1)}, u32[]{:S(2)}, u32[]{:S(2)}) %all-to-all-start.1) | async-done | bytes 1048608 | tf_op jit(solution)/shard_map/all_to_all | solution.py:335
  331.2 4.6 multiply_reduce_fusion.2
  339.5 8.9 %copy.44 = bf16[8,4,704,128]{3,0,2,1:T(8,128)(2,1)} copy(bf16[8,4,704,128]{3,2,1,0:T(8,128)(2,1)} %bitcast.198) | data formatting | bytes 11534336 | tf_op jit(solution)/shard_map/reshape | solution.py:304
  348.4 9.2 %copy.46 = bf16[8,4,704,128]{3,0,2,1:T(8,128)(2,1)} copy(bf16[8,4,704,128]{3,2,1,0:T(8,128)(2,1)} %bitcast.199) | data formatting | bytes 11534336 | tf_op jit(solution)/shard_map/reshape | solution.py:304
  357.6 49.0 %all-gather.17.cloned.1.call-done = bf16[22528,128]{1,0:T(8,128)(2,1)} async-done(((bf16[704,128]{1,0:T(8,128)(2,1)}), bf16[22528,128]{1,0:T(8,128)(2,1)}) %all-gather.17.cloned.1.call-update) | async-done | bytes 5767184 | tf_op jit(solution)/shard_map/all_gather | solution.py:303
  406.6 9.0 %copy.45 = bf16[8,4,704,128]{3,0,2,1:T(8,128)(2,1)} copy(bf16[8,4,704,128]{3,2,1,0:T(8,128)(2,1)} %bitcast.200) | data formatting | bytes 11534336 | tf_op jit(solution)/shard_map/reshape | solution.py:304
  415.6 8.9 %fusion.25 = f32[1024,2816]{1,0:T(8,128)} fusion(bf16[1024,1024]{1,0:T(8,128)(2,1)S(1)} %copy-done.14, bf16[352,8,8,128]{3,2,1,0:T(8,128)(2,1)S(1)} %bitcast.204), kind=kOutput, calls=%fused_computation.35 | convolution fusion | flops 5905580032 | bytes 19398656 | tf_op jit(solution)/shard_map/dot_general | solution.py:161
  424.5 8.9 %fusion.15 = f32[2816,1024]{0,1:T(8,128)} fusion(bf16[1024,1024]{1,0:T(8,128)(2,1)S(1)} %bitcast.221, bf16[352,8,8,128]{3,2,1,0:T(8,128)(2,1)S(1)} %bitcast.197), kind=kOutput, calls=%fused_computation.25 | convolution fusion | flops 5905580032 | bytes 19398656 | tf_op jit(solution)/shard_map/dot_general | solution.py:161
  433.4 21.9 %fusion.2 = (bf16[1024,2816]{1,0:T(8,128)(2,1)}, bf16[1024,2816]{1,0:T(8,128)(2,1)}, bf16[1024,2816]{1,0:T(8,128)(2,1)}) fusion(f32[2816,1024]{0,1:T(8,128)} %fusion.15, f32[1024,2816]{1,0:T(8,128)} %fusion.25, bf16[1024,1024]{1,0:T(8,128)(2,1)S(1)} %copy-done.15, bf16[352,8,8,128]{3,2,1,0:T(8,128)(2,1)} %bitcast.205), kind=kOutput, calls=%fused_computation.10 | convolution fusion | flops 5948833792 | bytes 48234496 | tf_op jit(solution)/shard_map/dot_general | solution.py:161
  455.3 11.3 %fusion.19 = f32[1024,1024]{1,0:T(8,128)} fusion(bf16[1024,2816]{1,0:T(8,128)(2,1)} %get-tuple-element.62, bf16[352,8,8,128]{3,2,1,0:T(8,128)(2,1)} %bitcast.206), kind=kOutput, calls=%fused_computation.29 | convolution fusion | flops 5905580032 | bytes 15728640 | tf_op jit(solution)/shard_map/dot_general | solution.py:161
  466.6 8.3 convolution_convert_fusion
  474.9 12.5 %multiply_reduce_fusion = (f32[1024]{0:T(1024)S(1)}, f32[1024]{0:T(1024)S(1)}, f32[1024,1024]{1,0:T(8,128)S(1)}) fusion(f32[1024,1024]{1,0:T(8,128)} %copy-done.8, f32[1024]{0:T(1024)S(1)} %get-tuple-element.108, f32[1024]{0:T(1024)S(1)} %bitcast.241, f32[1024,1024]{1,0:T(8,128)} %fusion.19, bf16[1024,2816]{1,0:T(8,128)(2,1)} %get-tuple-element.61, ...), kind=kOutput, calls=%fused_computation.57 | convolution fusion | flops 5912918016 | bytes 24133632 | tf_op jit(solution)/shard_map/dot_general | solution.py:161
  491.3 5.1 convolution_convert_fusion.4
  506.1 10.8 %convert_bitcast_fusion = bf16[1024,2816]{0,1:T(8,128)(2,1)} fusion(bf16[1024,2816]{1,0:T(8,128)(2,1)} %get-tuple-element.63, bf16[1024,1024]{1,0:T(8,128)(2,1)S(1)} %bitcast.222), kind=kOutput, calls=%fused_computation.37 | convolution fusion | flops 5908463616 | bytes 13631488 | tf_op jit(solution)/shard_map/dot_general | solution.py:161
  516.9 10.7 %convolution_convert_fusion.1 = bf16[1024,2816]{1,0:T(8,128)(2,1)} fusion(bf16[1024,1024]{1,0:T(8,128)(2,1)S(1)} %copy-done.16, bf16[1024,2816]{1,0:T(8,128)(2,1)} %get-tuple-element.61), kind=kOutput, calls=%fused_computation.39 | convolution fusion | flops 5908463616 | bytes 13631488 | tf_op jit(solution)/shard_map/dot_general | solution.py:161
  527.7 4.7 all-to-all-done.2
  533.6 8.3 copy.56
  547.2 25.5 %all-to-all-done.3 = bf16[4,256,512]{2,1,0:T(8,128)(2,1)S(1)} async-done(((bf16[4,256,512]{2,1,0:T(8,128)(2,1)}), bf16[4,256,512]{2,1,0:T(8,128)(2,1)S(1)}, u32[]{:S(2)}, u32[]{:S(2)}) %all-to-all-start.3) | async-done | bytes 1048608 | tf_op jit(solution)/shard_map/all_to_all | solution.py:369
  573.8 26.3 %attn_bwd.2 = bf16[3,256,2048]{2,1,0:T(8,128)(2,1)} custom-call(s32[4]{0:T(128)} %get-tuple-element.123.lo_ref, bf16[768,2048]{1,0:T(8,128)(2,1)} %pad_maximum_fusion.1.q_ref.k_ref.v_ref, bf16[768,2048]{1,0:T(8,128)(2,1)} %pad_maximum_fusion.1.q_ref.k_ref.v_ref, bf16[768,2048]{1,0:T(8,128)(2,1)} %pad_maximum_fusion.1.q_ref.k_ref.v_ref, ...), custom_call_target="tpu_custom_call" | custom-call | flops 10737418240 | bytes 10485760 | tf_op jit(solution)/shard_map/attn_bwd/pallas_call | solution.py:140
  600.2 5.9 convolution_convert_fusion.3
  608.2 26.3 %attn_bwd.3 = bf16[3,256,2048]{2,1,0:T(8,128)(2,1)} custom-call(s32[4]{0:T(128)} %get-tuple-element.122.lo_ref, bf16[768,2048]{1,0:T(8,128)(2,1)} %pad_maximum_fusion.2.q_ref.k_ref.v_ref, bf16[768,2048]{1,0:T(8,128)(2,1)} %pad_maximum_fusion.2.q_ref.k_ref.v_ref, bf16[768,2048]{1,0:T(8,128)(2,1)} %pad_maximum_fusion.2.q_ref.k_ref.v_ref, ...), custom_call_target="tpu_custom_call" | custom-call | flops 10737418240 | bytes 10485760 | tf_op jit(solution)/shard_map/attn_bwd/pallas_call | solution.py:140
  634.5 8.9 %fusion.14 = (f32[1024]{0:T(1024)S(1)}, bf16[2048,1024]{1,0:T(8,128)(2,1)}) fusion(f32[2048]{0:T(1024)S(1)} %copy-done.38, bf16[3584,1024]{1,0:T(8,128)(2,1)} %copy-done.12, s32[]{:T(128)S(6)} %select_n.131, bf16[768,2048]{1,0:T(8,128)(2,1)} %bitcast.261, bf16[1024,768]{1,0:T(8,128)(2,1)S(1)} %bitcast.227), kind=kOutput, calls=%fused_computation.24 | convolution fusion | flops 3233807360 | bytes 13119492 | tf_op jit(solution)/shard_map/dot_general | solution.py:161
  644.1 14.3 %all-to-all-start.5 = ((f32[32,32,2]{1,2,0:T(2,128)}), f32[32,32,2]{1,2,0:T(2,128)S(1)}, u32[]{:S(2)}, u32[]{:S(2)}) async-start(f32[32,32,2]{1,2,0:T(2,128)} %copy.53), calls=%async_computation.12 | async-start | bytes 65536 | tf_op jit(solution)/shard_map/all_to_all | solution.py:263
  661.3 5.0 collective-permute-start.12
  672.3 6.2 fusion.57
  682.2 6.6 collective-permute-done.12
  688.8 28.8 %collective-permute-start.19 = (bf16[512,1024]{1,0:T(8,128)(2,1)}, bf16[512,1024]{1,0:T(8,128)(2,1)}, u32[]{:S(2)}, u32[]{:S(2)}) collective-permute-start(bf16[512,1024]{1,0:T(8,128)(2,1)} %get-tuple-element.79), channel_id=1, source_target_pairs={{0,2},{4,6},{8,10},{12,14},{16,18},{20,22},{24,26},{28,30}} | collective-permute-start | bytes 3145736 | tf_op jit(solution)/shard_map/ppermute | solution.py:245
  720.9 5.6 add_convert_fusion.1
  728.4 5.4 add_convert_fusion.5
  737.5 18.9 %collective-permute-done.19 = bf16[512,1024]{1,0:T(8,128)(2,1)} collective-permute-done((bf16[512,1024]{1,0:T(8,128)(2,1)}, bf16[512,1024]{1,0:T(8,128)(2,1)}, u32[]{:S(2)}, u32[]{:S(2)}) %collective-permute-start.19) | collective-permute-done | bytes 1048608 | tf_op jit(solution)/shard_map/ppermute | solution.py:245
  756.4 4.7 add_convert_fusion.3
  761.1 13.3 %collective-permute-start.20 = (bf16[512,1024]{1,0:T(8,128)(2,1)}, bf16[512,1024]{1,0:T(8,128)(2,1)}, u32[]{:S(2)}, u32[]{:S(2)}) collective-permute-start(bf16[512,1024]{1,0:T(8,128)(2,1)} %get-tuple-element.74), channel_id=1, source_target_pairs={{0,1},{1,2},{2,3},{4,5},{5,6},{6,7},{8,9},{9,10},{10,11},{12,13},{... | collective-permute-start | bytes 3145736 | tf_op jit(solution)/shard_map/ppermute | solution.py:251
  782.0 11.5 %add_convert_fusion = bf16[1024,1024]{1,0:T(8,128)(2,1)} fusion(f32[1024,1024]{1,0:T(8,128)} %copy-done.8, bf16[1024,2816]{1,0:T(8,128)(2,1)} %get-tuple-element.63, bf16[352,8,8,128]{3,2,1,0:T(8,128)(2,1)} %bitcast.194), kind=kOutput, calls=%fused_computation.60 | convolution fusion | flops 5907677184 | bytes 17825792 | tf_op jit(solution)/shard_map/dot_general | solution.py:161
  794.0 8.7 all-to-all-done.4
  808.5 7.8 collective-permute-done.20
  824.6 5.4 fusion.38
  833.2 9.5 %reduce-scatter.21.cloned.1.call-done = bf16[1,128,704]{1,2,0:T(8,128)(2,1)} async-done(((bf16[4,128,704]{1,2,0:T(8,128)(2,1)}), bf16[1,128,704]{1,2,0:T(8,128)(2,1)}) %reduce-scatter.21.cloned.1.call-update) | async-done | bytes 180240 | tf_op jit(solution)/shard_map/reduce_scatter | solution.py:206
  844.4 22.7 %reduce-scatter.17.cloned.1.call-done = bf16[1,128,704]{1,2,0:T(8,128)(2,1)} async-done(((bf16[4,128,704]{1,2,0:T(8,128)(2,1)}), bf16[1,128,704]{1,2,0:T(8,128)(2,1)}) %reduce-scatter.17.cloned.1.call-update) | async-done | bytes 180240 | tf_op jit(solution)/shard_map/reduce_scatter | solution.py:206
  (274 shorter events, 160.4 us)
Async XLA Ops:
  7.2 111.2 %all-gather.11.cloned.1.call-start = ((), (), s32[]{:S(2)}) async-start(), calls=%async_computation.21 | async-start | bytes 1990656 | tf_op jit(solution)/shard_map/all_gather | solution.py:290
  10.0 27.8 %collective-permute-start = (bf16[512,1024]{1,0:T(8,128)(2,1)}, bf16[512,1024]{1,0:T(8,128)(2,1)}, u32[]{:S(2)}, u32[]{:S(2)}) collective-permute-start(bf16[512,1024]{1,0:T(8,128)(2,1)} %get-tuple-element.91), channel_id=1, source_target_pairs={{0,1},{1,2},{2,3},{4,5},{5,6},{6,7},{8,9},{9,10},{10,11},{12,13},{... | collective-permute-start | bytes 3145736 | tf_op jit(solution)/shard_map/ppermute | solution.py:219
  17.9 275.7 %all-gather.13.cloned.1.call-start = ((), (), s32[]{:S(2)}) async-start(), calls=%async_computation.22 | async-start | bytes 2162688 | tf_op jit(solution)/shard_map/all_gather | solution.py:303
  17.9 26.8 %collective-permute-start.3 = (bf16[512,1024]{1,0:T(8,128)(2,1)}, bf16[512,1024]{1,0:T(8,128)(2,1)}, u32[]{:S(2)}, u32[]{:S(2)}) collective-permute-start(bf16[512,1024]{1,0:T(8,128)(2,1)} %get-tuple-element.91), channel_id=1, source_target_pairs={{1,0},{2,1},{3,2},{5,4},{6,5},{7,6},{9,8},{10,9},{11,10},{13,12},{... | collective-permute-start | bytes 3145736 | tf_op jit(solution)/shard_map/ppermute | solution.py:220
  37.8 9.6 %collective-permute-start.1 = (bf16[512,1024]{1,0:T(8,128)(2,1)}, bf16[512,1024]{1,0:T(8,128)(2,1)}, u32[]{:S(2)}, u32[]{:S(2)}) collective-permute-start(bf16[512,1024]{1,0:T(8,128)(2,1)} %collective-permute-done), channel_id=1, source_target_pairs={{1,3},{5,7},{9,11},{13,15},{17,19},{21,23},{25,27},{29,31}} | collective-permute-start | bytes 3145736 | tf_op jit(solution)/shard_map/ppermute | solution.py:224
  39.5 9.2 %collective-permute-start.2 = (bf16[512,1024]{1,0:T(8,128)(2,1)}, bf16[512,1024]{1,0:T(8,128)(2,1)}, u32[]{:S(2)}, u32[]{:S(2)}) collective-permute-start(bf16[512,1024]{1,0:T(8,128)(2,1)} %collective-permute-done), channel_id=1, source_target_pairs={{1,2},{2,3},{5,6},{6,7},{9,10},{10,11},{13,14},{14,15},{17,18},{18... | collective-permute-start | bytes 3145736 | tf_op jit(solution)/shard_map/ppermute | solution.py:222
  44.7 28.6 %collective-permute-start.4 = (bf16[512,1024]{1,0:T(8,128)(2,1)}, bf16[512,1024]{1,0:T(8,128)(2,1)}, u32[]{:S(2)}, u32[]{:S(2)}) collective-permute-start(bf16[512,1024]{1,0:T(8,128)(2,1)} %collective-permute-done.3), channel_id=1, source_target_pairs={{1,0},{2,1},{5,4},{6,5},{9,8},{10,9},{13,12},{14,13},{17,16},{18,1... | collective-permute-start | bytes 3145736 | tf_op jit(solution)/shard_map/ppermute | solution.py:223
  46.0 49.9 %collective-permute-start.5 = (bf16[512,1024]{1,0:T(8,128)(2,1)}, bf16[512,1024]{1,0:T(8,128)(2,1)}, u32[]{:S(2)}, u32[]{:S(2)}) collective-permute-start(bf16[512,1024]{1,0:T(8,128)(2,1)} %collective-permute-done.3), channel_id=1, source_target_pairs={{2,0},{6,4},{10,8},{14,12},{18,16},{22,20},{26,24},{30,28}} | collective-permute-start | bytes 3145736 | tf_op jit(solution)/shard_map/ppermute | solution.py:225
  99.7 239.8 %all-gather.15.cloned.1.call-start = ((), (), s32[]{:S(2)}) async-start(), calls=%async_computation.23 | async-start | bytes 5947392 | tf_op jit(solution)/shard_map/all_gather | solution.py:303
  100.4 248.0 %all-gather.19.cloned.1.call-start = ((), (), s32[]{:S(2)}) async-start(), calls=%async_computation.25 | async-start | bytes 5947392 | tf_op jit(solution)/shard_map/all_gather | solution.py:303
  101.0 305.6 %all-gather.17.cloned.1.call-start = ((), (), s32[]{:S(2)}) async-start(), calls=%async_computation.24 | async-start | bytes 5947392 | tf_op jit(solution)/shard_map/all_gather | solution.py:303
  111.8 149.3 %copy-start.23 = (f32[32,2048]{1,0:T(8,128)}, f32[32,2048]{1,0:T(8,128)S(1)}, u32[]{:S(2)}) copy-start(f32[32,2048]{1,0:T(8,128)S(1)} %get-tuple-element.103.cos_ref) | copy-start | bytes 786436
  111.8 41.7 %collective-permute-start.6 = (bf16[512,1024]{1,0:T(8,128)(2,1)S(1)}, bf16[512,1024]{1,0:T(8,128)(2,1)}, u32[]{:S(2)}, u32[]{:S(2)}) collective-permute-start(bf16[512,1024]{1,0:T(8,128)(2,1)S(1)} %get-tuple-element.31), channel_id=1, source_target_pairs={{0,1},{1,2},{2,3},{4,5},{5,6},{6,7},{8,9},{9,10},{10,11},{12,13},{... | collective-permute-start | bytes 3145736 | tf_op jit(solution)/shard_map/ppermute | solution.py:219
  114.0 39.4 %collective-permute-start.7 = (bf16[512,1024]{1,0:T(8,128)(2,1)S(1)}, bf16[512,1024]{1,0:T(8,128)(2,1)}, u32[]{:S(2)}, u32[]{:S(2)}) collective-permute-start(bf16[512,1024]{1,0:T(8,128)(2,1)S(1)} %get-tuple-element.31), channel_id=1, source_target_pairs={{1,0},{2,1},{3,2},{5,4},{6,5},{7,6},{9,8},{10,9},{11,10},{13,12},{... | collective-permute-start | bytes 3145736 | tf_op jit(solution)/shard_map/ppermute | solution.py:220
  120.9 133.6 %copy-start.31 = (f32[8,1,128]{2,1,0:T(1,128)}, f32[8,1,128]{2,1,0:T(1,128)S(1)}, u32[]{:S(2)}) copy-start(f32[8,1,128]{2,1,0:T(1,128)S(1)} %get-tuple-element.100) | copy-start | bytes 12292
  153.5 20.8 %collective-permute-start.8 = (bf16[512,1024]{1,0:T(8,128)(2,1)}, bf16[512,1024]{1,0:T(8,128)(2,1)}, u32[]{:S(2)}, u32[]{:S(2)}) collective-permute-start(bf16[512,1024]{1,0:T(8,128)(2,1)} %collective-permute-done.6), channel_id=1, source_target_pairs={{1,3},{5,7},{9,11},{13,15},{17,19},{21,23},{25,27},{29,31}} | collective-permute-start | bytes 3145736 | tf_op jit(solution)/shard_map/ppermute | solution.py:224
  155.1 20.5 %collective-permute-start.9 = (bf16[512,1024]{1,0:T(8,128)(2,1)}, bf16[512,1024]{1,0:T(8,128)(2,1)}, u32[]{:S(2)}, u32[]{:S(2)}) collective-permute-start(bf16[512,1024]{1,0:T(8,128)(2,1)} %collective-permute-done.6), channel_id=1, source_target_pairs={{1,2},{2,3},{5,6},{6,7},{9,10},{10,11},{13,14},{14,15},{17,18},{18... | collective-permute-start | bytes 3145736 | tf_op jit(solution)/shard_map/ppermute | solution.py:222
  156.8 42.7 %collective-permute-start.10 = (bf16[512,1024]{1,0:T(8,128)(2,1)}, bf16[512,1024]{1,0:T(8,128)(2,1)}, u32[]{:S(2)}, u32[]{:S(2)}) collective-permute-start(bf16[512,1024]{1,0:T(8,128)(2,1)} %collective-permute-done.7), channel_id=1, source_target_pairs={{1,0},{2,1},{5,4},{6,5},{9,8},{10,9},{13,12},{14,13},{17,16},{18,1... | collective-permute-start | bytes 3145736 | tf_op jit(solution)/shard_map/ppermute | solution.py:223
  158.1 94.3 %collective-permute-start.11 = (bf16[512,1024]{1,0:T(8,128)(2,1)}, bf16[512,1024]{1,0:T(8,128)(2,1)}, u32[]{:S(2)}, u32[]{:S(2)}) collective-permute-start(bf16[512,1024]{1,0:T(8,128)(2,1)} %collective-permute-done.7), channel_id=1, source_target_pairs={{2,0},{6,4},{10,8},{14,12},{18,16},{22,20},{26,24},{30,28}} | collective-permute-start | bytes 3145736 | tf_op jit(solution)/shard_map/ppermute | solution.py:225
  161.7 127.9 %all-to-all-start = ((bf16[256,4,512]{2,0,1:T(8,128)(2,1)}), bf16[256,4,512]{2,0,1:T(8,128)(2,1)}, u32[]{:S(2)}, u32[]{:S(2)}) async-start(bf16[256,4,512]{2,0,1:T(8,128)(2,1)} %bitcast.188), calls=%async_computation | async-start | bytes 2097152 | tf_op jit(solution)/shard_map/all_to_all | solution.py:335
  179.6 77.1 %copy-start.21 = (bf16[8,128,768]{2,1,0:T(8,128)(2,1)S(1)}, bf16[8,128,768]{2,1,0:T(8,128)(2,1)}, u32[]{:S(2)}) copy-start(bf16[8,128,768]{2,1,0:T(8,128)(2,1)} %copy-done.20) | copy-start | bytes 4718596
  289.6 41.6 %all-to-all-start.1 = ((bf16[256,4,512]{2,0,1:T(8,128)(2,1)}), bf16[256,4,512]{2,0,1:T(8,128)(2,1)S(1)}, u32[]{:S(2)}, u32[]{:S(2)}) async-start(bf16[256,4,512]{2,0,1:T(8,128)(2,1)} %bitcast.187), calls=%async_computation.1 | async-start | bytes 2097152 | tf_op jit(solution)/shard_map/all_to_all | solution.py:335
  348.4 67.2 %slice-start.2 = ((s8[5767168]{0:T(1024)(128)(4,1)}), s8[1572864]{0:T(1024)(128)(4,1)S(1)}, s32[]{:S(2)}) async-start(s8[5767168]{0:T(1024)(128)(4,1)} %bitcast.202), calls=%async_computation.29 | async-start | bytes 3145728
  502.5 29.9 %all-to-all-start.2 = ((bf16[4,256,512]{2,1,0:T(8,128)(2,1)}), bf16[4,256,512]{2,1,0:T(8,128)(2,1)S(1)}, u32[]{:S(2)}, u32[]{:S(2)}) async-start(bf16[4,256,512]{2,1,0:T(8,128)(2,1)} %bitcast.37), calls=%async_computation.2 | async-start | bytes 2097152 | tf_op jit(solution)/shard_map/all_to_all | solution.py:369
  506.0 220.5 %reduce-scatter.11.cloned.1.call-start = ((), (), s32[]{:S(2)}) async-start(), calls=%async_computation.14 | async-start | bytes 2359296 | tf_op jit(solution)/shard_map/reduce_scatter | solution.py:206
  533.5 242.2 %reduce-scatter.25.cloned.1.call-start = ((), (), s32[]{:S(2)}) async-start(), calls=%async_computation.26 | async-start | bytes 6488064
  541.9 261.7 %reduce-scatter.19.cloned.1.call-start = ((), (), s32[]{:S(2)}) async-start(), calls=%async_computation.18 | async-start | bytes 6488064 | tf_op jit(solution)/shard_map/reduce_scatter | solution.py:206
  542.7 279.6 %reduce-scatter.15.cloned.1.call-start = ((), (), s32[]{:S(2)}) async-start(), calls=%async_computation.16 | async-start | bytes 6488064 | tf_op jit(solution)/shard_map/reduce_scatter | solution.py:206
  543.4 29.3 %all-to-all-start.3 = ((bf16[4,256,512]{2,1,0:T(8,128)(2,1)}), bf16[4,256,512]{2,1,0:T(8,128)(2,1)S(1)}, u32[]{:S(2)}, u32[]{:S(2)}) async-start(bf16[4,256,512]{2,1,0:T(8,128)(2,1)} %bitcast.41), calls=%async_computation.3 | async-start | bytes 2097152 | tf_op jit(solution)/shard_map/all_to_all | solution.py:369
  644.1 133.9 %all-to-all-start.5 = ((f32[32,32,2]{1,2,0:T(2,128)}), f32[32,32,2]{1,2,0:T(2,128)S(1)}, u32[]{:S(2)}, u32[]{:S(2)}) async-start(f32[32,32,2]{1,2,0:T(2,128)} %copy.53), calls=%async_computation.12 | async-start | bytes 65536 | tf_op jit(solution)/shard_map/all_to_all | solution.py:263
  658.4 171.6 %reduce-scatter.13.cloned.1.call-start = ((), (), s32[]{:S(2)}) async-start(), calls=%async_computation.15 | async-start | bytes 327680 | tf_op jit(solution)/shard_map/reduce_scatter | solution.py:206
  658.5 62.4 %slice-start.4 = ((s8[7340032]{0:T(1024)(128)(4,1)}), s8[4194304]{0:T(1024)(128)(4,1)S(1)}, s32[]{:S(2)}) async-start(s8[7340032]{0:T(1024)(128)(4,1)} %bitcast.213), calls=%async_computation.31 | async-start | bytes 8388608
  661.3 27.5 %collective-permute-start.12 = (bf16[512,1024]{1,0:T(8,128)(2,1)S(1)}, bf16[512,1024]{1,0:T(8,128)(2,1)}, u32[]{:S(2)}, u32[]{:S(2)}) collective-permute-start(bf16[512,1024]{1,0:T(8,128)(2,1)S(1)} %get-tuple-element.70), channel_id=1, source_target_pairs={{0,1},{1,2},{4,5},{5,6},{8,9},{9,10},{12,13},{13,14},{16,17},{17,1... | collective-permute-start | bytes 3145736 | tf_op jit(solution)/shard_map/ppermute | solution.py:243
  666.3 51.3 %collective-permute-start.13 = (bf16[512,1024]{1,0:T(8,128)(2,1)S(1)}, bf16[512,1024]{1,0:T(8,128)(2,1)}, u32[]{:S(2)}, u32[]{:S(2)}) collective-permute-start(bf16[512,1024]{1,0:T(8,128)(2,1)S(1)} %get-tuple-element.73), channel_id=1, source_target_pairs={{0,2},{4,6},{8,10},{12,14},{16,18},{20,22},{24,26},{28,30}} | collective-permute-start | bytes 3145736 | tf_op jit(solution)/shard_map/ppermute | solution.py:245
  668.6 50.7 %collective-permute-start.15 = (bf16[512,1024]{1,0:T(8,128)(2,1)S(1)}, bf16[512,1024]{1,0:T(8,128)(2,1)}, u32[]{:S(2)}, u32[]{:S(2)}) collective-permute-start(bf16[512,1024]{1,0:T(8,128)(2,1)S(1)} %get-tuple-element.72), channel_id=1, source_target_pairs={{3,2},{2,1},{7,6},{6,5},{11,10},{10,9},{15,14},{14,13},{19,18},{18... | collective-permute-start | bytes 3145736 | tf_op jit(solution)/shard_map/ppermute | solution.py:244
  670.3 58.1 %collective-permute-start.16 = (bf16[512,1024]{1,0:T(8,128)(2,1)S(1)}, bf16[512,1024]{1,0:T(8,128)(2,1)}, u32[]{:S(2)}, u32[]{:S(2)}) collective-permute-start(bf16[512,1024]{1,0:T(8,128)(2,1)S(1)} %get-tuple-element.71), channel_id=1, source_target_pairs={{3,1},{7,5},{11,9},{15,13},{19,17},{23,21},{27,25},{31,29}} | collective-permute-start | bytes 3145736 | tf_op jit(solution)/shard_map/ppermute | solution.py:246
  680.7 55.5 %collective-permute-start.18 = (bf16[512,1024]{1,0:T(8,128)(2,1)}, bf16[512,1024]{1,0:T(8,128)(2,1)S(1)}, u32[]{:S(2)}, u32[]{:S(2)}) collective-permute-start(bf16[512,1024]{1,0:T(8,128)(2,1)} %get-tuple-element.76), channel_id=1, source_target_pairs={{0,1},{1,2},{4,5},{5,6},{8,9},{9,10},{12,13},{13,14},{16,17},{17,1... | collective-permute-start | bytes 3145736 | tf_op jit(solution)/shard_map/ppermute | solution.py:243
  688.8 67.6 %collective-permute-start.19 = (bf16[512,1024]{1,0:T(8,128)(2,1)}, bf16[512,1024]{1,0:T(8,128)(2,1)}, u32[]{:S(2)}, u32[]{:S(2)}) collective-permute-start(bf16[512,1024]{1,0:T(8,128)(2,1)} %get-tuple-element.79), channel_id=1, source_target_pairs={{0,2},{4,6},{8,10},{12,14},{16,18},{20,22},{24,26},{28,30}} | collective-permute-start | bytes 3145736 | tf_op jit(solution)/shard_map/ppermute | solution.py:245
  717.6 38.8 %collective-permute-start.21 = (bf16[512,1024]{1,0:T(8,128)(2,1)}, bf16[512,1024]{1,0:T(8,128)(2,1)}, u32[]{:S(2)}, u32[]{:S(2)}) collective-permute-start(bf16[512,1024]{1,0:T(8,128)(2,1)} %get-tuple-element.78), channel_id=1, source_target_pairs={{3,2},{2,1},{7,6},{6,5},{11,10},{10,9},{15,14},{14,13},{19,18},{18... | collective-permute-start | bytes 3145736 | tf_op jit(solution)/shard_map/ppermute | solution.py:244
  719.3 37.1 %collective-permute-start.22 = (bf16[512,1024]{1,0:T(8,128)(2,1)}, bf16[512,1024]{1,0:T(8,128)(2,1)}, u32[]{:S(2)}, u32[]{:S(2)}) collective-permute-start(bf16[512,1024]{1,0:T(8,128)(2,1)} %get-tuple-element.77), channel_id=1, source_target_pairs={{3,1},{7,5},{11,9},{15,13},{19,17},{23,21},{27,25},{31,29}} | collective-permute-start | bytes 3145736 | tf_op jit(solution)/shard_map/ppermute | solution.py:246
  728.4 103.2 %reduce-scatter.23.cloned.1.call-start = ((), (), s32[]{:S(2)}) async-start(), calls=%async_computation.20 | async-start | bytes 901120 | tf_op jit(solution)/shard_map/reduce_scatter | solution.py:206
  733.9 72.1 %collective-permute-start.14 = (bf16[512,1024]{1,0:T(8,128)(2,1)}, bf16[512,1024]{1,0:T(8,128)(2,1)}, u32[]{:S(2)}, u32[]{:S(2)}) collective-permute-start(bf16[512,1024]{1,0:T(8,128)(2,1)} %get-tuple-element.68), channel_id=1, source_target_pairs={{0,1},{1,2},{2,3},{4,5},{5,6},{6,7},{8,9},{9,10},{10,11},{12,13},{... | collective-permute-start | bytes 3145736 | tf_op jit(solution)/shard_map/ppermute | solution.py:251
  736.2 69.8 %collective-permute-start.17 = (bf16[512,1024]{1,0:T(8,128)(2,1)S(1)}, bf16[512,1024]{1,0:T(8,128)(2,1)}, u32[]{:S(2)}, u32[]{:S(2)}) collective-permute-start(bf16[512,1024]{1,0:T(8,128)(2,1)S(1)} %get-tuple-element.69), channel_id=1, source_target_pairs={{1,0},{2,1},{3,2},{5,4},{6,5},{7,6},{9,8},{10,9},{11,10},{13,12},{... | collective-permute-start | bytes 3145736 | tf_op jit(solution)/shard_map/ppermute | solution.py:254
  761.1 55.2 %collective-permute-start.20 = (bf16[512,1024]{1,0:T(8,128)(2,1)}, bf16[512,1024]{1,0:T(8,128)(2,1)}, u32[]{:S(2)}, u32[]{:S(2)}) collective-permute-start(bf16[512,1024]{1,0:T(8,128)(2,1)} %get-tuple-element.74), channel_id=1, source_target_pairs={{0,1},{1,2},{2,3},{4,5},{5,6},{6,7},{8,9},{9,10},{10,11},{12,13},{... | collective-permute-start | bytes 3145736 | tf_op jit(solution)/shard_map/ppermute | solution.py:251
  774.4 41.9 %collective-permute-start.23 = (bf16[512,1024]{1,0:T(8,128)(2,1)}, bf16[512,1024]{1,0:T(8,128)(2,1)}, u32[]{:S(2)}, u32[]{:S(2)}) collective-permute-start(bf16[512,1024]{1,0:T(8,128)(2,1)} %get-tuple-element.75), channel_id=1, source_target_pairs={{1,0},{2,1},{3,2},{5,4},{6,5},{7,6},{9,8},{10,9},{11,10},{13,12},{... | collective-permute-start | bytes 3145736 | tf_op jit(solution)/shard_map/ppermute | solution.py:254
  778.0 24.7 %all-to-all-start.4 = ((bf16[8,128,768]{2,1,0:T(8,128)(2,1)}), bf16[8,128,768]{2,1,0:T(8,128)(2,1)S(1)}, u32[]{:S(2)}, u32[]{:S(2)}) async-start(bf16[8,128,768]{2,1,0:T(8,128)(2,1)} %bitcast.46), calls=%async_computation.4 | async-start | bytes 3145728 | tf_op jit(solution)/shard_map/all_to_all | solution.py:263
  781.7 61.0 %reduce-scatter.21.cloned.1.call-start = ((), (), s32[]{:S(2)}) async-start(), calls=%async_computation.19 | async-start | bytes 901120 | tf_op jit(solution)/shard_map/reduce_scatter | solution.py:206
  805.9 61.1 %reduce-scatter.17.cloned.1.call-start = ((), (), s32[]{:S(2)}) async-start(), calls=%async_computation.17 | async-start | bytes 901120 | tf_op jit(solution)/shard_map/reduce_scatter | solution.py:206
  (44 other events, 505.1 us)
Sparse Core Ops, SparseCore 0:
  18.0 25.6 all-gather.10
  99.8 55.7 all-gather.12
  158.4 93.6 all-gather.14
  254.8 77.3 all-gather.18
  334.9 71.6 all-gather.16
  533.6 39.2 reduce-scatter.10
  576.4 59.0 reduce-scatter.24
  638.9 59.0 reduce-scatter.18
  701.4 58.9 reduce-scatter.14
  763.1 21.2 reduce-scatter.12
  786.6 31.7 reduce-scatter.22
  820.6 22.0 reduce-scatter.20
  845.0 21.9 reduce-scatter.16
where the time goes:
time: 886 us; the launch traced here: 876 us
  waiting for transfers between devices  325 us (37%)
  matrix products  156 us (18%)
  starting transfers between devices  128 us (14%)
  local copies, waits for them, and re-layouts  98 us (11%)
  Pallas kernels  97.6 us (11%)
  other arithmetic  50.5 us (6%)
  between operations  20.6 us (2%)
    dot_general x18, matrix products, dot_dims(): lax.dot_general(left, right, (((left_dim,), (right_dim,)), ((), ())), pre...  156 us
    ppermute x2, waiting for transfers between devices, line_gather(): three_right = lax.ppermute(one_right, axis, [(2, 0)])  72.8 us
    pallas_call x2, Pallas kernels, attn_bwd(): pl.pallas_call(functools.partial(attn_bwd_kernel, bq=bq, bk=bk, heads=hps...  52.6 us
    all_gather x4, waiting for transfers between devices, whole(): every = lax.all_gather(piece, ('dp', 'mp'), axis=0, tiled=False)  49 us
    pallas_call x2, Pallas kernels, attn_fwd(): pl.pallas_call(functools.partial(attn_fwd_kernel, bq=bq, bk=bk, heads=hps...  45 us
    ppermute x2, waiting for transfers between devices, line_gather(): two_right = lax.ppermute(one_right, axis, [(1, 0), (2, 1)])  40.6 us
    unnamed x118, local copies, waits for them, and re-layouts  34.5 us
    all_to_all x2, waiting for transfers between devices, local(): lax.all_to_all(mixed[m], 'mp', split_axis=1, concat_axis=0, tiled=True)  33.4 us
  transfers between devices with their start and end apart: 43, of which 16 were waited for; matrix products, arithmetic and copies ran while one was open for 22% of the time, Pallas kernels for 11%

commit v1 on v0

--- a/solution.py
+++ b/solution.py
@@ -257,6 +257,36 @@
     return total(block(0), right, left)
 
 
+def plane_gather(piece, axis):
+    core, across, along = ([(i, i ^ bit) for i in range(8)] for bit in (1, 2, 4))
+    half = piece.shape[0] // 2
+    top, low = piece[:half], piece[half:]
+
+    def partner(part):
+        return lax.ppermute(part, axis, core)
+
+    top_x, low_y = lax.ppermute(top, axis, across), lax.ppermute(low, axis, along)
+    top_y, low_x = lax.ppermute(top, axis, along), lax.ppermute(low, axis, across)
+    top_xy, low_xy = lax.ppermute(top_x, axis, along), lax.ppermute(low_y, axis, across)
+    held = [(top, low), (top_x, low_x), (top_y, low_y), (top_xy, low_xy)]
+    parts = []
+    for pair in held:
+        parts += [pair, tuple(partner(part) for part in pair)]
+
+    def ordered(me):
+        def branch(*flat):
+            lanes = [
+                jnp.concatenate([flat[2 * (i ^ me)], flat[2 * (i ^ me) + 1]], axis=0)
+                for i in range(8)
+            ]
+            return jnp.concatenate(lanes, axis=1)
+
+        return branch
+
+    flat = [part for pair in parts for part in pair]
+    return lax.switch(lax.axis_index(axis), [ordered(me) for me in range(8)], *flat)
+
+
 def exchange_sum(partial_sum, axis):
     count = lax.axis_size(axis)
     parts = partial_sum.reshape((count, partial_sum.shape[0] // count) + partial_sum.shape[1:])
@@ -273,6 +303,7 @@
     batches, tokens, width = inputs.shape
     cols = w_query.shape[1]
     depth = w_query.shape[0]
+    hidden_part = w_gate.shape[1]
 
     def split16(gain):
         high = gain.astype(low)
@@ -293,20 +324,24 @@
     gain_one = (gains[:, 0] + gains[:, 1]).reshape(width)
     gain_two = (gains[:, 2] + gains[:, 3]).reshape(width)
 
+    rest_piece = jnp.concatenate([w_output, w_gate.T, w_up.T, w_down], axis=0)
+    sizes = (cols, hidden_part, hidden_part, hidden_part)
+    firsts = (0, cols, cols + hidden_part, cols + 2 * hidden_part)
+    if n_dp == 8:
+        rest_every = plane_gather(line_gather(rest_piece, "mp"), "dp")
+        rest_every = rest_every.reshape(n_mp, rest_piece.shape[0], width)
+    else:
+        rest_every = lax.all_gather(rest_piece, ("dp", "mp"), axis=0, tiled=False)
+        rest_every = rest_every.reshape((n_dp, n_mp) + rest_piece.shape).transpose(1, 2, 0, 3)
+        rest_every = rest_every.reshape(n_mp, rest_piece.shape[0], width)
+    output_full, gate_full, up_full, down_full = (
+        rest_every[:, first : first + size].reshape(n_mp * size, width)
+        for first, size in zip(firsts, sizes)
+    )
+
     first_rows = line_gather(inputs[0], "mp")
-    first_rows, second_piece, w_output, gate_t, up_t, w_down = lax.optimization_barrier(
-        (first_rows, inputs[1], w_output, w_gate.T, w_up.T, w_down)
-    )
+    first_rows, second_piece = lax.optimization_barrier((first_rows, inputs[1]))
     rows_all = [first_rows, None]
-
-    def whole(piece):
-        every = lax.all_gather(piece, ("dp", "mp"), axis=0, tiled=False)
-        every = every.reshape((n_dp, n_mp) + piece.shape)
-        return every.transpose(1, 2, 0, 3).reshape(n_mp * piece.shape[0], width)
-
-    output_full, gate_full, up_full, down_full = (
-        whole(piece) for piece in (w_output, gate_t, up_t, w_down)
-    )
 
     normed, factors, qkv, tables, starts, lows, mixed, logs = [], [], [], [], [], [], [], []
     for m in range(batches):
@@ -372,11 +407,10 @@
             )
         )
     grad_output = dot_dims(grad_branch, mixed_both, 0, 1).astype(low)
-    grad_mixed_rows[0], grad_down, grad_gate, grad_up, grad_output = lax.optimization_barrier(
-        (grad_mixed_rows[0], grad_down, grad_gate, grad_up, grad_output)
-    )
-
-    mine = [scatter(g, "dp", 0) for g in (grad_down, grad_gate, grad_up, grad_output)]
+
+    every_grad = jnp.concatenate([grad_output, grad_gate, grad_up, grad_down], axis=1)
+    grad_mixed_rows[0], every_grad = lax.optimization_barrier((grad_mixed_rows[0], every_grad))
+    mine = scatter(every_grad, "dp", 0)
 
 
     grad_qkv, grad_normed = [], []
@@ -397,11 +431,15 @@
         )
     grad_w = sum(dot_dims(normed[m], grad_qkv[m], 0, 1) for m in range(batches))
 
-    def owned(part):
-        parts = part.reshape(depth, n_mp, -1).transpose(1, 0, 2)
-        return scatter(parts, "mp", 0)[0].astype(jnp.float32)
-
-    own_down, own_gate, own_up, own_output = (owned(part) for part in mine)
+    own_parts = [
+        mine[:, n_mp * first : n_mp * (first + size)].reshape(depth, n_mp, size)
+        for first, size in zip(firsts, sizes)
+    ]
+    own_rest = jnp.concatenate(own_parts, axis=2).transpose(1, 2, 0)
+    own_rest = line_scatter(own_rest.reshape(-1, depth), "mp")
+    own_output, own_gate, own_up, own_down = (
+        own_rest[first : first + size] for first, size in zip(firsts, sizes)
+    )
     own_qkv = exchange_sum(grad_w.astype(low), "dp")
 
     grad_normed_attn = jnp.concatenate(grad_normed, axis=0)
@@ -414,10 +452,10 @@
         own_qkv[:, :cols],
         own_qkv[:, cols : 2 * cols],
         own_qkv[:, 2 * cols :],
-        own_output.T,
-        own_gate,
-        own_up,
-        own_down.T,
+        own_output,
+        own_gate.T,
+        own_up.T,
+        own_down,
         grad_norms[0],
         grad_norms[1],
     )

time: 886 us -> 929 us (1.049)
  waiting for transfers between devices: 325 us -> 228 us
  starting transfers between devices: 128 us -> 204 us
  other arithmetic: 50.5 us -> 103 us
  loops' own time: 0 us -> 36.4 us
  local copies, waits for them, and re-layouts: 98 us -> 73.4 us
    all_gather x4 -> x0, waiting for transfers between devices: 49 us -> none  [whole(): every = lax.all_gather(piece, ('dp', 'mp'), axis=0, tiled=False)]
    cond x0 -> x7, other arithmetic: none -> 43.1 us
    ppermute x0 -> x14, waiting for transfers between devices: none -> 38.1 us  [the longest x1 23.5 us: plane_gather(): lax.ppermute(top_x, axis, along)]
    another operation x0 -> x1, loops' own time: none -> 36.4 us  [plane_gather(): lax.switch(lax.axis_index(axis), [ordered(me) for me in range(8)], *flat)]
    ppermute x2 -> x3, waiting for transfers between devices: 72.8 us -> 39.6 us  [line_gather(): three_right = lax.ppermute(one_right, axis, [(2, 0)])]
    reshape x5 -> x1, local copies, waits for them, and re-layouts: 33.1 us -> 0.17 us  [local(): mine[:, n_mp * first:n_mp * (first + size)].reshape(depth, n_mp, size)]
    reduce_scatter x7 -> x1, waiting for transfers between devices: 32.1 us -> 0.01 us  [scatter(): lax.psum_scatter(partial_sum, axis, scatter_dimension=dim, tiled=True)]
    ppermute x0 -> x14, starting transfers between devices: none -> 26.8 us  [the longest x1 14.5 us: plane_gather(): lax.ppermute(top, axis, along)]
  transfers between devices with their start and end apart: 43 -> 58, of which waited for: 16 -> 19; matrix products, arithmetic and copies ran while one was open for 22% -> 23% of each run, Pallas kernels for 11% -> 11%
where the time goes in v1:
time: 929 us; the launch traced here: 918 us
  waiting for transfers between devices  228 us (25%)
  starting transfers between devices  204 us (22%)
  matrix products  153 us (16%)
  other arithmetic  103 us (11%)
  Pallas kernels  98.5 us (11%)
  local copies, waits for them, and re-layouts  73.4 us (8%)
  loops' own time  36.4 us (4%)
  between operations  21.1 us (2%)
    dot_general x18, matrix products, dot_dims(): lax.dot_general(left, right, (((left_dim,), (right_dim,)), ((), ())), pre...  153 us
    pallas_call x2, Pallas kernels, attn_bwd(): pl.pallas_call(functools.partial(attn_bwd_kernel, bq=bq, bk=bk, heads=hps...  53.5 us
    pallas_call x2, Pallas kernels, attn_fwd(): pl.pallas_call(functools.partial(attn_fwd_kernel, bq=bq, bk=bk, heads=hps...  45 us
    cond x7, other arithmetic  43.1 us
    ppermute x3, waiting for transfers between devices, line_gather(): three_right = lax.ppermute(one_right, axis, [(2, 0)])  39.6 us
    another operation x1, loops' own time, plane_gather(): lax.switch(lax.axis_index(axis), [ordered(me) for me in range(8)], *flat)  36.4 us
    ppermute x3, starting transfers between devices, line_scatter(): three_right = lax.ppermute(block(3), axis, [(0, 2)])  32.2 us
    all_to_all x2, waiting for transfers between devices, local(): lax.all_to_all(grad_mixed[:, m * tokens:(m + 1) * tokens], 'mp', split_ax...  30.4 us
  transfers between devices with their start and end apart: 58, of which 19 were waited for; matrix products, arithmetic and copies ran while one was open for 23% of the time, Pallas kernels for 11%

profile of v1, /device:TPU:0, one launch (start us, length us, event | category | flops | bytes accessed | tf_op | source)
XLA Modules:
  0.0 917.7 jit_solution(2603202258086505527)
XLA Ops:
  9.3 6.0 collective-permute-start
  32.5 17.2 %collective-permute-done.12 = bf16[2368,128]{1,0:T(8,128)(2,1)S(1)} collective-permute-done((bf16[2368,128]{1,0:T(8,128)(2,1)}, bf16[2368,128]{1,0:T(8,128)(2,1)S(1)}, u32[]{:S(2)}, u32[]{:S(2)}) %collective-permute-start.12) | collective-permute-done | bytes 606240 | tf_op jit(solution)/shard_map/ppermute | solution.py:219
  73.3 27.8 %collective-permute-done.4 = bf16[512,1024]{1,0:T(8,128)(2,1)S(1)} collective-permute-done((bf16[512,1024]{1,0:T(8,128)(2,1)}, bf16[512,1024]{1,0:T(8,128)(2,1)S(1)}, u32[]{:S(2)}, u32[]{:S(2)}) %collective-permute-start.4) | collective-permute-done | bytes 1048608 | tf_op jit(solution)/shard_map/ppermute | solution.py:223
  101.2 24.7 %collective-permute-done.5 = bf16[512,1024]{1,0:T(8,128)(2,1)S(1)} collective-permute-done((bf16[512,1024]{1,0:T(8,128)(2,1)}, bf16[512,1024]{1,0:T(8,128)(2,1)S(1)}, u32[]{:S(2)}, u32[]{:S(2)}) %collective-permute-start.5) | collective-permute-done | bytes 1048608 | tf_op jit(solution)/shard_map/ppermute | solution.py:225
  126.5 6.8 collective-permute-start.6
  148.4 22.4 %attn_fwd.2 = (bf16[256,2048]{1,0:T(8,128)(2,1)}, f32[4,1,2048]{2,1,0:T(1,128)}) custom-call(s32[4]{0:T(128)} %get-tuple-element.1132.lo_ref, bf16[768,2048]{1,0:T(8,128)(2,1)} %pad_maximum_fusion.2.q_ref.k_ref.v_ref, bf16[768,2048]{1,0:T(8,128)(2,1)} %pad_maximum_fusion.2.q_ref.k_ref.v_ref, bf16[768,2048]{1,0:T(8,128)(2,1)} %pad_maximum_fusion.2.q_ref.k_ref.v_ref, ...), custom_call_target="tpu_custom_call" | custom-call | flops 4294967296 | bytes 4194304 | tf_op jit(solution)/shard_map/attn_fwd/pallas_call | solution.py:120
  182.8 8.3 collective-permute-start.25
  192.1 13.0 %all-to-all-start = ((bf16[256,4,512]{2,0,1:T(8,128)(2,1)}), bf16[256,4,512]{2,0,1:T(8,128)(2,1)}, u32[]{:S(2)}, u32[]{:S(2)}) async-start(bf16[256,4,512]{2,0,1:T(8,128)(2,1)} %bitcast.142), calls=%async_computation | async-start | bytes 2097152 | tf_op jit(solution)/shard_map/all_to_all | solution.py:370
  207.3 14.5 %collective-permute-start.24 = (bf16[4736,128]{1,0:T(8,128)(2,1)S(1)}, bf16[4736,128]{1,0:T(8,128)(2,1)}, u32[]{:S(2)}, u32[]{:S(2)}) collective-permute-start(bf16[4736,128]{1,0:T(8,128)(2,1)S(1)} %get-tuple-element.1064), channel_id=1, source_target_pairs={{0,16},{4,20},{8,24},{12,28},{16,0},{20,4},{24,8},{28,12},{1,17},{... | collective-permute-start | bytes 3637256 | tf_op jit(solution)/shard_map/ppermute | solution.py:269
  228.5 14.9 %collective-permute-done.11 = bf16[512,1024]{1,0:T(8,128)(2,1)} collective-permute-done((bf16[512,1024]{1,0:T(8,128)(2,1)}, bf16[512,1024]{1,0:T(8,128)(2,1)}, u32[]{:S(2)}, u32[]{:S(2)}) %collective-permute-start.11) | collective-permute-done | bytes 1048608 | tf_op jit(solution)/shard_map/ppermute | solution.py:225
  245.6 14.1 %collective-permute-done.20 = bf16[4736,128]{1,0:T(8,128)(2,1)S(1)} collective-permute-done((bf16[4736,128]{1,0:T(8,128)(2,1)S(1)}, bf16[4736,128]{1,0:T(8,128)(2,1)S(1)}, u32[]{:S(2)}, u32[]{:S(2)}) %collective-permute-start.20) | collective-permute-done | bytes 1212448 | tf_op jit(solution)/shard_map/ppermute | solution.py:268
  265.4 23.5 %collective-permute-done.28 = bf16[4736,128]{1,0:T(8,128)(2,1)} collective-permute-done((bf16[4736,128]{1,0:T(8,128)(2,1)S(1)}, bf16[4736,128]{1,0:T(8,128)(2,1)}, u32[]{:S(2)}, u32[]{:S(2)}) %collective-permute-start.28) | collective-permute-done | bytes 1212448 | tf_op jit(solution)/shard_map/ppermute | solution.py:270
  292.9 22.5 %attn_fwd.3 = (bf16[256,2048]{1,0:T(8,128)(2,1)}, f32[4,1,2048]{2,1,0:T(1,128)}) custom-call(s32[4]{0:T(128)} %get-tuple-element.1131.lo_ref, bf16[768,2048]{1,0:T(8,128)(2,1)} %pad_maximum_fusion.3.q_ref.k_ref.v_ref, bf16[768,2048]{1,0:T(8,128)(2,1)} %pad_maximum_fusion.3.q_ref.k_ref.v_ref, bf16[768,2048]{1,0:T(8,128)(2,1)} %pad_maximum_fusion.3.q_ref.k_ref.v_ref, ...), custom_call_target="tpu_custom_call" | custom-call | flops 4294967296 | bytes 4194304 | tf_op jit(solution)/shard_map/attn_fwd/pallas_call | solution.py:120
  317.8 83.5 %conditional.1 = (bf16[4,2368,1024]{2,1,0:T(8,128)(2,1)}) conditional(s32[]{:T(128)} %clamp.3, (bf16[4736,128]{1,0:T(8,128)(2,1)S(1)}, bf16[4736,128]{1,0:T(8,128)(2,1)S(1)}, bf16[4736,128]{1,0:T(8,128)(2,1)}, bf16[4736,128]{1,0:T(8,128)(2,1)}, bf16[4736,128]{1,0:T(8,128)(2,1)}, ...), branch_computations={%region_8.9_spmd, %region_9.10_spmd, %region_10.11_spmd, %region_1... | conditional | flops 38797312 | bytes 58196088 | solution.py:287
  318.1 9.7 %maximum_dynamic-update-slice_fusion.7 = bf16[9472,1024]{1,0:T(8,128)(2,1)} fusion(bf16[4736,128]{1,0:T(8,128)(2,1)S(1)} %get-tuple-element.879, bf16[4736,128]{1,0:T(8,128)(2,1)S(1)} %get-tuple-element.878), kind=kLoop, calls=%fused_computation.7 | loop fusion | flops 4849663 | bytes 4849664 | tf_op jit(solution)/shard_map/cond
  327.8 9.5 %maximum_dynamic-update-slice_fusion.6 = bf16[9472,1024]{1,0:T(8,128)(2,1)} fusion(bf16[9472,1024]{1,0:T(8,128)(2,1)} %maximum_dynamic-update-slice_fusion.7, bf16[4736,128]{1,0:T(8,128)(2,1)S(1)} %copy-done.17, bf16[4736,128]{1,0:T(8,128)(2,1)S(1)} %copy-done.9), kind=kLoop, calls=%fused_computation.6 | loop fusion | flops 4849664 | bytes 4849664 | tf_op jit(solution)/shard_map/cond
  343.1 6.3 maximum_dynamic-update-slice_fusion.4
  404.5 13.4 %fusion.48 = (bf16[4,704,1024]{2,1,0:T(8,128)(2,1)}, bf16[4,704,1024]{2,1,0:T(8,128)(2,1)}, bf16[4,704,1024]{2,1,0:T(8,128)(2,1)}) fusion(bf16[4,2368,1024]{2,1,0:T(8,128)(2,1)} %get-tuple-element.1135), kind=kLoop, calls=%fused_computation.257 | loop fusion | bytes 34603008 | tf_op jit(solution)/shard_map/slice | solution.py:338
  417.8 16.6 %all-to-all-start.1 = ((bf16[256,4,512]{2,0,1:T(8,128)(2,1)}), bf16[256,4,512]{2,0,1:T(8,128)(2,1)S(1)}, u32[]{:S(2)}, u32[]{:S(2)}) async-start(bf16[256,4,512]{2,0,1:T(8,128)(2,1)} %bitcast.141), calls=%async_computation.1 | async-start | bytes 2097152 | tf_op jit(solution)/shard_map/all_to_all | solution.py:370
  434.4 12.1 %fusion.56 = f32[2816,1024]{0,1:T(8,128)} fusion(bf16[2816,1024]{1,0:T(8,128)(2,1)} %bitcast.151, bf16[1024,1024]{1,0:T(8,128)(2,1)} %bitcast.175), kind=kOutput, calls=%fused_computation.265 | convolution fusion | flops 5905580032 | bytes 19398656 | tf_op jit(solution)/shard_map/dot_general | solution.py:161
  446.5 7.9 all-to-all-done.1
  461.5 8.9 fusion.55
  470.4 21.8 %fusion.2 = (bf16[1024,2816]{1,0:T(8,128)(2,1)}, bf16[1024,2816]{1,0:T(8,128)(2,1)}, bf16[1024,2816]{1,0:T(8,128)(2,1)}) fusion(f32[2816,1024]{0,1:T(8,128)} %fusion.56, f32[1024,2816]{1,0:T(8,128)} %fusion.55, bf16[1024,1024]{1,0:T(8,128)(2,1)S(1)} %multiply_convert_fusion.1, bf16[2816,1024]{1,0:T(8,128)(2,1)} %bitcast.159), kind=kOutput, calls=%fused_computation.75 | convolution fusion | flops 5948833792 | bytes 48234496 | tf_op jit(solution)/shard_map/dot_general | solution.py:161
  492.3 10.6 %fusion.57 = f32[1024,1024]{1,0:T(8,128)S(1)} fusion(bf16[1024,2816]{1,0:T(8,128)(2,1)} %get-tuple-element.1054, bf16[2816,1024]{1,0:T(8,128)(2,1)} %bitcast.160), kind=kOutput, calls=%fused_computation.266 | convolution fusion | flops 5905580032 | bytes 15728640 | tf_op jit(solution)/shard_map/dot_general | solution.py:161
  502.9 8.3 convolution_convert_fusion
  511.2 8.3 convolution_convert_fusion.1
  519.6 6.7 multiply_reduce_fusion
  528.0 5.8 convolution_convert_fusion.4
  540.4 11.1 %convert_bitcast_fusion = bf16[1024,2816]{1,0:T(8,128)(2,1)} fusion(bf16[1024,2816]{1,0:T(8,128)(2,1)} %get-tuple-element.1055, bf16[1024,1024]{1,0:T(8,128)(2,1)} %bitcast.176), kind=kOutput, calls=%fused_computation.90 | convolution fusion | flops 5908463616 | bytes 13631488 | tf_op jit(solution)/shard_map/dot_general | solution.py:161
  556.5 15.9 %pad_maximum_fusion = bf16[1024,9472]{1,0:T(8,128)(2,1)} fusion(bf16[1024,2816]{1,0:T(8,128)(2,1)} %convert_bitcast_fusion, bf16[1024,2816]{1,0:T(8,128)(2,1)} %convolution_convert_fusion, bf16[1024,2816]{1,0:T(8,128)(2,1)} %convolution_convert_fusion.1, bf16[1024,1024]{1,0:T(8,128)(2,1)S(1)} %copy.45), kind=kLoop, calls=%fused_computation.64 | loop fusion | flops 77594624 | bytes 38797312 | tf_op jit(solution)/shard_map/concatenate | solution.py:411
  572.4 6.4 all-to-all-done.2
  584.0 24.0 %all-to-all-done.3 = bf16[4,256,512]{2,1,0:T(8,128)(2,1)S(1)} async-done(((bf16[4,256,512]{2,1,0:T(8,128)(2,1)}), bf16[4,256,512]{2,1,0:T(8,128)(2,1)S(1)}, u32[]{:S(2)}, u32[]{:S(2)}) %all-to-all-start.3) | async-done | bytes 1048608 | tf_op jit(solution)/shard_map/all_to_all | solution.py:404
  609.1 27.2 %attn_bwd.2 = bf16[3,256,2048]{2,1,0:T(8,128)(2,1)} custom-call(s32[4]{0:T(128)} %get-tuple-element.1132.lo_ref, bf16[768,2048]{1,0:T(8,128)(2,1)} %pad_maximum_fusion.2.q_ref.k_ref.v_ref, bf16[768,2048]{1,0:T(8,128)(2,1)} %pad_maximum_fusion.2.q_ref.k_ref.v_ref, bf16[768,2048]{1,0:T(8,128)(2,1)} %pad_maximum_fusion.2.q_ref.k_ref.v_ref, ...), custom_call_target="tpu_custom_call" | custom-call | flops 10737418240 | bytes 10485760 | tf_op jit(solution)/shard_map/attn_bwd/pallas_call | solution.py:140
  636.3 5.9 convolution_convert_fusion.3
  644.1 26.3 %attn_bwd.3 = bf16[3,256,2048]{2,1,0:T(8,128)(2,1)} custom-call(s32[4]{0:T(128)} %get-tuple-element.1131.lo_ref, bf16[768,2048]{1,0:T(8,128)(2,1)} %pad_maximum_fusion.3.q_ref.k_ref.v_ref, bf16[768,2048]{1,0:T(8,128)(2,1)} %pad_maximum_fusion.3.q_ref.k_ref.v_ref, bf16[768,2048]{1,0:T(8,128)(2,1)} %pad_maximum_fusion.3.q_ref.k_ref.v_ref, ...), custom_call_target="tpu_custom_call" | custom-call | flops 10737418240 | bytes 10485760 | tf_op jit(solution)/shard_map/attn_bwd/pallas_call | solution.py:140
  670.4 8.8 fusion.14
  680.0 22.2 %all-to-all-start.5 = ((f32[32,32,2]{1,2,0:T(2,128)}), f32[32,32,2]{1,2,0:T(2,128)S(1)}, u32[]{:S(2)}, u32[]{:S(2)}) async-start(f32[32,32,2]{1,2,0:T(2,128)} %copy.51), calls=%async_computation.6 | async-start | bytes 65536 | tf_op jit(solution)/shard_map/all_to_all | solution.py:293
  713.0 7.9 fusion.23
  724.5 7.9 collective-permute-done.32
  732.5 27.8 %collective-permute-start.39 = (bf16[512,1024]{1,0:T(8,128)(2,1)S(1)}, bf16[512,1024]{1,0:T(8,128)(2,1)S(1)}, u32[]{:S(2)}, u32[]{:S(2)}) collective-permute-start(bf16[512,1024]{1,0:T(8,128)(2,1)S(1)} %get-tuple-element.1076), channel_id=1, source_target_pairs={{0,2},{4,6},{8,10},{12,14},{16,18},{20,22},{24,26},{28,30}} | collective-permute-start | bytes 3145736 | tf_op jit(solution)/shard_map/ppermute | solution.py:245
  762.8 7.9 add_convert_fusion.1
  778.7 21.2 %collective-permute-done.39 = bf16[512,1024]{1,0:T(8,128)(2,1)S(1)} collective-permute-done((bf16[512,1024]{1,0:T(8,128)(2,1)S(1)}, bf16[512,1024]{1,0:T(8,128)(2,1)S(1)}, u32[]{:S(2)}, u32[]{:S(2)}) %collective-permute-start.39) | collective-permute-done | bytes 1048608 | tf_op jit(solution)/shard_map/ppermute | solution.py:245
  804.0 13.0 %collective-permute-start.40 = (bf16[512,1024]{1,0:T(8,128)(2,1)}, bf16[512,1024]{1,0:T(8,128)(2,1)}, u32[]{:S(2)}, u32[]{:S(2)}) collective-permute-start(bf16[512,1024]{1,0:T(8,128)(2,1)} %get-tuple-element.1071), channel_id=1, source_target_pairs={{0,1},{1,2},{2,3},{4,5},{5,6},{6,7},{8,9},{9,10},{10,11},{12,13},{... | collective-permute-start | bytes 3145736 | tf_op jit(solution)/shard_map/ppermute | solution.py:251
  822.4 11.4 %add_convert_fusion = bf16[1024,1024]{1,0:T(8,128)(2,1)} fusion(f32[1024,1024]{1,0:T(8,128)} %copy-done.47, bf16[1024,2816]{1,0:T(8,128)(2,1)} %get-tuple-element.1055, bf16[2816,1024]{1,0:T(8,128)(2,1)} %bitcast.152), kind=kOutput, calls=%fused_computation.107 | convolution fusion | flops 5907677184 | bytes 17825792 | tf_op jit(solution)/shard_map/dot_general | solution.py:161
  834.3 8.9 all-to-all-done.4
  870.0 9.2 %collective-permute-done.44 = bf16[2368,128]{1,0:T(8,128)(2,1)S(1)} collective-permute-done((bf16[2368,128]{1,0:T(8,128)(2,1)S(1)}, bf16[2368,128]{1,0:T(8,128)(2,1)S(1)}, u32[]{:S(2)}, u32[]{:S(2)}) %collective-permute-start.44) | collective-permute-done | bytes 606240 | tf_op jit(solution)/shard_map/ppermute | solution.py:243
  879.2 8.9 collective-permute-done.45
  888.6 7.7 collective-permute-start.46
  (352 shorter events, 219.2 us)
Async XLA Ops:
  7.3 128.2 %all-gather.3.cloned.1.call-start = ((), (), s32[]{:S(2)}) async-start(), calls=%async_computation.8 | async-start | bytes 1990656 | tf_op jit(solution)/shard_map/all_gather | solution.py:321
  9.3 48.1 %collective-permute-start = (bf16[512,1024]{1,0:T(8,128)(2,1)S(1)}, bf16[512,1024]{1,0:T(8,128)(2,1)}, u32[]{:S(2)}, u32[]{:S(2)}) collective-permute-start(bf16[512,1024]{1,0:T(8,128)(2,1)S(1)} %get-tuple-element.1097), channel_id=1, source_target_pairs={{0,1},{1,2},{2,3},{4,5},{5,6},{6,7},{8,9},{9,10},{10,11},{12,13},{... | collective-permute-start | bytes 3145736 | tf_op jit(solution)/shard_map/ppermute | solution.py:219
  15.3 42.8 %collective-permute-start.3 = (bf16[512,1024]{1,0:T(8,128)(2,1)S(1)}, bf16[512,1024]{1,0:T(8,128)(2,1)}, u32[]{:S(2)}, u32[]{:S(2)}) collective-permute-start(bf16[512,1024]{1,0:T(8,128)(2,1)S(1)} %get-tuple-element.1097), channel_id=1, source_target_pairs={{1,0},{2,1},{3,2},{5,4},{6,5},{7,6},{9,8},{10,9},{11,10},{13,12},{... | collective-permute-start | bytes 3145736 | tf_op jit(solution)/shard_map/ppermute | solution.py:220
  17.5 32.2 %collective-permute-start.12 = (bf16[2368,128]{1,0:T(8,128)(2,1)}, bf16[2368,128]{1,0:T(8,128)(2,1)S(1)}, u32[]{:S(2)}, u32[]{:S(2)}) collective-permute-start(bf16[2368,128]{1,0:T(8,128)(2,1)} %pad_maximum_fusion.10), channel_id=1, source_target_pairs={{0,1},{1,2},{2,3},{4,5},{5,6},{6,7},{8,9},{9,10},{10,11},{12,13},{... | collective-permute-start | bytes 1818632 | tf_op jit(solution)/shard_map/ppermute | solution.py:219
  22.1 34.0 %collective-permute-start.15 = (bf16[2368,128]{1,0:T(8,128)(2,1)}, bf16[2368,128]{1,0:T(8,128)(2,1)}, u32[]{:S(2)}, u32[]{:S(2)}) collective-permute-start(bf16[2368,128]{1,0:T(8,128)(2,1)} %pad_maximum_fusion.10), channel_id=1, source_target_pairs={{1,0},{2,1},{3,2},{5,4},{6,5},{7,6},{9,8},{10,9},{11,10},{13,12},{... | collective-permute-start | bytes 1818632 | tf_op jit(solution)/shard_map/ppermute | solution.py:220
  56.1 119.5 %collective-permute-start.16 = (bf16[2368,128]{1,0:T(8,128)(2,1)}, bf16[2368,128]{1,0:T(8,128)(2,1)}, u32[]{:S(2)}, u32[]{:S(2)}) collective-permute-start(bf16[2368,128]{1,0:T(8,128)(2,1)} %collective-permute-done.15), channel_id=1, source_target_pairs={{1,0},{2,1},{5,4},{6,5},{9,8},{10,9},{13,12},{14,13},{17,16},{18,1... | collective-permute-start | bytes 1818632 | tf_op jit(solution)/shard_map/ppermute | solution.py:223
  58.9 42.3 %collective-permute-start.4 = (bf16[512,1024]{1,0:T(8,128)(2,1)}, bf16[512,1024]{1,0:T(8,128)(2,1)S(1)}, u32[]{:S(2)}, u32[]{:S(2)}) collective-permute-start(bf16[512,1024]{1,0:T(8,128)(2,1)} %collective-permute-done.3), channel_id=1, source_target_pairs={{1,0},{2,1},{5,4},{6,5},{9,8},{10,9},{13,12},{14,13},{17,16},{18,1... | collective-permute-start | bytes 3145736 | tf_op jit(solution)/shard_map/ppermute | solution.py:223
  61.3 64.6 %collective-permute-start.5 = (bf16[512,1024]{1,0:T(8,128)(2,1)}, bf16[512,1024]{1,0:T(8,128)(2,1)S(1)}, u32[]{:S(2)}, u32[]{:S(2)}) collective-permute-start(bf16[512,1024]{1,0:T(8,128)(2,1)} %collective-permute-done.3), channel_id=1, source_target_pairs={{2,0},{6,4},{10,8},{14,12},{18,16},{22,20},{26,24},{30,28}} | collective-permute-start | bytes 3145736 | tf_op jit(solution)/shard_map/ppermute | solution.py:225
  69.2 108.4 %collective-permute-start.17 = (bf16[2368,128]{1,0:T(8,128)(2,1)}, bf16[2368,128]{1,0:T(8,128)(2,1)}, u32[]{:S(2)}, u32[]{:S(2)}) collective-permute-start(bf16[2368,128]{1,0:T(8,128)(2,1)} %collective-permute-done.15), channel_id=1, source_target_pairs={{2,0},{6,4},{10,8},{14,12},{18,16},{22,20},{26,24},{30,28}} | collective-permute-start | bytes 1818632 | tf_op jit(solution)/shard_map/ppermute | solution.py:225
  126.5 44.4 %collective-permute-start.6 = (bf16[512,1024]{1,0:T(8,128)(2,1)S(1)}, bf16[512,1024]{1,0:T(8,128)(2,1)}, u32[]{:S(2)}, u32[]{:S(2)}) collective-permute-start(bf16[512,1024]{1,0:T(8,128)(2,1)S(1)} %get-tuple-element.1030), channel_id=1, source_target_pairs={{0,1},{1,2},{2,3},{4,5},{5,6},{6,7},{8,9},{9,10},{10,11},{12,13},{... | collective-permute-start | bytes 3145736 | tf_op jit(solution)/shard_map/ppermute | solution.py:219
  133.3 37.6 %collective-permute-start.7 = (bf16[512,1024]{1,0:T(8,128)(2,1)S(1)}, bf16[512,1024]{1,0:T(8,128)(2,1)}, u32[]{:S(2)}, u32[]{:S(2)}) collective-permute-start(bf16[512,1024]{1,0:T(8,128)(2,1)S(1)} %get-tuple-element.1030), channel_id=1, source_target_pairs={{1,0},{2,1},{3,2},{5,4},{6,5},{7,6},{9,8},{10,9},{11,10},{13,12},{... | collective-permute-start | bytes 3145736 | tf_op jit(solution)/shard_map/ppermute | solution.py:220
  170.9 34.2 %collective-permute-start.8 = (bf16[512,1024]{1,0:T(8,128)(2,1)}, bf16[512,1024]{1,0:T(8,128)(2,1)}, u32[]{:S(2)}, u32[]{:S(2)}) collective-permute-start(bf16[512,1024]{1,0:T(8,128)(2,1)} %collective-permute-done.6), channel_id=1, source_target_pairs={{1,3},{5,7},{9,11},{13,15},{17,19},{21,23},{25,27},{29,31}} | collective-permute-start | bytes 3145736 | tf_op jit(solution)/shard_map/ppermute | solution.py:224
  172.7 34.1 %collective-permute-start.9 = (bf16[512,1024]{1,0:T(8,128)(2,1)}, bf16[512,1024]{1,0:T(8,128)(2,1)}, u32[]{:S(2)}, u32[]{:S(2)}) collective-permute-start(bf16[512,1024]{1,0:T(8,128)(2,1)} %collective-permute-done.6), channel_id=1, source_target_pairs={{1,2},{2,3},{5,6},{6,7},{9,10},{10,11},{13,14},{14,15},{17,18},{18... | collective-permute-start | bytes 3145736 | tf_op jit(solution)/shard_map/ppermute | solution.py:222
  174.3 33.0 %collective-permute-start.10 = (bf16[512,1024]{1,0:T(8,128)(2,1)}, bf16[512,1024]{1,0:T(8,128)(2,1)}, u32[]{:S(2)}, u32[]{:S(2)}) collective-permute-start(bf16[512,1024]{1,0:T(8,128)(2,1)} %collective-permute-done.7), channel_id=1, source_target_pairs={{1,0},{2,1},{5,4},{6,5},{9,8},{10,9},{13,12},{14,13},{17,16},{18,1... | collective-permute-start | bytes 3145736 | tf_op jit(solution)/shard_map/ppermute | solution.py:223
  179.5 63.9 %collective-permute-start.11 = (bf16[512,1024]{1,0:T(8,128)(2,1)}, bf16[512,1024]{1,0:T(8,128)(2,1)}, u32[]{:S(2)}, u32[]{:S(2)}) collective-permute-start(bf16[512,1024]{1,0:T(8,128)(2,1)} %collective-permute-done.7), channel_id=1, source_target_pairs={{2,0},{6,4},{10,8},{14,12},{18,16},{22,20},{26,24},{30,28}} | collective-permute-start | bytes 3145736 | tf_op jit(solution)/shard_map/ppermute | solution.py:225
  182.8 76.9 %collective-permute-start.25 = (bf16[4736,128]{1,0:T(8,128)(2,1)S(1)}, bf16[4736,128]{1,0:T(8,128)(2,1)}, u32[]{:S(2)}, u32[]{:S(2)}) collective-permute-start(bf16[4736,128]{1,0:T(8,128)(2,1)S(1)} %get-tuple-element.1063), channel_id=1, source_target_pairs={{0,16},{4,20},{8,24},{12,28},{16,0},{20,4},{24,8},{28,12},{1,17},{... | collective-permute-start | bytes 3637256 | tf_op jit(solution)/shard_map/ppermute | solution.py:268
  192.1 225.7 %all-to-all-start = ((bf16[256,4,512]{2,0,1:T(8,128)(2,1)}), bf16[256,4,512]{2,0,1:T(8,128)(2,1)}, u32[]{:S(2)}, u32[]{:S(2)}) async-start(bf16[256,4,512]{2,0,1:T(8,128)(2,1)} %bitcast.142), calls=%async_computation | async-start | bytes 2097152 | tf_op jit(solution)/shard_map/all_to_all | solution.py:370
  205.1 54.9 %collective-permute-start.21 = (bf16[4736,128]{1,0:T(8,128)(2,1)S(1)}, bf16[4736,128]{1,0:T(8,128)(2,1)}, u32[]{:S(2)}, u32[]{:S(2)}) collective-permute-start(bf16[4736,128]{1,0:T(8,128)(2,1)S(1)} %get-tuple-element.1063), channel_id=1, source_target_pairs={{0,8},{4,12},{8,0},{12,4},{16,24},{20,28},{24,16},{28,20},{1,9},{5... | collective-permute-start | bytes 3637256 | tf_op jit(solution)/shard_map/ppermute | solution.py:269
  206.8 52.9 %collective-permute-start.20 = (bf16[4736,128]{1,0:T(8,128)(2,1)S(1)}, bf16[4736,128]{1,0:T(8,128)(2,1)S(1)}, u32[]{:S(2)}, u32[]{:S(2)}) collective-permute-start(bf16[4736,128]{1,0:T(8,128)(2,1)S(1)} %get-tuple-element.1064), channel_id=1, source_target_pairs={{0,8},{4,12},{8,0},{12,4},{16,24},{20,28},{24,16},{28,20},{1,9},{5... | collective-permute-start | bytes 3637256 | tf_op jit(solution)/shard_map/ppermute | solution.py:268
  207.3 53.0 %collective-permute-start.24 = (bf16[4736,128]{1,0:T(8,128)(2,1)S(1)}, bf16[4736,128]{1,0:T(8,128)(2,1)}, u32[]{:S(2)}, u32[]{:S(2)}) collective-permute-start(bf16[4736,128]{1,0:T(8,128)(2,1)S(1)} %get-tuple-element.1064), channel_id=1, source_target_pairs={{0,16},{4,20},{8,24},{12,28},{16,0},{20,4},{24,8},{28,12},{1,17},{... | collective-permute-start | bytes 3637256 | tf_op jit(solution)/shard_map/ppermute | solution.py:269
  243.4 21.4 %collective-permute-start.18 = (bf16[4736,128]{1,0:T(8,128)(2,1)S(1)}, bf16[4736,128]{1,0:T(8,128)(2,1)S(1)}, u32[]{:S(2)}, u32[]{:S(2)}) collective-permute-start(bf16[4736,128]{1,0:T(8,128)(2,1)S(1)} %get-tuple-element.1064), channel_id=1, source_target_pairs={{0,4},{4,0},{8,12},{12,8},{16,20},{20,16},{24,28},{28,24},{1,5},{5... | collective-permute-start | bytes 3637256 | tf_op jit(solution)/shard_map/ppermute | solution.py:266
  259.7 29.2 %collective-permute-start.28 = (bf16[4736,128]{1,0:T(8,128)(2,1)S(1)}, bf16[4736,128]{1,0:T(8,128)(2,1)}, u32[]{:S(2)}, u32[]{:S(2)}) collective-permute-start(bf16[4736,128]{1,0:T(8,128)(2,1)S(1)} %collective-permute-done.20), channel_id=1, source_target_pairs={{0,16},{4,20},{8,24},{12,28},{16,0},{20,4},{24,8},{28,12},{1,17},{... | collective-permute-start | bytes 3637256 | tf_op jit(solution)/shard_map/ppermute | solution.py:270
  260.1 29.4 %collective-permute-start.22 = (bf16[4736,128]{1,0:T(8,128)(2,1)S(1)}, bf16[4736,128]{1,0:T(8,128)(2,1)S(1)}, u32[]{:S(2)}, u32[]{:S(2)}) collective-permute-start(bf16[4736,128]{1,0:T(8,128)(2,1)S(1)} %collective-permute-done.20), channel_id=1, source_target_pairs={{0,4},{4,0},{8,12},{12,8},{16,20},{20,16},{24,28},{28,24},{1,5},{5... | collective-permute-start | bytes 3637256 | tf_op jit(solution)/shard_map/ppermute | solution.py:266
  260.3 29.2 %collective-permute-start.29 = (bf16[4736,128]{1,0:T(8,128)(2,1)}, bf16[4736,128]{1,0:T(8,128)(2,1)}, u32[]{:S(2)}, u32[]{:S(2)}) collective-permute-start(bf16[4736,128]{1,0:T(8,128)(2,1)} %collective-permute-done.25), channel_id=1, source_target_pairs={{0,8},{4,12},{8,0},{12,4},{16,24},{20,28},{24,16},{28,20},{1,9},{5... | collective-permute-start | bytes 3637256 | tf_op jit(solution)/shard_map/ppermute | solution.py:270
  264.8 53.0 %collective-permute-start.27 = (bf16[4736,128]{1,0:T(8,128)(2,1)}, bf16[4736,128]{1,0:T(8,128)(2,1)}, u32[]{:S(2)}, u32[]{:S(2)}) collective-permute-start(bf16[4736,128]{1,0:T(8,128)(2,1)} %collective-permute-done.25), channel_id=1, source_target_pairs={{0,4},{4,0},{8,12},{12,8},{16,20},{20,16},{24,28},{28,24},{1,5},{5... | collective-permute-start | bytes 3637256 | tf_op jit(solution)/shard_map/ppermute | solution.py:266
  264.9 52.9 %collective-permute-start.23 = (bf16[4736,128]{1,0:T(8,128)(2,1)}, bf16[4736,128]{1,0:T(8,128)(2,1)}, u32[]{:S(2)}, u32[]{:S(2)}) collective-permute-start(bf16[4736,128]{1,0:T(8,128)(2,1)} %collective-permute-done.21), channel_id=1, source_target_pairs={{0,4},{4,0},{8,12},{12,8},{16,20},{20,16},{24,28},{28,24},{1,5},{5... | collective-permute-start | bytes 3637256 | tf_op jit(solution)/shard_map/ppermute | solution.py:266
  288.9 28.9 %collective-permute-start.26 = (bf16[4736,128]{1,0:T(8,128)(2,1)}, bf16[4736,128]{1,0:T(8,128)(2,1)}, u32[]{:S(2)}, u32[]{:S(2)}) collective-permute-start(bf16[4736,128]{1,0:T(8,128)(2,1)} %collective-permute-done.24), channel_id=1, source_target_pairs={{0,4},{4,0},{8,12},{12,8},{16,20},{20,16},{24,28},{28,24},{1,5},{5... | collective-permute-start | bytes 3637256 | tf_op jit(solution)/shard_map/ppermute | solution.py:266
  289.5 28.4 %collective-permute-start.30 = (bf16[4736,128]{1,0:T(8,128)(2,1)}, bf16[4736,128]{1,0:T(8,128)(2,1)}, u32[]{:S(2)}, u32[]{:S(2)}) collective-permute-start(bf16[4736,128]{1,0:T(8,128)(2,1)} %collective-permute-done.28), channel_id=1, source_target_pairs={{0,4},{4,0},{8,12},{12,8},{16,20},{20,16},{24,28},{28,24},{1,5},{5... | collective-permute-start | bytes 3637256 | tf_op jit(solution)/shard_map/ppermute | solution.py:266
  289.5 28.4 %collective-permute-start.31 = (bf16[4736,128]{1,0:T(8,128)(2,1)}, bf16[4736,128]{1,0:T(8,128)(2,1)}, u32[]{:S(2)}, u32[]{:S(2)}) collective-permute-start(bf16[4736,128]{1,0:T(8,128)(2,1)} %collective-permute-done.29), channel_id=1, source_target_pairs={{0,4},{4,0},{8,12},{12,8},{16,20},{20,16},{24,28},{28,24},{1,5},{5... | collective-permute-start | bytes 3637256 | tf_op jit(solution)/shard_map/ppermute | solution.py:266
  417.8 36.6 %all-to-all-start.1 = ((bf16[256,4,512]{2,0,1:T(8,128)(2,1)}), bf16[256,4,512]{2,0,1:T(8,128)(2,1)S(1)}, u32[]{:S(2)}, u32[]{:S(2)}) async-start(bf16[256,4,512]{2,0,1:T(8,128)(2,1)} %bitcast.141), calls=%async_computation.1 | async-start | bytes 2097152 | tf_op jit(solution)/shard_map/all_to_all | solution.py:370
  552.9 25.9 %all-to-all-start.2 = ((bf16[4,256,512]{2,1,0:T(8,128)(2,1)}), bf16[4,256,512]{2,1,0:T(8,128)(2,1)S(1)}, u32[]{:S(2)}, u32[]{:S(2)}) async-start(bf16[4,256,512]{2,1,0:T(8,128)(2,1)} %bitcast.165), calls=%async_computation.2 | async-start | bytes 2097152 | tf_op jit(solution)/shard_map/all_to_all | solution.py:404
  556.5 297.3 %reduce-scatter.2.cloned.1.call-start = ((), (), s32[]{:S(2)}) async-start(), calls=%async_computation.7 | async-start | bytes 21823488 | tf_op jit(solution)/shard_map/reduce_scatter | solution.py:206
  580.0 28.0 %all-to-all-start.3 = ((bf16[4,256,512]{2,1,0:T(8,128)(2,1)}), bf16[4,256,512]{2,1,0:T(8,128)(2,1)S(1)}, u32[]{:S(2)}, u32[]{:S(2)}) async-start(bf16[4,256,512]{2,1,0:T(8,128)(2,1)} %bitcast.45), calls=%async_computation.3 | async-start | bytes 2097152 | tf_op jit(solution)/shard_map/all_to_all | solution.py:404
  680.0 138.4 %all-to-all-start.5 = ((f32[32,32,2]{1,2,0:T(2,128)}), f32[32,32,2]{1,2,0:T(2,128)S(1)}, u32[]{:S(2)}, u32[]{:S(2)}) async-start(f32[32,32,2]{1,2,0:T(2,128)} %copy.51), calls=%async_computation.6 | async-start | bytes 65536 | tf_op jit(solution)/shard_map/all_to_all | solution.py:293
  705.0 27.5 %collective-permute-start.32 = (bf16[512,1024]{1,0:T(8,128)(2,1)S(1)}, bf16[512,1024]{1,0:T(8,128)(2,1)S(1)}, u32[]{:S(2)}, u32[]{:S(2)}) collective-permute-start(bf16[512,1024]{1,0:T(8,128)(2,1)S(1)} %get-tuple-element.1067), channel_id=1, source_target_pairs={{0,1},{1,2},{4,5},{5,6},{8,9},{9,10},{12,13},{13,14},{16,17},{17,1... | collective-permute-start | bytes 3145736 | tf_op jit(solution)/shard_map/ppermute | solution.py:243
  709.0 51.2 %collective-permute-start.33 = (bf16[512,1024]{1,0:T(8,128)(2,1)S(1)}, bf16[512,1024]{1,0:T(8,128)(2,1)S(1)}, u32[]{:S(2)}, u32[]{:S(2)}) collective-permute-start(bf16[512,1024]{1,0:T(8,128)(2,1)S(1)} %get-tuple-element.1070), channel_id=1, source_target_pairs={{0,2},{4,6},{8,10},{12,14},{16,18},{20,22},{24,26},{28,30}} | collective-permute-start | bytes 3145736 | tf_op jit(solution)/shard_map/ppermute | solution.py:245
  711.2 49.8 %collective-permute-start.35 = (bf16[512,1024]{1,0:T(8,128)(2,1)S(1)}, bf16[512,1024]{1,0:T(8,128)(2,1)S(1)}, u32[]{:S(2)}, u32[]{:S(2)}) collective-permute-start(bf16[512,1024]{1,0:T(8,128)(2,1)S(1)} %get-tuple-element.1069), channel_id=1, source_target_pairs={{3,2},{2,1},{7,6},{6,5},{11,10},{10,9},{15,14},{14,13},{19,18},{18... | collective-permute-start | bytes 3145736 | tf_op jit(solution)/shard_map/ppermute | solution.py:244
  712.0 58.7 %collective-permute-start.36 = (bf16[512,1024]{1,0:T(8,128)(2,1)S(1)}, bf16[512,1024]{1,0:T(8,128)(2,1)S(1)}, u32[]{:S(2)}, u32[]{:S(2)}) collective-permute-start(bf16[512,1024]{1,0:T(8,128)(2,1)S(1)} %get-tuple-element.1068), channel_id=1, source_target_pairs={{3,1},{7,5},{11,9},{15,13},{19,17},{23,21},{27,25},{31,29}} | collective-permute-start | bytes 3145736 | tf_op jit(solution)/shard_map/ppermute | solution.py:246
  721.4 56.1 %collective-permute-start.38 = (bf16[512,1024]{1,0:T(8,128)(2,1)S(1)}, bf16[512,1024]{1,0:T(8,128)(2,1)S(1)}, u32[]{:S(2)}, u32[]{:S(2)}) collective-permute-start(bf16[512,1024]{1,0:T(8,128)(2,1)S(1)} %get-tuple-element.1073), channel_id=1, source_target_pairs={{0,1},{1,2},{4,5},{5,6},{8,9},{9,10},{12,13},{13,14},{16,17},{17,1... | collective-permute-start | bytes 3145736 | tf_op jit(solution)/shard_map/ppermute | solution.py:243
  732.5 67.5 %collective-permute-start.39 = (bf16[512,1024]{1,0:T(8,128)(2,1)S(1)}, bf16[512,1024]{1,0:T(8,128)(2,1)S(1)}, u32[]{:S(2)}, u32[]{:S(2)}) collective-permute-start(bf16[512,1024]{1,0:T(8,128)(2,1)S(1)} %get-tuple-element.1076), channel_id=1, source_target_pairs={{0,2},{4,6},{8,10},{12,14},{16,18},{20,22},{24,26},{28,30}} | collective-permute-start | bytes 3145736 | tf_op jit(solution)/shard_map/ppermute | solution.py:245
  760.2 39.7 %collective-permute-start.41 = (bf16[512,1024]{1,0:T(8,128)(2,1)S(1)}, bf16[512,1024]{1,0:T(8,128)(2,1)S(1)}, u32[]{:S(2)}, u32[]{:S(2)}) collective-permute-start(bf16[512,1024]{1,0:T(8,128)(2,1)S(1)} %get-tuple-element.1075), channel_id=1, source_target_pairs={{3,2},{2,1},{7,6},{6,5},{11,10},{10,9},{15,14},{14,13},{19,18},{18... | collective-permute-start | bytes 3145736 | tf_op jit(solution)/shard_map/ppermute | solution.py:244
  761.0 39.0 %collective-permute-start.42 = (bf16[512,1024]{1,0:T(8,128)(2,1)S(1)}, bf16[512,1024]{1,0:T(8,128)(2,1)}, u32[]{:S(2)}, u32[]{:S(2)}) collective-permute-start(bf16[512,1024]{1,0:T(8,128)(2,1)S(1)} %get-tuple-element.1074), channel_id=1, source_target_pairs={{3,1},{7,5},{11,9},{15,13},{19,17},{23,21},{27,25},{31,29}} | collective-permute-start | bytes 3145736 | tf_op jit(solution)/shard_map/ppermute | solution.py:246
  773.2 71.0 %collective-permute-start.34 = (bf16[512,1024]{1,0:T(8,128)(2,1)}, bf16[512,1024]{1,0:T(8,128)(2,1)}, u32[]{:S(2)}, u32[]{:S(2)}) collective-permute-start(bf16[512,1024]{1,0:T(8,128)(2,1)} %get-tuple-element.1065), channel_id=1, source_target_pairs={{0,1},{1,2},{2,3},{4,5},{5,6},{6,7},{8,9},{9,10},{10,11},{12,13},{... | collective-permute-start | bytes 3145736 | tf_op jit(solution)/shard_map/ppermute | solution.py:251
  777.5 66.8 %collective-permute-start.37 = (bf16[512,1024]{1,0:T(8,128)(2,1)S(1)}, bf16[512,1024]{1,0:T(8,128)(2,1)}, u32[]{:S(2)}, u32[]{:S(2)}) collective-permute-start(bf16[512,1024]{1,0:T(8,128)(2,1)S(1)} %get-tuple-element.1066), channel_id=1, source_target_pairs={{1,0},{2,1},{3,2},{5,4},{6,5},{7,6},{9,8},{10,9},{11,10},{13,12},{... | collective-permute-start | bytes 3145736 | tf_op jit(solution)/shard_map/ppermute | solution.py:254
  804.0 42.7 %collective-permute-start.40 = (bf16[512,1024]{1,0:T(8,128)(2,1)}, bf16[512,1024]{1,0:T(8,128)(2,1)}, u32[]{:S(2)}, u32[]{:S(2)}) collective-permute-start(bf16[512,1024]{1,0:T(8,128)(2,1)} %get-tuple-element.1071), channel_id=1, source_target_pairs={{0,1},{1,2},{2,3},{4,5},{5,6},{6,7},{8,9},{9,10},{10,11},{12,13},{... | collective-permute-start | bytes 3145736 | tf_op jit(solution)/shard_map/ppermute | solution.py:251
  817.0 29.7 %collective-permute-start.43 = (bf16[512,1024]{1,0:T(8,128)(2,1)}, bf16[512,1024]{1,0:T(8,128)(2,1)}, u32[]{:S(2)}, u32[]{:S(2)}) collective-permute-start(bf16[512,1024]{1,0:T(8,128)(2,1)} %get-tuple-element.1072), channel_id=1, source_target_pairs={{1,0},{2,1},{3,2},{5,4},{6,5},{7,6},{9,8},{10,9},{11,10},{13,12},{... | collective-permute-start | bytes 3145736 | tf_op jit(solution)/shard_map/ppermute | solution.py:254
  818.3 24.9 %all-to-all-start.4 = ((bf16[8,128,768]{2,1,0:T(8,128)(2,1)}), bf16[8,128,768]{2,1,0:T(8,128)(2,1)S(1)}, u32[]{:S(2)}, u32[]{:S(2)}) async-start(bf16[8,128,768]{2,1,0:T(8,128)(2,1)} %bitcast.182), calls=%async_computation.4 | async-start | bytes 3145728 | tf_op jit(solution)/shard_map/all_to_all | solution.py:293
  865.2 22.9 %collective-permute-start.45 = (bf16[2368,128]{1,0:T(8,128)(2,1)S(1)}, bf16[2368,128]{1,0:T(8,128)(2,1)S(1)}, u32[]{:S(2)}, u32[]{:S(2)}) collective-permute-start(bf16[2368,128]{1,0:T(8,128)(2,1)S(1)} %get-tuple-element.1090), channel_id=1, source_target_pairs={{0,2},{4,6},{8,10},{12,14},{16,18},{20,22},{24,26},{28,30}} | collective-permute-start | bytes 1818632 | tf_op jit(solution)/shard_map/ppermute | solution.py:245
  (77 other events, 1310.4 us)
Sparse Core Ops, SparseCore 0:
  25.3 29.3 all-gather.2
  580.1 135.2 reduce-scatter.1

commit v2 on v1

--- a/solution.py
+++ b/solution.py
@@ -154,6 +154,147 @@
     )(lo, qkv_t, qkv_t, qkv_t, do_t, o_t, lse, start, cos, sin)
 
 
+def assemble_kernel(lane_ref, *refs, sizes, parts):
+    pieces, outs = refs[: 2 * parts], refs[2 * parts : 2 * parts + len(sizes)]
+    held, in_sem, out_sem = refs[2 * parts + len(sizes) :]
+    slots = held.shape[0]
+    total = sum(sizes)
+    steps = [
+        (block, part, sum(sizes[:part])) for block in range(4) for part in range(len(sizes))
+    ]
+
+    def fetch(step):
+        block, part, first = steps[step]
+        rows = pl.ds((block % 2) * total + first, sizes[part])
+        slot = step % slots
+        return [
+            pltpu.make_async_copy(
+                pieces[2 * r + block // 2].at[rows],
+                held.at[slot, pl.ds(0, sizes[part]), pl.ds(pl.multiple_of(lane_ref[r], 128), 128)],
+                in_sem.at[slot, r],
+            )
+            for r in range(parts)
+        ]
+
+    def put(step):
+        block, part, _ = steps[step]
+        slot = step % slots
+        return pltpu.make_async_copy(
+            held.at[slot, pl.ds(0, sizes[part])],
+            outs[part].at[pl.ds(block * sizes[part], sizes[part])],
+            out_sem.at[slot],
+        )
+
+    ahead = slots // 2
+    for step in range(ahead):
+        for copy in fetch(step):
+            copy.start()
+    for step in range(len(steps)):
+        later = step + ahead
+        if later < len(steps):
+            if later >= slots:
+                put(later - slots).wait()
+            for copy in fetch(later):
+                copy.start()
+        for copy in fetch(step):
+            copy.wait()
+        put(step).start()
+    for step in range(len(steps) - slots, len(steps)):
+        put(step).wait()
+
+
+def assemble(lanes, pieces, sizes, width):
+    parts = len(pieces) // 2
+    whole = pl.BlockSpec(memory_space=pl.ANY)
+    return pl.pallas_call(
+        functools.partial(assemble_kernel, sizes=sizes, parts=parts),
+        out_shape=[jax.ShapeDtypeStruct((4 * size, width), jnp.bfloat16) for size in sizes],
+        grid_spec=pltpu.PrefetchScalarGridSpec(
+            num_scalar_prefetch=1,
+            grid=(1,),
+            in_specs=[whole] * len(pieces),
+            out_specs=[whole] * len(sizes),
+            scratch_shapes=[
+                pltpu.VMEM((4, max(sizes), width), jnp.bfloat16),
+                pltpu.SemaphoreType.DMA((4, parts)),
+                pltpu.SemaphoreType.DMA((4,)),
+            ],
+        ),
+        cost_estimate=pl.CostEstimate(
+            flops=0, bytes_accessed=16 * sum(sizes) * width, transcendentals=0
+        ),
+        name="assemble",
+    )(lanes, *pieces)
+
+
+def dot_in(left, right, left_dim, right_dim):
+    return lax.dot_general(
+        left, right, (((left_dim,), (right_dim,)), ((), ())), preferred_element_type=jnp.float32
+    )
+
+
+def ffn_main_kernel(x_ref, c_ref, gate_ref, up_ref, down_ref, h_ref, dg_ref, du_ref, *, step):
+    for first in range(0, x_ref.shape[0], step):
+        rows = slice(first, first + step)
+        gate = dot_in(x_ref[rows], gate_ref[...], 1, 1)
+        up = dot_in(x_ref[rows], up_ref[...], 1, 1)
+        grad_hidden = dot_in(c_ref[rows], down_ref[...], 1, 1)
+        sig = jax.nn.sigmoid(gate)
+        silu = gate * sig
+        h_ref[rows] = (silu * up).astype(jnp.bfloat16)
+        dg = (grad_hidden * up * sig * (1.0 + gate * (1.0 - sig))).astype(jnp.bfloat16)
+        du = (grad_hidden * silu).astype(jnp.bfloat16)
+        dg_ref[rows] = dg
+        du_ref[rows] = du
+
+
+def ffn_grad_kernel(x_ref, c_ref, h_ref, dg_ref, du_ref, g_ref):
+    for place, (left, right) in enumerate(((dg_ref, x_ref), (du_ref, x_ref), (h_ref, c_ref))):
+        grad = dot_in(left[...], right[...], 0, 0).astype(jnp.bfloat16)
+        for i in range(g_ref.shape[0]):
+            g_ref[i, place] = grad[:, i * g_ref.shape[3] : (i + 1) * g_ref.shape[3]]
+
+
+def ffn_main(x, c, gate, up, down, tile=256, step=256):
+    tokens, width = x.shape
+    units = gate.shape[0]
+    full = pl.BlockSpec((tokens, width), lambda t: (0, 0))
+    weight = pl.BlockSpec((tile, width), lambda t: (t, 0))
+    column = pl.BlockSpec((tokens, tile), lambda t: (0, t))
+    return pl.pallas_call(
+        functools.partial(ffn_main_kernel, step=step),
+        out_shape=[jax.ShapeDtypeStruct((tokens, units), jnp.bfloat16)] * 3,
+        grid=(units // tile,),
+        in_specs=[full, full, weight, weight, weight],
+        out_specs=[column, column, column],
+        cost_estimate=pl.CostEstimate(
+            flops=6 * tokens * width * units, bytes_accessed=6 * units * (width + tokens),
+            transcendentals=tokens * units,
+        ),
+        name="ffn_main",
+    )(x, c, gate, up, down)
+
+
+def ffn_grad(x, c, hidden, dg, du, chunks, tile=256):
+    tokens, width = x.shape
+    units = hidden.shape[1]
+    full = pl.BlockSpec((tokens, width), lambda t: (0, 0))
+    column = pl.BlockSpec((tokens, tile), lambda t: (0, t))
+    piece = width // chunks
+    return pl.pallas_call(
+        ffn_grad_kernel,
+        out_shape=jax.ShapeDtypeStruct((chunks, 3, units, piece), jnp.bfloat16),
+        grid=(units // tile,),
+        in_specs=[full, full, column, column, column],
+        out_specs=pl.BlockSpec((chunks, 3, tile, piece), lambda t: (0, 0, t, 0)),
+        cost_estimate=pl.CostEstimate(
+            flops=6 * tokens * width * units, bytes_accessed=6 * units * (width + tokens),
+            transcendentals=0,
+        ),
+        name="ffn_grad",
+    )(x, c, hidden, dg, du)
+
+
 eps_norm = 1e-05
 
 
@@ -257,7 +398,7 @@
     return total(block(0), right, left)
 
 
-def plane_gather(piece, axis):
+def plane_gather(piece, axis, sizes):
     core, across, along = ([(i, i ^ bit) for i in range(8)] for bit in (1, 2, 4))
     half = piece.shape[0] // 2
     top, low = piece[:half], piece[half:]
@@ -273,18 +414,9 @@
     for pair in held:
         parts += [pair, tuple(partner(part) for part in pair)]
 
-    def ordered(me):
-        def branch(*flat):
-            lanes = [
-                jnp.concatenate([flat[2 * (i ^ me)], flat[2 * (i ^ me) + 1]], axis=0)
-                for i in range(8)
-            ]
-            return jnp.concatenate(lanes, axis=1)
-
-        return branch
-
     flat = [part for pair in parts for part in pair]
-    return lax.switch(lax.axis_index(axis), [ordered(me) for me in range(8)], *flat)
+    lanes = jnp.arange(8, dtype=jnp.int32) ^ lax.axis_index(axis).astype(jnp.int32)
+    return assemble(lanes * piece.shape[1], flat, sizes, 8 * piece.shape[1])
 
 
 def exchange_sum(partial_sum, axis):
@@ -327,17 +459,16 @@
     rest_piece = jnp.concatenate([w_output, w_gate.T, w_up.T, w_down], axis=0)
     sizes = (cols, hidden_part, hidden_part, hidden_part)
     firsts = (0, cols, cols + hidden_part, cols + 2 * hidden_part)
-    if n_dp == 8:
-        rest_every = plane_gather(line_gather(rest_piece, "mp"), "dp")
-        rest_every = rest_every.reshape(n_mp, rest_piece.shape[0], width)
+    if n_dp == 8 and depth == 128:
+        output_full, gate_full, up_full, down_full = plane_gather(line_gather(rest_piece, "mp"), "dp", sizes)
     else:
         rest_every = lax.all_gather(rest_piece, ("dp", "mp"), axis=0, tiled=False)
         rest_every = rest_every.reshape((n_dp, n_mp) + rest_piece.shape).transpose(1, 2, 0, 3)
         rest_every = rest_every.reshape(n_mp, rest_piece.shape[0], width)
-    output_full, gate_full, up_full, down_full = (
-        rest_every[:, first : first + size].reshape(n_mp * size, width)
-        for first, size in zip(firsts, sizes)
-    )
+        output_full, gate_full, up_full, down_full = (
+            rest_every[:, first : first + size].reshape(n_mp * size, width)
+            for first, size in zip(firsts, sizes)
+        )
 
     first_rows = line_gather(inputs[0], "mp")
     first_rows, second_piece = lax.optimization_barrier((first_rows, inputs[1]))
@@ -366,34 +497,29 @@
         out, log = attn_fwd(qkv[m], starts[m], lows[m])
         mixed.append(out)
         logs.append(log)
-    mixed_own = [
-        lax.all_to_all(mixed[m], "mp", split_axis=1, concat_axis=0, tiled=True)
-        for m in range(batches)
-    ]
+    mixed_own = []
+    for m in range(batches):
+        mixed_own.append(
+            lax.all_to_all(mixed[m], "mp", split_axis=1, concat_axis=0, tiled=True)
+        )
     in_float = inputs.astype(jnp.float32).reshape(batches * tokens, width)
     mixed_both = jnp.concatenate(mixed_own, axis=1)
     hidden_in = in_float + dot_dims(mixed_both, output_full, 0, 0)
     factor_ffn = rms_factor(hidden_in)
     normed_ffn = (hidden_in * factor_ffn * gain_two).astype(low)
-    gate_pre = dot_dims(normed_ffn, gate_full, 1, 1)
-    up_pre = dot_dims(normed_ffn, up_full, 1, 1)
-    sig_gate = jax.nn.sigmoid(gate_pre)
-    silu_gate = gate_pre * sig_gate
-    hidden = (silu_gate * up_pre).astype(low)
-    result = (hidden_in + dot_dims(hidden, down_full, 1, 0)).astype(low)
-
     grad_top = cotangent.reshape(batches * tokens, width)
-    grad_down = dot_dims(grad_top, hidden, 0, 0).astype(low)
-    grad_hidden = dot_dims(grad_top, down_full, 1, 1)
-    grad_gate_pre = (
-        grad_hidden * up_pre * sig_gate * (1.0 + gate_pre * (1.0 - sig_gate))
-    ).astype(low)
-    grad_up_pre = (grad_hidden * silu_gate).astype(low)
-    grad_gate = dot_dims(normed_ffn, grad_gate_pre, 0, 0).astype(low)
-    grad_up = dot_dims(normed_ffn, grad_up_pre, 0, 0).astype(low)
+    hidden, grad_gate_pre, grad_up_pre = ffn_main(
+        normed_ffn, grad_top, gate_full, up_full, down_full
+    )
     grad_normed_ffn = dot_dims(grad_gate_pre, gate_full, 1, 0) + dot_dims(
         grad_up_pre, up_full, 1, 0
     )
+    result = (hidden_in + dot_dims(hidden, down_full, 1, 0)).astype(low)
+    chunks = width // 128
+    every_grad = ffn_grad(normed_ffn, grad_top, hidden, grad_gate_pre, grad_up_pre, chunks)
+    if n_dp != chunks:
+        every_grad = every_grad.reshape(chunks, 3, n_mp * hidden_part, n_dp // chunks, depth)
+        every_grad = every_grad.transpose(0, 3, 1, 2, 4).reshape(n_dp, 3, -1, depth)
     grad_middle, gain_ffn_part = rms_back(hidden_in, factor_ffn, gain_two, grad_normed_ffn)
     grad_hidden_in = grad_top.astype(jnp.float32) + grad_middle
     grad_branch = grad_hidden_in.astype(low)
@@ -408,7 +534,6 @@
         )
     grad_output = dot_dims(grad_branch, mixed_both, 0, 1).astype(low)
 
-    every_grad = jnp.concatenate([grad_output, grad_gate, grad_up, grad_down], axis=1)
     grad_mixed_rows[0], every_grad = lax.optimization_barrier((grad_mixed_rows[0], every_grad))
     mine = scatter(every_grad, "dp", 0)
 
@@ -431,12 +556,11 @@
         )
     grad_w = sum(dot_dims(normed[m], grad_qkv[m], 0, 1) for m in range(batches))
 
-    own_parts = [
-        mine[:, n_mp * first : n_mp * (first + size)].reshape(depth, n_mp, size)
-        for first, size in zip(firsts, sizes)
-    ]
-    own_rest = jnp.concatenate(own_parts, axis=2).transpose(1, 2, 0)
-    own_rest = line_scatter(own_rest.reshape(-1, depth), "mp")
+    own_out = exchange_sum(grad_output, "dp").astype(low).T.reshape(n_mp, cols, depth)
+    own_ffn = mine.reshape(3, n_mp, hidden_part, depth).transpose(1, 0, 2, 3)
+    own_rest = jnp.concatenate([own_out, own_ffn.reshape(n_mp, -1, depth)], axis=1)
+    own_rest = own_rest.reshape(-1, depth)
+    own_rest = line_scatter(own_rest, "mp")
     own_output, own_gate, own_up, own_down = (
         own_rest[first : first + size] for first, size in zip(firsts, sizes)
     )

time: 929 us -> 786 us (0.85)
  matrix products: 153 us -> 86.2 us
  Pallas kernels: 98.5 us -> 163 us
  other arithmetic: 103 us -> 43.7 us
  loops' own time: 36.4 us -> 0 us
  starting transfers between devices: 204 us -> 181 us
  local copies, waits for them, and re-layouts: 73.4 us -> 58.7 us
    dot_general x18 -> x12, matrix products: 153 us -> 86.2 us  [dot_dims(): lax.dot_general(left, right, (((left_dim,), (right_dim,)), ((), ())), pre...]
    pallas_call x0 -> x3, Pallas kernels: none -> 65.2 us  [the longest x1 25.8 us: ffn_main(): pl.pallas_call(functools.partial(ffn_main_kernel, step=step), out_shape=[...]
    cond x7 -> x0, other arithmetic: 43.1 us -> none
    another operation x1 -> x0, loops' own time: 36.4 us -> none  [plane_gather(): lax.switch(lax.axis_index(axis), [ordered(me) for me in range(8)], *flat)]
    concatenate x3 -> x1, other arithmetic: 21.5 us -> 0.16 us  [local(): jnp.concatenate([own_out, own_ffn.reshape(n_mp, -1, depth)], axis=1)]
    slice x8 -> x0, local copies, waits for them, and re-layouts: 20.8 us -> none  [the longest x2 16.5 us: local(): rest_every[:, first:first + size].reshape(n_mp * size, width)]
    ppermute x1, waiting for transfers between devices: 0.01 us -> 15.2 us  [plane_gather(): lax.ppermute(low, axis, along)]
    ppermute x1, starting transfers between devices: 14.5 us -> 0.07 us  [plane_gather(): lax.ppermute(top, axis, along)]
  transfers between devices with their start and end apart: 58 -> 59, of which waited for: 19 -> 21; matrix products, arithmetic and copies ran while one was open for 23% -> 18% of each run, Pallas kernels for 11% -> 18%
where the time goes in v2:
time: 786 us; the launch traced here: 774 us
  waiting for transfers between devices  220 us (28%)
  starting transfers between devices  181 us (23%)
  Pallas kernels  163 us (21%)
  matrix products  86.2 us (11%)
  local copies, waits for them, and re-layouts  58.7 us (7%)
  other arithmetic  43.7 us (6%)
  between operations  21.1 us (3%)
    dot_general x12, matrix products, dot_dims(): lax.dot_general(left, right, (((left_dim,), (right_dim,)), ((), ())), pre...  86.2 us
    pallas_call x2, Pallas kernels, attn_bwd(): pl.pallas_call(functools.partial(attn_bwd_kernel, bq=bq, bk=bk, heads=hps...  52.9 us
    pallas_call x2, Pallas kernels, attn_fwd(): pl.pallas_call(functools.partial(attn_fwd_kernel, bq=bq, bk=bk, heads=hps...  44.9 us
    ppermute x3, waiting for transfers between devices, line_gather(): three_right = lax.ppermute(one_right, axis, [(2, 0)])  39 us
    ppermute x3, waiting for transfers between devices, line_gather(): two_right = lax.ppermute(one_right, axis, [(1, 0), (2, 1)])  32.2 us
    ppermute x3, waiting for transfers between devices, line_scatter(): two_right = lax.ppermute(block(2), axis, [(0, 1), (1, 2)])  31.5 us
    all_to_all x3, starting transfers between devices, exchange_sum(): lax.all_to_all(parts, axis, split_axis=0, concat_axis=0, tiled=True)  29.3 us
    unnamed x125, local copies, waits for them, and re-layouts  28.7 us
  transfers between devices with their start and end apart: 59, of which 21 were waited for; matrix products, arithmetic and copies ran while one was open for 18% of the time, Pallas kernels for 18%

profile of v2, /device:TPU:0, one launch (start us, length us, event | category | flops | bytes accessed | tf_op | source)
XLA Modules:
  0.0 774.2 jit_solution(7418069859320451547)
XLA Ops:
  9.3 5.1 collective-permute-start.12
  17.4 5.6 collective-permute-start
  41.0 8.9 %collective-permute-done = bf16[512,1024]{1,0:T(8,128)(2,1)} collective-permute-done((bf16[512,1024]{1,0:T(8,128)(2,1)S(1)}, bf16[512,1024]{1,0:T(8,128)(2,1)}, u32[]{:S(2)}, u32[]{:S(2)}) %collective-permute-start) | collective-permute-done | bytes 1048608 | tf_op jit(solution)/shard_map/ppermute | solution.py:360
  50.7 4.9 collective-permute-done.3
  70.8 27.4 %collective-permute-done.4 = bf16[512,1024]{1,0:T(8,128)(2,1)S(1)} collective-permute-done((bf16[512,1024]{1,0:T(8,128)(2,1)}, bf16[512,1024]{1,0:T(8,128)(2,1)S(1)}, u32[]{:S(2)}, u32[]{:S(2)}) %collective-permute-start.4) | collective-permute-done | bytes 1048608 | tf_op jit(solution)/shard_map/ppermute | solution.py:364
  98.3 21.2 %collective-permute-done.5 = bf16[512,1024]{1,0:T(8,128)(2,1)S(1)} collective-permute-done((bf16[512,1024]{1,0:T(8,128)(2,1)}, bf16[512,1024]{1,0:T(8,128)(2,1)S(1)}, u32[]{:S(2)}, u32[]{:S(2)}) %collective-permute-start.5) | collective-permute-done | bytes 1048608 | tf_op jit(solution)/shard_map/ppermute | solution.py:366
  120.1 8.9 %collective-permute-start.6 = (bf16[512,1024]{1,0:T(8,128)(2,1)S(1)}, bf16[512,1024]{1,0:T(8,128)(2,1)}, u32[]{:S(2)}, u32[]{:S(2)}) collective-permute-start(bf16[512,1024]{1,0:T(8,128)(2,1)S(1)} %get-tuple-element.31), channel_id=1, source_target_pairs={{0,1},{1,2},{2,3},{4,5},{5,6},{6,7},{8,9},{9,10},{10,11},{12,13},{... | collective-permute-start | bytes 3145736 | tf_op jit(solution)/shard_map/ppermute | solution.py:360
  133.7 5.7 fusion.20
  143.2 22.5 %attn_fwd.2 = (bf16[256,2048]{1,0:T(8,128)(2,1)}, f32[4,1,2048]{2,1,0:T(1,128)}) custom-call(s32[4]{0:T(128)} %get-tuple-element.131.lo_ref, bf16[768,2048]{1,0:T(8,128)(2,1)} %pad_maximum_fusion.1.q_ref.k_ref.v_ref, bf16[768,2048]{1,0:T(8,128)(2,1)} %pad_maximum_fusion.1.q_ref.k_ref.v_ref, bf16[768,2048]{1,0:T(8,128)(2,1)} %pad_maximum_fusion.1.q_ref.k_ref.v_ref, ...), custom_call_target="tpu_custom_call" | custom-call | flops 4294967296 | bytes 4194304 | tf_op jit(solution)/shard_map/attn_fwd/pallas_call | solution.py:120
  179.9 13.1 %all-to-all-start = ((bf16[256,4,512]{2,0,1:T(8,128)(2,1)}), bf16[256,4,512]{2,0,1:T(8,128)(2,1)}, u32[]{:S(2)}, u32[]{:S(2)}) async-start(bf16[256,4,512]{2,0,1:T(8,128)(2,1)} %bitcast.117), calls=%async_computation | async-start | bytes 2097152 | tf_op jit(solution)/shard_map/all_to_all | solution.py:503
  193.0 9.9 %collective-permute-start.20 = (bf16[4736,128]{1,0:T(8,128)(2,1)}, bf16[4736,128]{1,0:T(8,128)(2,1)}, u32[]{:S(2)}, u32[]{:S(2)}) collective-permute-start(bf16[4736,128]{1,0:T(8,128)(2,1)} %get-tuple-element.66.refs_0_), channel_id=1, source_target_pairs={{0,8},{4,12},{8,0},{12,4},{16,24},{20,28},{24,16},{28,20},{1,9},{5... | collective-permute-start | bytes 3637256 | tf_op jit(solution)/shard_map/ppermute | solution.py:409
  208.3 4.8 collective-permute-done.10
  213.1 10.1 %collective-permute-start.21 = (bf16[4736,128]{1,0:T(8,128)(2,1)S(1)}, bf16[4736,128]{1,0:T(8,128)(2,1)}, u32[]{:S(2)}, u32[]{:S(2)}) collective-permute-start(bf16[4736,128]{1,0:T(8,128)(2,1)S(1)} %get-tuple-element.65.refs_1_), channel_id=1, source_target_pairs={{0,8},{4,12},{8,0},{12,4},{16,24},{20,28},{24,16},{28,20},{1,9},{5... | collective-permute-start | bytes 3637256 | tf_op jit(solution)/shard_map/ppermute | solution.py:410
  224.5 17.8 %collective-permute-done.11 = bf16[512,1024]{1,0:T(8,128)(2,1)} collective-permute-done((bf16[512,1024]{1,0:T(8,128)(2,1)}, bf16[512,1024]{1,0:T(8,128)(2,1)}, u32[]{:S(2)}, u32[]{:S(2)}) %collective-permute-start.11) | collective-permute-done | bytes 1048608 | tf_op jit(solution)/shard_map/ppermute | solution.py:366
  242.3 8.2 %collective-permute-start.25 = (bf16[4736,128]{1,0:T(8,128)(2,1)S(1)}, bf16[4736,128]{1,0:T(8,128)(2,1)}, u32[]{:S(2)}, u32[]{:S(2)}) collective-permute-start(bf16[4736,128]{1,0:T(8,128)(2,1)S(1)} %get-tuple-element.65.refs_1_), channel_id=1, source_target_pairs={{0,16},{4,20},{8,24},{12,28},{16,0},{20,4},{24,8},{28,12},{1,17},{... | collective-permute-start | bytes 3637256 | tf_op jit(solution)/shard_map/ppermute | solution.py:409
  262.9 15.2 %collective-permute-done.25.refs_9_ = bf16[4736,128]{1,0:T(8,128)(2,1)} collective-permute-done((bf16[4736,128]{1,0:T(8,128)(2,1)S(1)}, bf16[4736,128]{1,0:T(8,128)(2,1)}, u32[]{:S(2)}, u32[]{:S(2)}) %collective-permute-start.25) | collective-permute-done | bytes 1212448 | tf_op jit(solution)/shard_map/ppermute | solution.py:409
  280.2 22.4 %attn_fwd.3 = (bf16[256,2048]{1,0:T(8,128)(2,1)}, f32[4,1,2048]{2,1,0:T(1,128)}) custom-call(s32[4]{0:T(128)} %get-tuple-element.130.lo_ref, bf16[768,2048]{1,0:T(8,128)(2,1)} %pad_maximum_fusion.2.q_ref.k_ref.v_ref, bf16[768,2048]{1,0:T(8,128)(2,1)} %pad_maximum_fusion.2.q_ref.k_ref.v_ref, bf16[768,2048]{1,0:T(8,128)(2,1)} %pad_maximum_fusion.2.q_ref.k_ref.v_ref, ...), custom_call_target="tpu_custom_call" | custom-call | flops 4294967296 | bytes 4194304 | tf_op jit(solution)/shard_map/attn_fwd/pallas_call | solution.py:120
  304.9 4.6 all-to-all-start.1
  310.2 17.0 %collective-permute-done.28.refs_12_ = bf16[4736,128]{1,0:T(8,128)(2,1)} collective-permute-done((bf16[4736,128]{1,0:T(8,128)(2,1)}, bf16[4736,128]{1,0:T(8,128)(2,1)}, u32[]{:S(2)}, u32[]{:S(2)}) %collective-permute-start.28) | collective-permute-done | bytes 1212448 | tf_op jit(solution)/shard_map/ppermute | solution.py:411
  332.1 14.5 %assemble.1 = (bf16[1024,1024]{1,0:T(8,128)(2,1)}, bf16[2816,1024]{1,0:T(8,128)(2,1)}, bf16[2816,1024]{1,0:T(8,128)(2,1)}, bf16[2816,1024]{1,0:T(8,128)(2,1)}) custom-call(s32[8]{0:T(128)} %xor_multiply_fusion.lane_ref, bf16[4736,128]{1,0:T(8,128)(2,1)} %get-tuple-element.66.refs_0_, bf16[4736,128]{1,0:T(8,128)(2,1)} %copy-done.15, ...), custom_call_target="tpu_custom_call" | custom-call | bytes 38797312 | tf_op jit(solution)/shard_map/assemble/pallas_call | solution.py:209
  346.6 4.9 multiply_reduce_fusion.2
  355.2 25.8 %ffn_main.1 = (bf16[1024,2816]{1,0:T(8,128)(2,1)}, bf16[1024,2816]{1,0:T(8,128)(2,1)}, bf16[1024,2816]{1,0:T(8,128)(2,1)}) custom-call(bf16[1024,1024]{1,0:T(8,128)(2,1)} %multiply_convert_fusion.x_ref, bf16[1024,1024]{1,0:T(8,128)(2,1)} %bitcast.126, bf16[2816,1024]{1,0:T(8,128)(2,1)} %get-tuple-element.39.gate_ref, ...), custom_call_target="tpu_custom_call" | custom-call | flops 17716740096 | bytes 34603008 | tf_op jit(solution)/shard_map/ffn_main/pallas_call | solution.py:264
  381.0 10.0 %fusion.48 = f32[1024,1024]{1,0:T(8,128)S(1)} fusion(bf16[1024,2816]{1,0:T(8,128)(2,1)} %get-tuple-element.44.du_ref, bf16[2816,1024]{1,0:T(8,128)(2,1)} %get-tuple-element.40.up_ref), kind=kOutput, calls=%fused_computation.186 | convolution fusion | flops 5905580032 | bytes 15728640 | tf_op jit(solution)/shard_map/dot_general | solution.py:302
  391.0 9.0 %multiply_reduce_fusion = (f32[1024]{0:T(1024)S(1)}, f32[1024]{0:T(1024)S(1)}, f32[1024,1024]{1,0:T(8,128)S(1)}) fusion(f32[1024,1024]{1,0:T(8,128)S(1)} %copy-done.12, f32[1024]{0:T(1024)S(1)} %get-tuple-element.116, f32[1024]{0:T(1024)S(1)} %bitcast.146, f32[1024,1024]{1,0:T(8,128)S(1)} %fusion.48, bf16[1024,2816]{1,0:T(8,128)(2,1)S(1)} %copy-done.48, ...), kind=kOutput, calls=%fused_computation.27 | convolution fusion | flops 5912918016 | bytes 24133632 | tf_op jit(solution)/shard_map/dot_general | solution.py:302
  409.1 24.9 %ffn_grad.1 = bf16[8,3,2816,128]{3,2,1,0:T(8,128)(2,1)} custom-call(bf16[1024,1024]{1,0:T(8,128)(2,1)} %multiply_convert_fusion.x_ref, bf16[1024,1024]{1,0:T(8,128)(2,1)} %bitcast.127, bf16[1024,2816]{1,0:T(8,128)(2,1)} %get-tuple-element.42.h_ref, bf16[1024,2816]{1,0:T(8,128)(2,1)} %get-tuple-element.43.dg_ref, bf16[1024,2816]{1,0:T(8,128)(2,1)} %get-tuple-element.44.du_ref), custom_call_target="tpu_custom_call" | custom-call | flops 17716740096 | bytes 34603008 | tf_op jit(solution)/shard_map/ffn_grad/pallas_call | solution.py:284
  440.4 7.2 convolution_convert_fusion.2
  447.6 18.4 %all-to-all-done.3 = bf16[4,256,512]{2,1,0:T(8,128)(2,1)S(1)} async-done(((bf16[4,256,512]{2,1,0:T(8,128)(2,1)}), bf16[4,256,512]{2,1,0:T(8,128)(2,1)S(1)}, u32[]{:S(2)}, u32[]{:S(2)}) %all-to-all-start.3) | async-done | bytes 1048608 | tf_op jit(solution)/shard_map/all_to_all | solution.py:530
  467.2 26.3 %attn_bwd.2 = bf16[3,256,2048]{2,1,0:T(8,128)(2,1)} custom-call(s32[4]{0:T(128)} %get-tuple-element.131.lo_ref, bf16[768,2048]{1,0:T(8,128)(2,1)} %pad_maximum_fusion.1.q_ref.k_ref.v_ref, bf16[768,2048]{1,0:T(8,128)(2,1)} %pad_maximum_fusion.1.q_ref.k_ref.v_ref, bf16[768,2048]{1,0:T(8,128)(2,1)} %pad_maximum_fusion.1.q_ref.k_ref.v_ref, ...), custom_call_target="tpu_custom_call" | custom-call | flops 10737418240 | bytes 10485760 | tf_op jit(solution)/shard_map/attn_bwd/pallas_call | solution.py:140
  493.5 7.2 convolution_convert_fusion.1
  500.7 26.5 %attn_bwd.3 = bf16[3,256,2048]{2,1,0:T(8,128)(2,1)} custom-call(s32[4]{0:T(128)} %get-tuple-element.130.lo_ref, bf16[768,2048]{1,0:T(8,128)(2,1)} %pad_maximum_fusion.2.q_ref.k_ref.v_ref, bf16[768,2048]{1,0:T(8,128)(2,1)} %pad_maximum_fusion.2.q_ref.k_ref.v_ref, bf16[768,2048]{1,0:T(8,128)(2,1)} %pad_maximum_fusion.2.q_ref.k_ref.v_ref, ...), custom_call_target="tpu_custom_call" | custom-call | flops 10737418240 | bytes 10485760 | tf_op jit(solution)/shard_map/attn_bwd/pallas_call | solution.py:140
  527.3 8.2 %fusion.9 = (f32[1024]{0:T(1024)S(1)}, bf16[2048,1024]{1,0:T(8,128)(2,1)S(1)}) fusion(f32[2048]{0:T(1024)S(1)} %add_rsqrt_fusion, bf16[3584,1024]{1,0:T(8,128)(2,1)} %copy-done.18, s32[]{:T(128)S(6)} %select_n.155, bf16[768,2048]{1,0:T(8,128)(2,1)} %bitcast.166, bf16[1024,768]{1,0:T(8,128)(2,1)S(1)} %bitcast.132), kind=kOutput, calls=%fused_computation.15 | convolution fusion | flops 3233807360 | bytes 13119492 | tf_op jit(solution)/shard_map/dot_general | solution.py:302
  547.7 14.6 %all-to-all-start.6 = ((f32[32,32,2]{1,2,0:T(2,128)}), f32[32,32,2]{1,2,0:T(2,128)S(1)}, u32[]{:S(2)}, u32[]{:S(2)}) async-start(f32[32,32,2]{1,2,0:T(2,128)} %copy.36), calls=%async_computation.7 | async-start | bytes 65536 | tf_op jit(solution)/shard_map/all_to_all | solution.py:425
  562.3 8.7 %fusion.18 = f32[1024,768]{1,0:T(8,128)} fusion(bf16[768,2048]{1,0:T(8,128)(2,1)} %bitcast.169, bf16[2048,1024]{1,0:T(8,128)(2,1)} %copy-done, f32[1024]{0:T(1024)S(1)} %bitcast.152, f32[2048]{0:T(1024)S(1)} %copy-done.40), kind=kOutput, calls=%fused_computation.59 | convolution fusion | flops 3229614080 | bytes 10498048 | tf_op jit(solution)/shard_map/dot_general | solution.py:302
  572.6 13.7 %all-to-all-done.6 = f32[32,32,2]{1,2,0:T(2,128)S(1)} async-done(((f32[32,32,2]{1,2,0:T(2,128)}), f32[32,32,2]{1,2,0:T(2,128)S(1)}, u32[]{:S(2)}, u32[]{:S(2)}) %all-to-all-start.6) | async-done | bytes 8224 | tf_op jit(solution)/shard_map/all_to_all | solution.py:425
  586.4 10.4 %all-to-all-start.5 = ((bf16[8,128,1024]{2,1,0:T(8,128)(2,1)}), bf16[8,128,1024]{2,1,0:T(8,128)(2,1)S(1)}, u32[]{:S(2)}, u32[]{:S(2)}) async-start(bf16[8,128,1024]{2,1,0:T(8,128)(2,1)} %bitcast.125), calls=%async_computation.5 | async-start | bytes 4194304 | tf_op jit(solution)/shard_map/all_to_all | solution.py:425
  599.6 7.6 collective-permute-start.33
  610.2 7.7 add_convert_fusion.1
  617.9 4.8 add_convert_fusion.3
  624.0 6.7 collective-permute-done.33
  633.0 20.2 %collective-permute-done.32 = bf16[512,1024]{1,0:T(8,128)(2,1)S(1)} collective-permute-done((bf16[512,1024]{1,0:T(8,128)(2,1)S(1)}, bf16[512,1024]{1,0:T(8,128)(2,1)S(1)}, u32[]{:S(2)}, u32[]{:S(2)}) %collective-permute-start.32) | collective-permute-done | bytes 1048608 | tf_op jit(solution)/shard_map/ppermute | solution.py:384
  657.0 9.9 %collective-permute-start.34 = (bf16[512,1024]{1,0:T(8,128)(2,1)S(1)}, bf16[512,1024]{1,0:T(8,128)(2,1)}, u32[]{:S(2)}, u32[]{:S(2)}) collective-permute-start(bf16[512,1024]{1,0:T(8,128)(2,1)S(1)} %get-tuple-element.67), channel_id=1, source_target_pairs={{0,1},{1,2},{2,3},{4,5},{5,6},{6,7},{8,9},{9,10},{10,11},{12,13},{... | collective-permute-start | bytes 3145736 | tf_op jit(solution)/shard_map/ppermute | solution.py:392
  671.2 11.4 %add_convert_fusion = bf16[1024,1024]{1,0:T(8,128)(2,1)} fusion(f32[1024,1024]{1,0:T(8,128)} %copy-done.11, bf16[1024,2816]{1,0:T(8,128)(2,1)} %get-tuple-element.42.h_ref, bf16[2816,1024]{1,0:T(8,128)(2,1)} %get-tuple-element.41.down_ref), kind=kOutput, calls=%fused_computation.30 | convolution fusion | flops 5907677184 | bytes 17825792 | tf_op jit(solution)/shard_map/dot_general | solution.py:302
  685.4 6.8 all-to-all-done.4
  706.0 9.2 %collective-permute-start.45 = (bf16[2368,128]{1,0:T(8,128)(2,1)S(1)}, bf16[2368,128]{1,0:T(8,128)(2,1)S(1)}, u32[]{:S(2)}, u32[]{:S(2)}) collective-permute-start(bf16[2368,128]{1,0:T(8,128)(2,1)S(1)} %get-tuple-element.92), channel_id=1, source_target_pairs={{0,2},{4,6},{8,10},{12,14},{16,18},{20,22},{24,26},{28,30}} | collective-permute-start | bytes 1818632 | tf_op jit(solution)/shard_map/ppermute | solution.py:386
  719.4 9.9 %collective-permute-done.45 = bf16[2368,128]{1,0:T(8,128)(2,1)S(1)} collective-permute-done((bf16[2368,128]{1,0:T(8,128)(2,1)S(1)}, bf16[2368,128]{1,0:T(8,128)(2,1)S(1)}, u32[]{:S(2)}, u32[]{:S(2)}) %collective-permute-start.45) | collective-permute-done | bytes 606240 | tf_op jit(solution)/shard_map/ppermute | solution.py:386
  729.3 11.3 %collective-permute-done.44 = bf16[2368,128]{1,0:T(8,128)(2,1)S(1)} collective-permute-done((bf16[2368,128]{1,0:T(8,128)(2,1)S(1)}, bf16[2368,128]{1,0:T(8,128)(2,1)S(1)}, u32[]{:S(2)}, u32[]{:S(2)}) %collective-permute-start.44) | collective-permute-done | bytes 606240 | tf_op jit(solution)/shard_map/ppermute | solution.py:384
  742.3 9.6 %collective-permute-start.46 = (bf16[2368,128]{1,0:T(8,128)(2,1)S(1)}, bf16[2368,128]{1,0:T(8,128)(2,1)S(1)}, u32[]{:S(2)}, u32[]{:S(2)}) collective-permute-start(bf16[2368,128]{1,0:T(8,128)(2,1)S(1)} %get-tuple-element.87), channel_id=1, source_target_pairs={{0,1},{1,2},{2,3},{4,5},{5,6},{6,7},{8,9},{9,10},{10,11},{12,13},{... | collective-permute-start | bytes 1818632 | tf_op jit(solution)/shard_map/ppermute | solution.py:392
  754.8 9.1 %collective-permute-done.49 = bf16[2368,128]{1,0:T(8,128)(2,1)S(1)} collective-permute-done((bf16[2368,128]{1,0:T(8,128)(2,1)S(1)}, bf16[2368,128]{1,0:T(8,128)(2,1)S(1)}, u32[]{:S(2)}, u32[]{:S(2)}) %collective-permute-start.49) | collective-permute-done | bytes 606240 | tf_op jit(solution)/shard_map/ppermute | solution.py:395
  (298 shorter events, 165.2 us)
Async XLA Ops:
  7.2 124.0 %all-gather.3.cloned.1.call-start = ((), (), s32[]{:S(2)}) async-start(), calls=%async_computation.9 | async-start | bytes 1990656 | tf_op jit(solution)/shard_map/all_gather | solution.py:453
  9.3 24.1 %collective-permute-start.12 = (bf16[2368,128]{1,0:T(8,128)(2,1)}, bf16[2368,128]{1,0:T(8,128)(2,1)S(1)}, u32[]{:S(2)}, u32[]{:S(2)}) collective-permute-start(bf16[2368,128]{1,0:T(8,128)(2,1)} %pad_maximum_fusion.9), channel_id=1, source_target_pairs={{0,1},{1,2},{2,3},{4,5},{5,6},{6,7},{8,9},{9,10},{10,11},{12,13},{... | collective-permute-start | bytes 1818632 | tf_op jit(solution)/shard_map/ppermute | solution.py:360
  14.4 25.4 %collective-permute-start.15 = (bf16[2368,128]{1,0:T(8,128)(2,1)}, bf16[2368,128]{1,0:T(8,128)(2,1)}, u32[]{:S(2)}, u32[]{:S(2)}) collective-permute-start(bf16[2368,128]{1,0:T(8,128)(2,1)} %pad_maximum_fusion.9), channel_id=1, source_target_pairs={{1,0},{2,1},{3,2},{5,4},{6,5},{7,6},{9,8},{10,9},{11,10},{13,12},{... | collective-permute-start | bytes 1818632 | tf_op jit(solution)/shard_map/ppermute | solution.py:361
  17.4 32.5 %collective-permute-start = (bf16[512,1024]{1,0:T(8,128)(2,1)S(1)}, bf16[512,1024]{1,0:T(8,128)(2,1)}, u32[]{:S(2)}, u32[]{:S(2)}) collective-permute-start(bf16[512,1024]{1,0:T(8,128)(2,1)S(1)} %get-tuple-element.96), channel_id=1, source_target_pairs={{0,1},{1,2},{2,3},{4,5},{5,6},{6,7},{8,9},{9,10},{10,11},{12,13},{... | collective-permute-start | bytes 3145736 | tf_op jit(solution)/shard_map/ppermute | solution.py:360
  23.0 32.6 %collective-permute-start.3 = (bf16[512,1024]{1,0:T(8,128)(2,1)S(1)}, bf16[512,1024]{1,0:T(8,128)(2,1)}, u32[]{:S(2)}, u32[]{:S(2)}) collective-permute-start(bf16[512,1024]{1,0:T(8,128)(2,1)S(1)} %get-tuple-element.96), channel_id=1, source_target_pairs={{1,0},{2,1},{3,2},{5,4},{6,5},{7,6},{9,8},{10,9},{11,10},{13,12},{... | collective-permute-start | bytes 3145736 | tf_op jit(solution)/shard_map/ppermute | solution.py:361
  34.9 23.9 %collective-permute-start.14 = (bf16[2368,128]{1,0:T(8,128)(2,1)S(1)}, bf16[2368,128]{1,0:T(8,128)(2,1)}, u32[]{:S(2)}, u32[]{:S(2)}) collective-permute-start(bf16[2368,128]{1,0:T(8,128)(2,1)S(1)} %collective-permute-done.12), channel_id=1, source_target_pairs={{1,2},{2,3},{5,6},{6,7},{9,10},{10,11},{13,14},{14,15},{17,18},{18... | collective-permute-start | bytes 1818632 | tf_op jit(solution)/shard_map/ppermute | solution.py:363
  39.8 127.8 %collective-permute-start.16 = (bf16[2368,128]{1,0:T(8,128)(2,1)}, bf16[2368,128]{1,0:T(8,128)(2,1)}, u32[]{:S(2)}, u32[]{:S(2)}) collective-permute-start(bf16[2368,128]{1,0:T(8,128)(2,1)} %collective-permute-done.15), channel_id=1, source_target_pairs={{1,0},{2,1},{5,4},{6,5},{9,8},{10,9},{13,12},{14,13},{17,16},{18,1... | collective-permute-start | bytes 1818632 | tf_op jit(solution)/shard_map/ppermute | solution.py:364
  56.4 41.9 %collective-permute-start.4 = (bf16[512,1024]{1,0:T(8,128)(2,1)}, bf16[512,1024]{1,0:T(8,128)(2,1)S(1)}, u32[]{:S(2)}, u32[]{:S(2)}) collective-permute-start(bf16[512,1024]{1,0:T(8,128)(2,1)} %collective-permute-done.3), channel_id=1, source_target_pairs={{1,0},{2,1},{5,4},{6,5},{9,8},{10,9},{13,12},{14,13},{17,16},{18,1... | collective-permute-start | bytes 3145736 | tf_op jit(solution)/shard_map/ppermute | solution.py:364
  58.8 60.7 %collective-permute-start.5 = (bf16[512,1024]{1,0:T(8,128)(2,1)}, bf16[512,1024]{1,0:T(8,128)(2,1)S(1)}, u32[]{:S(2)}, u32[]{:S(2)}) collective-permute-start(bf16[512,1024]{1,0:T(8,128)(2,1)} %collective-permute-done.3), channel_id=1, source_target_pairs={{2,0},{6,4},{10,8},{14,12},{18,16},{22,20},{26,24},{30,28}} | collective-permute-start | bytes 3145736 | tf_op jit(solution)/shard_map/ppermute | solution.py:366
  66.7 104.4 %collective-permute-start.17 = (bf16[2368,128]{1,0:T(8,128)(2,1)}, bf16[2368,128]{1,0:T(8,128)(2,1)}, u32[]{:S(2)}, u32[]{:S(2)}) collective-permute-start(bf16[2368,128]{1,0:T(8,128)(2,1)} %collective-permute-done.15), channel_id=1, source_target_pairs={{2,0},{6,4},{10,8},{14,12},{18,16},{22,20},{26,24},{30,28}} | collective-permute-start | bytes 1818632 | tf_op jit(solution)/shard_map/ppermute | solution.py:366
  120.1 45.7 %collective-permute-start.6 = (bf16[512,1024]{1,0:T(8,128)(2,1)S(1)}, bf16[512,1024]{1,0:T(8,128)(2,1)}, u32[]{:S(2)}, u32[]{:S(2)}) collective-permute-start(bf16[512,1024]{1,0:T(8,128)(2,1)S(1)} %get-tuple-element.31), channel_id=1, source_target_pairs={{0,1},{1,2},{2,3},{4,5},{5,6},{6,7},{8,9},{9,10},{10,11},{12,13},{... | collective-permute-start | bytes 3145736 | tf_op jit(solution)/shard_map/ppermute | solution.py:360
  129.0 36.8 %collective-permute-start.7 = (bf16[512,1024]{1,0:T(8,128)(2,1)S(1)}, bf16[512,1024]{1,0:T(8,128)(2,1)}, u32[]{:S(2)}, u32[]{:S(2)}) collective-permute-start(bf16[512,1024]{1,0:T(8,128)(2,1)S(1)} %get-tuple-element.31), channel_id=1, source_target_pairs={{1,0},{2,1},{3,2},{5,4},{6,5},{7,6},{9,8},{10,9},{11,10},{13,12},{... | collective-permute-start | bytes 3145736 | tf_op jit(solution)/shard_map/ppermute | solution.py:361
  165.7 27.3 %collective-permute-start.8 = (bf16[512,1024]{1,0:T(8,128)(2,1)}, bf16[512,1024]{1,0:T(8,128)(2,1)}, u32[]{:S(2)}, u32[]{:S(2)}) collective-permute-start(bf16[512,1024]{1,0:T(8,128)(2,1)} %collective-permute-done.6), channel_id=1, source_target_pairs={{1,3},{5,7},{9,11},{13,15},{17,19},{21,23},{25,27},{29,31}} | collective-permute-start | bytes 3145736 | tf_op jit(solution)/shard_map/ppermute | solution.py:365
  169.5 34.8 %collective-permute-start.9 = (bf16[512,1024]{1,0:T(8,128)(2,1)}, bf16[512,1024]{1,0:T(8,128)(2,1)}, u32[]{:S(2)}, u32[]{:S(2)}) collective-permute-start(bf16[512,1024]{1,0:T(8,128)(2,1)} %collective-permute-done.6), channel_id=1, source_target_pairs={{1,2},{2,3},{5,6},{6,7},{9,10},{10,11},{13,14},{14,15},{17,18},{18... | collective-permute-start | bytes 3145736 | tf_op jit(solution)/shard_map/ppermute | solution.py:363
  173.0 40.0 %collective-permute-start.10 = (bf16[512,1024]{1,0:T(8,128)(2,1)}, bf16[512,1024]{1,0:T(8,128)(2,1)}, u32[]{:S(2)}, u32[]{:S(2)}) collective-permute-start(bf16[512,1024]{1,0:T(8,128)(2,1)} %collective-permute-done.7), channel_id=1, source_target_pairs={{1,0},{2,1},{5,4},{6,5},{9,8},{10,9},{13,12},{14,13},{17,16},{18,1... | collective-permute-start | bytes 3145736 | tf_op jit(solution)/shard_map/ppermute | solution.py:364
  174.3 67.9 %collective-permute-start.11 = (bf16[512,1024]{1,0:T(8,128)(2,1)}, bf16[512,1024]{1,0:T(8,128)(2,1)}, u32[]{:S(2)}, u32[]{:S(2)}) collective-permute-start(bf16[512,1024]{1,0:T(8,128)(2,1)} %collective-permute-done.7), channel_id=1, source_target_pairs={{2,0},{6,4},{10,8},{14,12},{18,16},{22,20},{26,24},{30,28}} | collective-permute-start | bytes 3145736 | tf_op jit(solution)/shard_map/ppermute | solution.py:366
  178.7 82.0 %collective-permute-start.18 = (bf16[4736,128]{1,0:T(8,128)(2,1)}, bf16[4736,128]{1,0:T(8,128)(2,1)}, u32[]{:S(2)}, u32[]{:S(2)}) collective-permute-start(bf16[4736,128]{1,0:T(8,128)(2,1)} %get-tuple-element.66.refs_0_), channel_id=1, source_target_pairs={{0,4},{4,0},{8,12},{12,8},{16,20},{20,16},{24,28},{28,24},{1,5},{5... | collective-permute-start | bytes 3637256 | tf_op jit(solution)/shard_map/ppermute | solution.py:407
  179.9 125.0 %all-to-all-start = ((bf16[256,4,512]{2,0,1:T(8,128)(2,1)}), bf16[256,4,512]{2,0,1:T(8,128)(2,1)}, u32[]{:S(2)}, u32[]{:S(2)}) async-start(bf16[256,4,512]{2,0,1:T(8,128)(2,1)} %bitcast.117), calls=%async_computation | async-start | bytes 2097152 | tf_op jit(solution)/shard_map/all_to_all | solution.py:503
  193.0 67.7 %collective-permute-start.20 = (bf16[4736,128]{1,0:T(8,128)(2,1)}, bf16[4736,128]{1,0:T(8,128)(2,1)}, u32[]{:S(2)}, u32[]{:S(2)}) collective-permute-start(bf16[4736,128]{1,0:T(8,128)(2,1)} %get-tuple-element.66.refs_0_), channel_id=1, source_target_pairs={{0,8},{4,12},{8,0},{12,4},{16,24},{20,28},{24,16},{28,20},{1,9},{5... | collective-permute-start | bytes 3637256 | tf_op jit(solution)/shard_map/ppermute | solution.py:409
  204.2 56.6 %collective-permute-start.19 = (bf16[4736,128]{1,0:T(8,128)(2,1)S(1)}, bf16[4736,128]{1,0:T(8,128)(2,1)S(1)}, u32[]{:S(2)}, u32[]{:S(2)}) collective-permute-start(bf16[4736,128]{1,0:T(8,128)(2,1)S(1)} %get-tuple-element.65.refs_1_), channel_id=1, source_target_pairs={{0,4},{4,0},{8,12},{12,8},{16,20},{20,16},{24,28},{28,24},{1,5},{5... | collective-permute-start | bytes 3637256 | tf_op jit(solution)/shard_map/ppermute | solution.py:407
  213.1 96.4 %collective-permute-start.21 = (bf16[4736,128]{1,0:T(8,128)(2,1)S(1)}, bf16[4736,128]{1,0:T(8,128)(2,1)}, u32[]{:S(2)}, u32[]{:S(2)}) collective-permute-start(bf16[4736,128]{1,0:T(8,128)(2,1)S(1)} %get-tuple-element.65.refs_1_), channel_id=1, source_target_pairs={{0,8},{4,12},{8,0},{12,4},{16,24},{20,28},{24,16},{28,20},{1,9},{5... | collective-permute-start | bytes 3637256 | tf_op jit(solution)/shard_map/ppermute | solution.py:410
  242.3 35.8 %collective-permute-start.25 = (bf16[4736,128]{1,0:T(8,128)(2,1)S(1)}, bf16[4736,128]{1,0:T(8,128)(2,1)}, u32[]{:S(2)}, u32[]{:S(2)}) collective-permute-start(bf16[4736,128]{1,0:T(8,128)(2,1)S(1)} %get-tuple-element.65.refs_1_), channel_id=1, source_target_pairs={{0,16},{4,20},{8,24},{12,28},{16,0},{20,4},{24,8},{28,12},{1,17},{... | collective-permute-start | bytes 3637256 | tf_op jit(solution)/shard_map/ppermute | solution.py:409
  260.7 48.9 %collective-permute-start.24 = (bf16[4736,128]{1,0:T(8,128)(2,1)}, bf16[4736,128]{1,0:T(8,128)(2,1)}, u32[]{:S(2)}, u32[]{:S(2)}) collective-permute-start(bf16[4736,128]{1,0:T(8,128)(2,1)} %get-tuple-element.66.refs_0_), channel_id=1, source_target_pairs={{0,16},{4,20},{8,24},{12,28},{16,0},{20,4},{24,8},{28,12},{1,17},{... | collective-permute-start | bytes 3637256 | tf_op jit(solution)/shard_map/ppermute | solution.py:410
  260.8 49.3 %collective-permute-start.22 = (bf16[4736,128]{1,0:T(8,128)(2,1)}, bf16[4736,128]{1,0:T(8,128)(2,1)}, u32[]{:S(2)}, u32[]{:S(2)}) collective-permute-start(bf16[4736,128]{1,0:T(8,128)(2,1)} %collective-permute-done.20.refs_4_), channel_id=1, source_target_pairs={{0,4},{4,0},{8,12},{12,8},{16,20},{20,16},{24,28},{28,24},{1,5},{5... | collective-permute-start | bytes 3637256 | tf_op jit(solution)/shard_map/ppermute | solution.py:407
  260.9 66.3 %collective-permute-start.28 = (bf16[4736,128]{1,0:T(8,128)(2,1)}, bf16[4736,128]{1,0:T(8,128)(2,1)}, u32[]{:S(2)}, u32[]{:S(2)}) collective-permute-start(bf16[4736,128]{1,0:T(8,128)(2,1)} %collective-permute-done.20.refs_4_), channel_id=1, source_target_pairs={{0,16},{4,20},{8,24},{12,28},{16,0},{20,4},{24,8},{28,12},{1,17},{... | collective-permute-start | bytes 3637256 | tf_op jit(solution)/shard_map/ppermute | solution.py:411
  278.1 49.1 %collective-permute-start.29 = (bf16[4736,128]{1,0:T(8,128)(2,1)}, bf16[4736,128]{1,0:T(8,128)(2,1)}, u32[]{:S(2)}, u32[]{:S(2)}) collective-permute-start(bf16[4736,128]{1,0:T(8,128)(2,1)} %collective-permute-done.25.refs_9_), channel_id=1, source_target_pairs={{0,8},{4,12},{8,0},{12,4},{16,24},{20,28},{24,16},{28,20},{1,9},{5... | collective-permute-start | bytes 3637256 | tf_op jit(solution)/shard_map/ppermute | solution.py:411
  304.9 41.7 %all-to-all-start.1 = ((bf16[256,4,512]{2,0,1:T(8,128)(2,1)}), bf16[256,4,512]{2,0,1:T(8,128)(2,1)}, u32[]{:S(2)}, u32[]{:S(2)}) async-start(bf16[256,4,512]{2,0,1:T(8,128)(2,1)} %bitcast.118), calls=%async_computation.1 | async-start | bytes 2097152 | tf_op jit(solution)/shard_map/all_to_all | solution.py:503
  405.6 29.8 %all-to-all-start.2 = ((bf16[4,256,512]{2,1,0:T(8,128)(2,1)}), bf16[4,256,512]{2,1,0:T(8,128)(2,1)S(1)}, u32[]{:S(2)}, u32[]{:S(2)}) async-start(bf16[4,256,512]{2,1,0:T(8,128)(2,1)} %bitcast.28), calls=%async_computation.2 | async-start | bytes 2097152 | tf_op jit(solution)/shard_map/all_to_all | solution.py:530
  409.1 294.8 %reduce-scatter.2.cloned.1.call-start = ((), (), s32[]{:S(2)}) async-start(), calls=%async_computation.8 | async-start | bytes 19464192 | tf_op jit(solution)/shard_map/reduce_scatter | solution.py:347
  436.5 29.6 %all-to-all-start.3 = ((bf16[4,256,512]{2,1,0:T(8,128)(2,1)}), bf16[4,256,512]{2,1,0:T(8,128)(2,1)S(1)}, u32[]{:S(2)}, u32[]{:S(2)}) async-start(bf16[4,256,512]{2,1,0:T(8,128)(2,1)} %bitcast.31), calls=%async_computation.3 | async-start | bytes 2097152 | tf_op jit(solution)/shard_map/all_to_all | solution.py:530
  539.6 67.6 %collective-permute-start.39 = (bf16[512,1024]{1,0:T(8,128)(2,1)}, bf16[512,1024]{1,0:T(8,128)(2,1)S(1)}, u32[]{:S(2)}, u32[]{:S(2)}) collective-permute-start(bf16[512,1024]{1,0:T(8,128)(2,1)} %get-tuple-element.78), channel_id=1, source_target_pairs={{0,2},{4,6},{8,10},{12,14},{16,18},{20,22},{24,26},{28,30}} | collective-permute-start | bytes 3145736 | tf_op jit(solution)/shard_map/ppermute | solution.py:386
  541.5 67.1 %collective-permute-start.38 = (bf16[512,1024]{1,0:T(8,128)(2,1)}, bf16[512,1024]{1,0:T(8,128)(2,1)}, u32[]{:S(2)}, u32[]{:S(2)}) collective-permute-start(bf16[512,1024]{1,0:T(8,128)(2,1)} %get-tuple-element.75), channel_id=1, source_target_pairs={{0,1},{1,2},{4,5},{5,6},{8,9},{9,10},{12,13},{13,14},{16,17},{17,1... | collective-permute-start | bytes 3145736 | tf_op jit(solution)/shard_map/ppermute | solution.py:384
  543.7 65.6 %collective-permute-start.42 = (bf16[512,1024]{1,0:T(8,128)(2,1)}, bf16[512,1024]{1,0:T(8,128)(2,1)}, u32[]{:S(2)}, u32[]{:S(2)}) collective-permute-start(bf16[512,1024]{1,0:T(8,128)(2,1)} %get-tuple-element.76), channel_id=1, source_target_pairs={{3,1},{7,5},{11,9},{15,13},{19,17},{23,21},{27,25},{31,29}} | collective-permute-start | bytes 3145736 | tf_op jit(solution)/shard_map/ppermute | solution.py:387
  547.7 38.7 %all-to-all-start.6 = ((f32[32,32,2]{1,2,0:T(2,128)}), f32[32,32,2]{1,2,0:T(2,128)S(1)}, u32[]{:S(2)}, u32[]{:S(2)}) async-start(f32[32,32,2]{1,2,0:T(2,128)} %copy.36), calls=%async_computation.7 | async-start | bytes 65536 | tf_op jit(solution)/shard_map/all_to_all | solution.py:425
  571.0 46.9 %collective-permute-start.41 = (bf16[512,1024]{1,0:T(8,128)(2,1)}, bf16[512,1024]{1,0:T(8,128)(2,1)}, u32[]{:S(2)}, u32[]{:S(2)}) collective-permute-start(bf16[512,1024]{1,0:T(8,128)(2,1)} %get-tuple-element.77), channel_id=1, source_target_pairs={{3,2},{2,1},{7,6},{6,5},{11,10},{10,9},{15,14},{14,13},{19,18},{18... | collective-permute-start | bytes 3145736 | tf_op jit(solution)/shard_map/ppermute | solution.py:385
  586.4 80.5 %all-to-all-start.5 = ((bf16[8,128,1024]{2,1,0:T(8,128)(2,1)}), bf16[8,128,1024]{2,1,0:T(8,128)(2,1)S(1)}, u32[]{:S(2)}, u32[]{:S(2)}) async-start(bf16[8,128,1024]{2,1,0:T(8,128)(2,1)} %bitcast.125), calls=%async_computation.5 | async-start | bytes 4194304 | tf_op jit(solution)/shard_map/all_to_all | solution.py:425
  599.6 31.1 %collective-permute-start.33 = (bf16[512,1024]{1,0:T(8,128)(2,1)S(1)}, bf16[512,1024]{1,0:T(8,128)(2,1)S(1)}, u32[]{:S(2)}, u32[]{:S(2)}) collective-permute-start(bf16[512,1024]{1,0:T(8,128)(2,1)S(1)} %get-tuple-element.72), channel_id=1, source_target_pairs={{0,2},{4,6},{8,10},{12,14},{16,18},{20,22},{24,26},{28,30}} | collective-permute-start | bytes 3145736 | tf_op jit(solution)/shard_map/ppermute | solution.py:386
  607.2 46.0 %collective-permute-start.32 = (bf16[512,1024]{1,0:T(8,128)(2,1)S(1)}, bf16[512,1024]{1,0:T(8,128)(2,1)S(1)}, u32[]{:S(2)}, u32[]{:S(2)}) collective-permute-start(bf16[512,1024]{1,0:T(8,128)(2,1)S(1)} %get-tuple-element.69), channel_id=1, source_target_pairs={{0,1},{1,2},{4,5},{5,6},{8,9},{9,10},{12,13},{13,14},{16,17},{17,1... | collective-permute-start | bytes 3145736 | tf_op jit(solution)/shard_map/ppermute | solution.py:384
  608.6 44.6 %collective-permute-start.36 = (bf16[512,1024]{1,0:T(8,128)(2,1)S(1)}, bf16[512,1024]{1,0:T(8,128)(2,1)S(1)}, u32[]{:S(2)}, u32[]{:S(2)}) collective-permute-start(bf16[512,1024]{1,0:T(8,128)(2,1)S(1)} %get-tuple-element.70), channel_id=1, source_target_pairs={{3,1},{7,5},{11,9},{15,13},{19,17},{23,21},{27,25},{31,29}} | collective-permute-start | bytes 3145736 | tf_op jit(solution)/shard_map/ppermute | solution.py:387
  609.4 43.8 %collective-permute-start.35 = (bf16[512,1024]{1,0:T(8,128)(2,1)S(1)}, bf16[512,1024]{1,0:T(8,128)(2,1)S(1)}, u32[]{:S(2)}, u32[]{:S(2)}) collective-permute-start(bf16[512,1024]{1,0:T(8,128)(2,1)S(1)} %get-tuple-element.71), channel_id=1, source_target_pairs={{3,2},{2,1},{7,6},{6,5},{11,10},{10,9},{15,14},{14,13},{19,18},{18... | collective-permute-start | bytes 3145736 | tf_op jit(solution)/shard_map/ppermute | solution.py:385
  622.7 71.9 %collective-permute-start.43 = (bf16[512,1024]{1,0:T(8,128)(2,1)}, bf16[512,1024]{1,0:T(8,128)(2,1)}, u32[]{:S(2)}, u32[]{:S(2)}) collective-permute-start(bf16[512,1024]{1,0:T(8,128)(2,1)} %get-tuple-element.74), channel_id=1, source_target_pairs={{1,0},{2,1},{3,2},{5,4},{6,5},{7,6},{9,8},{10,9},{11,10},{13,12},{... | collective-permute-start | bytes 3145736 | tf_op jit(solution)/shard_map/ppermute | solution.py:395
  630.7 63.9 %collective-permute-start.40 = (bf16[512,1024]{1,0:T(8,128)(2,1)}, bf16[512,1024]{1,0:T(8,128)(2,1)}, u32[]{:S(2)}, u32[]{:S(2)}) collective-permute-start(bf16[512,1024]{1,0:T(8,128)(2,1)} %get-tuple-element.73), channel_id=1, source_target_pairs={{0,1},{1,2},{2,3},{4,5},{5,6},{6,7},{8,9},{9,10},{10,11},{12,13},{... | collective-permute-start | bytes 3145736 | tf_op jit(solution)/shard_map/ppermute | solution.py:392
  655.7 41.3 %collective-permute-start.37 = (bf16[512,1024]{1,0:T(8,128)(2,1)}, bf16[512,1024]{1,0:T(8,128)(2,1)}, u32[]{:S(2)}, u32[]{:S(2)}) collective-permute-start(bf16[512,1024]{1,0:T(8,128)(2,1)} %get-tuple-element.68), channel_id=1, source_target_pairs={{1,0},{2,1},{3,2},{5,4},{6,5},{7,6},{9,8},{10,9},{11,10},{13,12},{... | collective-permute-start | bytes 3145736 | tf_op jit(solution)/shard_map/ppermute | solution.py:395
  657.0 40.5 %collective-permute-start.34 = (bf16[512,1024]{1,0:T(8,128)(2,1)S(1)}, bf16[512,1024]{1,0:T(8,128)(2,1)}, u32[]{:S(2)}, u32[]{:S(2)}) collective-permute-start(bf16[512,1024]{1,0:T(8,128)(2,1)S(1)} %get-tuple-element.67), channel_id=1, source_target_pairs={{0,1},{1,2},{2,3},{4,5},{5,6},{6,7},{8,9},{9,10},{10,11},{12,13},{... | collective-permute-start | bytes 3145736 | tf_op jit(solution)/shard_map/ppermute | solution.py:392
  666.9 25.3 %all-to-all-start.4 = ((bf16[8,128,768]{2,1,0:T(8,128)(2,1)}), bf16[8,128,768]{2,1,0:T(8,128)(2,1)}, u32[]{:S(2)}, u32[]{:S(2)}) async-start(bf16[8,128,768]{2,1,0:T(8,128)(2,1)} %bitcast.133), calls=%async_computation.4 | async-start | bytes 3145728 | tf_op jit(solution)/shard_map/all_to_all | solution.py:425
  706.0 23.3 %collective-permute-start.45 = (bf16[2368,128]{1,0:T(8,128)(2,1)S(1)}, bf16[2368,128]{1,0:T(8,128)(2,1)S(1)}, u32[]{:S(2)}, u32[]{:S(2)}) collective-permute-start(bf16[2368,128]{1,0:T(8,128)(2,1)S(1)} %get-tuple-element.92), channel_id=1, source_target_pairs={{0,2},{4,6},{8,10},{12,14},{16,18},{20,22},{24,26},{28,30}} | collective-permute-start | bytes 1818632 | tf_op jit(solution)/shard_map/ppermute | solution.py:386
  715.2 25.3 %collective-permute-start.44 = (bf16[2368,128]{1,0:T(8,128)(2,1)S(1)}, bf16[2368,128]{1,0:T(8,128)(2,1)S(1)}, u32[]{:S(2)}, u32[]{:S(2)}) collective-permute-start(bf16[2368,128]{1,0:T(8,128)(2,1)S(1)} %get-tuple-element.89), channel_id=1, source_target_pairs={{0,1},{1,2},{4,5},{5,6},{8,9},{9,10},{12,13},{13,14},{16,17},{17,1... | collective-permute-start | bytes 1818632 | tf_op jit(solution)/shard_map/ppermute | solution.py:384
  716.6 24.0 %collective-permute-start.48 = (bf16[2368,128]{1,0:T(8,128)(2,1)S(1)}, bf16[2368,128]{1,0:T(8,128)(2,1)S(1)}, u32[]{:S(2)}, u32[]{:S(2)}) collective-permute-start(bf16[2368,128]{1,0:T(8,128)(2,1)S(1)} %get-tuple-element.90), channel_id=1, source_target_pairs={{3,1},{7,5},{11,9},{15,13},{19,17},{23,21},{27,25},{31,29}} | collective-permute-start | bytes 1818632 | tf_op jit(solution)/shard_map/ppermute | solution.py:387
  (60 other events, 1282.9 us)
Sparse Core Ops, SparseCore 0:
  26.2 29.5 all-gather.2
  436.6 118.1 reduce-scatter.1

commit v3 on v2

--- a/solution.py
+++ b/solution.py
@@ -353,13 +353,12 @@
     return near_right, near_left
 
 
-def line_gather(piece, axis, hold=lambda *arrays: arrays):
+def line_gather(piece, axis):
     count, me = lax.axis_size(axis), lax.axis_index(axis)
     assert count == 4
     near_right, near_left = line_steps(count)
     one_left = lax.ppermute(piece, axis, near_right)
     one_right = lax.ppermute(piece, axis, near_left)
-    one_left, one_right = hold(one_left, one_right)
     two_left = lax.ppermute(one_left, axis, [(1, 2), (2, 3)])
     two_right = lax.ppermute(one_right, axis, [(1, 0), (2, 1)])
     three_left = lax.ppermute(one_left, axis, [(1, 3)])
@@ -482,11 +481,7 @@
         starts.append(start[None])
         lows.append(start[::BQ] // BK)
         if m == 1:
-            def after_first(left, right):
-                left, right, mixed[0] = lax.optimization_barrier((left, right, mixed[0]))
-                return left, right
-
-            rows_all[1] = line_gather(second_piece, "mp", after_first)
+            rows_all[1] = line_gather(second_piece, "mp")
         rows = rows_all[m].astype(jnp.float32)
         factors.append(rms_factor(rows))
         normed.append((rows * factors[m] * gain_one).astype(low))
@@ -554,7 +549,9 @@
         gain_attn_part = gain_attn_part + jnp.sum(
             spread.astype(jnp.float32) * rows_all[m].astype(jnp.float32) * factors[m], axis=0
         )
-    grad_w = sum(dot_dims(normed[m], grad_qkv[m], 0, 1) for m in range(batches))
+    grad_w = 0.0
+    for m in range(batches):
+        grad_w = grad_w + dot_dims(normed[m], grad_qkv[m], 0, 1)
 
     own_out = exchange_sum(grad_output, "dp").astype(low).T.reshape(n_mp, cols, depth)
     own_ffn = mine.reshape(3, n_mp, hidden_part, depth).transpose(1, 0, 2, 3)
@@ -569,7 +566,9 @@
     grad_normed_attn = jnp.concatenate(grad_normed, axis=0)
     grad_lower, _ = rms_back(in_float, rms_factor(in_float), gain_one, grad_normed_attn)
     grad_inputs = (grad_hidden_in + grad_lower).astype(low)
-    grad_norms = exchange_sum(jnp.stack([gain_attn_part, gain_ffn_part], axis=1), ("dp", "mp")).T
+    grad_norms = exchange_sum(
+        jnp.stack([gain_attn_part, gain_ffn_part], axis=1), ("dp", "mp")
+    ).T
     return (
         result.reshape(inputs.shape),
         grad_inputs.reshape(inputs.shape),

time: 786 us -> 759 us (0.966)
  waiting for transfers between devices: 220 us -> 205 us
  starting transfers between devices: 181 us -> 167 us
    ppermute x1, starting transfers between devices: 10.1 us -> 0.08 us  [plane_gather(): lax.ppermute(low, axis, across)]
    ppermute x1, waiting for transfers between devices: 17 us -> 7.51 us  [plane_gather(): lax.ppermute(top_x, axis, along)]
    ppermute x3, waiting for transfers between devices: 32.2 us -> 40.8 us  [line_gather(): two_right = lax.ppermute(one_right, axis, [(1, 0), (2, 1)])]
    ppermute x1, starting transfers between devices: 8.2 us -> 0.32 us  [plane_gather(): lax.ppermute(low, axis, along)]
    unnamed x125 -> x113, local copies, waits for them, and re-layouts: 28.7 us -> 28.6 us
  transfers between devices with their start and end apart: 59 -> 59, of which waited for: 21 -> 21; matrix products, arithmetic and copies ran while one was open for 18% -> 19% of each run, Pallas kernels for 18% -> 18%
where the time goes in v3:
time: 759 us; the launch traced here: 748 us
  waiting for transfers between devices  205 us (27%)
  starting transfers between devices  167 us (22%)
  Pallas kernels  163 us (21%)
  matrix products  86.3 us (11%)
  local copies, waits for them, and re-layouts  59.5 us (8%)
  other arithmetic  46.2 us (6%)
  between operations  21 us (3%)
    dot_general x12, matrix products, dot_dims(): lax.dot_general(left, right, (((left_dim,), (right_dim,)), ((), ())), pre...  86.3 us
    pallas_call x2, Pallas kernels, attn_bwd(): pl.pallas_call(functools.partial(attn_bwd_kernel, bq=bq, bk=bk, heads=hps...  52.8 us
    pallas_call x2, Pallas kernels, attn_fwd(): pl.pallas_call(functools.partial(attn_fwd_kernel, bq=bq, bk=bk, heads=hps...  44.9 us
    ppermute x3, waiting for transfers between devices, line_gather(): two_right = lax.ppermute(one_right, axis, [(1, 0), (2, 1)])  40.8 us
    ppermute x3, waiting for transfers between devices, line_gather(): three_right = lax.ppermute(one_right, axis, [(2, 0)])  35.7 us
    ppermute x3, waiting for transfers between devices, line_scatter(): two_right = lax.ppermute(block(2), axis, [(0, 1), (1, 2)])  31.5 us
    all_to_all x3, starting transfers between devices, exchange_sum(): lax.all_to_all(parts, axis, split_axis=0, concat_axis=0, tiled=True)  29.9 us
    unnamed x113, local copies, waits for them, and re-layouts  28.6 us
  transfers between devices with their start and end apart: 59, of which 21 were waited for; matrix products, arithmetic and copies ran while one was open for 19% of the time, Pallas kernels for 18%

profile of v3, /device:TPU:0, one launch (start us, length us, event | category | flops | bytes accessed | tf_op | source)
XLA Modules:
  0.0 747.9 jit_solution(17806110383284329412)
XLA Ops:
  8.4 5.1 collective-permute-start.12
  17.5 5.7 collective-permute-start
  58.3 14.6 %collective-permute-done.16 = bf16[2368,128]{1,0:T(8,128)(2,1)S(1)} collective-permute-done((bf16[2368,128]{1,0:T(8,128)(2,1)S(1)}, bf16[2368,128]{1,0:T(8,128)(2,1)S(1)}, u32[]{:S(2)}, u32[]{:S(2)}) %collective-permute-start.16) | collective-permute-done | bytes 606240 | tf_op jit(solution)/shard_map/ppermute | solution.py:363
  74.3 14.0 %collective-permute-done.17 = bf16[2368,128]{1,0:T(8,128)(2,1)S(1)} collective-permute-done((bf16[2368,128]{1,0:T(8,128)(2,1)S(1)}, bf16[2368,128]{1,0:T(8,128)(2,1)S(1)}, u32[]{:S(2)}, u32[]{:S(2)}) %collective-permute-start.17) | collective-permute-done | bytes 606240 | tf_op jit(solution)/shard_map/ppermute | solution.py:365
  93.3 26.1 %collective-permute-done.4 = bf16[512,1024]{1,0:T(8,128)(2,1)S(1)} collective-permute-done((bf16[512,1024]{1,0:T(8,128)(2,1)}, bf16[512,1024]{1,0:T(8,128)(2,1)S(1)}, u32[]{:S(2)}, u32[]{:S(2)}) %collective-permute-start.4) | collective-permute-done | bytes 1048608 | tf_op jit(solution)/shard_map/ppermute | solution.py:363
  119.5 11.2 %collective-permute-done.5 = bf16[512,1024]{1,0:T(8,128)(2,1)S(1)} collective-permute-done((bf16[512,1024]{1,0:T(8,128)(2,1)}, bf16[512,1024]{1,0:T(8,128)(2,1)S(1)}, u32[]{:S(2)}, u32[]{:S(2)}) %collective-permute-start.5) | collective-permute-done | bytes 1048608 | tf_op jit(solution)/shard_map/ppermute | solution.py:365
  138.3 5.7 fusion.20
  156.5 22.5 %attn_fwd.2 = (bf16[256,2048]{1,0:T(8,128)(2,1)}, f32[4,1,2048]{2,1,0:T(1,128)}) custom-call(s32[4]{0:T(128)} %get-tuple-element.125.lo_ref, bf16[768,2048]{1,0:T(8,128)(2,1)} %pad_maximum_fusion.1.q_ref.k_ref.v_ref, bf16[768,2048]{1,0:T(8,128)(2,1)} %pad_maximum_fusion.1.q_ref.k_ref.v_ref, bf16[768,2048]{1,0:T(8,128)(2,1)} %pad_maximum_fusion.1.q_ref.k_ref.v_ref, ...), custom_call_target="tpu_custom_call" | custom-call | flops 4294967296 | bytes 4194304 | tf_op jit(solution)/shard_map/attn_fwd/pallas_call | solution.py:120
  181.4 14.2 %all-to-all-start = ((bf16[256,4,512]{2,0,1:T(8,128)(2,1)}), bf16[256,4,512]{2,0,1:T(8,128)(2,1)}, u32[]{:S(2)}, u32[]{:S(2)}) async-start(bf16[256,4,512]{2,0,1:T(8,128)(2,1)} %bitcast.117), calls=%async_computation | async-start | bytes 2097152 | tf_op jit(solution)/shard_map/all_to_all | solution.py:498
  195.5 9.9 %collective-permute-start.20 = (bf16[4736,128]{1,0:T(8,128)(2,1)}, bf16[4736,128]{1,0:T(8,128)(2,1)}, u32[]{:S(2)}, u32[]{:S(2)}) collective-permute-start(bf16[4736,128]{1,0:T(8,128)(2,1)} %get-tuple-element.60.refs_0_), channel_id=1, source_target_pairs={{0,8},{4,12},{8,0},{12,4},{16,24},{20,28},{24,16},{28,20},{1,9},{5... | collective-permute-start | bytes 3637256 | tf_op jit(solution)/shard_map/ppermute | solution.py:408
  213.5 10.5 %collective-permute-done.11 = bf16[512,1024]{1,0:T(8,128)(2,1)} collective-permute-done((bf16[512,1024]{1,0:T(8,128)(2,1)}, bf16[512,1024]{1,0:T(8,128)(2,1)}, u32[]{:S(2)}, u32[]{:S(2)}) %collective-permute-start.11) | collective-permute-done | bytes 1048608 | tf_op jit(solution)/shard_map/ppermute | solution.py:365
  228.6 3.9 fusion.25
  236.7 16.9 %collective-permute-done.25.refs_9_ = bf16[4736,128]{1,0:T(8,128)(2,1)} collective-permute-done((bf16[4736,128]{1,0:T(8,128)(2,1)S(1)}, bf16[4736,128]{1,0:T(8,128)(2,1)}, u32[]{:S(2)}, u32[]{:S(2)}) %collective-permute-start.25) | collective-permute-done | bytes 1212448 | tf_op jit(solution)/shard_map/ppermute | solution.py:408
  257.2 22.4 %attn_fwd.3 = (bf16[256,2048]{1,0:T(8,128)(2,1)}, f32[4,1,2048]{2,1,0:T(1,128)}) custom-call(s32[4]{0:T(128)} %get-tuple-element.124.lo_ref, bf16[768,2048]{1,0:T(8,128)(2,1)} %pad_maximum_fusion.2.q_ref.k_ref.v_ref, bf16[768,2048]{1,0:T(8,128)(2,1)} %pad_maximum_fusion.2.q_ref.k_ref.v_ref, bf16[768,2048]{1,0:T(8,128)(2,1)} %pad_maximum_fusion.2.q_ref.k_ref.v_ref, ...), custom_call_target="tpu_custom_call" | custom-call | flops 4294967296 | bytes 4194304 | tf_op jit(solution)/shard_map/attn_fwd/pallas_call | solution.py:120
  281.9 4.7 all-to-all-start.1
  287.2 7.5 %collective-permute-done.28.refs_12_ = bf16[4736,128]{1,0:T(8,128)(2,1)} collective-permute-done((bf16[4736,128]{1,0:T(8,128)(2,1)}, bf16[4736,128]{1,0:T(8,128)(2,1)}, u32[]{:S(2)}, u32[]{:S(2)}) %collective-permute-start.28) | collective-permute-done | bytes 1212448 | tf_op jit(solution)/shard_map/ppermute | solution.py:410
  299.7 14.4 %assemble.1 = (bf16[1024,1024]{1,0:T(8,128)(2,1)}, bf16[2816,1024]{1,0:T(8,128)(2,1)}, bf16[2816,1024]{1,0:T(8,128)(2,1)}, bf16[2816,1024]{1,0:T(8,128)(2,1)}) custom-call(s32[8]{0:T(128)} %xor_multiply_fusion.lane_ref, bf16[4736,128]{1,0:T(8,128)(2,1)} %get-tuple-element.60.refs_0_, bf16[4736,128]{1,0:T(8,128)(2,1)} %copy-done.15, ...), custom_call_target="tpu_custom_call" | custom-call | bytes 38797312 | tf_op jit(solution)/shard_map/assemble/pallas_call | solution.py:209
  314.1 4.9 multiply_reduce_fusion.2
  322.7 25.9 %ffn_main.1 = (bf16[1024,2816]{1,0:T(8,128)(2,1)}, bf16[1024,2816]{1,0:T(8,128)(2,1)}, bf16[1024,2816]{1,0:T(8,128)(2,1)}) custom-call(bf16[1024,1024]{1,0:T(8,128)(2,1)} %multiply_convert_fusion.x_ref, bf16[1024,1024]{1,0:T(8,128)(2,1)} %bitcast.126, bf16[2816,1024]{1,0:T(8,128)(2,1)} %get-tuple-element.33.gate_ref, ...), custom_call_target="tpu_custom_call" | custom-call | flops 17716740096 | bytes 34603008 | tf_op jit(solution)/shard_map/ffn_main/pallas_call | solution.py:264
  348.6 10.0 %fusion.48 = f32[1024,1024]{1,0:T(8,128)S(1)} fusion(bf16[1024,2816]{1,0:T(8,128)(2,1)} %get-tuple-element.38.du_ref, bf16[2816,1024]{1,0:T(8,128)(2,1)} %get-tuple-element.34.up_ref), kind=kOutput, calls=%fused_computation.186 | convolution fusion | flops 5905580032 | bytes 15728640 | tf_op jit(solution)/shard_map/dot_general | solution.py:302
  358.6 9.0 %multiply_reduce_fusion = (f32[1024]{0:T(1024)S(1)}, f32[1024]{0:T(1024)S(1)}, f32[1024,1024]{1,0:T(8,128)S(1)}) fusion(f32[1024,1024]{1,0:T(8,128)S(1)} %copy-done.12, f32[1024]{0:T(1024)S(1)} %get-tuple-element.110, f32[1024]{0:T(1024)S(1)} %bitcast.146, f32[1024,1024]{1,0:T(8,128)S(1)} %fusion.48, bf16[1024,2816]{1,0:T(8,128)(2,1)S(1)} %copy-done.42, ...), kind=kOutput, calls=%fused_computation.27 | convolution fusion | flops 5912918016 | bytes 24133632 | tf_op jit(solution)/shard_map/dot_general | solution.py:302
  373.1 11.0 %all-to-all-start.2 = ((bf16[4,256,512]{2,1,0:T(8,128)(2,1)}), bf16[4,256,512]{2,1,0:T(8,128)(2,1)S(1)}, u32[]{:S(2)}, u32[]{:S(2)}) async-start(bf16[4,256,512]{2,1,0:T(8,128)(2,1)} %bitcast.28), calls=%async_computation.2 | async-start | bytes 2097152 | tf_op jit(solution)/shard_map/all_to_all | solution.py:525
  384.1 24.8 %ffn_grad.1 = bf16[8,3,2816,128]{3,2,1,0:T(8,128)(2,1)} custom-call(bf16[1024,1024]{1,0:T(8,128)(2,1)} %multiply_convert_fusion.x_ref, bf16[1024,1024]{1,0:T(8,128)(2,1)} %bitcast.127, bf16[1024,2816]{1,0:T(8,128)(2,1)} %get-tuple-element.36.h_ref, bf16[1024,2816]{1,0:T(8,128)(2,1)} %get-tuple-element.37.dg_ref, bf16[1024,2816]{1,0:T(8,128)(2,1)} %get-tuple-element.38.du_ref), custom_call_target="tpu_custom_call" | custom-call | flops 17716740096 | bytes 34603008 | tf_op jit(solution)/shard_map/ffn_grad/pallas_call | solution.py:284
  411.3 4.1 all-to-all-start.3
  415.5 7.2 convolution_convert_fusion.2
  422.6 18.2 %all-to-all-done.3 = bf16[4,256,512]{2,1,0:T(8,128)(2,1)S(1)} async-done(((bf16[4,256,512]{2,1,0:T(8,128)(2,1)}), bf16[4,256,512]{2,1,0:T(8,128)(2,1)S(1)}, u32[]{:S(2)}, u32[]{:S(2)}) %all-to-all-start.3) | async-done | bytes 1048608 | tf_op jit(solution)/shard_map/all_to_all | solution.py:525
  441.9 26.3 %attn_bwd.2 = bf16[3,256,2048]{2,1,0:T(8,128)(2,1)} custom-call(s32[4]{0:T(128)} %get-tuple-element.125.lo_ref, bf16[768,2048]{1,0:T(8,128)(2,1)} %pad_maximum_fusion.1.q_ref.k_ref.v_ref, bf16[768,2048]{1,0:T(8,128)(2,1)} %pad_maximum_fusion.1.q_ref.k_ref.v_ref, bf16[768,2048]{1,0:T(8,128)(2,1)} %pad_maximum_fusion.1.q_ref.k_ref.v_ref, ...), custom_call_target="tpu_custom_call" | custom-call | flops 10737418240 | bytes 10485760 | tf_op jit(solution)/shard_map/attn_bwd/pallas_call | solution.py:140
  468.2 7.3 convolution_convert_fusion.1
  475.5 26.5 %attn_bwd.3 = bf16[3,256,2048]{2,1,0:T(8,128)(2,1)} custom-call(s32[4]{0:T(128)} %get-tuple-element.124.lo_ref, bf16[768,2048]{1,0:T(8,128)(2,1)} %pad_maximum_fusion.2.q_ref.k_ref.v_ref, bf16[768,2048]{1,0:T(8,128)(2,1)} %pad_maximum_fusion.2.q_ref.k_ref.v_ref, bf16[768,2048]{1,0:T(8,128)(2,1)} %pad_maximum_fusion.2.q_ref.k_ref.v_ref, ...), custom_call_target="tpu_custom_call" | custom-call | flops 10737418240 | bytes 10485760 | tf_op jit(solution)/shard_map/attn_bwd/pallas_call | solution.py:140
  502.0 8.2 %fusion.9 = (f32[1024]{0:T(1024)S(1)}, bf16[2048,1024]{1,0:T(8,128)(2,1)S(1)}) fusion(f32[2048]{0:T(1024)S(1)} %add_rsqrt_fusion, bf16[3584,1024]{1,0:T(8,128)(2,1)} %copy-done.16, s32[]{:T(128)S(6)} %select_n.159, bf16[768,2048]{1,0:T(8,128)(2,1)} %bitcast.166, bf16[1024,768]{1,0:T(8,128)(2,1)S(1)} %bitcast.132), kind=kOutput, calls=%fused_computation.15 | convolution fusion | flops 3233807360 | bytes 13119492 | tf_op jit(solution)/shard_map/dot_general | solution.py:302
  522.5 15.9 %all-to-all-start.6 = ((f32[32,32,2]{1,2,0:T(2,128)}), f32[32,32,2]{1,2,0:T(2,128)S(1)}, u32[]{:S(2)}, u32[]{:S(2)}) async-start(f32[32,32,2]{1,2,0:T(2,128)} %copy.36), calls=%async_computation.7 | async-start | bytes 65536 | tf_op jit(solution)/shard_map/all_to_all | solution.py:424
  538.4 8.7 %fusion.18 = f32[1024,768]{1,0:T(8,128)} fusion(bf16[768,2048]{1,0:T(8,128)(2,1)} %bitcast.169, bf16[2048,1024]{1,0:T(8,128)(2,1)} %copy-done, f32[1024]{0:T(1024)S(1)} %bitcast.152, f32[2048]{0:T(1024)S(1)} %copy-done.36), kind=kOutput, calls=%fused_computation.59 | convolution fusion | flops 3229614080 | bytes 10498048 | tf_op jit(solution)/shard_map/dot_general | solution.py:302
  548.8 12.0 %all-to-all-done.6 = f32[32,32,2]{1,2,0:T(2,128)S(1)} async-done(((f32[32,32,2]{1,2,0:T(2,128)}), f32[32,32,2]{1,2,0:T(2,128)S(1)}, u32[]{:S(2)}, u32[]{:S(2)}) %all-to-all-start.6) | async-done | bytes 8224 | tf_op jit(solution)/shard_map/all_to_all | solution.py:424
  560.8 9.7 %all-to-all-start.5 = ((bf16[8,128,1024]{2,1,0:T(8,128)(2,1)}), bf16[8,128,1024]{2,1,0:T(8,128)(2,1)S(1)}, u32[]{:S(2)}, u32[]{:S(2)}) async-start(bf16[8,128,1024]{2,1,0:T(8,128)(2,1)} %bitcast.125), calls=%async_computation.5 | async-start | bytes 4194304 | tf_op jit(solution)/shard_map/all_to_all | solution.py:424
  573.3 7.6 %collective-permute-start.33 = (bf16[512,1024]{1,0:T(8,128)(2,1)S(1)}, bf16[512,1024]{1,0:T(8,128)(2,1)S(1)}, u32[]{:S(2)}, u32[]{:S(2)}) collective-permute-start(bf16[512,1024]{1,0:T(8,128)(2,1)S(1)} %get-tuple-element.66), channel_id=1, source_target_pairs={{0,2},{4,6},{8,10},{12,14},{16,18},{20,22},{24,26},{28,30}} | collective-permute-start | bytes 3145736 | tf_op jit(solution)/shard_map/ppermute | solution.py:385
  584.0 7.7 %add_convert_fusion.1 = bf16[1024,768]{1,0:T(8,128)(2,1)} fusion(f32[1024,768]{1,0:T(8,128)S(1)} %copy-done.41, bf16[768,2048]{1,0:T(8,128)(2,1)S(1)} %bitcast.167, f32[2048]{0:T(1024)S(1)} %add_rsqrt_fusion, f32[1024]{0:T(1024)S(1)} %bitcast.153, bf16[3584,1024]{1,0:T(8,128)(2,1)} %copy-done.16, s32[]{:T(128)S(6)} %select_n.159), kind=kOutput, calls=%fused_computation.38 | convolution fusion | flops 3231186944 | bytes 12070916 | tf_op jit(solution)/shard_map/dot_general | solution.py:302
  591.7 4.8 add_convert_fusion.3
  597.8 6.7 collective-permute-done.33
  606.7 20.2 %collective-permute-done.32 = bf16[512,1024]{1,0:T(8,128)(2,1)S(1)} collective-permute-done((bf16[512,1024]{1,0:T(8,128)(2,1)S(1)}, bf16[512,1024]{1,0:T(8,128)(2,1)S(1)}, u32[]{:S(2)}, u32[]{:S(2)}) %collective-permute-start.32) | collective-permute-done | bytes 1048608 | tf_op jit(solution)/shard_map/ppermute | solution.py:383
  630.7 9.8 %collective-permute-start.34 = (bf16[512,1024]{1,0:T(8,128)(2,1)S(1)}, bf16[512,1024]{1,0:T(8,128)(2,1)}, u32[]{:S(2)}, u32[]{:S(2)}) collective-permute-start(bf16[512,1024]{1,0:T(8,128)(2,1)S(1)} %get-tuple-element.61), channel_id=1, source_target_pairs={{0,1},{1,2},{2,3},{4,5},{5,6},{6,7},{8,9},{9,10},{10,11},{12,13},{... | collective-permute-start | bytes 3145736 | tf_op jit(solution)/shard_map/ppermute | solution.py:391
  640.6 4.3 all-to-all-start.4
  644.9 11.4 %add_convert_fusion = bf16[1024,1024]{1,0:T(8,128)(2,1)} fusion(f32[1024,1024]{1,0:T(8,128)} %copy-done.11, bf16[1024,2816]{1,0:T(8,128)(2,1)} %get-tuple-element.36.h_ref, bf16[2816,1024]{1,0:T(8,128)(2,1)} %get-tuple-element.35.down_ref), kind=kOutput, calls=%fused_computation.30 | convolution fusion | flops 5907677184 | bytes 17825792 | tf_op jit(solution)/shard_map/dot_general | solution.py:302
  659.1 6.8 all-to-all-done.4
  679.7 9.2 %collective-permute-start.45 = (bf16[2368,128]{1,0:T(8,128)(2,1)S(1)}, bf16[2368,128]{1,0:T(8,128)(2,1)S(1)}, u32[]{:S(2)}, u32[]{:S(2)}) collective-permute-start(bf16[2368,128]{1,0:T(8,128)(2,1)S(1)} %get-tuple-element.86), channel_id=1, source_target_pairs={{0,2},{4,6},{8,10},{12,14},{16,18},{20,22},{24,26},{28,30}} | collective-permute-start | bytes 1818632 | tf_op jit(solution)/shard_map/ppermute | solution.py:385
  693.1 9.9 %collective-permute-done.45 = bf16[2368,128]{1,0:T(8,128)(2,1)S(1)} collective-permute-done((bf16[2368,128]{1,0:T(8,128)(2,1)S(1)}, bf16[2368,128]{1,0:T(8,128)(2,1)S(1)}, u32[]{:S(2)}, u32[]{:S(2)}) %collective-permute-start.45) | collective-permute-done | bytes 606240 | tf_op jit(solution)/shard_map/ppermute | solution.py:385
  703.0 11.3 %collective-permute-done.44 = bf16[2368,128]{1,0:T(8,128)(2,1)S(1)} collective-permute-done((bf16[2368,128]{1,0:T(8,128)(2,1)S(1)}, bf16[2368,128]{1,0:T(8,128)(2,1)S(1)}, u32[]{:S(2)}, u32[]{:S(2)}) %collective-permute-start.44) | collective-permute-done | bytes 606240 | tf_op jit(solution)/shard_map/ppermute | solution.py:383
  716.1 9.6 %collective-permute-start.46 = (bf16[2368,128]{1,0:T(8,128)(2,1)S(1)}, bf16[2368,128]{1,0:T(8,128)(2,1)S(1)}, u32[]{:S(2)}, u32[]{:S(2)}) collective-permute-start(bf16[2368,128]{1,0:T(8,128)(2,1)S(1)} %get-tuple-element.81), channel_id=1, source_target_pairs={{0,1},{1,2},{2,3},{4,5},{5,6},{6,7},{8,9},{9,10},{10,11},{12,13},{... | collective-permute-start | bytes 1818632 | tf_op jit(solution)/shard_map/ppermute | solution.py:391
  728.5 9.1 %collective-permute-done.49 = bf16[2368,128]{1,0:T(8,128)(2,1)S(1)} collective-permute-done((bf16[2368,128]{1,0:T(8,128)(2,1)S(1)}, bf16[2368,128]{1,0:T(8,128)(2,1)S(1)}, u32[]{:S(2)}, u32[]{:S(2)}) %collective-permute-start.49) | collective-permute-done | bytes 606240 | tf_op jit(solution)/shard_map/ppermute | solution.py:394
  (286 shorter events, 159.4 us)
Async XLA Ops:
  7.2 128.6 %all-gather.3.cloned.1.call-start = ((), (), s32[]{:S(2)}) async-start(), calls=%async_computation.9 | async-start | bytes 1990656 | tf_op jit(solution)/shard_map/all_gather | solution.py:452
  8.4 35.4 %collective-permute-start.12 = (bf16[2368,128]{1,0:T(8,128)(2,1)S(1)}, bf16[2368,128]{1,0:T(8,128)(2,1)S(1)}, u32[]{:S(2)}, u32[]{:S(2)}) collective-permute-start(bf16[2368,128]{1,0:T(8,128)(2,1)S(1)} %pad_maximum_fusion.9), channel_id=1, source_target_pairs={{0,1},{1,2},{2,3},{4,5},{5,6},{6,7},{8,9},{9,10},{10,11},{12,13},{... | collective-permute-start | bytes 1818632 | tf_op jit(solution)/shard_map/ppermute | solution.py:360
  13.6 36.7 %collective-permute-start.15 = (bf16[2368,128]{1,0:T(8,128)(2,1)S(1)}, bf16[2368,128]{1,0:T(8,128)(2,1)S(1)}, u32[]{:S(2)}, u32[]{:S(2)}) collective-permute-start(bf16[2368,128]{1,0:T(8,128)(2,1)S(1)} %pad_maximum_fusion.9), channel_id=1, source_target_pairs={{1,0},{2,1},{3,2},{5,4},{6,5},{7,6},{9,8},{10,9},{11,10},{13,12},{... | collective-permute-start | bytes 1818632 | tf_op jit(solution)/shard_map/ppermute | solution.py:361
  17.5 34.0 %collective-permute-start = (bf16[512,1024]{1,0:T(8,128)(2,1)S(1)}, bf16[512,1024]{1,0:T(8,128)(2,1)}, u32[]{:S(2)}, u32[]{:S(2)}) collective-permute-start(bf16[512,1024]{1,0:T(8,128)(2,1)S(1)} %get-tuple-element.90), channel_id=1, source_target_pairs={{0,1},{1,2},{2,3},{4,5},{5,6},{6,7},{8,9},{9,10},{10,11},{12,13},{... | collective-permute-start | bytes 3145736 | tf_op jit(solution)/shard_map/ppermute | solution.py:360
  23.2 31.5 %collective-permute-start.3 = (bf16[512,1024]{1,0:T(8,128)(2,1)S(1)}, bf16[512,1024]{1,0:T(8,128)(2,1)}, u32[]{:S(2)}, u32[]{:S(2)}) collective-permute-start(bf16[512,1024]{1,0:T(8,128)(2,1)S(1)} %get-tuple-element.90), channel_id=1, source_target_pairs={{1,0},{2,1},{3,2},{5,4},{6,5},{7,6},{9,8},{10,9},{11,10},{13,12},{... | collective-permute-start | bytes 3145736 | tf_op jit(solution)/shard_map/ppermute | solution.py:361
  51.6 36.7 %collective-permute-start.17 = (bf16[2368,128]{1,0:T(8,128)(2,1)S(1)}, bf16[2368,128]{1,0:T(8,128)(2,1)S(1)}, u32[]{:S(2)}, u32[]{:S(2)}) collective-permute-start(bf16[2368,128]{1,0:T(8,128)(2,1)S(1)} %collective-permute-done.15), channel_id=1, source_target_pairs={{2,0},{6,4},{10,8},{14,12},{18,16},{22,20},{26,24},{30,28}} | collective-permute-start | bytes 1818632 | tf_op jit(solution)/shard_map/ppermute | solution.py:365
  52.9 36.7 %collective-permute-start.1 = (bf16[512,1024]{1,0:T(8,128)(2,1)}, bf16[512,1024]{1,0:T(8,128)(2,1)S(1)}, u32[]{:S(2)}, u32[]{:S(2)}) collective-permute-start(bf16[512,1024]{1,0:T(8,128)(2,1)} %collective-permute-done), channel_id=1, source_target_pairs={{1,3},{5,7},{9,11},{13,15},{17,19},{21,23},{25,27},{29,31}} | collective-permute-start | bytes 3145736 | tf_op jit(solution)/shard_map/ppermute | solution.py:364
  54.8 34.9 %collective-permute-start.2 = (bf16[512,1024]{1,0:T(8,128)(2,1)}, bf16[512,1024]{1,0:T(8,128)(2,1)S(1)}, u32[]{:S(2)}, u32[]{:S(2)}) collective-permute-start(bf16[512,1024]{1,0:T(8,128)(2,1)} %collective-permute-done), channel_id=1, source_target_pairs={{1,2},{2,3},{5,6},{6,7},{9,10},{10,11},{13,14},{14,15},{17,18},{18... | collective-permute-start | bytes 3145736 | tf_op jit(solution)/shard_map/ppermute | solution.py:362
  55.5 63.9 %collective-permute-start.4 = (bf16[512,1024]{1,0:T(8,128)(2,1)}, bf16[512,1024]{1,0:T(8,128)(2,1)S(1)}, u32[]{:S(2)}, u32[]{:S(2)}) collective-permute-start(bf16[512,1024]{1,0:T(8,128)(2,1)} %collective-permute-done.3), channel_id=1, source_target_pairs={{1,0},{2,1},{5,4},{6,5},{9,8},{10,9},{13,12},{14,13},{17,16},{18,1... | collective-permute-start | bytes 3145736 | tf_op jit(solution)/shard_map/ppermute | solution.py:363
  72.9 57.8 %collective-permute-start.5 = (bf16[512,1024]{1,0:T(8,128)(2,1)}, bf16[512,1024]{1,0:T(8,128)(2,1)S(1)}, u32[]{:S(2)}, u32[]{:S(2)}) collective-permute-start(bf16[512,1024]{1,0:T(8,128)(2,1)} %collective-permute-done.3), channel_id=1, source_target_pairs={{2,0},{6,4},{10,8},{14,12},{18,16},{22,20},{26,24},{30,28}} | collective-permute-start | bytes 3145736 | tf_op jit(solution)/shard_map/ppermute | solution.py:365
  89.6 144.9 %collective-permute-start.18 = (bf16[4736,128]{1,0:T(8,128)(2,1)}, bf16[4736,128]{1,0:T(8,128)(2,1)}, u32[]{:S(2)}, u32[]{:S(2)}) collective-permute-start(bf16[4736,128]{1,0:T(8,128)(2,1)} %get-tuple-element.60.refs_0_), channel_id=1, source_target_pairs={{0,4},{4,0},{8,12},{12,8},{16,20},{20,16},{24,28},{28,24},{1,5},{5... | collective-permute-start | bytes 3637256 | tf_op jit(solution)/shard_map/ppermute | solution.py:406
  148.3 47.2 %collective-permute-start.7 = (bf16[512,1024]{1,0:T(8,128)(2,1)}, bf16[512,1024]{1,0:T(8,128)(2,1)}, u32[]{:S(2)}, u32[]{:S(2)}) collective-permute-start(bf16[512,1024]{1,0:T(8,128)(2,1)} %collective-permute-done.6), channel_id=1, source_target_pairs={{1,3},{5,7},{9,11},{13,15},{17,19},{21,23},{25,27},{29,31}} | collective-permute-start | bytes 3145736 | tf_op jit(solution)/shard_map/ppermute | solution.py:364
  150.3 56.5 %collective-permute-start.8 = (bf16[512,1024]{1,0:T(8,128)(2,1)}, bf16[512,1024]{1,0:T(8,128)(2,1)}, u32[]{:S(2)}, u32[]{:S(2)}) collective-permute-start(bf16[512,1024]{1,0:T(8,128)(2,1)} %collective-permute-done.6), channel_id=1, source_target_pairs={{1,2},{2,3},{5,6},{6,7},{9,10},{10,11},{13,14},{14,15},{17,18},{18... | collective-permute-start | bytes 3145736 | tf_op jit(solution)/shard_map/ppermute | solution.py:362
  153.9 58.1 %collective-permute-start.10 = (bf16[512,1024]{1,0:T(8,128)(2,1)}, bf16[512,1024]{1,0:T(8,128)(2,1)}, u32[]{:S(2)}, u32[]{:S(2)}) collective-permute-start(bf16[512,1024]{1,0:T(8,128)(2,1)} %collective-permute-done.9), channel_id=1, source_target_pairs={{1,0},{2,1},{5,4},{6,5},{9,8},{10,9},{13,12},{14,13},{17,16},{18,1... | collective-permute-start | bytes 3145736 | tf_op jit(solution)/shard_map/ppermute | solution.py:363
  155.2 68.8 %collective-permute-start.11 = (bf16[512,1024]{1,0:T(8,128)(2,1)}, bf16[512,1024]{1,0:T(8,128)(2,1)}, u32[]{:S(2)}, u32[]{:S(2)}) collective-permute-start(bf16[512,1024]{1,0:T(8,128)(2,1)} %collective-permute-done.9), channel_id=1, source_target_pairs={{2,0},{6,4},{10,8},{14,12},{18,16},{22,20},{26,24},{30,28}} | collective-permute-start | bytes 3145736 | tf_op jit(solution)/shard_map/ppermute | solution.py:365
  181.4 100.5 %all-to-all-start = ((bf16[256,4,512]{2,0,1:T(8,128)(2,1)}), bf16[256,4,512]{2,0,1:T(8,128)(2,1)}, u32[]{:S(2)}, u32[]{:S(2)}) async-start(bf16[256,4,512]{2,0,1:T(8,128)(2,1)} %bitcast.117), calls=%async_computation | async-start | bytes 2097152 | tf_op jit(solution)/shard_map/all_to_all | solution.py:498
  195.5 40.8 %collective-permute-start.20 = (bf16[4736,128]{1,0:T(8,128)(2,1)}, bf16[4736,128]{1,0:T(8,128)(2,1)}, u32[]{:S(2)}, u32[]{:S(2)}) collective-permute-start(bf16[4736,128]{1,0:T(8,128)(2,1)} %get-tuple-element.60.refs_0_), channel_id=1, source_target_pairs={{0,8},{4,12},{8,0},{12,4},{16,24},{20,28},{24,16},{28,20},{1,9},{5... | collective-permute-start | bytes 3637256 | tf_op jit(solution)/shard_map/ppermute | solution.py:408
  206.7 29.6 %collective-permute-start.19 = (bf16[4736,128]{1,0:T(8,128)(2,1)S(1)}, bf16[4736,128]{1,0:T(8,128)(2,1)S(1)}, u32[]{:S(2)}, u32[]{:S(2)}) collective-permute-start(bf16[4736,128]{1,0:T(8,128)(2,1)S(1)} %get-tuple-element.59.refs_1_), channel_id=1, source_target_pairs={{0,4},{4,0},{8,12},{12,8},{16,20},{20,16},{24,28},{28,24},{1,5},{5... | collective-permute-start | bytes 3637256 | tf_op jit(solution)/shard_map/ppermute | solution.py:406
  212.0 74.5 %collective-permute-start.21 = (bf16[4736,128]{1,0:T(8,128)(2,1)S(1)}, bf16[4736,128]{1,0:T(8,128)(2,1)}, u32[]{:S(2)}, u32[]{:S(2)}) collective-permute-start(bf16[4736,128]{1,0:T(8,128)(2,1)S(1)} %get-tuple-element.59.refs_1_), channel_id=1, source_target_pairs={{0,8},{4,12},{8,0},{12,4},{16,24},{20,28},{24,16},{28,20},{1,9},{5... | collective-permute-start | bytes 3637256 | tf_op jit(solution)/shard_map/ppermute | solution.py:409
  224.0 29.7 %collective-permute-start.25 = (bf16[4736,128]{1,0:T(8,128)(2,1)S(1)}, bf16[4736,128]{1,0:T(8,128)(2,1)}, u32[]{:S(2)}, u32[]{:S(2)}) collective-permute-start(bf16[4736,128]{1,0:T(8,128)(2,1)S(1)} %get-tuple-element.59.refs_1_), channel_id=1, source_target_pairs={{0,16},{4,20},{8,24},{12,28},{16,0},{20,4},{24,8},{28,12},{1,17},{... | collective-permute-start | bytes 3637256 | tf_op jit(solution)/shard_map/ppermute | solution.py:408
  234.5 52.1 %collective-permute-start.24 = (bf16[4736,128]{1,0:T(8,128)(2,1)}, bf16[4736,128]{1,0:T(8,128)(2,1)}, u32[]{:S(2)}, u32[]{:S(2)}) collective-permute-start(bf16[4736,128]{1,0:T(8,128)(2,1)} %get-tuple-element.60.refs_0_), channel_id=1, source_target_pairs={{0,16},{4,20},{8,24},{12,28},{16,0},{20,4},{24,8},{28,12},{1,17},{... | collective-permute-start | bytes 3637256 | tf_op jit(solution)/shard_map/ppermute | solution.py:409
  236.3 50.8 %collective-permute-start.22 = (bf16[4736,128]{1,0:T(8,128)(2,1)}, bf16[4736,128]{1,0:T(8,128)(2,1)}, u32[]{:S(2)}, u32[]{:S(2)}) collective-permute-start(bf16[4736,128]{1,0:T(8,128)(2,1)} %collective-permute-done.20.refs_4_), channel_id=1, source_target_pairs={{0,4},{4,0},{8,12},{12,8},{16,20},{20,16},{24,28},{28,24},{1,5},{5... | collective-permute-start | bytes 3637256 | tf_op jit(solution)/shard_map/ppermute | solution.py:406
  236.3 58.4 %collective-permute-start.28 = (bf16[4736,128]{1,0:T(8,128)(2,1)}, bf16[4736,128]{1,0:T(8,128)(2,1)}, u32[]{:S(2)}, u32[]{:S(2)}) collective-permute-start(bf16[4736,128]{1,0:T(8,128)(2,1)} %collective-permute-done.20.refs_4_), channel_id=1, source_target_pairs={{0,16},{4,20},{8,24},{12,28},{16,0},{20,4},{24,8},{28,12},{1,17},{... | collective-permute-start | bytes 3637256 | tf_op jit(solution)/shard_map/ppermute | solution.py:410
  253.7 41.1 %collective-permute-start.29 = (bf16[4736,128]{1,0:T(8,128)(2,1)}, bf16[4736,128]{1,0:T(8,128)(2,1)}, u32[]{:S(2)}, u32[]{:S(2)}) collective-permute-start(bf16[4736,128]{1,0:T(8,128)(2,1)} %collective-permute-done.25.refs_9_), channel_id=1, source_target_pairs={{0,8},{4,12},{8,0},{12,4},{16,24},{20,28},{24,16},{28,20},{1,9},{5... | collective-permute-start | bytes 3637256 | tf_op jit(solution)/shard_map/ppermute | solution.py:410
  281.9 32.2 %all-to-all-start.1 = ((bf16[256,4,512]{2,0,1:T(8,128)(2,1)}), bf16[256,4,512]{2,0,1:T(8,128)(2,1)}, u32[]{:S(2)}, u32[]{:S(2)}) async-start(bf16[256,4,512]{2,0,1:T(8,128)(2,1)} %bitcast.118), calls=%async_computation.1 | async-start | bytes 2097152 | tf_op jit(solution)/shard_map/all_to_all | solution.py:498
  373.1 37.0 %all-to-all-start.2 = ((bf16[4,256,512]{2,1,0:T(8,128)(2,1)}), bf16[4,256,512]{2,1,0:T(8,128)(2,1)S(1)}, u32[]{:S(2)}, u32[]{:S(2)}) async-start(bf16[4,256,512]{2,1,0:T(8,128)(2,1)} %bitcast.28), calls=%async_computation.2 | async-start | bytes 2097152 | tf_op jit(solution)/shard_map/all_to_all | solution.py:525
  384.1 293.5 %reduce-scatter.2.cloned.1.call-start = ((), (), s32[]{:S(2)}) async-start(), calls=%async_computation.8 | async-start | bytes 19464192 | tf_op jit(solution)/shard_map/reduce_scatter | solution.py:347
  411.3 29.6 %all-to-all-start.3 = ((bf16[4,256,512]{2,1,0:T(8,128)(2,1)}), bf16[4,256,512]{2,1,0:T(8,128)(2,1)S(1)}, u32[]{:S(2)}, u32[]{:S(2)}) async-start(bf16[4,256,512]{2,1,0:T(8,128)(2,1)} %bitcast.31), calls=%async_computation.3 | async-start | bytes 2097152 | tf_op jit(solution)/shard_map/all_to_all | solution.py:525
  514.4 66.5 %collective-permute-start.39 = (bf16[512,1024]{1,0:T(8,128)(2,1)}, bf16[512,1024]{1,0:T(8,128)(2,1)S(1)}, u32[]{:S(2)}, u32[]{:S(2)}) collective-permute-start(bf16[512,1024]{1,0:T(8,128)(2,1)} %get-tuple-element.72), channel_id=1, source_target_pairs={{0,2},{4,6},{8,10},{12,14},{16,18},{20,22},{24,26},{28,30}} | collective-permute-start | bytes 3145736 | tf_op jit(solution)/shard_map/ppermute | solution.py:385
  516.3 66.1 %collective-permute-start.38 = (bf16[512,1024]{1,0:T(8,128)(2,1)}, bf16[512,1024]{1,0:T(8,128)(2,1)}, u32[]{:S(2)}, u32[]{:S(2)}) collective-permute-start(bf16[512,1024]{1,0:T(8,128)(2,1)} %get-tuple-element.69), channel_id=1, source_target_pairs={{0,1},{1,2},{4,5},{5,6},{8,9},{9,10},{12,13},{13,14},{16,17},{17,1... | collective-permute-start | bytes 3145736 | tf_op jit(solution)/shard_map/ppermute | solution.py:383
  518.5 64.5 %collective-permute-start.42 = (bf16[512,1024]{1,0:T(8,128)(2,1)}, bf16[512,1024]{1,0:T(8,128)(2,1)}, u32[]{:S(2)}, u32[]{:S(2)}) collective-permute-start(bf16[512,1024]{1,0:T(8,128)(2,1)} %get-tuple-element.70), channel_id=1, source_target_pairs={{3,1},{7,5},{11,9},{15,13},{19,17},{23,21},{27,25},{31,29}} | collective-permute-start | bytes 3145736 | tf_op jit(solution)/shard_map/ppermute | solution.py:386
  522.5 38.3 %all-to-all-start.6 = ((f32[32,32,2]{1,2,0:T(2,128)}), f32[32,32,2]{1,2,0:T(2,128)S(1)}, u32[]{:S(2)}, u32[]{:S(2)}) async-start(f32[32,32,2]{1,2,0:T(2,128)} %copy.36), calls=%async_computation.7 | async-start | bytes 65536 | tf_op jit(solution)/shard_map/all_to_all | solution.py:424
  547.1 44.5 %collective-permute-start.41 = (bf16[512,1024]{1,0:T(8,128)(2,1)}, bf16[512,1024]{1,0:T(8,128)(2,1)}, u32[]{:S(2)}, u32[]{:S(2)}) collective-permute-start(bf16[512,1024]{1,0:T(8,128)(2,1)} %get-tuple-element.71), channel_id=1, source_target_pairs={{3,2},{2,1},{7,6},{6,5},{11,10},{10,9},{15,14},{14,13},{19,18},{18... | collective-permute-start | bytes 3145736 | tf_op jit(solution)/shard_map/ppermute | solution.py:384
  560.8 79.8 %all-to-all-start.5 = ((bf16[8,128,1024]{2,1,0:T(8,128)(2,1)}), bf16[8,128,1024]{2,1,0:T(8,128)(2,1)S(1)}, u32[]{:S(2)}, u32[]{:S(2)}) async-start(bf16[8,128,1024]{2,1,0:T(8,128)(2,1)} %bitcast.125), calls=%async_computation.5 | async-start | bytes 4194304 | tf_op jit(solution)/shard_map/all_to_all | solution.py:424
  573.3 31.1 %collective-permute-start.33 = (bf16[512,1024]{1,0:T(8,128)(2,1)S(1)}, bf16[512,1024]{1,0:T(8,128)(2,1)S(1)}, u32[]{:S(2)}, u32[]{:S(2)}) collective-permute-start(bf16[512,1024]{1,0:T(8,128)(2,1)S(1)} %get-tuple-element.66), channel_id=1, source_target_pairs={{0,2},{4,6},{8,10},{12,14},{16,18},{20,22},{24,26},{28,30}} | collective-permute-start | bytes 3145736 | tf_op jit(solution)/shard_map/ppermute | solution.py:385
  581.0 46.0 %collective-permute-start.32 = (bf16[512,1024]{1,0:T(8,128)(2,1)S(1)}, bf16[512,1024]{1,0:T(8,128)(2,1)S(1)}, u32[]{:S(2)}, u32[]{:S(2)}) collective-permute-start(bf16[512,1024]{1,0:T(8,128)(2,1)S(1)} %get-tuple-element.63), channel_id=1, source_target_pairs={{0,1},{1,2},{4,5},{5,6},{8,9},{9,10},{12,13},{13,14},{16,17},{17,1... | collective-permute-start | bytes 3145736 | tf_op jit(solution)/shard_map/ppermute | solution.py:383
  582.3 44.6 %collective-permute-start.36 = (bf16[512,1024]{1,0:T(8,128)(2,1)S(1)}, bf16[512,1024]{1,0:T(8,128)(2,1)S(1)}, u32[]{:S(2)}, u32[]{:S(2)}) collective-permute-start(bf16[512,1024]{1,0:T(8,128)(2,1)S(1)} %get-tuple-element.64), channel_id=1, source_target_pairs={{3,1},{7,5},{11,9},{15,13},{19,17},{23,21},{27,25},{31,29}} | collective-permute-start | bytes 3145736 | tf_op jit(solution)/shard_map/ppermute | solution.py:386
  583.1 43.8 %collective-permute-start.35 = (bf16[512,1024]{1,0:T(8,128)(2,1)S(1)}, bf16[512,1024]{1,0:T(8,128)(2,1)S(1)}, u32[]{:S(2)}, u32[]{:S(2)}) collective-permute-start(bf16[512,1024]{1,0:T(8,128)(2,1)S(1)} %get-tuple-element.65), channel_id=1, source_target_pairs={{3,2},{2,1},{7,6},{6,5},{11,10},{10,9},{15,14},{14,13},{19,18},{18... | collective-permute-start | bytes 3145736 | tf_op jit(solution)/shard_map/ppermute | solution.py:384
  596.5 71.8 %collective-permute-start.43 = (bf16[512,1024]{1,0:T(8,128)(2,1)}, bf16[512,1024]{1,0:T(8,128)(2,1)}, u32[]{:S(2)}, u32[]{:S(2)}) collective-permute-start(bf16[512,1024]{1,0:T(8,128)(2,1)} %get-tuple-element.68), channel_id=1, source_target_pairs={{1,0},{2,1},{3,2},{5,4},{6,5},{7,6},{9,8},{10,9},{11,10},{13,12},{... | collective-permute-start | bytes 3145736 | tf_op jit(solution)/shard_map/ppermute | solution.py:394
  604.5 63.8 %collective-permute-start.40 = (bf16[512,1024]{1,0:T(8,128)(2,1)}, bf16[512,1024]{1,0:T(8,128)(2,1)}, u32[]{:S(2)}, u32[]{:S(2)}) collective-permute-start(bf16[512,1024]{1,0:T(8,128)(2,1)} %get-tuple-element.67), channel_id=1, source_target_pairs={{0,1},{1,2},{2,3},{4,5},{5,6},{6,7},{8,9},{9,10},{10,11},{12,13},{... | collective-permute-start | bytes 3145736 | tf_op jit(solution)/shard_map/ppermute | solution.py:391
  629.4 41.3 %collective-permute-start.37 = (bf16[512,1024]{1,0:T(8,128)(2,1)}, bf16[512,1024]{1,0:T(8,128)(2,1)}, u32[]{:S(2)}, u32[]{:S(2)}) collective-permute-start(bf16[512,1024]{1,0:T(8,128)(2,1)} %get-tuple-element.62), channel_id=1, source_target_pairs={{1,0},{2,1},{3,2},{5,4},{6,5},{7,6},{9,8},{10,9},{11,10},{13,12},{... | collective-permute-start | bytes 3145736 | tf_op jit(solution)/shard_map/ppermute | solution.py:394
  630.7 40.6 %collective-permute-start.34 = (bf16[512,1024]{1,0:T(8,128)(2,1)S(1)}, bf16[512,1024]{1,0:T(8,128)(2,1)}, u32[]{:S(2)}, u32[]{:S(2)}) collective-permute-start(bf16[512,1024]{1,0:T(8,128)(2,1)S(1)} %get-tuple-element.61), channel_id=1, source_target_pairs={{0,1},{1,2},{2,3},{4,5},{5,6},{6,7},{8,9},{9,10},{10,11},{12,13},{... | collective-permute-start | bytes 3145736 | tf_op jit(solution)/shard_map/ppermute | solution.py:391
  640.6 25.3 %all-to-all-start.4 = ((bf16[8,128,768]{2,1,0:T(8,128)(2,1)}), bf16[8,128,768]{2,1,0:T(8,128)(2,1)}, u32[]{:S(2)}, u32[]{:S(2)}) async-start(bf16[8,128,768]{2,1,0:T(8,128)(2,1)} %bitcast.133), calls=%async_computation.4 | async-start | bytes 3145728 | tf_op jit(solution)/shard_map/all_to_all | solution.py:424
  679.7 23.3 %collective-permute-start.45 = (bf16[2368,128]{1,0:T(8,128)(2,1)S(1)}, bf16[2368,128]{1,0:T(8,128)(2,1)S(1)}, u32[]{:S(2)}, u32[]{:S(2)}) collective-permute-start(bf16[2368,128]{1,0:T(8,128)(2,1)S(1)} %get-tuple-element.86), channel_id=1, source_target_pairs={{0,2},{4,6},{8,10},{12,14},{16,18},{20,22},{24,26},{28,30}} | collective-permute-start | bytes 1818632 | tf_op jit(solution)/shard_map/ppermute | solution.py:385
  689.0 25.3 %collective-permute-start.44 = (bf16[2368,128]{1,0:T(8,128)(2,1)S(1)}, bf16[2368,128]{1,0:T(8,128)(2,1)S(1)}, u32[]{:S(2)}, u32[]{:S(2)}) collective-permute-start(bf16[2368,128]{1,0:T(8,128)(2,1)S(1)} %get-tuple-element.83), channel_id=1, source_target_pairs={{0,1},{1,2},{4,5},{5,6},{8,9},{9,10},{12,13},{13,14},{16,17},{17,1... | collective-permute-start | bytes 1818632 | tf_op jit(solution)/shard_map/ppermute | solution.py:383
  690.3 24.0 %collective-permute-start.48 = (bf16[2368,128]{1,0:T(8,128)(2,1)S(1)}, bf16[2368,128]{1,0:T(8,128)(2,1)S(1)}, u32[]{:S(2)}, u32[]{:S(2)}) collective-permute-start(bf16[2368,128]{1,0:T(8,128)(2,1)S(1)} %get-tuple-element.84), channel_id=1, source_target_pairs={{3,1},{7,5},{11,9},{15,13},{19,17},{23,21},{27,25},{31,29}} | collective-permute-start | bytes 1818632 | tf_op jit(solution)/shard_map/ppermute | solution.py:386
  691.2 23.0 %collective-permute-start.47 = (bf16[2368,128]{1,0:T(8,128)(2,1)S(1)}, bf16[2368,128]{1,0:T(8,128)(2,1)S(1)}, u32[]{:S(2)}, u32[]{:S(2)}) collective-permute-start(bf16[2368,128]{1,0:T(8,128)(2,1)S(1)} %get-tuple-element.85), channel_id=1, source_target_pairs={{3,2},{2,1},{7,6},{6,5},{11,10},{10,9},{15,14},{14,13},{19,18},{18... | collective-permute-start | bytes 1818632 | tf_op jit(solution)/shard_map/ppermute | solution.py:384
  714.8 22.8 %collective-permute-start.49 = (bf16[2368,128]{1,0:T(8,128)(2,1)S(1)}, bf16[2368,128]{1,0:T(8,128)(2,1)S(1)}, u32[]{:S(2)}, u32[]{:S(2)}) collective-permute-start(bf16[2368,128]{1,0:T(8,128)(2,1)S(1)} %get-tuple-element.82), channel_id=1, source_target_pairs={{1,0},{2,1},{3,2},{5,4},{6,5},{7,6},{9,8},{10,9},{11,10},{13,12},{... | collective-permute-start | bytes 1818632 | tf_op jit(solution)/shard_map/ppermute | solution.py:394
  (54 other events, 1025.3 us)
Sparse Core Ops, SparseCore 0:
  36.7 28.7 all-gather.2
  411.4 118.3 reduce-scatter.1

commit v4 on v3

--- a/solution.py
+++ b/solution.py
@@ -12,7 +12,8 @@
 HD = 64
 BQ = 512
 BK = 256
-HPS = 2
+BK_FORWARD = 512
+HPS = 4
 
 
 def attn_fwd_kernel(lo_ref, q_ref, k_ref, v_ref, start_ref, o_ref, lse_ref, k_scr, *, bq, bk, heads):
@@ -111,7 +112,7 @@
         out_ref[2, h * HD:(h + 1) * HD, :] = dv_scr[h].T.astype(jnp.bfloat16)
 
 
-def attn_fwd(qkv_t, start, lo, bq=BQ, bk=BK, hps=HPS):
+def attn_fwd(qkv_t, start, lo, bq=BQ, bk=BK_FORWARD, hps=HPS):
     cols3, length = qkv_t.shape
     cols = cols3 // 3
     steps = cols // (HD * hps)
@@ -418,13 +419,6 @@
     return assemble(lanes * piece.shape[1], flat, sizes, 8 * piece.shape[1])
 
 
-def exchange_sum(partial_sum, axis):
-    count = lax.axis_size(axis)
-    parts = partial_sum.reshape((count, partial_sum.shape[0] // count) + partial_sum.shape[1:])
-    swapped = lax.all_to_all(parts, axis, split_axis=0, concat_axis=0, tiled=True)
-    return jnp.sum(swapped.astype(jnp.float32), axis=0)
-
-
 def local(
     inputs, segments, w_query, w_key, w_value, w_output, w_gate, w_up, w_down,
     gain_attn, gain_ffn, cotangent,
@@ -479,7 +473,7 @@
         cos_table, sin_table = rope_tables(start)
         tables.append((cos_table, sin_table))
         starts.append(start[None])
-        lows.append(start[::BQ] // BK)
+        lows.append((start[::BQ] // BK_FORWARD, start[::BQ] // BK))
         if m == 1:
             rows_all[1] = line_gather(second_piece, "mp")
         rows = rows_all[m].astype(jnp.float32)
@@ -489,7 +483,7 @@
         turned_q = rotate(pre[:cols], cos_table, sin_table) * HD ** -0.5
         turned_k = rotate(pre[cols : 2 * cols], cos_table, sin_table)
         qkv.append(jnp.concatenate([turned_q, turned_k, pre[2 * cols :]], axis=0).astype(low))
-        out, log = attn_fwd(qkv[m], starts[m], lows[m])
+        out, log = attn_fwd(qkv[m], starts[m], lows[m][0])
         mixed.append(out)
         logs.append(log)
     mixed_own = []
@@ -538,7 +532,7 @@
     for m in range(batches):
         cos_table, sin_table = tables[m]
         back = attn_bwd(
-            qkv[m], grad_mixed_rows[m], mixed[m], logs[m], starts[m], lows[m], cos_table,
+            qkv[m], grad_mixed_rows[m], mixed[m], logs[m], starts[m], lows[m][1], cos_table,
             sin_table,
         ).reshape(3 * cols, n_mp * tokens)
         grad_qkv.append(back)
@@ -553,22 +547,42 @@
     for m in range(batches):
         grad_w = grad_w + dot_dims(normed[m], grad_qkv[m], 0, 1)
 
-    own_out = exchange_sum(grad_output, "dp").astype(low).T.reshape(n_mp, cols, depth)
+    gain_parts = jnp.stack([gain_attn_part, gain_ffn_part]).astype(low)
+    gain_parts = gain_parts.reshape(2, n_dp, depth).transpose(1, 0, 2).reshape(n_dp, 1, 2 * depth)
+    sums = jnp.concatenate(
+        [
+            grad_w.astype(low).reshape(n_dp, depth, 3 * cols),
+            grad_output.reshape(n_dp, depth, n_mp * cols),
+        ],
+        axis=2,
+    )
+    gain_rows = jnp.pad(gain_parts, ((0, 0), (0, 15), (0, sums.shape[2] - 2 * depth)))
+    sums = jnp.concatenate([sums, gain_rows], axis=1)
+    sums = lax.all_to_all(sums, "dp", split_axis=0, concat_axis=0, tiled=True)
+    sums = jnp.sum(sums.astype(jnp.float32), axis=0)
+    own_qkv, own_out = sums[:depth, : 3 * cols], sums[:depth, 3 * cols :]
+    own_gain = sums[depth, : 2 * depth].reshape(2, n_mp, depth // n_mp).transpose(1, 0, 2)
+    own_gain = own_gain.reshape(n_mp, 1, 2 * depth // n_mp)
+    own_gain = jnp.pad(own_gain.astype(low), ((0, 0), (0, 15), (0, depth - own_gain.shape[2])))
     own_ffn = mine.reshape(3, n_mp, hidden_part, depth).transpose(1, 0, 2, 3)
-    own_rest = jnp.concatenate([own_out, own_ffn.reshape(n_mp, -1, depth)], axis=1)
+    own_rest = jnp.concatenate(
+        [
+            own_out.T.astype(low).reshape(n_mp, cols, depth),
+            own_ffn.reshape(n_mp, -1, depth),
+            own_gain,
+        ],
+        axis=1,
+    )
     own_rest = own_rest.reshape(-1, depth)
     own_rest = line_scatter(own_rest, "mp")
     own_output, own_gate, own_up, own_down = (
         own_rest[first : first + size] for first, size in zip(firsts, sizes)
     )
-    own_qkv = exchange_sum(grad_w.astype(low), "dp")
+    grad_norms = own_rest[sum(sizes), : 2 * depth // n_mp].reshape(2, -1)
 
     grad_normed_attn = jnp.concatenate(grad_normed, axis=0)
     grad_lower, _ = rms_back(in_float, rms_factor(in_float), gain_one, grad_normed_attn)
     grad_inputs = (grad_hidden_in + grad_lower).astype(low)
-    grad_norms = exchange_sum(
-        jnp.stack([gain_attn_part, gain_ffn_part], axis=1), ("dp", "mp")
-    ).T
     return (
         result.reshape(inputs.shape),
         grad_inputs.reshape(inputs.shape),

time: 759 us -> 752 us (level)
  the two profiles are of different devices: /device:TPU:0 before, /device:TPU:18 now
where the time goes in v4:
time: 752 us; the launch traced here: 741 us
  waiting for transfers between devices  240 us (32%)
  Pallas kernels  173 us (23%)
  starting transfers between devices  126 us (17%)
  matrix products  77.2 us (10%)
  local copies, waits for them, and re-layouts  58.9 us (8%)
  other arithmetic  44.7 us (6%)
  between operations  21 us (3%)
    dot_general x12, matrix products, dot_dims(): lax.dot_general(left, right, (((left_dim,), (right_dim,)), ((), ())), pre...  77.2 us
    pallas_call x2, Pallas kernels, attn_bwd(): pl.pallas_call(functools.partial(attn_bwd_kernel, bq=bq, bk=bk, heads=hps...  61.2 us
    ppermute x3, waiting for transfers between devices, line_gather(): two_left = lax.ppermute(one_left, axis, [(1, 2), (2, 3)])  60.1 us
    pallas_call x2, Pallas kernels, attn_fwd(): pl.pallas_call(functools.partial(attn_fwd_kernel, bq=bq, bk=bk, heads=hps...  47.1 us
    ppermute x3, waiting for transfers between devices, line_scatter(): two_right = lax.ppermute(block(2), axis, [(0, 1), (1, 2)])  43.6 us
    unnamed x120, local copies, waits for them, and re-layouts  28 us
    ppermute x3, waiting for transfers between devices, line_scatter(): lax.ppermute(total(block(-1), two_left, three_left).astype(jnp.bfloat16),...  27.3 us
    pallas_call x1, Pallas kernels, ffn_main(): pl.pallas_call(functools.partial(ffn_main_kernel, step=step), out_shape=[...  25.8 us
  transfers between devices with their start and end apart: 57, of which 23 were waited for; matrix products, arithmetic and copies ran while one was open for 18% of the time, Pallas kernels for 20%

profile of v4, /device:TPU:18, one launch (start us, length us, event | category | flops | bytes accessed | tf_op | source)
XLA Modules:
  0.0 741.0 jit_solution(9166465065879352623)
XLA Ops:
  43.9 4.3 collective-permute-start.14
  51.7 5.0 collective-permute-start.16
  62.8 6.0 collective-permute-start.2
  68.8 26.2 %collective-permute-done.14 = bf16[2368,128]{1,0:T(8,128)(2,1)} collective-permute-done((bf16[2368,128]{1,0:T(8,128)(2,1)S(1)}, bf16[2368,128]{1,0:T(8,128)(2,1)}, u32[]{:S(2)}, u32[]{:S(2)}) %collective-permute-start.14) | collective-permute-done | bytes 606240 | tf_op jit(solution)/shard_map/ppermute | solution.py:363
  100.7 18.6 %collective-permute-done.2 = bf16[512,1024]{1,0:T(8,128)(2,1)S(1)} collective-permute-done((bf16[512,1024]{1,0:T(8,128)(2,1)}, bf16[512,1024]{1,0:T(8,128)(2,1)S(1)}, u32[]{:S(2)}, u32[]{:S(2)}) %collective-permute-start.2) | collective-permute-done | bytes 1048608 | tf_op jit(solution)/shard_map/ppermute | solution.py:363
  122.2 4.1 collective-permute-done.5
  136.1 5.7 fusion.24
  143.4 5.2 collective-permute-done.6
  156.5 6.3 collective-permute-start.10
  165.5 23.6 %attn_fwd.2 = (bf16[256,2048]{1,0:T(8,128)(2,1)}, f32[4,1,2048]{2,1,0:T(1,128)}) custom-call(s32[4]{0:T(128)} %get-tuple-element.128.lo_ref, bf16[768,2048]{1,0:T(8,128)(2,1)} %pad_maximum_fusion.1.q_ref.k_ref.v_ref, bf16[768,2048]{1,0:T(8,128)(2,1)} %pad_maximum_fusion.1.q_ref.k_ref.v_ref, bf16[768,2048]{1,0:T(8,128)(2,1)} %pad_maximum_fusion.1.q_ref.k_ref.v_ref, ...), custom_call_target="tpu_custom_call" | custom-call | flops 4294967296 | bytes 4194304 | tf_op jit(solution)/shard_map/attn_fwd/pallas_call | solution.py:121
  191.5 4.3 all-to-all-start
  197.1 15.3 %collective-permute-done.8 = bf16[512,1024]{1,0:T(8,128)(2,1)} collective-permute-done((bf16[512,1024]{1,0:T(8,128)(2,1)}, bf16[512,1024]{1,0:T(8,128)(2,1)}, u32[]{:S(2)}, u32[]{:S(2)}) %collective-permute-start.8) | collective-permute-done | bytes 1048608 | tf_op jit(solution)/shard_map/ppermute | solution.py:363
  233.3 16.0 %collective-permute-done.25.refs_9_ = bf16[4736,128]{1,0:T(8,128)(2,1)} collective-permute-done((bf16[4736,128]{1,0:T(8,128)(2,1)S(1)}, bf16[4736,128]{1,0:T(8,128)(2,1)}, u32[]{:S(2)}, u32[]{:S(2)}) %collective-permute-start.25) | collective-permute-done | bytes 1212448 | tf_op jit(solution)/shard_map/ppermute | solution.py:409
  252.8 23.6 %attn_fwd.3 = (bf16[256,2048]{1,0:T(8,128)(2,1)}, f32[4,1,2048]{2,1,0:T(1,128)}) custom-call(s32[4]{0:T(128)} %get-tuple-element.116.lo_ref, bf16[768,2048]{1,0:T(8,128)(2,1)} %pad_maximum_fusion.2.q_ref.k_ref.v_ref, bf16[768,2048]{1,0:T(8,128)(2,1)} %pad_maximum_fusion.2.q_ref.k_ref.v_ref, bf16[768,2048]{1,0:T(8,128)(2,1)} %pad_maximum_fusion.2.q_ref.k_ref.v_ref, ...), custom_call_target="tpu_custom_call" | custom-call | flops 4294967296 | bytes 4194304 | tf_op jit(solution)/shard_map/attn_fwd/pallas_call | solution.py:121
  278.6 6.7 all-to-all-start.1
  286.0 14.6 %collective-permute-done.28.refs_12_ = bf16[4736,128]{1,0:T(8,128)(2,1)} collective-permute-done((bf16[4736,128]{1,0:T(8,128)(2,1)}, bf16[4736,128]{1,0:T(8,128)(2,1)}, u32[]{:S(2)}, u32[]{:S(2)}) %collective-permute-start.28) | collective-permute-done | bytes 1212448 | tf_op jit(solution)/shard_map/ppermute | solution.py:411
  305.6 14.4 %assemble.1 = (bf16[1024,1024]{1,0:T(8,128)(2,1)}, bf16[2816,1024]{1,0:T(8,128)(2,1)}, bf16[2816,1024]{1,0:T(8,128)(2,1)}, bf16[2816,1024]{1,0:T(8,128)(2,1)}) custom-call(s32[8]{0:T(128)} %xor_multiply_fusion.lane_ref, bf16[4736,128]{1,0:T(8,128)(2,1)} %get-tuple-element.60.refs_0_, bf16[4736,128]{1,0:T(8,128)(2,1)} %copy-done.16, ...), custom_call_target="tpu_custom_call" | custom-call | bytes 38797312 | tf_op jit(solution)/shard_map/assemble/pallas_call | solution.py:210
  320.0 4.9 multiply_reduce_fusion.2
  328.6 25.8 %ffn_main.1 = (bf16[1024,2816]{1,0:T(8,128)(2,1)}, bf16[1024,2816]{1,0:T(8,128)(2,1)}, bf16[1024,2816]{1,0:T(8,128)(2,1)}) custom-call(bf16[1024,1024]{1,0:T(8,128)(2,1)} %multiply_convert_fusion.x_ref, bf16[1024,1024]{1,0:T(8,128)(2,1)} %bitcast.140, bf16[2816,1024]{1,0:T(8,128)(2,1)} %get-tuple-element.33.gate_ref, ...), custom_call_target="tpu_custom_call" | custom-call | flops 17716740096 | bytes 34603008 | tf_op jit(solution)/shard_map/ffn_main/pallas_call | solution.py:265
  354.5 9.9 %fusion.53 = f32[1024,1024]{1,0:T(8,128)S(1)} fusion(bf16[1024,2816]{1,0:T(8,128)(2,1)} %get-tuple-element.38.du_ref, bf16[2816,1024]{1,0:T(8,128)(2,1)} %get-tuple-element.34.up_ref), kind=kOutput, calls=%fused_computation.203 | convolution fusion | flops 5905580032 | bytes 15728640 | tf_op jit(solution)/shard_map/dot_general | solution.py:303
  364.4 9.0 %multiply_reduce_fusion = (bf16[1024]{0:T(1024)(128)(2,1)S(1)}, f32[1024]{0:T(1024)S(1)}, f32[1024,1024]{1,0:T(8,128)S(1)}) fusion(f32[1024,1024]{1,0:T(8,128)S(1)} %copy-done.13, f32[1024]{0:T(1024)S(1)} %get-tuple-element.112, f32[1024]{0:T(1024)S(1)} %bitcast.159, f32[1024,1024]{1,0:T(8,128)S(1)} %fusion.53, bf16[1024,2816]{1,0:T(8,128)(2,1)S(1)} %copy-done.43, ...), kind=kOutput, calls=%fused_computation.32 | convolution fusion | flops 5912918016 | bytes 24131584 | tf_op jit(solution)/shard_map/dot_general | solution.py:303
  379.0 4.2 all-to-all-start.2
  383.4 24.9 %ffn_grad.1 = bf16[8,3,2816,128]{3,2,1,0:T(8,128)(2,1)} custom-call(bf16[1024,1024]{1,0:T(8,128)(2,1)} %multiply_convert_fusion.x_ref, bf16[1024,1024]{1,0:T(8,128)(2,1)} %bitcast.141, bf16[1024,2816]{1,0:T(8,128)(2,1)} %get-tuple-element.36.h_ref, bf16[1024,2816]{1,0:T(8,128)(2,1)} %get-tuple-element.37.dg_ref, bf16[1024,2816]{1,0:T(8,128)(2,1)} %get-tuple-element.38.du_ref), custom_call_target="tpu_custom_call" | custom-call | flops 17716740096 | bytes 34603008 | tf_op jit(solution)/shard_map/ffn_grad/pallas_call | solution.py:285
  409.4 5.1 all-to-all-start.3
  414.5 5.9 convolution_convert_fusion.2
  420.4 16.3 %all-to-all-done.3 = bf16[4,256,512]{2,1,0:T(8,128)(2,1)S(1)} async-done(((bf16[4,256,512]{2,1,0:T(8,128)(2,1)}), bf16[4,256,512]{2,1,0:T(8,128)(2,1)S(1)}, u32[]{:S(2)}, u32[]{:S(2)}) %all-to-all-start.3) | async-done | bytes 1048608 | tf_op jit(solution)/shard_map/all_to_all | solution.py:519
  437.8 32.6 %attn_bwd.2 = bf16[3,256,2048]{2,1,0:T(8,128)(2,1)} custom-call(s32[4]{0:T(128)} %get-tuple-element.129.lo_ref, bf16[768,2048]{1,0:T(8,128)(2,1)} %pad_maximum_fusion.1.q_ref.k_ref.v_ref, bf16[768,2048]{1,0:T(8,128)(2,1)} %pad_maximum_fusion.1.q_ref.k_ref.v_ref, bf16[768,2048]{1,0:T(8,128)(2,1)} %pad_maximum_fusion.1.q_ref.k_ref.v_ref, ...), custom_call_target="tpu_custom_call" | custom-call | flops 10737418240 | bytes 10485760 | tf_op jit(solution)/shard_map/attn_bwd/pallas_call | solution.py:141
  470.5 7.9 %convolution_convert_fusion.1 = bf16[2048,1024]{1,0:T(8,128)(2,1)} fusion(bf16[768,2048]{1,0:T(8,128)(2,1)} %bitcast.182, bf16[1024,768]{1,0:T(8,128)(2,1)} %bitcast.144), kind=kOutput, calls=%fused_computation.40 | convolution fusion | flops 3223322624 | bytes 8912896 | tf_op jit(solution)/shard_map/dot_general | solution.py:303
  478.4 28.6 %attn_bwd.3 = bf16[3,256,2048]{2,1,0:T(8,128)(2,1)} custom-call(s32[4]{0:T(128)} %get-tuple-element.115.lo_ref, bf16[768,2048]{1,0:T(8,128)(2,1)} %pad_maximum_fusion.2.q_ref.k_ref.v_ref, bf16[768,2048]{1,0:T(8,128)(2,1)} %pad_maximum_fusion.2.q_ref.k_ref.v_ref, bf16[768,2048]{1,0:T(8,128)(2,1)} %pad_maximum_fusion.2.q_ref.k_ref.v_ref, ...), custom_call_target="tpu_custom_call" | custom-call | flops 10737418240 | bytes 10485760 | tf_op jit(solution)/shard_map/attn_bwd/pallas_call | solution.py:141
  506.9 8.6 %fusion.9 = (f32[1024]{0:T(1024)S(1)}, bf16[2048,1024]{1,0:T(8,128)(2,1)S(1)}) fusion(f32[2048]{0:T(1024)S(1)} %add_rsqrt_fusion, bf16[3584,1024]{1,0:T(8,128)(2,1)} %copy-done.17, s32[]{:T(128)S(6)} %select_n.165, bf16[768,2048]{1,0:T(8,128)(2,1)} %bitcast.180, bf16[1024,768]{1,0:T(8,128)(2,1)} %bitcast.145), kind=kOutput, calls=%fused_computation.15 | convolution fusion | flops 3233807360 | bytes 13119492 | tf_op jit(solution)/shard_map/dot_general | solution.py:303
  522.8 4.5 collective-permute-start.41
  529.0 4.1 fusion.22
  536.8 4.1 add_convert_fusion.1
  540.9 6.6 collective-permute-done.39
  548.8 21.2 %collective-permute-done.38 = bf16[512,1024]{1,0:T(8,128)(2,1)} collective-permute-done((bf16[512,1024]{1,0:T(8,128)(2,1)S(1)}, bf16[512,1024]{1,0:T(8,128)(2,1)}, u32[]{:S(2)}, u32[]{:S(2)}) %collective-permute-start.38) | collective-permute-done | bytes 1048608 | tf_op jit(solution)/shard_map/ppermute | solution.py:384
  576.0 4.5 all-to-all-start.4
  580.5 4.4 add_convert_fusion.3
  586.9 5.5 collective-permute-done.33
  594.8 11.4 %collective-permute-done.32 = bf16[512,1024]{1,0:T(8,128)(2,1)} collective-permute-done((bf16[512,1024]{1,0:T(8,128)(2,1)}, bf16[512,1024]{1,0:T(8,128)(2,1)}, u32[]{:S(2)}, u32[]{:S(2)}) %collective-permute-start.32) | collective-permute-done | bytes 1048608 | tf_op jit(solution)/shard_map/ppermute | solution.py:384
  606.2 14.6 %collective-permute-done.35 = bf16[512,1024]{1,0:T(8,128)(2,1)} collective-permute-done((bf16[512,1024]{1,0:T(8,128)(2,1)}, bf16[512,1024]{1,0:T(8,128)(2,1)}, u32[]{:S(2)}, u32[]{:S(2)}) %collective-permute-start.35) | collective-permute-done | bytes 1048608 | tf_op jit(solution)/shard_map/ppermute | solution.py:385
  626.0 4.0 collective-permute-start.34
  630.0 10.8 %add_convert_fusion = bf16[1024,1024]{1,0:T(8,128)(2,1)} fusion(f32[1024,1024]{1,0:T(8,128)S(1)} %copy-done.14, bf16[1024,2816]{1,0:T(8,128)(2,1)} %get-tuple-element.36.h_ref, bf16[2816,1024]{1,0:T(8,128)(2,1)} %get-tuple-element.35.down_ref), kind=kOutput, calls=%fused_computation.35 | convolution fusion | flops 5907677184 | bytes 17825792 | tf_op jit(solution)/shard_map/dot_general | solution.py:303
  644.9 17.9 %collective-permute-done.37 = bf16[512,1024]{1,0:T(8,128)(2,1)S(1)} collective-permute-done((bf16[512,1024]{1,0:T(8,128)(2,1)S(1)}, bf16[512,1024]{1,0:T(8,128)(2,1)S(1)}, u32[]{:S(2)}, u32[]{:S(2)}) %collective-permute-start.37) | collective-permute-done | bytes 1048608 | tf_op jit(solution)/shard_map/ppermute | solution.py:395
  679.5 5.1 collective-permute-start.47
  684.7 10.8 %collective-permute-done.45 = bf16[2384,128]{1,0:T(8,128)(2,1)S(1)} collective-permute-done((bf16[2384,128]{1,0:T(8,128)(2,1)S(1)}, bf16[2384,128]{1,0:T(8,128)(2,1)S(1)}, u32[]{:S(2)}, u32[]{:S(2)}) %collective-permute-start.45) | collective-permute-done | bytes 610336 | tf_op jit(solution)/shard_map/ppermute | solution.py:386
  695.5 11.0 %collective-permute-done.44 = bf16[2384,128]{1,0:T(8,128)(2,1)S(1)} collective-permute-done((bf16[2384,128]{1,0:T(8,128)(2,1)S(1)}, bf16[2384,128]{1,0:T(8,128)(2,1)S(1)}, u32[]{:S(2)}, u32[]{:S(2)}) %collective-permute-start.44) | collective-permute-done | bytes 610336 | tf_op jit(solution)/shard_map/ppermute | solution.py:384
  720.3 7.1 collective-permute-done.49
  727.4 4.1 collective-permute-done.46
  (292 shorter events, 184.8 us)
Async XLA Ops:
  7.2 126.4 %all-gather.3.cloned.1.call-start = ((), (), s32[]{:S(2)}) async-start(), calls=%async_computation.7 | async-start | bytes 1990656 | tf_op jit(solution)/shard_map/all_gather | solution.py:446
  8.4 34.0 %collective-permute-start.12 = (bf16[2368,128]{1,0:T(8,128)(2,1)S(1)}, bf16[2368,128]{1,0:T(8,128)(2,1)S(1)}, u32[]{:S(2)}, u32[]{:S(2)}) collective-permute-start(bf16[2368,128]{1,0:T(8,128)(2,1)S(1)} %pad_maximum_fusion.8), channel_id=1, source_target_pairs={{0,1},{1,2},{2,3},{4,5},{5,6},{6,7},{8,9},{9,10},{10,11},{12,13},{... | collective-permute-start | bytes 1818632 | tf_op jit(solution)/shard_map/ppermute | solution.py:361
  12.0 39.6 %collective-permute-start.15 = (bf16[2368,128]{1,0:T(8,128)(2,1)S(1)}, bf16[2368,128]{1,0:T(8,128)(2,1)S(1)}, u32[]{:S(2)}, u32[]{:S(2)}) collective-permute-start(bf16[2368,128]{1,0:T(8,128)(2,1)S(1)} %pad_maximum_fusion.8), channel_id=1, source_target_pairs={{1,0},{2,1},{3,2},{5,4},{6,5},{7,6},{9,8},{10,9},{11,10},{13,12},{... | collective-permute-start | bytes 1818632 | tf_op jit(solution)/shard_map/ppermute | solution.py:362
  17.1 42.5 %collective-permute-start = (bf16[512,1024]{1,0:T(8,128)(2,1)S(1)}, bf16[512,1024]{1,0:T(8,128)(2,1)}, u32[]{:S(2)}, u32[]{:S(2)}) collective-permute-start(bf16[512,1024]{1,0:T(8,128)(2,1)S(1)} %get-tuple-element.90), channel_id=1, source_target_pairs={{0,1},{1,2},{2,3},{4,5},{5,6},{6,7},{8,9},{9,10},{10,11},{12,13},{... | collective-permute-start | bytes 3145736 | tf_op jit(solution)/shard_map/ppermute | solution.py:361
  20.8 42.1 %collective-permute-start.3 = (bf16[512,1024]{1,0:T(8,128)(2,1)S(1)}, bf16[512,1024]{1,0:T(8,128)(2,1)}, u32[]{:S(2)}, u32[]{:S(2)}) collective-permute-start(bf16[512,1024]{1,0:T(8,128)(2,1)S(1)} %get-tuple-element.90), channel_id=1, source_target_pairs={{1,0},{2,1},{3,2},{5,4},{6,5},{7,6},{9,8},{10,9},{11,10},{13,12},{... | collective-permute-start | bytes 3145736 | tf_op jit(solution)/shard_map/ppermute | solution.py:362
  43.9 51.1 %collective-permute-start.14 = (bf16[2368,128]{1,0:T(8,128)(2,1)S(1)}, bf16[2368,128]{1,0:T(8,128)(2,1)}, u32[]{:S(2)}, u32[]{:S(2)}) collective-permute-start(bf16[2368,128]{1,0:T(8,128)(2,1)S(1)} %collective-permute-done.12), channel_id=1, source_target_pairs={{1,2},{2,3},{5,6},{6,7},{9,10},{10,11},{13,14},{14,15},{17,18},{18... | collective-permute-start | bytes 1818632 | tf_op jit(solution)/shard_map/ppermute | solution.py:363
  51.7 46.2 %collective-permute-start.16 = (bf16[2368,128]{1,0:T(8,128)(2,1)S(1)}, bf16[2368,128]{1,0:T(8,128)(2,1)S(1)}, u32[]{:S(2)}, u32[]{:S(2)}) collective-permute-start(bf16[2368,128]{1,0:T(8,128)(2,1)S(1)} %collective-permute-done.15), channel_id=1, source_target_pairs={{1,0},{2,1},{5,4},{6,5},{9,8},{10,9},{13,12},{14,13},{17,16},{18,1... | collective-permute-start | bytes 1818632 | tf_op jit(solution)/shard_map/ppermute | solution.py:364
  59.6 39.7 %collective-permute-start.17 = (bf16[2368,128]{1,0:T(8,128)(2,1)S(1)}, bf16[2368,128]{1,0:T(8,128)(2,1)S(1)}, u32[]{:S(2)}, u32[]{:S(2)}) collective-permute-start(bf16[2368,128]{1,0:T(8,128)(2,1)S(1)} %collective-permute-done.15), channel_id=1, source_target_pairs={{2,0},{6,4},{10,8},{14,12},{18,16},{22,20},{26,24},{30,28}} | collective-permute-start | bytes 1818632 | tf_op jit(solution)/shard_map/ppermute | solution.py:366
  61.0 39.7 %collective-permute-start.1 = (bf16[512,1024]{1,0:T(8,128)(2,1)}, bf16[512,1024]{1,0:T(8,128)(2,1)S(1)}, u32[]{:S(2)}, u32[]{:S(2)}) collective-permute-start(bf16[512,1024]{1,0:T(8,128)(2,1)} %collective-permute-done), channel_id=1, source_target_pairs={{1,3},{5,7},{9,11},{13,15},{17,19},{21,23},{25,27},{29,31}} | collective-permute-start | bytes 3145736 | tf_op jit(solution)/shard_map/ppermute | solution.py:365
  62.8 56.5 %collective-permute-start.2 = (bf16[512,1024]{1,0:T(8,128)(2,1)}, bf16[512,1024]{1,0:T(8,128)(2,1)S(1)}, u32[]{:S(2)}, u32[]{:S(2)}) collective-permute-start(bf16[512,1024]{1,0:T(8,128)(2,1)} %collective-permute-done), channel_id=1, source_target_pairs={{1,2},{2,3},{5,6},{6,7},{9,10},{10,11},{13,14},{14,15},{17,18},{18... | collective-permute-start | bytes 3145736 | tf_op jit(solution)/shard_map/ppermute | solution.py:363
  95.0 27.1 %collective-permute-start.4 = (bf16[512,1024]{1,0:T(8,128)(2,1)}, bf16[512,1024]{1,0:T(8,128)(2,1)S(1)}, u32[]{:S(2)}, u32[]{:S(2)}) collective-permute-start(bf16[512,1024]{1,0:T(8,128)(2,1)} %collective-permute-done.3), channel_id=1, source_target_pairs={{1,0},{2,1},{5,4},{6,5},{9,8},{10,9},{13,12},{14,13},{17,16},{18,1... | collective-permute-start | bytes 3145736 | tf_op jit(solution)/shard_map/ppermute | solution.py:364
  97.9 28.4 %collective-permute-start.5 = (bf16[512,1024]{1,0:T(8,128)(2,1)}, bf16[512,1024]{1,0:T(8,128)(2,1)S(1)}, u32[]{:S(2)}, u32[]{:S(2)}) collective-permute-start(bf16[512,1024]{1,0:T(8,128)(2,1)} %collective-permute-done.3), channel_id=1, source_target_pairs={{2,0},{6,4},{10,8},{14,12},{18,16},{22,20},{26,24},{30,28}} | collective-permute-start | bytes 3145736 | tf_op jit(solution)/shard_map/ppermute | solution.py:366
  100.7 130.4 %collective-permute-start.18 = (bf16[4736,128]{1,0:T(8,128)(2,1)}, bf16[4736,128]{1,0:T(8,128)(2,1)}, u32[]{:S(2)}, u32[]{:S(2)}) collective-permute-start(bf16[4736,128]{1,0:T(8,128)(2,1)} %get-tuple-element.60.refs_0_), channel_id=1, source_target_pairs={{0,4},{4,0},{8,12},{12,8},{16,20},{20,16},{24,28},{28,24},{1,5},{5... | collective-permute-start | bytes 3637256 | tf_op jit(solution)/shard_map/ppermute | solution.py:407
  126.8 21.8 %collective-permute-start.6 = (bf16[512,1024]{1,0:T(8,128)(2,1)}, bf16[512,1024]{1,0:T(8,128)(2,1)}, u32[]{:S(2)}, u32[]{:S(2)}) collective-permute-start(bf16[512,1024]{1,0:T(8,128)(2,1)} %get-tuple-element.30), channel_id=1, source_target_pairs={{0,1},{1,2},{2,3},{4,5},{5,6},{6,7},{8,9},{9,10},{10,11},{12,13},{... | collective-permute-start | bytes 3145736 | tf_op jit(solution)/shard_map/ppermute | solution.py:361
  128.8 27.8 %collective-permute-start.9 = (bf16[512,1024]{1,0:T(8,128)(2,1)}, bf16[512,1024]{1,0:T(8,128)(2,1)}, u32[]{:S(2)}, u32[]{:S(2)}) collective-permute-start(bf16[512,1024]{1,0:T(8,128)(2,1)} %get-tuple-element.30), channel_id=1, source_target_pairs={{1,0},{2,1},{3,2},{5,4},{6,5},{7,6},{9,8},{10,9},{11,10},{13,12},{... | collective-permute-start | bytes 3145736 | tf_op jit(solution)/shard_map/ppermute | solution.py:362
  148.7 47.1 %collective-permute-start.7 = (bf16[512,1024]{1,0:T(8,128)(2,1)}, bf16[512,1024]{1,0:T(8,128)(2,1)}, u32[]{:S(2)}, u32[]{:S(2)}) collective-permute-start(bf16[512,1024]{1,0:T(8,128)(2,1)} %collective-permute-done.6), channel_id=1, source_target_pairs={{1,3},{5,7},{9,11},{13,15},{17,19},{21,23},{25,27},{29,31}} | collective-permute-start | bytes 3145736 | tf_op jit(solution)/shard_map/ppermute | solution.py:365
  150.5 61.9 %collective-permute-start.8 = (bf16[512,1024]{1,0:T(8,128)(2,1)}, bf16[512,1024]{1,0:T(8,128)(2,1)}, u32[]{:S(2)}, u32[]{:S(2)}) collective-permute-start(bf16[512,1024]{1,0:T(8,128)(2,1)} %collective-permute-done.6), channel_id=1, source_target_pairs={{1,2},{2,3},{5,6},{6,7},{9,10},{10,11},{13,14},{14,15},{17,18},{18... | collective-permute-start | bytes 3145736 | tf_op jit(solution)/shard_map/ppermute | solution.py:363
  156.5 61.1 %collective-permute-start.10 = (bf16[512,1024]{1,0:T(8,128)(2,1)}, bf16[512,1024]{1,0:T(8,128)(2,1)}, u32[]{:S(2)}, u32[]{:S(2)}) collective-permute-start(bf16[512,1024]{1,0:T(8,128)(2,1)} %collective-permute-done.9), channel_id=1, source_target_pairs={{1,0},{2,1},{5,4},{6,5},{9,8},{10,9},{13,12},{14,13},{17,16},{18,1... | collective-permute-start | bytes 3145736 | tf_op jit(solution)/shard_map/ppermute | solution.py:364
  162.8 56.7 %collective-permute-start.11 = (bf16[512,1024]{1,0:T(8,128)(2,1)}, bf16[512,1024]{1,0:T(8,128)(2,1)}, u32[]{:S(2)}, u32[]{:S(2)}) collective-permute-start(bf16[512,1024]{1,0:T(8,128)(2,1)} %collective-permute-done.9), channel_id=1, source_target_pairs={{2,0},{6,4},{10,8},{14,12},{18,16},{22,20},{26,24},{30,28}} | collective-permute-start | bytes 3145736 | tf_op jit(solution)/shard_map/ppermute | solution.py:366
  191.5 87.2 %all-to-all-start = ((bf16[256,4,512]{2,0,1:T(8,128)(2,1)}), bf16[256,4,512]{2,0,1:T(8,128)(2,1)}, u32[]{:S(2)}, u32[]{:S(2)}) async-start(bf16[256,4,512]{2,0,1:T(8,128)(2,1)} %bitcast.129), calls=%async_computation | async-start | bytes 2097152 | tf_op jit(solution)/shard_map/all_to_all | solution.py:492
  195.7 36.1 %collective-permute-start.20 = (bf16[4736,128]{1,0:T(8,128)(2,1)}, bf16[4736,128]{1,0:T(8,128)(2,1)}, u32[]{:S(2)}, u32[]{:S(2)}) collective-permute-start(bf16[4736,128]{1,0:T(8,128)(2,1)} %get-tuple-element.60.refs_0_), channel_id=1, source_target_pairs={{0,8},{4,12},{8,0},{12,4},{16,24},{20,28},{24,16},{28,20},{1,9},{5... | collective-permute-start | bytes 3637256 | tf_op jit(solution)/shard_map/ppermute | solution.py:409
  217.6 67.7 %collective-permute-start.21 = (bf16[4736,128]{1,0:T(8,128)(2,1)S(1)}, bf16[4736,128]{1,0:T(8,128)(2,1)}, u32[]{:S(2)}, u32[]{:S(2)}) collective-permute-start(bf16[4736,128]{1,0:T(8,128)(2,1)S(1)} %get-tuple-element.59.refs_1_), channel_id=1, source_target_pairs={{0,8},{4,12},{8,0},{12,4},{16,24},{20,28},{24,16},{28,20},{1,9},{5... | collective-permute-start | bytes 3637256 | tf_op jit(solution)/shard_map/ppermute | solution.py:410
  219.5 29.7 %collective-permute-start.25 = (bf16[4736,128]{1,0:T(8,128)(2,1)S(1)}, bf16[4736,128]{1,0:T(8,128)(2,1)}, u32[]{:S(2)}, u32[]{:S(2)}) collective-permute-start(bf16[4736,128]{1,0:T(8,128)(2,1)S(1)} %get-tuple-element.59.refs_1_), channel_id=1, source_target_pairs={{0,16},{4,20},{8,24},{12,28},{16,0},{20,4},{24,8},{28,12},{1,17},{... | collective-permute-start | bytes 3637256 | tf_op jit(solution)/shard_map/ppermute | solution.py:409
  231.1 54.3 %collective-permute-start.24 = (bf16[4736,128]{1,0:T(8,128)(2,1)}, bf16[4736,128]{1,0:T(8,128)(2,1)}, u32[]{:S(2)}, u32[]{:S(2)}) collective-permute-start(bf16[4736,128]{1,0:T(8,128)(2,1)} %get-tuple-element.60.refs_0_), channel_id=1, source_target_pairs={{0,16},{4,20},{8,24},{12,28},{16,0},{20,4},{24,8},{28,12},{1,17},{... | collective-permute-start | bytes 3637256 | tf_op jit(solution)/shard_map/ppermute | solution.py:410
  231.8 54.1 %collective-permute-start.22 = (bf16[4736,128]{1,0:T(8,128)(2,1)}, bf16[4736,128]{1,0:T(8,128)(2,1)}, u32[]{:S(2)}, u32[]{:S(2)}) collective-permute-start(bf16[4736,128]{1,0:T(8,128)(2,1)} %collective-permute-done.20.refs_4_), channel_id=1, source_target_pairs={{0,4},{4,0},{8,12},{12,8},{16,20},{20,16},{24,28},{28,24},{1,5},{5... | collective-permute-start | bytes 3637256 | tf_op jit(solution)/shard_map/ppermute | solution.py:407
  231.8 68.8 %collective-permute-start.28 = (bf16[4736,128]{1,0:T(8,128)(2,1)}, bf16[4736,128]{1,0:T(8,128)(2,1)}, u32[]{:S(2)}, u32[]{:S(2)}) collective-permute-start(bf16[4736,128]{1,0:T(8,128)(2,1)} %collective-permute-done.20.refs_4_), channel_id=1, source_target_pairs={{0,16},{4,20},{8,24},{12,28},{16,0},{20,4},{24,8},{28,12},{1,17},{... | collective-permute-start | bytes 3637256 | tf_op jit(solution)/shard_map/ppermute | solution.py:411
  249.2 51.4 %collective-permute-start.29 = (bf16[4736,128]{1,0:T(8,128)(2,1)}, bf16[4736,128]{1,0:T(8,128)(2,1)}, u32[]{:S(2)}, u32[]{:S(2)}) collective-permute-start(bf16[4736,128]{1,0:T(8,128)(2,1)} %collective-permute-done.25.refs_9_), channel_id=1, source_target_pairs={{0,8},{4,12},{8,0},{12,4},{16,24},{20,28},{24,16},{28,20},{1,9},{5... | collective-permute-start | bytes 3637256 | tf_op jit(solution)/shard_map/ppermute | solution.py:411
  278.6 41.4 %all-to-all-start.1 = ((bf16[256,4,512]{2,0,1:T(8,128)(2,1)}), bf16[256,4,512]{2,0,1:T(8,128)(2,1)}, u32[]{:S(2)}, u32[]{:S(2)}) async-start(bf16[256,4,512]{2,0,1:T(8,128)(2,1)} %bitcast.130), calls=%async_computation.1 | async-start | bytes 2097152 | tf_op jit(solution)/shard_map/all_to_all | solution.py:492
  379.0 29.3 %all-to-all-start.2 = ((bf16[4,256,512]{2,1,0:T(8,128)(2,1)}), bf16[4,256,512]{2,1,0:T(8,128)(2,1)S(1)}, u32[]{:S(2)}, u32[]{:S(2)}) async-start(bf16[4,256,512]{2,1,0:T(8,128)(2,1)} %bitcast.28), calls=%async_computation.2 | async-start | bytes 2097152 | tf_op jit(solution)/shard_map/all_to_all | solution.py:519
  383.2 290.4 %reduce-scatter.2.cloned.1.call-start = ((), (), s32[]{:S(2)}) async-start(), calls=%async_computation.6 | async-start | bytes 19464192 | tf_op jit(solution)/shard_map/reduce_scatter | solution.py:348
  409.4 27.3 %all-to-all-start.3 = ((bf16[4,256,512]{2,1,0:T(8,128)(2,1)}), bf16[4,256,512]{2,1,0:T(8,128)(2,1)S(1)}, u32[]{:S(2)}, u32[]{:S(2)}) async-start(bf16[4,256,512]{2,1,0:T(8,128)(2,1)} %bitcast.31), calls=%async_computation.3 | async-start | bytes 2097152 | tf_op jit(solution)/shard_map/all_to_all | solution.py:519
  518.2 29.3 %collective-permute-start.39 = (bf16[512,1024]{1,0:T(8,128)(2,1)S(1)}, bf16[512,1024]{1,0:T(8,128)(2,1)}, u32[]{:S(2)}, u32[]{:S(2)}) collective-permute-start(bf16[512,1024]{1,0:T(8,128)(2,1)S(1)} %get-tuple-element.72), channel_id=1, source_target_pairs={{0,2},{4,6},{8,10},{12,14},{16,18},{20,22},{24,26},{28,30}} | collective-permute-start | bytes 3145736 | tf_op jit(solution)/shard_map/ppermute | solution.py:386
  519.8 50.3 %collective-permute-start.38 = (bf16[512,1024]{1,0:T(8,128)(2,1)S(1)}, bf16[512,1024]{1,0:T(8,128)(2,1)}, u32[]{:S(2)}, u32[]{:S(2)}) collective-permute-start(bf16[512,1024]{1,0:T(8,128)(2,1)S(1)} %get-tuple-element.69), channel_id=1, source_target_pairs={{0,1},{1,2},{4,5},{5,6},{8,9},{9,10},{12,13},{13,14},{16,17},{17,1... | collective-permute-start | bytes 3145736 | tf_op jit(solution)/shard_map/ppermute | solution.py:384
  521.2 50.5 %collective-permute-start.42 = (bf16[512,1024]{1,0:T(8,128)(2,1)S(1)}, bf16[512,1024]{1,0:T(8,128)(2,1)}, u32[]{:S(2)}, u32[]{:S(2)}) collective-permute-start(bf16[512,1024]{1,0:T(8,128)(2,1)S(1)} %get-tuple-element.70), channel_id=1, source_target_pairs={{3,1},{7,5},{11,9},{15,13},{19,17},{23,21},{27,25},{31,29}} | collective-permute-start | bytes 3145736 | tf_op jit(solution)/shard_map/ppermute | solution.py:387
  522.8 57.7 %collective-permute-start.41 = (bf16[512,1024]{1,0:T(8,128)(2,1)}, bf16[512,1024]{1,0:T(8,128)(2,1)}, u32[]{:S(2)}, u32[]{:S(2)}) collective-permute-start(bf16[512,1024]{1,0:T(8,128)(2,1)} %get-tuple-element.71), channel_id=1, source_target_pairs={{3,2},{2,1},{7,6},{6,5},{11,10},{10,9},{15,14},{14,13},{19,18},{18... | collective-permute-start | bytes 3145736 | tf_op jit(solution)/shard_map/ppermute | solution.py:385
  535.3 57.1 %collective-permute-start.33 = (bf16[512,1024]{1,0:T(8,128)(2,1)}, bf16[512,1024]{1,0:T(8,128)(2,1)S(1)}, u32[]{:S(2)}, u32[]{:S(2)}) collective-permute-start(bf16[512,1024]{1,0:T(8,128)(2,1)} %get-tuple-element.66), channel_id=1, source_target_pairs={{0,2},{4,6},{8,10},{12,14},{16,18},{20,22},{24,26},{28,30}} | collective-permute-start | bytes 3145736 | tf_op jit(solution)/shard_map/ppermute | solution.py:386
  547.5 58.6 %collective-permute-start.32 = (bf16[512,1024]{1,0:T(8,128)(2,1)}, bf16[512,1024]{1,0:T(8,128)(2,1)}, u32[]{:S(2)}, u32[]{:S(2)}) collective-permute-start(bf16[512,1024]{1,0:T(8,128)(2,1)} %get-tuple-element.63), channel_id=1, source_target_pairs={{0,1},{1,2},{4,5},{5,6},{8,9},{9,10},{12,13},{13,14},{16,17},{17,1... | collective-permute-start | bytes 3145736 | tf_op jit(solution)/shard_map/ppermute | solution.py:384
  570.0 36.1 %collective-permute-start.36 = (bf16[512,1024]{1,0:T(8,128)(2,1)}, bf16[512,1024]{1,0:T(8,128)(2,1)}, u32[]{:S(2)}, u32[]{:S(2)}) collective-permute-start(bf16[512,1024]{1,0:T(8,128)(2,1)} %get-tuple-element.64), channel_id=1, source_target_pairs={{3,1},{7,5},{11,9},{15,13},{19,17},{23,21},{27,25},{31,29}} | collective-permute-start | bytes 3145736 | tf_op jit(solution)/shard_map/ppermute | solution.py:387
  571.7 49.0 %collective-permute-start.35 = (bf16[512,1024]{1,0:T(8,128)(2,1)}, bf16[512,1024]{1,0:T(8,128)(2,1)}, u32[]{:S(2)}, u32[]{:S(2)}) collective-permute-start(bf16[512,1024]{1,0:T(8,128)(2,1)} %get-tuple-element.65), channel_id=1, source_target_pairs={{3,2},{2,1},{7,6},{6,5},{11,10},{10,9},{15,14},{14,13},{19,18},{18... | collective-permute-start | bytes 3145736 | tf_op jit(solution)/shard_map/ppermute | solution.py:385
  576.0 90.9 %all-to-all-start.4 = ((bf16[8,144,1792]{2,1,0:T(8,128)(2,1)}), bf16[8,144,1792]{2,1,0:T(8,128)(2,1)}, u32[]{:S(2)}, u32[]{:S(2)}) async-start(bf16[8,144,1792]{2,1,0:T(8,128)(2,1)} %fusion.18), calls=%async_computation.4 | async-start | bytes 8257536 | tf_op jit(solution)/shard_map/all_to_all | solution.py:561
  585.0 58.1 %collective-permute-start.43 = (bf16[512,1024]{1,0:T(8,128)(2,1)S(1)}, bf16[512,1024]{1,0:T(8,128)(2,1)S(1)}, u32[]{:S(2)}, u32[]{:S(2)}) collective-permute-start(bf16[512,1024]{1,0:T(8,128)(2,1)S(1)} %get-tuple-element.68), channel_id=1, source_target_pairs={{1,0},{2,1},{3,2},{5,4},{6,5},{7,6},{9,8},{10,9},{11,10},{13,12},{... | collective-permute-start | bytes 3145736 | tf_op jit(solution)/shard_map/ppermute | solution.py:395
  592.4 50.7 %collective-permute-start.40 = (bf16[512,1024]{1,0:T(8,128)(2,1)S(1)}, bf16[512,1024]{1,0:T(8,128)(2,1)S(1)}, u32[]{:S(2)}, u32[]{:S(2)}) collective-permute-start(bf16[512,1024]{1,0:T(8,128)(2,1)S(1)} %get-tuple-element.67), channel_id=1, source_target_pairs={{0,1},{1,2},{2,3},{4,5},{5,6},{6,7},{8,9},{9,10},{10,11},{12,13},{... | collective-permute-start | bytes 3145736 | tf_op jit(solution)/shard_map/ppermute | solution.py:392
  624.1 38.7 %collective-permute-start.37 = (bf16[512,1024]{1,0:T(8,128)(2,1)S(1)}, bf16[512,1024]{1,0:T(8,128)(2,1)S(1)}, u32[]{:S(2)}, u32[]{:S(2)}) collective-permute-start(bf16[512,1024]{1,0:T(8,128)(2,1)S(1)} %get-tuple-element.62), channel_id=1, source_target_pairs={{1,0},{2,1},{3,2},{5,4},{6,5},{7,6},{9,8},{10,9},{11,10},{13,12},{... | collective-permute-start | bytes 3145736 | tf_op jit(solution)/shard_map/ppermute | solution.py:395
  626.0 36.8 %collective-permute-start.34 = (bf16[512,1024]{1,0:T(8,128)(2,1)S(1)}, bf16[512,1024]{1,0:T(8,128)(2,1)S(1)}, u32[]{:S(2)}, u32[]{:S(2)}) collective-permute-start(bf16[512,1024]{1,0:T(8,128)(2,1)S(1)} %get-tuple-element.61), channel_id=1, source_target_pairs={{0,1},{1,2},{2,3},{4,5},{5,6},{6,7},{8,9},{9,10},{10,11},{12,13},{... | collective-permute-start | bytes 3145736 | tf_op jit(solution)/shard_map/ppermute | solution.py:392
  675.8 19.7 %collective-permute-start.45 = (bf16[2384,128]{1,0:T(8,128)(2,1)S(1)}, bf16[2384,128]{1,0:T(8,128)(2,1)S(1)}, u32[]{:S(2)}, u32[]{:S(2)}) collective-permute-start(bf16[2384,128]{1,0:T(8,128)(2,1)S(1)} %get-tuple-element.86), channel_id=1, source_target_pairs={{0,2},{4,6},{8,10},{12,14},{16,18},{20,22},{24,26},{28,30}} | collective-permute-start | bytes 1830920 | tf_op jit(solution)/shard_map/ppermute | solution.py:386
  677.3 29.2 %collective-permute-start.44 = (bf16[2384,128]{1,0:T(8,128)(2,1)S(1)}, bf16[2384,128]{1,0:T(8,128)(2,1)S(1)}, u32[]{:S(2)}, u32[]{:S(2)}) collective-permute-start(bf16[2384,128]{1,0:T(8,128)(2,1)S(1)} %get-tuple-element.83), channel_id=1, source_target_pairs={{0,1},{1,2},{4,5},{5,6},{8,9},{9,10},{12,13},{13,14},{16,17},{17,1... | collective-permute-start | bytes 1830920 | tf_op jit(solution)/shard_map/ppermute | solution.py:384
  678.8 27.8 %collective-permute-start.48 = (bf16[2384,128]{1,0:T(8,128)(2,1)S(1)}, bf16[2384,128]{1,0:T(8,128)(2,1)S(1)}, u32[]{:S(2)}, u32[]{:S(2)}) collective-permute-start(bf16[2384,128]{1,0:T(8,128)(2,1)S(1)} %get-tuple-element.84), channel_id=1, source_target_pairs={{3,1},{7,5},{11,9},{15,13},{19,17},{23,21},{27,25},{31,29}} | collective-permute-start | bytes 1830920 | tf_op jit(solution)/shard_map/ppermute | solution.py:387
  679.5 30.9 %collective-permute-start.47 = (bf16[2384,128]{1,0:T(8,128)(2,1)S(1)}, bf16[2384,128]{1,0:T(8,128)(2,1)S(1)}, u32[]{:S(2)}, u32[]{:S(2)}) collective-permute-start(bf16[2384,128]{1,0:T(8,128)(2,1)S(1)} %get-tuple-element.85), channel_id=1, source_target_pairs={{3,2},{2,1},{7,6},{6,5},{11,10},{10,9},{15,14},{14,13},{19,18},{18... | collective-permute-start | bytes 1830920 | tf_op jit(solution)/shard_map/ppermute | solution.py:385
  (55 other events, 1262.5 us)
Sparse Core Ops, SparseCore 0:
  35.2 28.4 all-gather.2
  409.5 118.9 reduce-scatter.1

commit v5 on v4

--- a/solution.py
+++ b/solution.py
@@ -12,7 +12,7 @@
 HD = 64
 BQ = 512
 BK = 256
-BK_FORWARD = 512
+BK_FORWARD = 256
 HPS = 4
 
 
@@ -27,26 +27,31 @@
         start = start_ref[:, qcols]
         q_idx = q0 + lax.broadcasted_iota(jnp.int32, (1, bq), 1)
 
-        def k_step(kb, state):
+        def visit(kb, state, first):
             k0 = pl.multiple_of(kb * bk, bk)
-            k_idx = k0 + lax.broadcasted_iota(jnp.int32, (bk, bq), 0)
-            allowed = (k_idx >= start) & (k_idx <= q_idx)
+            wide = bq - first
+            k_idx = k0 + lax.broadcasted_iota(jnp.int32, (bk, wide), 0)
+            allowed = (k_idx >= start[:, first:]) & (k_idx <= q_idx[:, first:])
             out = []
             for h in range(heads):
-                peak, total, acc = state[h]
-                s = jnp.dot(k_scr[pl.ds(k0, bk), h * HD:(h + 1) * HD], q_blk[h * HD:(h + 1) * HD], preferred_element_type=jnp.float32)
+                peak, total, acc = (part[:, first:] for part in state[h])
+                s = jnp.dot(k_scr[pl.ds(k0, bk), h * HD:(h + 1) * HD], q_blk[h * HD:(h + 1) * HD, first:], preferred_element_type=jnp.float32)
                 s = jnp.where(allowed, s, -1e30)
                 new_peak = jnp.maximum(peak, jnp.max(s, axis=0, keepdims=True))
                 p = jnp.exp(s - new_peak)
                 fade = jnp.exp(peak - new_peak)
                 total = total * fade + jnp.sum(p, axis=0, keepdims=True)
                 acc = acc * fade + jnp.dot(v_ref[h * HD:(h + 1) * HD, pl.ds(k0, bk)], p.astype(jnp.bfloat16), preferred_element_type=jnp.float32)
-                out.append((new_peak, total, acc))
+                fresh = (new_peak, total, acc)
+                if first:
+                    fresh = tuple(jnp.concatenate([old[:, :first], new], axis=1) for old, new in zip(state[h], fresh))
+                out.append(fresh)
             return tuple(out)
 
         init = tuple((jnp.full((1, bq), -1e30, jnp.float32), jnp.zeros((1, bq), jnp.float32), jnp.zeros((HD, bq), jnp.float32)) for _ in range(heads))
         hi = (q0 + bq - 1) // bk
-        state = lax.fori_loop(lo_ref[qi], hi + 1, k_step, init)
+        state = lax.fori_loop(lo_ref[qi], hi, lambda kb, state: visit(kb, state, 0), init)
+        state = visit(hi, state, bq - bk)
         for h in range(heads):
             peak, total, acc = state[h]
             o_ref[h * HD:(h + 1) * HD, qcols] = (acc / total).astype(jnp.bfloat16)
@@ -81,26 +86,32 @@
         deltas = [jnp.sum(prod[h * HD:(h + 1) * HD], axis=0, keepdims=True) for h in range(heads)]
         lses = [lse_ref[h, :, qcols] for h in range(heads)]
 
-        def k_step(kb, state):
+        def visit(kb, state, first):
             k0 = pl.multiple_of(kb * bk, bk)
             rows = pl.ds(k0, bk)
-            k_idx = k0 + lax.broadcasted_iota(jnp.int32, (bk, bq), 0)
-            allowed = (k_idx >= start) & (k_idx <= q_idx)
+            k_idx = k0 + lax.broadcasted_iota(jnp.int32, (bk, bq - first), 0)
+            allowed = (k_idx >= start[:, first:]) & (k_idx <= q_idx[:, first:])
             out = []
             for h in range(heads):
                 hs = slice(h * HD, (h + 1) * HD)
-                s = jnp.dot(k_scr[rows, hs], q_blk[hs], preferred_element_type=jnp.float32)
-                p = jnp.exp(jnp.where(allowed, s - lses[h], -1e30))
-                dp = jnp.dot(v_scr[rows, hs], do_blk[hs], preferred_element_type=jnp.float32)
-                ds = (p * (dp - deltas[h])).astype(jnp.bfloat16)
-                dv_scr[h, rows, :] += jnp.dot(p.astype(jnp.bfloat16), do_t[:, hs], preferred_element_type=jnp.float32)
-                dk_scr[h, rows, :] += jnp.dot(ds, q_t[:, hs], preferred_element_type=jnp.float32)
-                out.append(state[h] + jnp.dot(k_ref[hs, rows], ds, preferred_element_type=jnp.float32))
+                s = jnp.dot(k_scr[rows, hs], q_blk[hs, first:], preferred_element_type=jnp.float32)
+                p = jnp.exp(jnp.where(allowed, s - lses[h][:, first:], -1e30))
+                dp = jnp.dot(v_scr[rows, hs], do_blk[hs, first:], preferred_element_type=jnp.float32)
+                ds = (p * (dp - deltas[h][:, first:])).astype(jnp.bfloat16)
+                dv_scr[h, rows, :] += jnp.dot(p.astype(jnp.bfloat16), do_t[first:, hs], preferred_element_type=jnp.float32)
+                dk_scr[h, rows, :] += jnp.dot(ds, q_t[first:, hs], preferred_element_type=jnp.float32)
+                part = jnp.dot(k_ref[hs, rows], ds, preferred_element_type=jnp.float32)
+                if first:
+                    part = jnp.concatenate([state[h][:, :first], state[h][:, first:] + part], axis=1)
+                else:
+                    part = state[h] + part
+                out.append(part)
             return tuple(out)
 
         init = tuple(jnp.zeros((HD, bq), jnp.float32) for _ in range(heads))
         hi = (q0 + bq - 1) // bk
-        state = lax.fori_loop(lo_ref[qi], hi + 1, k_step, init)
+        state = lax.fori_loop(lo_ref[qi], hi, lambda kb, state: visit(kb, state, 0), init)
+        state = visit(hi, state, bq - bk)
         cos, sin = cos_ref[:, qcols], sin_ref[:, qcols]
         for h in range(heads):
             out_ref[0, h * HD:(h + 1) * HD, qcols] = unrotate(state[h] * HD ** -0.5, cos, sin)
@@ -371,31 +382,37 @@
     return lax.dynamic_slice_in_dim(slots, (count - 1 - me) * rows, count * rows, axis=0)
 
 
-def line_scatter(partial_sum, axis):
-    count, me = lax.axis_size(axis), lax.axis_index(axis)
+def line_scatter(blocks, axis):
+    count = lax.axis_size(axis)
     assert count == 4
-    rows = partial_sum.shape[0] // count
     near_right, near_left = line_steps(count)
-
-    def block(offset):
-        first = jnp.clip(me + offset, 0, count - 1) * rows
-        return lax.dynamic_slice_in_dim(partial_sum, first, rows, axis=0)
-
-    two_right = lax.ppermute(block(2), axis, [(0, 1), (1, 2)])
-    two_left = lax.ppermute(block(-2), axis, [(3, 2), (2, 1)])
-    three_right = lax.ppermute(block(3), axis, [(0, 2)])
-    three_left = lax.ppermute(block(-3), axis, [(3, 1)])
+    own, next_one, opposite, last = blocks
+    two_right = lax.ppermute(opposite, axis, [(0, 1), (1, 2)])
+    two_left = lax.ppermute(opposite, axis, [(3, 2), (2, 1)])
+    three_right = lax.ppermute(last, axis, [(0, 2)])
+    three_left = lax.ppermute(next_one, axis, [(3, 1)])
+
+    own, next_one, last = lax.optimization_barrier((own, next_one, last))
 
     def total(*parts):
         return sum(part.astype(jnp.float32) for part in parts)
 
     right = lax.ppermute(
-        total(block(1), two_right, three_right).astype(jnp.bfloat16), axis, near_right
+        total(next_one, two_right, three_right).astype(jnp.bfloat16), axis, near_right
     )
     left = lax.ppermute(
-        total(block(-1), two_left, three_left).astype(jnp.bfloat16), axis, near_left
-    )
-    return total(block(0), right, left)
+        total(last, two_left, three_left).astype(jnp.bfloat16), axis, near_left
+    )
+    return total(own, right, left)
+
+
+def turned_blocks(whole, axis, dim):
+    count, me = lax.axis_size(axis), lax.axis_index(axis)
+    size = whole.shape[dim] // count
+    return [
+        lax.dynamic_slice_in_dim(whole, (me + place) % count * size, size, axis=dim)
+        for place in range(count)
+    ]
 
 
 def plane_gather(piece, axis, sizes):
@@ -536,13 +553,13 @@
             sin_table,
         ).reshape(3 * cols, n_mp * tokens)
         grad_qkv.append(back)
-        spread = dot_dims(back, w_qkv, 0, 1).astype(low)
-        if m == 0:
-            spread, grad_mixed_rows[1] = lax.optimization_barrier((spread, grad_mixed_rows[1]))
+        spread = [
+            dot_dims(part, w_qkv, 0, 1).astype(low) for part in turned_blocks(back, "mp", 1)
+        ]
         grad_normed.append(line_scatter(spread, "mp"))
-        gain_attn_part = gain_attn_part + jnp.sum(
-            spread.astype(jnp.float32) * rows_all[m].astype(jnp.float32) * factors[m], axis=0
-        )
+        scaled_rows = rows_all[m].astype(jnp.float32) * factors[m]
+        for part, rows in zip(spread, turned_blocks(scaled_rows, "mp", 0)):
+            gain_attn_part = gain_attn_part + jnp.sum(part.astype(jnp.float32) * rows, axis=0)
     grad_w = 0.0
     for m in range(batches):
         grad_w = grad_w + dot_dims(normed[m], grad_qkv[m], 0, 1)
@@ -574,6 +591,7 @@
         axis=1,
     )
     own_rest = own_rest.reshape(-1, depth)
+    own_rest = turned_blocks(own_rest, "mp", 0)
     own_rest = line_scatter(own_rest, "mp")
     own_output, own_gate, own_up, own_down = (
         own_rest[first : first + size] for first, size in zip(firsts, sizes)

time: 752 us -> 718 us (0.955)
  the two profiles are of different devices: /device:TPU:18 before, /device:TPU:20 now
where the time goes in v5:
time: 718 us; the launch traced here: 707 us
  waiting for transfers between devices  185 us (26%)
  Pallas kernels  164 us (23%)
  starting transfers between devices  140 us (19%)
  matrix products  84.7 us (12%)
  other arithmetic  60.2 us (8%)
  local copies, waits for them, and re-layouts  52.7 us (7%)
  between operations  21.3 us (3%)
    dot_general x18, matrix products, dot_dims(): lax.dot_general(left, right, (((left_dim,), (right_dim,)), ((), ())), pre...  84.7 us
    pallas_call x2, Pallas kernels, attn_bwd(): pl.pallas_call(functools.partial(attn_bwd_kernel, bq=bq, bk=bk, heads=hps...  52.6 us
    pallas_call x2, Pallas kernels, attn_fwd(): pl.pallas_call(functools.partial(attn_fwd_kernel, bq=bq, bk=bk, heads=hps...  46.1 us
    ppermute x3, waiting for transfers between devices, line_gather(): two_left = lax.ppermute(one_left, axis, [(1, 2), (2, 3)])  44.8 us
    ppermute x3, waiting for transfers between devices, line_scatter(): lax.ppermute(total(next_one, two_right, three_right).astype(jnp.bfloat16)...  30.7 us
    pallas_call x1, Pallas kernels, ffn_main(): pl.pallas_call(functools.partial(ffn_main_kernel, step=step), out_shape=[...  25.8 us
    unnamed x128, local copies, waits for them, and re-layouts  25.5 us
    ppermute x3, waiting for transfers between devices, line_scatter(): two_left = lax.ppermute(opposite, axis, [(3, 2), (2, 1)])  25.1 us
  transfers between devices with their start and end apart: 57, of which 18 were waited for; matrix products, arithmetic and copies ran while one was open for 22% of the time, Pallas kernels for 20%

profile of v5, /device:TPU:20, one launch (start us, length us, event | category | flops | bytes accessed | tf_op | source)
XLA Modules:
  0.0 707.0 jit_solution(1268577393597257554)
XLA Ops:
  17.1 3.6 collective-permute-start
  44.0 4.3 collective-permute-start.14
  51.7 5.0 collective-permute-start.16
  62.8 6.0 collective-permute-start.2
  68.8 26.2 %collective-permute-done.14 = bf16[2368,128]{1,0:T(8,128)(2,1)} collective-permute-done((bf16[2368,128]{1,0:T(8,128)(2,1)S(1)}, bf16[2368,128]{1,0:T(8,128)(2,1)}, u32[]{:S(2)}, u32[]{:S(2)}) %collective-permute-start.14) | collective-permute-done | bytes 606240 | tf_op jit(solution)/shard_map/ppermute | solution.py:374
  100.7 18.6 %collective-permute-done.2 = bf16[512,1024]{1,0:T(8,128)(2,1)S(1)} collective-permute-done((bf16[512,1024]{1,0:T(8,128)(2,1)}, bf16[512,1024]{1,0:T(8,128)(2,1)S(1)}, u32[]{:S(2)}, u32[]{:S(2)}) %collective-permute-start.2) | collective-permute-done | bytes 1048608 | tf_op jit(solution)/shard_map/ppermute | solution.py:374
  122.2 4.2 collective-permute-done.5
  128.8 3.9 collective-permute-start.9
  136.2 5.7 fusion.15
  143.5 5.2 collective-permute-done.6
  150.6 3.9 collective-permute-start.8
  156.6 6.3 collective-permute-start.10
  165.3 26.2 %attn_fwd.2 = (bf16[256,2048]{1,0:T(8,128)(2,1)}, f32[4,1,2048]{2,1,0:T(1,128)}) custom-call(s32[4]{0:T(128)} %get-tuple-element.133.lo_ref, bf16[768,2048]{1,0:T(8,128)(2,1)} %pad_maximum_fusion.1.q_ref.k_ref.v_ref, bf16[768,2048]{1,0:T(8,128)(2,1)} %pad_maximum_fusion.1.q_ref.k_ref.v_ref, bf16[768,2048]{1,0:T(8,128)(2,1)} %pad_maximum_fusion.1.q_ref.k_ref.v_ref, ...), custom_call_target="tpu_custom_call" | custom-call | flops 4294967296 | bytes 4194304 | tf_op jit(solution)/shard_map/attn_fwd/pallas_call | solution.py:132
  193.8 4.2 all-to-all-start
  208.1 11.4 %collective-permute-done.11 = bf16[512,1024]{1,0:T(8,128)(2,1)} collective-permute-done((bf16[512,1024]{1,0:T(8,128)(2,1)}, bf16[512,1024]{1,0:T(8,128)(2,1)}, u32[]{:S(2)}, u32[]{:S(2)}) %collective-permute-start.11) | collective-permute-done | bytes 1048608 | tf_op jit(solution)/shard_map/ppermute | solution.py:377
  223.3 3.9 fusion.16
  231.4 17.7 %collective-permute-done.25.refs_9_ = bf16[4736,128]{1,0:T(8,128)(2,1)} collective-permute-done((bf16[4736,128]{1,0:T(8,128)(2,1)S(1)}, bf16[4736,128]{1,0:T(8,128)(2,1)}, u32[]{:S(2)}, u32[]{:S(2)}) %collective-permute-start.25) | collective-permute-done | bytes 1212448 | tf_op jit(solution)/shard_map/ppermute | solution.py:426
  252.8 20.0 %attn_fwd.3 = (bf16[256,2048]{1,0:T(8,128)(2,1)}, f32[4,1,2048]{2,1,0:T(1,128)}) custom-call(s32[4]{0:T(128)} %get-tuple-element.132.lo_ref, bf16[768,2048]{1,0:T(8,128)(2,1)} %pad_maximum_fusion.2.q_ref.k_ref.v_ref, bf16[768,2048]{1,0:T(8,128)(2,1)} %pad_maximum_fusion.2.q_ref.k_ref.v_ref, bf16[768,2048]{1,0:T(8,128)(2,1)} %pad_maximum_fusion.2.q_ref.k_ref.v_ref, ...), custom_call_target="tpu_custom_call" | custom-call | flops 4294967296 | bytes 4194304 | tf_op jit(solution)/shard_map/attn_fwd/pallas_call | solution.py:132
  275.0 7.8 %all-to-all-start.1 = ((bf16[256,4,512]{2,0,1:T(8,128)(2,1)}), bf16[256,4,512]{2,0,1:T(8,128)(2,1)}, u32[]{:S(2)}, u32[]{:S(2)}) async-start(bf16[256,4,512]{2,0,1:T(8,128)(2,1)} %bitcast.147), calls=%async_computation.1 | async-start | bytes 2097152 | tf_op jit(solution)/shard_map/all_to_all | solution.py:509
  283.5 16.7 %collective-permute-done.28.refs_12_ = bf16[4736,128]{1,0:T(8,128)(2,1)} collective-permute-done((bf16[4736,128]{1,0:T(8,128)(2,1)}, bf16[4736,128]{1,0:T(8,128)(2,1)}, u32[]{:S(2)}, u32[]{:S(2)}) %collective-permute-start.28) | collective-permute-done | bytes 1212448 | tf_op jit(solution)/shard_map/ppermute | solution.py:428
  305.2 14.4 %assemble.1 = (bf16[1024,1024]{1,0:T(8,128)(2,1)}, bf16[2816,1024]{1,0:T(8,128)(2,1)}, bf16[2816,1024]{1,0:T(8,128)(2,1)}, bf16[2816,1024]{1,0:T(8,128)(2,1)}) custom-call(s32[8]{0:T(128)} %xor_multiply_fusion.lane_ref, bf16[4736,128]{1,0:T(8,128)(2,1)} %get-tuple-element.82.refs_0_, bf16[4736,128]{1,0:T(8,128)(2,1)} %copy-done.18, ...), custom_call_target="tpu_custom_call" | custom-call | bytes 38797312 | tf_op jit(solution)/shard_map/assemble/pallas_call | solution.py:221
  319.6 4.9 multiply_reduce_fusion.2
  328.2 25.8 %ffn_main.1 = (bf16[1024,2816]{1,0:T(8,128)(2,1)}, bf16[1024,2816]{1,0:T(8,128)(2,1)}, bf16[1024,2816]{1,0:T(8,128)(2,1)}) custom-call(bf16[1024,1024]{1,0:T(8,128)(2,1)} %multiply_convert_fusion.2.x_ref, bf16[1024,1024]{1,0:T(8,128)(2,1)} %bitcast.156, bf16[2816,1024]{1,0:T(8,128)(2,1)} %get-tuple-element.40.gate_ref, ...), custom_call_target="tpu_custom_call" | custom-call | flops 17716740096 | bytes 34603008 | tf_op jit(solution)/shard_map/ffn_main/pallas_call | solution.py:276
  354.0 10.0 %fusion.55 = f32[1024,1024]{1,0:T(8,128)S(1)} fusion(bf16[1024,2816]{1,0:T(8,128)(2,1)} %get-tuple-element.45.du_ref, bf16[2816,1024]{1,0:T(8,128)(2,1)} %get-tuple-element.41.up_ref), kind=kOutput, calls=%fused_computation.209 | convolution fusion | flops 5905580032 | bytes 15728640 | tf_op jit(solution)/shard_map/dot_general | solution.py:314
  364.0 9.0 %multiply_reduce_fusion = (bf16[1024]{0:T(1024)(128)(2,1)S(1)}, f32[1024]{0:T(1024)S(1)}, f32[1024,1024]{1,0:T(8,128)S(1)}) fusion(f32[1024,1024]{1,0:T(8,128)S(1)} %copy-done.12, f32[1024]{0:T(1024)S(1)} %get-tuple-element.120, f32[1024]{0:T(1024)S(1)} %bitcast.181, f32[1024,1024]{1,0:T(8,128)S(1)} %fusion.55, bf16[1024,2816]{1,0:T(8,128)(2,1)S(1)} %copy-done.43, ...), kind=kOutput, calls=%fused_computation.24 | convolution fusion | flops 5912918016 | bytes 24131584 | tf_op jit(solution)/shard_map/dot_general | solution.py:314
  378.5 4.2 all-to-all-start.2
  383.1 24.9 %ffn_grad.1 = bf16[8,3,2816,128]{3,2,1,0:T(8,128)(2,1)} custom-call(bf16[1024,1024]{1,0:T(8,128)(2,1)} %multiply_convert_fusion.2.x_ref, bf16[1024,1024]{1,0:T(8,128)(2,1)} %bitcast.157, bf16[1024,2816]{1,0:T(8,128)(2,1)} %get-tuple-element.43.h_ref, bf16[1024,2816]{1,0:T(8,128)(2,1)} %get-tuple-element.44.dg_ref, bf16[1024,2816]{1,0:T(8,128)(2,1)} %get-tuple-element.45.du_ref), custom_call_target="tpu_custom_call" | custom-call | flops 17716740096 | bytes 34603008 | tf_op jit(solution)/shard_map/ffn_grad/pallas_call | solution.py:296
  409.2 5.1 all-to-all-start.3
  414.4 8.2 %convert_multiply_fusion.2 = f32[2048,1024]{1,0:T(8,128)} fusion(bf16[2048,1024]{1,0:T(8,128)(2,1)} %copy-done, f32[2048]{0:T(1024)S(1)} %add_rsqrt_fusion.1), kind=kLoop, calls=%fused_computation.2 | loop fusion | flops 4194304 | bytes 12591104 | tf_op jit(solution)/shard_map/mul | solution.py:498
  422.6 8.4 %convert_multiply_fusion = f32[2048,1024]{1,0:T(8,128)} fusion(f32[2048]{0:T(1024)S(1)} %add_rsqrt_fusion, bf16[3584,1024]{1,0:T(8,128)(2,1)} %copy-done.17, s32[]{:T(128)S(6)} %select_n.199), kind=kLoop, calls=%fused_computation | loop fusion | flops 4194304 | bytes 12591108 | tf_op jit(solution)/shard_map/mul | solution.py:498
  430.9 5.7 convolution_convert_fusion
  437.8 23.3 %attn_bwd.3 = bf16[3,256,2048]{2,1,0:T(8,128)(2,1)} custom-call(s32[4]{0:T(128)} %get-tuple-element.132.lo_ref, bf16[768,2048]{1,0:T(8,128)(2,1)} %pad_maximum_fusion.2.q_ref.k_ref.v_ref, bf16[768,2048]{1,0:T(8,128)(2,1)} %pad_maximum_fusion.2.q_ref.k_ref.v_ref, bf16[768,2048]{1,0:T(8,128)(2,1)} %pad_maximum_fusion.2.q_ref.k_ref.v_ref, ...), custom_call_target="tpu_custom_call" | custom-call | flops 10737418240 | bytes 10485760 | tf_op jit(solution)/shard_map/attn_bwd/pallas_call | solution.py:152
  475.4 29.3 %attn_bwd.2 = bf16[3,256,2048]{2,1,0:T(8,128)(2,1)} custom-call(s32[4]{0:T(128)} %get-tuple-element.133.lo_ref, bf16[768,2048]{1,0:T(8,128)(2,1)} %pad_maximum_fusion.1.q_ref.k_ref.v_ref, bf16[768,2048]{1,0:T(8,128)(2,1)} %pad_maximum_fusion.1.q_ref.k_ref.v_ref, bf16[768,2048]{1,0:T(8,128)(2,1)} %pad_maximum_fusion.1.q_ref.k_ref.v_ref, ...), custom_call_target="tpu_custom_call" | custom-call | flops 10737418240 | bytes 10485760 | tf_op jit(solution)/shard_map/attn_bwd/pallas_call | solution.py:152
  508.1 5.2 collective-permute-start.35
  517.2 5.3 multiply_reduce_fusion.6
  522.5 4.6 multiply_reduce_fusion.9
  527.1 4.1 fusion.14
  531.3 4.4 add_convert_fusion.1
  542.1 7.8 %all-to-all-start.4 = ((bf16[8,144,1792]{2,1,0:T(8,128)(2,1)}), bf16[8,144,1792]{2,1,0:T(8,128)(2,1)}, u32[]{:S(2)}, u32[]{:S(2)}) async-start(bf16[8,144,1792]{2,1,0:T(8,128)(2,1)} %fusion.10), calls=%async_computation.4 | async-start | bytes 8257536 | tf_op jit(solution)/shard_map/all_to_all | solution.py:578
  552.4 4.2 collective-permute-start.43
  559.2 9.9 %collective-permute-start.40 = (bf16[512,1024]{1,0:T(8,128)(2,1)S(1)}, bf16[512,1024]{1,0:T(8,128)(2,1)S(1)}, u32[]{:S(2)}, u32[]{:S(2)}) collective-permute-start(bf16[512,1024]{1,0:T(8,128)(2,1)S(1)} %add_convert_fusion.3), channel_id=1, source_target_pairs={{0,1},{1,2},{2,3},{4,5},{5,6},{6,7},{8,9},{9,10},{10,11},{12,13},{... | collective-permute-start | bytes 3145736 | tf_op jit(solution)/shard_map/ppermute | solution.py:400
  571.6 3.9 collective-permute-start.37
  575.5 11.6 %collective-permute-done.32 = bf16[512,1024]{1,0:T(8,128)(2,1)S(1)} collective-permute-done((bf16[512,1024]{1,0:T(8,128)(2,1)}, bf16[512,1024]{1,0:T(8,128)(2,1)S(1)}, u32[]{:S(2)}, u32[]{:S(2)}) %collective-permute-start.32) | collective-permute-done | bytes 1048608 | tf_op jit(solution)/shard_map/ppermute | solution.py:390
  591.1 10.8 %add_convert_fusion = bf16[1024,1024]{1,0:T(8,128)(2,1)} fusion(f32[1024,1024]{1,0:T(8,128)S(1)} %copy-done.13, bf16[1024,2816]{1,0:T(8,128)(2,1)} %get-tuple-element.43.h_ref, bf16[2816,1024]{1,0:T(8,128)(2,1)} %get-tuple-element.42.down_ref), kind=kOutput, calls=%fused_computation.27 | convolution fusion | flops 5907677184 | bytes 17825792 | tf_op jit(solution)/shard_map/dot_general | solution.py:314
  601.9 7.8 %collective-permute-done.40 = bf16[512,1024]{1,0:T(8,128)(2,1)S(1)} collective-permute-done((bf16[512,1024]{1,0:T(8,128)(2,1)S(1)}, bf16[512,1024]{1,0:T(8,128)(2,1)S(1)}, u32[]{:S(2)}, u32[]{:S(2)}) %collective-permute-start.40) | collective-permute-done | bytes 1048608 | tf_op jit(solution)/shard_map/ppermute | solution.py:400
  612.5 19.6 %collective-permute-done.34 = bf16[512,1024]{1,0:T(8,128)(2,1)S(1)} collective-permute-done((bf16[512,1024]{1,0:T(8,128)(2,1)S(1)}, bf16[512,1024]{1,0:T(8,128)(2,1)S(1)}, u32[]{:S(2)}, u32[]{:S(2)}) %collective-permute-start.34) | collective-permute-done | bytes 1048608 | tf_op jit(solution)/shard_map/ppermute | solution.py:400
  650.8 25.1 %collective-permute-done.47 = bf16[2384,128]{1,0:T(8,128)(2,1)S(1)} collective-permute-done((bf16[2384,128]{1,0:T(8,128)(2,1)S(1)}, bf16[2384,128]{1,0:T(8,128)(2,1)S(1)}, u32[]{:S(2)}, u32[]{:S(2)}) %collective-permute-start.47) | collective-permute-done | bytes 610336 | tf_op jit(solution)/shard_map/ppermute | solution.py:391
  685.8 8.0 %collective-permute-done.49 = bf16[2384,128]{1,0:T(8,128)(2,1)S(1)} collective-permute-done((bf16[2384,128]{1,0:T(8,128)(2,1)S(1)}, bf16[2384,128]{1,0:T(8,128)(2,1)S(1)}, u32[]{:S(2)}, u32[]{:S(2)}) %collective-permute-start.49) | collective-permute-done | bytes 610336 | tf_op jit(solution)/shard_map/ppermute | solution.py:403
  (310 shorter events, 179.4 us)
Async XLA Ops:
  7.2 126.5 %all-gather.3.cloned.1.call-start = ((), (), s32[]{:S(2)}) async-start(), calls=%async_computation.7 | async-start | bytes 1990656 | tf_op jit(solution)/shard_map/all_gather | solution.py:463
  8.4 34.0 %collective-permute-start.12 = (bf16[2368,128]{1,0:T(8,128)(2,1)S(1)}, bf16[2368,128]{1,0:T(8,128)(2,1)S(1)}, u32[]{:S(2)}, u32[]{:S(2)}) collective-permute-start(bf16[2368,128]{1,0:T(8,128)(2,1)S(1)} %pad_maximum_fusion.8), channel_id=1, source_target_pairs={{0,1},{1,2},{2,3},{4,5},{5,6},{6,7},{8,9},{9,10},{10,11},{12,13},{... | collective-permute-start | bytes 1818632 | tf_op jit(solution)/shard_map/ppermute | solution.py:372
  12.0 39.7 %collective-permute-start.15 = (bf16[2368,128]{1,0:T(8,128)(2,1)S(1)}, bf16[2368,128]{1,0:T(8,128)(2,1)S(1)}, u32[]{:S(2)}, u32[]{:S(2)}) collective-permute-start(bf16[2368,128]{1,0:T(8,128)(2,1)S(1)} %pad_maximum_fusion.8), channel_id=1, source_target_pairs={{1,0},{2,1},{3,2},{5,4},{6,5},{7,6},{9,8},{10,9},{11,10},{13,12},{... | collective-permute-start | bytes 1818632 | tf_op jit(solution)/shard_map/ppermute | solution.py:373
  17.1 42.5 %collective-permute-start = (bf16[512,1024]{1,0:T(8,128)(2,1)S(1)}, bf16[512,1024]{1,0:T(8,128)(2,1)}, u32[]{:S(2)}, u32[]{:S(2)}) collective-permute-start(bf16[512,1024]{1,0:T(8,128)(2,1)S(1)} %get-tuple-element.98), channel_id=1, source_target_pairs={{0,1},{1,2},{2,3},{4,5},{5,6},{6,7},{8,9},{9,10},{10,11},{12,13},{... | collective-permute-start | bytes 3145736 | tf_op jit(solution)/shard_map/ppermute | solution.py:372
  20.8 42.1 %collective-permute-start.3 = (bf16[512,1024]{1,0:T(8,128)(2,1)S(1)}, bf16[512,1024]{1,0:T(8,128)(2,1)}, u32[]{:S(2)}, u32[]{:S(2)}) collective-permute-start(bf16[512,1024]{1,0:T(8,128)(2,1)S(1)} %get-tuple-element.98), channel_id=1, source_target_pairs={{1,0},{2,1},{3,2},{5,4},{6,5},{7,6},{9,8},{10,9},{11,10},{13,12},{... | collective-permute-start | bytes 3145736 | tf_op jit(solution)/shard_map/ppermute | solution.py:373
  44.0 51.1 %collective-permute-start.14 = (bf16[2368,128]{1,0:T(8,128)(2,1)S(1)}, bf16[2368,128]{1,0:T(8,128)(2,1)}, u32[]{:S(2)}, u32[]{:S(2)}) collective-permute-start(bf16[2368,128]{1,0:T(8,128)(2,1)S(1)} %collective-permute-done.12), channel_id=1, source_target_pairs={{1,2},{2,3},{5,6},{6,7},{9,10},{10,11},{13,14},{14,15},{17,18},{18... | collective-permute-start | bytes 1818632 | tf_op jit(solution)/shard_map/ppermute | solution.py:374
  51.7 46.1 %collective-permute-start.16 = (bf16[2368,128]{1,0:T(8,128)(2,1)S(1)}, bf16[2368,128]{1,0:T(8,128)(2,1)S(1)}, u32[]{:S(2)}, u32[]{:S(2)}) collective-permute-start(bf16[2368,128]{1,0:T(8,128)(2,1)S(1)} %collective-permute-done.15), channel_id=1, source_target_pairs={{1,0},{2,1},{5,4},{6,5},{9,8},{10,9},{13,12},{14,13},{17,16},{18,1... | collective-permute-start | bytes 1818632 | tf_op jit(solution)/shard_map/ppermute | solution.py:375
  59.6 39.7 %collective-permute-start.17 = (bf16[2368,128]{1,0:T(8,128)(2,1)S(1)}, bf16[2368,128]{1,0:T(8,128)(2,1)S(1)}, u32[]{:S(2)}, u32[]{:S(2)}) collective-permute-start(bf16[2368,128]{1,0:T(8,128)(2,1)S(1)} %collective-permute-done.15), channel_id=1, source_target_pairs={{2,0},{6,4},{10,8},{14,12},{18,16},{22,20},{26,24},{30,28}} | collective-permute-start | bytes 1818632 | tf_op jit(solution)/shard_map/ppermute | solution.py:377
  60.9 39.7 %collective-permute-start.1 = (bf16[512,1024]{1,0:T(8,128)(2,1)}, bf16[512,1024]{1,0:T(8,128)(2,1)S(1)}, u32[]{:S(2)}, u32[]{:S(2)}) collective-permute-start(bf16[512,1024]{1,0:T(8,128)(2,1)} %collective-permute-done), channel_id=1, source_target_pairs={{1,3},{5,7},{9,11},{13,15},{17,19},{21,23},{25,27},{29,31}} | collective-permute-start | bytes 3145736 | tf_op jit(solution)/shard_map/ppermute | solution.py:376
  62.8 56.5 %collective-permute-start.2 = (bf16[512,1024]{1,0:T(8,128)(2,1)}, bf16[512,1024]{1,0:T(8,128)(2,1)S(1)}, u32[]{:S(2)}, u32[]{:S(2)}) collective-permute-start(bf16[512,1024]{1,0:T(8,128)(2,1)} %collective-permute-done), channel_id=1, source_target_pairs={{1,2},{2,3},{5,6},{6,7},{9,10},{10,11},{13,14},{14,15},{17,18},{18... | collective-permute-start | bytes 3145736 | tf_op jit(solution)/shard_map/ppermute | solution.py:374
  95.0 27.1 %collective-permute-start.4 = (bf16[512,1024]{1,0:T(8,128)(2,1)}, bf16[512,1024]{1,0:T(8,128)(2,1)S(1)}, u32[]{:S(2)}, u32[]{:S(2)}) collective-permute-start(bf16[512,1024]{1,0:T(8,128)(2,1)} %collective-permute-done.3), channel_id=1, source_target_pairs={{1,0},{2,1},{5,4},{6,5},{9,8},{10,9},{13,12},{14,13},{17,16},{18,1... | collective-permute-start | bytes 3145736 | tf_op jit(solution)/shard_map/ppermute | solution.py:375
  97.9 28.5 %collective-permute-start.5 = (bf16[512,1024]{1,0:T(8,128)(2,1)}, bf16[512,1024]{1,0:T(8,128)(2,1)S(1)}, u32[]{:S(2)}, u32[]{:S(2)}) collective-permute-start(bf16[512,1024]{1,0:T(8,128)(2,1)} %collective-permute-done.3), channel_id=1, source_target_pairs={{2,0},{6,4},{10,8},{14,12},{18,16},{22,20},{26,24},{30,28}} | collective-permute-start | bytes 3145736 | tf_op jit(solution)/shard_map/ppermute | solution.py:377
  100.6 128.6 %collective-permute-start.18 = (bf16[4736,128]{1,0:T(8,128)(2,1)}, bf16[4736,128]{1,0:T(8,128)(2,1)}, u32[]{:S(2)}, u32[]{:S(2)}) collective-permute-start(bf16[4736,128]{1,0:T(8,128)(2,1)} %get-tuple-element.82.refs_0_), channel_id=1, source_target_pairs={{0,4},{4,0},{8,12},{12,8},{16,20},{20,16},{24,28},{28,24},{1,5},{5... | collective-permute-start | bytes 3637256 | tf_op jit(solution)/shard_map/ppermute | solution.py:424
  126.9 21.7 %collective-permute-start.6 = (bf16[512,1024]{1,0:T(8,128)(2,1)}, bf16[512,1024]{1,0:T(8,128)(2,1)}, u32[]{:S(2)}, u32[]{:S(2)}) collective-permute-start(bf16[512,1024]{1,0:T(8,128)(2,1)} %get-tuple-element.37), channel_id=1, source_target_pairs={{0,1},{1,2},{2,3},{4,5},{5,6},{6,7},{8,9},{9,10},{10,11},{12,13},{... | collective-permute-start | bytes 3145736 | tf_op jit(solution)/shard_map/ppermute | solution.py:372
  128.8 27.7 %collective-permute-start.9 = (bf16[512,1024]{1,0:T(8,128)(2,1)}, bf16[512,1024]{1,0:T(8,128)(2,1)}, u32[]{:S(2)}, u32[]{:S(2)}) collective-permute-start(bf16[512,1024]{1,0:T(8,128)(2,1)} %get-tuple-element.37), channel_id=1, source_target_pairs={{1,0},{2,1},{3,2},{5,4},{6,5},{7,6},{9,8},{10,9},{11,10},{13,12},{... | collective-permute-start | bytes 3145736 | tf_op jit(solution)/shard_map/ppermute | solution.py:373
  148.7 49.4 %collective-permute-start.7 = (bf16[512,1024]{1,0:T(8,128)(2,1)}, bf16[512,1024]{1,0:T(8,128)(2,1)}, u32[]{:S(2)}, u32[]{:S(2)}) collective-permute-start(bf16[512,1024]{1,0:T(8,128)(2,1)} %collective-permute-done.6), channel_id=1, source_target_pairs={{1,3},{5,7},{9,11},{13,15},{17,19},{21,23},{25,27},{29,31}} | collective-permute-start | bytes 3145736 | tf_op jit(solution)/shard_map/ppermute | solution.py:376
  150.6 48.8 %collective-permute-start.8 = (bf16[512,1024]{1,0:T(8,128)(2,1)}, bf16[512,1024]{1,0:T(8,128)(2,1)}, u32[]{:S(2)}, u32[]{:S(2)}) collective-permute-start(bf16[512,1024]{1,0:T(8,128)(2,1)} %collective-permute-done.6), channel_id=1, source_target_pairs={{1,2},{2,3},{5,6},{6,7},{9,10},{10,11},{13,14},{14,15},{17,18},{18... | collective-permute-start | bytes 3145736 | tf_op jit(solution)/shard_map/ppermute | solution.py:374
  156.6 48.2 %collective-permute-start.10 = (bf16[512,1024]{1,0:T(8,128)(2,1)}, bf16[512,1024]{1,0:T(8,128)(2,1)}, u32[]{:S(2)}, u32[]{:S(2)}) collective-permute-start(bf16[512,1024]{1,0:T(8,128)(2,1)} %collective-permute-done.9), channel_id=1, source_target_pairs={{1,0},{2,1},{5,4},{6,5},{9,8},{10,9},{13,12},{14,13},{17,16},{18,1... | collective-permute-start | bytes 3145736 | tf_op jit(solution)/shard_map/ppermute | solution.py:375
  162.9 56.6 %collective-permute-start.11 = (bf16[512,1024]{1,0:T(8,128)(2,1)}, bf16[512,1024]{1,0:T(8,128)(2,1)}, u32[]{:S(2)}, u32[]{:S(2)}) collective-permute-start(bf16[512,1024]{1,0:T(8,128)(2,1)} %collective-permute-done.9), channel_id=1, source_target_pairs={{2,0},{6,4},{10,8},{14,12},{18,16},{22,20},{26,24},{30,28}} | collective-permute-start | bytes 3145736 | tf_op jit(solution)/shard_map/ppermute | solution.py:377
  193.8 81.2 %all-to-all-start = ((bf16[256,4,512]{2,0,1:T(8,128)(2,1)}), bf16[256,4,512]{2,0,1:T(8,128)(2,1)}, u32[]{:S(2)}, u32[]{:S(2)}) async-start(bf16[256,4,512]{2,0,1:T(8,128)(2,1)} %bitcast.146), calls=%async_computation | async-start | bytes 2097152 | tf_op jit(solution)/shard_map/all_to_all | solution.py:509
  198.0 31.7 %collective-permute-start.20 = (bf16[4736,128]{1,0:T(8,128)(2,1)}, bf16[4736,128]{1,0:T(8,128)(2,1)}, u32[]{:S(2)}, u32[]{:S(2)}) collective-permute-start(bf16[4736,128]{1,0:T(8,128)(2,1)} %get-tuple-element.82.refs_0_), channel_id=1, source_target_pairs={{0,8},{4,12},{8,0},{12,4},{16,24},{20,28},{24,16},{28,20},{1,9},{5... | collective-permute-start | bytes 3637256 | tf_op jit(solution)/shard_map/ppermute | solution.py:426
  199.4 30.3 %collective-permute-start.19 = (bf16[4736,128]{1,0:T(8,128)(2,1)S(1)}, bf16[4736,128]{1,0:T(8,128)(2,1)S(1)}, u32[]{:S(2)}, u32[]{:S(2)}) collective-permute-start(bf16[4736,128]{1,0:T(8,128)(2,1)S(1)} %get-tuple-element.81.refs_1_), channel_id=1, source_target_pairs={{0,4},{4,0},{8,12},{12,8},{16,20},{20,16},{24,28},{28,24},{1,5},{5... | collective-permute-start | bytes 3637256 | tf_op jit(solution)/shard_map/ppermute | solution.py:424
  204.7 78.1 %collective-permute-start.21 = (bf16[4736,128]{1,0:T(8,128)(2,1)S(1)}, bf16[4736,128]{1,0:T(8,128)(2,1)}, u32[]{:S(2)}, u32[]{:S(2)}) collective-permute-start(bf16[4736,128]{1,0:T(8,128)(2,1)S(1)} %get-tuple-element.81.refs_1_), channel_id=1, source_target_pairs={{0,8},{4,12},{8,0},{12,4},{16,24},{20,28},{24,16},{28,20},{1,9},{5... | collective-permute-start | bytes 3637256 | tf_op jit(solution)/shard_map/ppermute | solution.py:427
  219.5 29.6 %collective-permute-start.25 = (bf16[4736,128]{1,0:T(8,128)(2,1)S(1)}, bf16[4736,128]{1,0:T(8,128)(2,1)}, u32[]{:S(2)}, u32[]{:S(2)}) collective-permute-start(bf16[4736,128]{1,0:T(8,128)(2,1)S(1)} %get-tuple-element.81.refs_1_), channel_id=1, source_target_pairs={{0,16},{4,20},{8,24},{12,28},{16,0},{20,4},{24,8},{28,12},{1,17},{... | collective-permute-start | bytes 3637256 | tf_op jit(solution)/shard_map/ppermute | solution.py:426
  229.2 53.7 %collective-permute-start.24 = (bf16[4736,128]{1,0:T(8,128)(2,1)}, bf16[4736,128]{1,0:T(8,128)(2,1)}, u32[]{:S(2)}, u32[]{:S(2)}) collective-permute-start(bf16[4736,128]{1,0:T(8,128)(2,1)} %get-tuple-element.82.refs_0_), channel_id=1, source_target_pairs={{0,16},{4,20},{8,24},{12,28},{16,0},{20,4},{24,8},{28,12},{1,17},{... | collective-permute-start | bytes 3637256 | tf_op jit(solution)/shard_map/ppermute | solution.py:427
  229.8 53.7 %collective-permute-start.22 = (bf16[4736,128]{1,0:T(8,128)(2,1)}, bf16[4736,128]{1,0:T(8,128)(2,1)}, u32[]{:S(2)}, u32[]{:S(2)}) collective-permute-start(bf16[4736,128]{1,0:T(8,128)(2,1)} %collective-permute-done.20.refs_4_), channel_id=1, source_target_pairs={{0,4},{4,0},{8,12},{12,8},{16,20},{20,16},{24,28},{28,24},{1,5},{5... | collective-permute-start | bytes 3637256 | tf_op jit(solution)/shard_map/ppermute | solution.py:424
  229.8 70.4 %collective-permute-start.28 = (bf16[4736,128]{1,0:T(8,128)(2,1)}, bf16[4736,128]{1,0:T(8,128)(2,1)}, u32[]{:S(2)}, u32[]{:S(2)}) collective-permute-start(bf16[4736,128]{1,0:T(8,128)(2,1)} %collective-permute-done.20.refs_4_), channel_id=1, source_target_pairs={{0,16},{4,20},{8,24},{12,28},{16,0},{20,4},{24,8},{28,12},{1,17},{... | collective-permute-start | bytes 3637256 | tf_op jit(solution)/shard_map/ppermute | solution.py:428
  249.2 51.0 %collective-permute-start.29 = (bf16[4736,128]{1,0:T(8,128)(2,1)}, bf16[4736,128]{1,0:T(8,128)(2,1)}, u32[]{:S(2)}, u32[]{:S(2)}) collective-permute-start(bf16[4736,128]{1,0:T(8,128)(2,1)} %collective-permute-done.25.refs_9_), channel_id=1, source_target_pairs={{0,8},{4,12},{8,0},{12,4},{16,24},{20,28},{24,16},{28,20},{1,9},{5... | collective-permute-start | bytes 3637256 | tf_op jit(solution)/shard_map/ppermute | solution.py:428
  275.0 44.6 %all-to-all-start.1 = ((bf16[256,4,512]{2,0,1:T(8,128)(2,1)}), bf16[256,4,512]{2,0,1:T(8,128)(2,1)}, u32[]{:S(2)}, u32[]{:S(2)}) async-start(bf16[256,4,512]{2,0,1:T(8,128)(2,1)} %bitcast.147), calls=%async_computation.1 | async-start | bytes 2097152 | tf_op jit(solution)/shard_map/all_to_all | solution.py:509
  378.5 29.5 %all-to-all-start.2 = ((bf16[4,256,512]{2,1,0:T(8,128)(2,1)}), bf16[4,256,512]{2,1,0:T(8,128)(2,1)S(1)}, u32[]{:S(2)}, u32[]{:S(2)}) async-start(bf16[4,256,512]{2,1,0:T(8,128)(2,1)} %bitcast.28), calls=%async_computation.2 | async-start | bytes 2097152 | tf_op jit(solution)/shard_map/all_to_all | solution.py:536
  382.7 260.1 %reduce-scatter.2.cloned.1.call-start = ((), (), s32[]{:S(2)}) async-start(), calls=%async_computation.6 | async-start | bytes 19464192 | tf_op jit(solution)/shard_map/reduce_scatter | solution.py:359
  409.2 27.4 %all-to-all-start.3 = ((bf16[4,256,512]{2,1,0:T(8,128)(2,1)}), bf16[4,256,512]{2,1,0:T(8,128)(2,1)S(1)}, u32[]{:S(2)}, u32[]{:S(2)}) async-start(bf16[4,256,512]{2,1,0:T(8,128)(2,1)} %bitcast.31), calls=%async_computation.3 | async-start | bytes 2097152 | tf_op jit(solution)/shard_map/all_to_all | solution.py:536
  464.5 72.5 %collective-permute-start.41 = (bf16[512,1024]{1,0:T(8,128)(2,1)}, bf16[512,1024]{1,0:T(8,128)(2,1)}, u32[]{:S(2)}, u32[]{:S(2)}) collective-permute-start(bf16[512,1024]{1,0:T(8,128)(2,1)} %convolution_convert_fusion.2), channel_id=1, source_target_pairs={{3,2},{2,1},{7,6},{6,5},{11,10},{10,9},{15,14},{14,13},{19,18},{18... | collective-permute-start | bytes 3145736 | tf_op jit(solution)/shard_map/ppermute | solution.py:391
  467.0 85.4 %collective-permute-start.38 = (bf16[512,1024]{1,0:T(8,128)(2,1)}, bf16[512,1024]{1,0:T(8,128)(2,1)}, u32[]{:S(2)}, u32[]{:S(2)}) collective-permute-start(bf16[512,1024]{1,0:T(8,128)(2,1)} %convolution_convert_fusion.2), channel_id=1, source_target_pairs={{0,1},{1,2},{4,5},{5,6},{8,9},{9,10},{12,13},{13,14},{16,17},{17,1... | collective-permute-start | bytes 3145736 | tf_op jit(solution)/shard_map/ppermute | solution.py:390
  470.5 65.3 %collective-permute-start.42 = (bf16[512,1024]{1,0:T(8,128)(2,1)}, bf16[512,1024]{1,0:T(8,128)(2,1)}, u32[]{:S(2)}, u32[]{:S(2)}) collective-permute-start(bf16[512,1024]{1,0:T(8,128)(2,1)} %convolution_convert_fusion.4), channel_id=1, source_target_pairs={{3,1},{7,5},{11,9},{15,13},{19,17},{23,21},{27,25},{31,29}} | collective-permute-start | bytes 3145736 | tf_op jit(solution)/shard_map/ppermute | solution.py:393
  474.2 64.2 %collective-permute-start.39 = (bf16[512,1024]{1,0:T(8,128)(2,1)}, bf16[512,1024]{1,0:T(8,128)(2,1)}, u32[]{:S(2)}, u32[]{:S(2)}) collective-permute-start(bf16[512,1024]{1,0:T(8,128)(2,1)} %convolution_convert_fusion.3), channel_id=1, source_target_pairs={{0,2},{4,6},{8,10},{12,14},{16,18},{20,22},{24,26},{28,30}} | collective-permute-start | bytes 3145736 | tf_op jit(solution)/shard_map/ppermute | solution.py:392
  508.1 61.0 %collective-permute-start.35 = (bf16[512,1024]{1,0:T(8,128)(2,1)}, bf16[512,1024]{1,0:T(8,128)(2,1)}, u32[]{:S(2)}, u32[]{:S(2)}) collective-permute-start(bf16[512,1024]{1,0:T(8,128)(2,1)} %convolution_convert_fusion.6), channel_id=1, source_target_pairs={{3,2},{2,1},{7,6},{6,5},{11,10},{10,9},{15,14},{14,13},{19,18},{18... | collective-permute-start | bytes 3145736 | tf_op jit(solution)/shard_map/ppermute | solution.py:391
  535.7 39.8 %collective-permute-start.33 = (bf16[512,1024]{1,0:T(8,128)(2,1)}, bf16[512,1024]{1,0:T(8,128)(2,1)S(1)}, u32[]{:S(2)}, u32[]{:S(2)}) collective-permute-start(bf16[512,1024]{1,0:T(8,128)(2,1)} %convolution_convert_fusion.7), channel_id=1, source_target_pairs={{0,2},{4,6},{8,10},{12,14},{16,18},{20,22},{24,26},{28,30}} | collective-permute-start | bytes 3145736 | tf_op jit(solution)/shard_map/ppermute | solution.py:392
  537.1 50.1 %collective-permute-start.32 = (bf16[512,1024]{1,0:T(8,128)(2,1)}, bf16[512,1024]{1,0:T(8,128)(2,1)S(1)}, u32[]{:S(2)}, u32[]{:S(2)}) collective-permute-start(bf16[512,1024]{1,0:T(8,128)(2,1)} %convolution_convert_fusion.6), channel_id=1, source_target_pairs={{0,1},{1,2},{4,5},{5,6},{8,9},{9,10},{12,13},{13,14},{16,17},{17,1... | collective-permute-start | bytes 3145736 | tf_op jit(solution)/shard_map/ppermute | solution.py:390
  538.4 20.8 %collective-permute-start.36 = (bf16[512,1024]{1,0:T(8,128)(2,1)}, bf16[512,1024]{1,0:T(8,128)(2,1)}, u32[]{:S(2)}, u32[]{:S(2)}) collective-permute-start(bf16[512,1024]{1,0:T(8,128)(2,1)} %get-tuple-element.49), channel_id=1, source_target_pairs={{3,1},{7,5},{11,9},{15,13},{19,17},{23,21},{27,25},{31,29}} | collective-permute-start | bytes 3145736 | tf_op jit(solution)/shard_map/ppermute | solution.py:393
  542.1 94.0 %all-to-all-start.4 = ((bf16[8,144,1792]{2,1,0:T(8,128)(2,1)}), bf16[8,144,1792]{2,1,0:T(8,128)(2,1)}, u32[]{:S(2)}, u32[]{:S(2)}) async-start(bf16[8,144,1792]{2,1,0:T(8,128)(2,1)} %fusion.10), calls=%async_computation.4 | async-start | bytes 8257536 | tf_op jit(solution)/shard_map/all_to_all | solution.py:578
  552.4 49.5 %collective-permute-start.43 = (bf16[512,1024]{1,0:T(8,128)(2,1)S(1)}, bf16[512,1024]{1,0:T(8,128)(2,1)S(1)}, u32[]{:S(2)}, u32[]{:S(2)}) collective-permute-start(bf16[512,1024]{1,0:T(8,128)(2,1)S(1)} %add_convert_fusion.2), channel_id=1, source_target_pairs={{1,0},{2,1},{3,2},{5,4},{6,5},{7,6},{9,8},{10,9},{11,10},{13,12},{... | collective-permute-start | bytes 3145736 | tf_op jit(solution)/shard_map/ppermute | solution.py:403
  559.2 50.5 %collective-permute-start.40 = (bf16[512,1024]{1,0:T(8,128)(2,1)S(1)}, bf16[512,1024]{1,0:T(8,128)(2,1)S(1)}, u32[]{:S(2)}, u32[]{:S(2)}) collective-permute-start(bf16[512,1024]{1,0:T(8,128)(2,1)S(1)} %add_convert_fusion.3), channel_id=1, source_target_pairs={{0,1},{1,2},{2,3},{4,5},{5,6},{6,7},{8,9},{9,10},{10,11},{12,13},{... | collective-permute-start | bytes 3145736 | tf_op jit(solution)/shard_map/ppermute | solution.py:400
  571.6 40.9 %collective-permute-start.37 = (bf16[512,1024]{1,0:T(8,128)(2,1)S(1)}, bf16[512,1024]{1,0:T(8,128)(2,1)S(1)}, u32[]{:S(2)}, u32[]{:S(2)}) collective-permute-start(bf16[512,1024]{1,0:T(8,128)(2,1)S(1)} %add_convert_fusion.4), channel_id=1, source_target_pairs={{1,0},{2,1},{3,2},{5,4},{6,5},{7,6},{9,8},{10,9},{11,10},{13,12},{... | collective-permute-start | bytes 3145736 | tf_op jit(solution)/shard_map/ppermute | solution.py:403
  589.0 43.1 %collective-permute-start.34 = (bf16[512,1024]{1,0:T(8,128)(2,1)S(1)}, bf16[512,1024]{1,0:T(8,128)(2,1)S(1)}, u32[]{:S(2)}, u32[]{:S(2)}) collective-permute-start(bf16[512,1024]{1,0:T(8,128)(2,1)S(1)} %add_convert_fusion.5), channel_id=1, source_target_pairs={{0,1},{1,2},{2,3},{4,5},{5,6},{6,7},{8,9},{9,10},{10,11},{12,13},{... | collective-permute-start | bytes 3145736 | tf_op jit(solution)/shard_map/ppermute | solution.py:400
  645.8 30.0 %collective-permute-start.47 = (bf16[2384,128]{1,0:T(8,128)(2,1)S(1)}, bf16[2384,128]{1,0:T(8,128)(2,1)S(1)}, u32[]{:S(2)}, u32[]{:S(2)}) collective-permute-start(bf16[2384,128]{1,0:T(8,128)(2,1)S(1)} %get-tuple-element.92), channel_id=1, source_target_pairs={{3,2},{2,1},{7,6},{6,5},{11,10},{10,9},{15,14},{14,13},{19,18},{18... | collective-permute-start | bytes 1830920 | tf_op jit(solution)/shard_map/ppermute | solution.py:391
  648.2 31.3 %collective-permute-start.44 = (bf16[2384,128]{1,0:T(8,128)(2,1)S(1)}, bf16[2384,128]{1,0:T(8,128)(2,1)S(1)}, u32[]{:S(2)}, u32[]{:S(2)}) collective-permute-start(bf16[2384,128]{1,0:T(8,128)(2,1)S(1)} %get-tuple-element.92), channel_id=1, source_target_pairs={{0,1},{1,2},{4,5},{5,6},{8,9},{9,10},{12,13},{13,14},{16,17},{17,1... | collective-permute-start | bytes 1830920 | tf_op jit(solution)/shard_map/ppermute | solution.py:390
  649.5 30.0 %collective-permute-start.45 = (bf16[2384,128]{1,0:T(8,128)(2,1)S(1)}, bf16[2384,128]{1,0:T(8,128)(2,1)S(1)}, u32[]{:S(2)}, u32[]{:S(2)}) collective-permute-start(bf16[2384,128]{1,0:T(8,128)(2,1)S(1)} %get-tuple-element.58), channel_id=1, source_target_pairs={{0,2},{4,6},{8,10},{12,14},{16,18},{20,22},{24,26},{28,30}} | collective-permute-start | bytes 1830920 | tf_op jit(solution)/shard_map/ppermute | solution.py:392
  (59 other events, 1272.0 us)
Sparse Core Ops, SparseCore 0:
  35.3 28.3 all-gather.2
  409.3 119.2 reduce-scatter.1

commit v6 on v5

--- a/solution.py
+++ b/solution.py
@@ -557,9 +557,12 @@
             dot_dims(part, w_qkv, 0, 1).astype(low) for part in turned_blocks(back, "mp", 1)
         ]
         grad_normed.append(line_scatter(spread, "mp"))
-        scaled_rows = rows_all[m].astype(jnp.float32) * factors[m]
-        for part, rows in zip(spread, turned_blocks(scaled_rows, "mp", 0)):
-            gain_attn_part = gain_attn_part + jnp.sum(part.astype(jnp.float32) * rows, axis=0)
+        own_rows = turned_blocks(rows_all[m], "mp", 0)
+        own_factors = turned_blocks(factors[m], "mp", 0)
+        for part, rows, factor in zip(spread, own_rows, own_factors):
+            gain_attn_part = gain_attn_part + jnp.sum(
+                part.astype(jnp.float32) * rows.astype(jnp.float32) * factor, axis=0
+            )
     grad_w = 0.0
     for m in range(batches):
         grad_w = grad_w + dot_dims(normed[m], grad_qkv[m], 0, 1)

time: 718 us -> 717 us (level)
  waiting for transfers between devices: 185 us -> 208 us
  other arithmetic: 60.2 us -> 41.9 us
    mul x2 -> x0, other arithmetic: 16.6 us -> none  [local(): normed.append((rows * factors[m] * gain_one).astype(low))]
    all_to_all x2, waiting for transfers between devices: 0.01 us -> 16.1 us  [local(): lax.all_to_all(grad_mixed[:, m * tokens:(m + 1) * tokens], 'mp', split_ax...]
    ppermute x3, waiting for transfers between devices: 8 us -> 23.2 us  [line_gather(): one_left = lax.ppermute(piece, axis, near_right)]
    unnamed x128 -> x118, local copies, waits for them, and re-layouts: 25.5 us -> 22.2 us
  transfers between devices with their start and end apart: 57 -> 57, of which waited for: 18 -> 18; matrix products, arithmetic and copies ran while one was open for 22% -> 18% of each run, Pallas kernels for 20% -> 19%
where the time goes in v6:
time: 717 us; the launch traced here: 706 us
  waiting for transfers between devices  208 us (29%)
  Pallas kernels  163 us (23%)
  starting transfers between devices  138 us (19%)
  matrix products  85.8 us (12%)
  local copies, waits for them, and re-layouts  47.5 us (7%)
  other arithmetic  41.9 us (6%)
  between operations  21.2 us (3%)
    dot_general x18, matrix products, dot_dims(): lax.dot_general(left, right, (((left_dim,), (right_dim,)), ((), ())), pre...  85.8 us
    pallas_call x2, Pallas kernels, attn_bwd(): pl.pallas_call(functools.partial(attn_bwd_kernel, bq=bq, bk=bk, heads=hps...  52.2 us
    pallas_call x2, Pallas kernels, attn_fwd(): pl.pallas_call(functools.partial(attn_fwd_kernel, bq=bq, bk=bk, heads=hps...  46.1 us
    ppermute x3, waiting for transfers between devices, line_gather(): two_left = lax.ppermute(one_left, axis, [(1, 2), (2, 3)])  44.5 us
    ppermute x3, waiting for transfers between devices, line_scatter(): lax.ppermute(total(next_one, two_right, three_right).astype(jnp.bfloat16)...  29.7 us
    pallas_call x1, Pallas kernels, ffn_main(): pl.pallas_call(functools.partial(ffn_main_kernel, step=step), out_shape=[...  25.8 us
    ppermute x3, waiting for transfers between devices, line_scatter(): two_left = lax.ppermute(opposite, axis, [(3, 2), (2, 1)])  25.1 us
    pallas_call x1, Pallas kernels, ffn_grad(): pl.pallas_call(ffn_grad_kernel, out_shape=jax.ShapeDtypeStruct((chunks, 3...  24.9 us
  transfers between devices with their start and end apart: 57, of which 18 were waited for; matrix products, arithmetic and copies ran while one was open for 18% of the time, Pallas kernels for 19%

profile of v6, /device:TPU:20, one launch (start us, length us, event | category | flops | bytes accessed | tf_op | source)
XLA Modules:
  0.0 706.2 jit_solution(11491698733528686233)
XLA Ops:
  8.4 3.5 collective-permute-start.12
  17.0 3.6 collective-permute-start
  34.5 4.2 collective-permute-start.14
  42.2 5.0 collective-permute-start.16
  47.2 13.7 %collective-permute-done = bf16[512,1024]{1,0:T(8,128)(2,1)} collective-permute-done((bf16[512,1024]{1,0:T(8,128)(2,1)S(1)}, bf16[512,1024]{1,0:T(8,128)(2,1)}, u32[]{:S(2)}, u32[]{:S(2)}) %collective-permute-start) | collective-permute-done | bytes 1048608 | tf_op jit(solution)/shard_map/ppermute | solution.py:372
  64.2 4.9 collective-permute-start.2
  69.0 27.4 %collective-permute-done.14 = bf16[2368,128]{1,0:T(8,128)(2,1)} collective-permute-done((bf16[2368,128]{1,0:T(8,128)(2,1)S(1)}, bf16[2368,128]{1,0:T(8,128)(2,1)}, u32[]{:S(2)}, u32[]{:S(2)}) %collective-permute-start.14) | collective-permute-done | bytes 606240 | tf_op jit(solution)/shard_map/ppermute | solution.py:374
  102.1 17.1 %collective-permute-done.2 = bf16[512,1024]{1,0:T(8,128)(2,1)S(1)} collective-permute-done((bf16[512,1024]{1,0:T(8,128)(2,1)}, bf16[512,1024]{1,0:T(8,128)(2,1)S(1)}, u32[]{:S(2)}, u32[]{:S(2)}) %collective-permute-start.2) | collective-permute-done | bytes 1048608 | tf_op jit(solution)/shard_map/ppermute | solution.py:374
  132.1 5.7 fusion.20
  139.4 9.5 %collective-permute-done.6 = bf16[512,1024]{1,0:T(8,128)(2,1)} collective-permute-done((bf16[512,1024]{1,0:T(8,128)(2,1)}, bf16[512,1024]{1,0:T(8,128)(2,1)}, u32[]{:S(2)}, u32[]{:S(2)}) %collective-permute-start.6) | collective-permute-done | bytes 1048608 | tf_op jit(solution)/shard_map/ppermute | solution.py:372
  155.9 6.3 collective-permute-start.10
  164.9 26.1 %attn_fwd.2 = (bf16[256,2048]{1,0:T(8,128)(2,1)}, f32[4,1,2048]{2,1,0:T(1,128)}) custom-call(s32[4]{0:T(128)} %get-tuple-element.141.lo_ref, bf16[768,2048]{1,0:T(8,128)(2,1)} %pad_maximum_fusion.1.q_ref.k_ref.v_ref, bf16[768,2048]{1,0:T(8,128)(2,1)} %pad_maximum_fusion.1.q_ref.k_ref.v_ref, bf16[768,2048]{1,0:T(8,128)(2,1)} %pad_maximum_fusion.1.q_ref.k_ref.v_ref, ...), custom_call_target="tpu_custom_call" | custom-call | flops 4294967296 | bytes 4194304 | tf_op jit(solution)/shard_map/attn_fwd/pallas_call | solution.py:132
  193.4 4.2 all-to-all-start
  207.7 11.1 %collective-permute-done.11 = bf16[512,1024]{1,0:T(8,128)(2,1)} collective-permute-done((bf16[512,1024]{1,0:T(8,128)(2,1)}, bf16[512,1024]{1,0:T(8,128)(2,1)}, u32[]{:S(2)}, u32[]{:S(2)}) %collective-permute-start.11) | collective-permute-done | bytes 1048608 | tf_op jit(solution)/shard_map/ppermute | solution.py:377
  224.6 3.8 fusion.33
  232.7 15.8 %collective-permute-done.25.refs_9_ = bf16[4736,128]{1,0:T(8,128)(2,1)} collective-permute-done((bf16[4736,128]{1,0:T(8,128)(2,1)S(1)}, bf16[4736,128]{1,0:T(8,128)(2,1)}, u32[]{:S(2)}, u32[]{:S(2)}) %collective-permute-start.25) | collective-permute-done | bytes 1212448 | tf_op jit(solution)/shard_map/ppermute | solution.py:426
  252.0 20.0 %attn_fwd.3 = (bf16[256,2048]{1,0:T(8,128)(2,1)}, f32[4,1,2048]{2,1,0:T(1,128)}) custom-call(s32[4]{0:T(128)} %get-tuple-element.140.lo_ref, bf16[768,2048]{1,0:T(8,128)(2,1)} %pad_maximum_fusion.2.q_ref.k_ref.v_ref, bf16[768,2048]{1,0:T(8,128)(2,1)} %pad_maximum_fusion.2.q_ref.k_ref.v_ref, bf16[768,2048]{1,0:T(8,128)(2,1)} %pad_maximum_fusion.2.q_ref.k_ref.v_ref, ...), custom_call_target="tpu_custom_call" | custom-call | flops 4294967296 | bytes 4194304 | tf_op jit(solution)/shard_map/attn_fwd/pallas_call | solution.py:132
  274.3 7.8 %all-to-all-start.1 = ((bf16[256,4,512]{2,0,1:T(8,128)(2,1)}), bf16[256,4,512]{2,0,1:T(8,128)(2,1)}, u32[]{:S(2)}, u32[]{:S(2)}) async-start(bf16[256,4,512]{2,0,1:T(8,128)(2,1)} %bitcast.132), calls=%async_computation.1 | async-start | bytes 2097152 | tf_op jit(solution)/shard_map/all_to_all | solution.py:509
  282.7 16.8 %collective-permute-done.28.refs_12_ = bf16[4736,128]{1,0:T(8,128)(2,1)} collective-permute-done((bf16[4736,128]{1,0:T(8,128)(2,1)}, bf16[4736,128]{1,0:T(8,128)(2,1)}, u32[]{:S(2)}, u32[]{:S(2)}) %collective-permute-start.28) | collective-permute-done | bytes 1212448 | tf_op jit(solution)/shard_map/ppermute | solution.py:428
  304.5 14.4 %assemble.1 = (bf16[1024,1024]{1,0:T(8,128)(2,1)}, bf16[2816,1024]{1,0:T(8,128)(2,1)}, bf16[2816,1024]{1,0:T(8,128)(2,1)}, bf16[2816,1024]{1,0:T(8,128)(2,1)}) custom-call(s32[8]{0:T(128)} %xor_multiply_fusion.lane_ref, bf16[4736,128]{1,0:T(8,128)(2,1)} %get-tuple-element.82.refs_0_, bf16[4736,128]{1,0:T(8,128)(2,1)} %copy-done.13, ...), custom_call_target="tpu_custom_call" | custom-call | bytes 38797312 | tf_op jit(solution)/shard_map/assemble/pallas_call | solution.py:221
  318.9 4.9 multiply_reduce_fusion.2
  326.4 25.8 %ffn_main.1 = (bf16[1024,2816]{1,0:T(8,128)(2,1)}, bf16[1024,2816]{1,0:T(8,128)(2,1)}, bf16[1024,2816]{1,0:T(8,128)(2,1)}) custom-call(bf16[1024,1024]{1,0:T(8,128)(2,1)} %multiply_convert_fusion.x_ref, bf16[1024,1024]{1,0:T(8,128)(2,1)} %bitcast.142, bf16[2816,1024]{1,0:T(8,128)(2,1)} %get-tuple-element.40.gate_ref, ...), custom_call_target="tpu_custom_call" | custom-call | flops 17716740096 | bytes 34603008 | tf_op jit(solution)/shard_map/ffn_main/pallas_call | solution.py:276
  352.2 10.0 %fusion.67 = f32[1024,1024]{1,0:T(8,128)S(1)} fusion(bf16[1024,2816]{1,0:T(8,128)(2,1)} %get-tuple-element.45.du_ref, bf16[2816,1024]{1,0:T(8,128)(2,1)} %get-tuple-element.41.up_ref), kind=kOutput, calls=%fused_computation.215 | convolution fusion | flops 5905580032 | bytes 15728640 | tf_op jit(solution)/shard_map/dot_general | solution.py:314
  362.2 9.0 %multiply_reduce_fusion = (bf16[1024]{0:T(1024)(128)(2,1)S(1)}, f32[1024]{0:T(1024)S(1)}, f32[1024,1024]{1,0:T(8,128)S(1)}) fusion(f32[1024,1024]{1,0:T(8,128)S(1)} %copy-done.11, f32[1024]{0:T(1024)S(1)} %get-tuple-element.128, f32[1024]{0:T(1024)S(1)} %bitcast.167, f32[1024,1024]{1,0:T(8,128)S(1)} %fusion.67, bf16[1024,2816]{1,0:T(8,128)(2,1)S(1)} %copy-done.42, ...), kind=kOutput, calls=%fused_computation.26 | convolution fusion | flops 5912918016 | bytes 24131584 | tf_op jit(solution)/shard_map/dot_general | solution.py:314
  376.8 4.2 all-to-all-start.2
  381.2 24.9 %ffn_grad.1 = bf16[8,3,2816,128]{3,2,1,0:T(8,128)(2,1)} custom-call(bf16[1024,1024]{1,0:T(8,128)(2,1)} %multiply_convert_fusion.x_ref, bf16[1024,1024]{1,0:T(8,128)(2,1)} %bitcast.143, bf16[1024,2816]{1,0:T(8,128)(2,1)} %get-tuple-element.43.h_ref, bf16[1024,2816]{1,0:T(8,128)(2,1)} %get-tuple-element.44.dg_ref, bf16[1024,2816]{1,0:T(8,128)(2,1)} %get-tuple-element.45.du_ref), custom_call_target="tpu_custom_call" | custom-call | flops 17716740096 | bytes 34603008 | tf_op jit(solution)/shard_map/ffn_grad/pallas_call | solution.py:296
  407.3 5.1 all-to-all-start.3
  412.6 5.9 convolution_convert_fusion
  418.5 16.1 %all-to-all-done.3 = bf16[4,256,512]{2,1,0:T(8,128)(2,1)S(1)} async-done(((bf16[4,256,512]{2,1,0:T(8,128)(2,1)}), bf16[4,256,512]{2,1,0:T(8,128)(2,1)S(1)}, u32[]{:S(2)}, u32[]{:S(2)}) %all-to-all-start.3) | async-done | bytes 1048608 | tf_op jit(solution)/shard_map/all_to_all | solution.py:536
  435.7 23.2 %attn_bwd.3 = bf16[3,256,2048]{2,1,0:T(8,128)(2,1)} custom-call(s32[4]{0:T(128)} %get-tuple-element.140.lo_ref, bf16[768,2048]{1,0:T(8,128)(2,1)} %pad_maximum_fusion.2.q_ref.k_ref.v_ref, bf16[768,2048]{1,0:T(8,128)(2,1)} %pad_maximum_fusion.2.q_ref.k_ref.v_ref, bf16[768,2048]{1,0:T(8,128)(2,1)} %pad_maximum_fusion.2.q_ref.k_ref.v_ref, ...), custom_call_target="tpu_custom_call" | custom-call | flops 10737418240 | bytes 10485760 | tf_op jit(solution)/shard_map/attn_bwd/pallas_call | solution.py:152
  458.9 4.1 convolution_convert_fusion.2
  474.2 29.1 %attn_bwd.2 = bf16[3,256,2048]{2,1,0:T(8,128)(2,1)} custom-call(s32[4]{0:T(128)} %get-tuple-element.141.lo_ref, bf16[768,2048]{1,0:T(8,128)(2,1)} %pad_maximum_fusion.1.q_ref.k_ref.v_ref, bf16[768,2048]{1,0:T(8,128)(2,1)} %pad_maximum_fusion.1.q_ref.k_ref.v_ref, bf16[768,2048]{1,0:T(8,128)(2,1)} %pad_maximum_fusion.1.q_ref.k_ref.v_ref, ...), custom_call_target="tpu_custom_call" | custom-call | flops 10737418240 | bytes 10485760 | tf_op jit(solution)/shard_map/attn_bwd/pallas_call | solution.py:152
  503.3 3.8 convolution_convert_fusion.6
  507.0 5.1 collective-permute-start.35
  516.8 4.1 fusion.18
  520.9 4.1 add_convert_fusion.1
  525.0 4.6 multiply_reduce_fusion.9
  529.6 5.3 multiply_reduce_fusion.6
  541.4 7.3 %all-to-all-start.4 = ((bf16[8,144,1792]{2,1,0:T(8,128)(2,1)}), bf16[8,144,1792]{2,1,0:T(8,128)(2,1)}, u32[]{:S(2)}, u32[]{:S(2)}) async-start(bf16[8,144,1792]{2,1,0:T(8,128)(2,1)} %fusion.14), calls=%async_computation.4 | async-start | bytes 8257536 | tf_op jit(solution)/shard_map/all_to_all | solution.py:581
  551.2 4.1 collective-permute-start.43
  557.8 10.6 %collective-permute-start.40 = (bf16[512,1024]{1,0:T(8,128)(2,1)S(1)}, bf16[512,1024]{1,0:T(8,128)(2,1)S(1)}, u32[]{:S(2)}, u32[]{:S(2)}) collective-permute-start(bf16[512,1024]{1,0:T(8,128)(2,1)S(1)} %add_convert_fusion.3), channel_id=1, source_target_pairs={{0,1},{1,2},{2,3},{4,5},{5,6},{6,7},{8,9},{9,10},{10,11},{12,13},{... | collective-permute-start | bytes 3145736 | tf_op jit(solution)/shard_map/ppermute | solution.py:400
  570.9 4.1 collective-permute-start.37
  575.0 11.4 %collective-permute-done.32 = bf16[512,1024]{1,0:T(8,128)(2,1)} collective-permute-done((bf16[512,1024]{1,0:T(8,128)(2,1)}, bf16[512,1024]{1,0:T(8,128)(2,1)}, u32[]{:S(2)}, u32[]{:S(2)}) %collective-permute-start.32) | collective-permute-done | bytes 1048608 | tf_op jit(solution)/shard_map/ppermute | solution.py:390
  591.0 11.0 %add_convert_fusion = bf16[1024,1024]{1,0:T(8,128)(2,1)} fusion(f32[1024,1024]{1,0:T(8,128)S(1)} %copy-done.12, bf16[1024,2816]{1,0:T(8,128)(2,1)} %get-tuple-element.43.h_ref, bf16[2816,1024]{1,0:T(8,128)(2,1)} %get-tuple-element.42.down_ref), kind=kOutput, calls=%fused_computation.29 | convolution fusion | flops 5907677184 | bytes 17825792 | tf_op jit(solution)/shard_map/dot_general | solution.py:314
  602.1 6.8 collective-permute-done.40
  611.8 19.6 %collective-permute-done.34 = bf16[512,1024]{1,0:T(8,128)(2,1)S(1)} collective-permute-done((bf16[512,1024]{1,0:T(8,128)(2,1)S(1)}, bf16[512,1024]{1,0:T(8,128)(2,1)S(1)}, u32[]{:S(2)}, u32[]{:S(2)}) %collective-permute-start.34) | collective-permute-done | bytes 1048608 | tf_op jit(solution)/shard_map/ppermute | solution.py:400
  650.0 25.1 %collective-permute-done.47 = bf16[2384,128]{1,0:T(8,128)(2,1)S(1)} collective-permute-done((bf16[2384,128]{1,0:T(8,128)(2,1)S(1)}, bf16[2384,128]{1,0:T(8,128)(2,1)S(1)}, u32[]{:S(2)}, u32[]{:S(2)}) %collective-permute-start.47) | collective-permute-done | bytes 610336 | tf_op jit(solution)/shard_map/ppermute | solution.py:391
  685.0 8.0 %collective-permute-done.49 = bf16[2384,128]{1,0:T(8,128)(2,1)S(1)} collective-permute-done((bf16[2384,128]{1,0:T(8,128)(2,1)S(1)}, bf16[2384,128]{1,0:T(8,128)(2,1)S(1)}, u32[]{:S(2)}, u32[]{:S(2)}) %collective-permute-start.49) | collective-permute-done | bytes 610336 | tf_op jit(solution)/shard_map/ppermute | solution.py:403
  (298 shorter events, 166.9 us)
Async XLA Ops:
  7.2 122.2 %all-gather.3.cloned.1.call-start = ((), (), s32[]{:S(2)}) async-start(), calls=%async_computation.7 | async-start | bytes 1990656 | tf_op jit(solution)/shard_map/all_gather | solution.py:463
  8.4 24.6 %collective-permute-start.12 = (bf16[2368,128]{1,0:T(8,128)(2,1)S(1)}, bf16[2368,128]{1,0:T(8,128)(2,1)S(1)}, u32[]{:S(2)}, u32[]{:S(2)}) collective-permute-start(bf16[2368,128]{1,0:T(8,128)(2,1)S(1)} %pad_maximum_fusion.8), channel_id=1, source_target_pairs={{0,1},{1,2},{2,3},{4,5},{5,6},{6,7},{8,9},{9,10},{10,11},{12,13},{... | collective-permute-start | bytes 1818632 | tf_op jit(solution)/shard_map/ppermute | solution.py:372
  11.9 30.3 %collective-permute-start.15 = (bf16[2368,128]{1,0:T(8,128)(2,1)S(1)}, bf16[2368,128]{1,0:T(8,128)(2,1)S(1)}, u32[]{:S(2)}, u32[]{:S(2)}) collective-permute-start(bf16[2368,128]{1,0:T(8,128)(2,1)S(1)} %pad_maximum_fusion.8), channel_id=1, source_target_pairs={{1,0},{2,1},{3,2},{5,4},{6,5},{7,6},{9,8},{10,9},{11,10},{13,12},{... | collective-permute-start | bytes 1818632 | tf_op jit(solution)/shard_map/ppermute | solution.py:373
  17.0 44.0 %collective-permute-start = (bf16[512,1024]{1,0:T(8,128)(2,1)S(1)}, bf16[512,1024]{1,0:T(8,128)(2,1)}, u32[]{:S(2)}, u32[]{:S(2)}) collective-permute-start(bf16[512,1024]{1,0:T(8,128)(2,1)S(1)} %get-tuple-element.98), channel_id=1, source_target_pairs={{0,1},{1,2},{2,3},{4,5},{5,6},{6,7},{8,9},{9,10},{10,11},{12,13},{... | collective-permute-start | bytes 3145736 | tf_op jit(solution)/shard_map/ppermute | solution.py:372
  20.6 43.6 %collective-permute-start.3 = (bf16[512,1024]{1,0:T(8,128)(2,1)S(1)}, bf16[512,1024]{1,0:T(8,128)(2,1)}, u32[]{:S(2)}, u32[]{:S(2)}) collective-permute-start(bf16[512,1024]{1,0:T(8,128)(2,1)S(1)} %get-tuple-element.98), channel_id=1, source_target_pairs={{1,0},{2,1},{3,2},{5,4},{6,5},{7,6},{9,8},{10,9},{11,10},{13,12},{... | collective-permute-start | bytes 3145736 | tf_op jit(solution)/shard_map/ppermute | solution.py:373
  33.0 29.3 %collective-permute-start.13 = (bf16[2368,128]{1,0:T(8,128)(2,1)S(1)}, bf16[2368,128]{1,0:T(8,128)(2,1)}, u32[]{:S(2)}, u32[]{:S(2)}) collective-permute-start(bf16[2368,128]{1,0:T(8,128)(2,1)S(1)} %collective-permute-done.12), channel_id=1, source_target_pairs={{1,3},{5,7},{9,11},{13,15},{17,19},{21,23},{25,27},{29,31}} | collective-permute-start | bytes 1818632 | tf_op jit(solution)/shard_map/ppermute | solution.py:376
  34.5 61.9 %collective-permute-start.14 = (bf16[2368,128]{1,0:T(8,128)(2,1)S(1)}, bf16[2368,128]{1,0:T(8,128)(2,1)}, u32[]{:S(2)}, u32[]{:S(2)}) collective-permute-start(bf16[2368,128]{1,0:T(8,128)(2,1)S(1)} %collective-permute-done.12), channel_id=1, source_target_pairs={{1,2},{2,3},{5,6},{6,7},{9,10},{10,11},{13,14},{14,15},{17,18},{18... | collective-permute-start | bytes 1818632 | tf_op jit(solution)/shard_map/ppermute | solution.py:374
  42.2 57.1 %collective-permute-start.16 = (bf16[2368,128]{1,0:T(8,128)(2,1)S(1)}, bf16[2368,128]{1,0:T(8,128)(2,1)S(1)}, u32[]{:S(2)}, u32[]{:S(2)}) collective-permute-start(bf16[2368,128]{1,0:T(8,128)(2,1)S(1)} %collective-permute-done.15), channel_id=1, source_target_pairs={{1,0},{2,1},{5,4},{6,5},{9,8},{10,9},{13,12},{14,13},{17,16},{18,1... | collective-permute-start | bytes 1818632 | tf_op jit(solution)/shard_map/ppermute | solution.py:375
  61.0 39.7 %collective-permute-start.17 = (bf16[2368,128]{1,0:T(8,128)(2,1)S(1)}, bf16[2368,128]{1,0:T(8,128)(2,1)S(1)}, u32[]{:S(2)}, u32[]{:S(2)}) collective-permute-start(bf16[2368,128]{1,0:T(8,128)(2,1)S(1)} %collective-permute-done.15), channel_id=1, source_target_pairs={{2,0},{6,4},{10,8},{14,12},{18,16},{22,20},{26,24},{30,28}} | collective-permute-start | bytes 1818632 | tf_op jit(solution)/shard_map/ppermute | solution.py:377
  62.3 39.7 %collective-permute-start.1 = (bf16[512,1024]{1,0:T(8,128)(2,1)}, bf16[512,1024]{1,0:T(8,128)(2,1)S(1)}, u32[]{:S(2)}, u32[]{:S(2)}) collective-permute-start(bf16[512,1024]{1,0:T(8,128)(2,1)} %collective-permute-done), channel_id=1, source_target_pairs={{1,3},{5,7},{9,11},{13,15},{17,19},{21,23},{25,27},{29,31}} | collective-permute-start | bytes 3145736 | tf_op jit(solution)/shard_map/ppermute | solution.py:376
  64.2 55.0 %collective-permute-start.2 = (bf16[512,1024]{1,0:T(8,128)(2,1)}, bf16[512,1024]{1,0:T(8,128)(2,1)S(1)}, u32[]{:S(2)}, u32[]{:S(2)}) collective-permute-start(bf16[512,1024]{1,0:T(8,128)(2,1)} %collective-permute-done), channel_id=1, source_target_pairs={{1,2},{2,3},{5,6},{6,7},{9,10},{10,11},{13,14},{14,15},{17,18},{18... | collective-permute-start | bytes 3145736 | tf_op jit(solution)/shard_map/ppermute | solution.py:374
  96.4 25.6 %collective-permute-start.4 = (bf16[512,1024]{1,0:T(8,128)(2,1)}, bf16[512,1024]{1,0:T(8,128)(2,1)S(1)}, u32[]{:S(2)}, u32[]{:S(2)}) collective-permute-start(bf16[512,1024]{1,0:T(8,128)(2,1)} %collective-permute-done.3), channel_id=1, source_target_pairs={{1,0},{2,1},{5,4},{6,5},{9,8},{10,9},{13,12},{14,13},{17,16},{18,1... | collective-permute-start | bytes 3145736 | tf_op jit(solution)/shard_map/ppermute | solution.py:375
  99.3 22.8 %collective-permute-start.5 = (bf16[512,1024]{1,0:T(8,128)(2,1)}, bf16[512,1024]{1,0:T(8,128)(2,1)S(1)}, u32[]{:S(2)}, u32[]{:S(2)}) collective-permute-start(bf16[512,1024]{1,0:T(8,128)(2,1)} %collective-permute-done.3), channel_id=1, source_target_pairs={{2,0},{6,4},{10,8},{14,12},{18,16},{22,20},{26,24},{30,28}} | collective-permute-start | bytes 3145736 | tf_op jit(solution)/shard_map/ppermute | solution.py:377
  102.0 128.5 %collective-permute-start.18 = (bf16[4736,128]{1,0:T(8,128)(2,1)}, bf16[4736,128]{1,0:T(8,128)(2,1)}, u32[]{:S(2)}, u32[]{:S(2)}) collective-permute-start(bf16[4736,128]{1,0:T(8,128)(2,1)} %get-tuple-element.82.refs_0_), channel_id=1, source_target_pairs={{0,4},{4,0},{8,12},{12,8},{16,20},{20,16},{24,28},{28,24},{1,5},{5... | collective-permute-start | bytes 3637256 | tf_op jit(solution)/shard_map/ppermute | solution.py:424
  122.6 26.3 %collective-permute-start.6 = (bf16[512,1024]{1,0:T(8,128)(2,1)}, bf16[512,1024]{1,0:T(8,128)(2,1)}, u32[]{:S(2)}, u32[]{:S(2)}) collective-permute-start(bf16[512,1024]{1,0:T(8,128)(2,1)} %get-tuple-element.37), channel_id=1, source_target_pairs={{0,1},{1,2},{2,3},{4,5},{5,6},{6,7},{8,9},{9,10},{10,11},{12,13},{... | collective-permute-start | bytes 3145736 | tf_op jit(solution)/shard_map/ppermute | solution.py:372
  126.0 29.9 %collective-permute-start.9 = (bf16[512,1024]{1,0:T(8,128)(2,1)}, bf16[512,1024]{1,0:T(8,128)(2,1)}, u32[]{:S(2)}, u32[]{:S(2)}) collective-permute-start(bf16[512,1024]{1,0:T(8,128)(2,1)} %get-tuple-element.37), channel_id=1, source_target_pairs={{1,0},{2,1},{3,2},{5,4},{6,5},{7,6},{9,8},{10,9},{11,10},{13,12},{... | collective-permute-start | bytes 3145736 | tf_op jit(solution)/shard_map/ppermute | solution.py:373
  148.9 48.8 %collective-permute-start.7 = (bf16[512,1024]{1,0:T(8,128)(2,1)}, bf16[512,1024]{1,0:T(8,128)(2,1)}, u32[]{:S(2)}, u32[]{:S(2)}) collective-permute-start(bf16[512,1024]{1,0:T(8,128)(2,1)} %collective-permute-done.6), channel_id=1, source_target_pairs={{1,3},{5,7},{9,11},{13,15},{17,19},{21,23},{25,27},{29,31}} | collective-permute-start | bytes 3145736 | tf_op jit(solution)/shard_map/ppermute | solution.py:376
  150.8 48.3 %collective-permute-start.8 = (bf16[512,1024]{1,0:T(8,128)(2,1)}, bf16[512,1024]{1,0:T(8,128)(2,1)}, u32[]{:S(2)}, u32[]{:S(2)}) collective-permute-start(bf16[512,1024]{1,0:T(8,128)(2,1)} %collective-permute-done.6), channel_id=1, source_target_pairs={{1,2},{2,3},{5,6},{6,7},{9,10},{10,11},{13,14},{14,15},{17,18},{18... | collective-permute-start | bytes 3145736 | tf_op jit(solution)/shard_map/ppermute | solution.py:374
  155.9 48.4 %collective-permute-start.10 = (bf16[512,1024]{1,0:T(8,128)(2,1)}, bf16[512,1024]{1,0:T(8,128)(2,1)}, u32[]{:S(2)}, u32[]{:S(2)}) collective-permute-start(bf16[512,1024]{1,0:T(8,128)(2,1)} %collective-permute-done.9), channel_id=1, source_target_pairs={{1,0},{2,1},{5,4},{6,5},{9,8},{10,9},{13,12},{14,13},{17,16},{18,1... | collective-permute-start | bytes 3145736 | tf_op jit(solution)/shard_map/ppermute | solution.py:375
  162.2 56.6 %collective-permute-start.11 = (bf16[512,1024]{1,0:T(8,128)(2,1)}, bf16[512,1024]{1,0:T(8,128)(2,1)}, u32[]{:S(2)}, u32[]{:S(2)}) collective-permute-start(bf16[512,1024]{1,0:T(8,128)(2,1)} %collective-permute-done.9), channel_id=1, source_target_pairs={{2,0},{6,4},{10,8},{14,12},{18,16},{22,20},{26,24},{30,28}} | collective-permute-start | bytes 3145736 | tf_op jit(solution)/shard_map/ppermute | solution.py:377
  193.4 80.9 %all-to-all-start = ((bf16[256,4,512]{2,0,1:T(8,128)(2,1)}), bf16[256,4,512]{2,0,1:T(8,128)(2,1)}, u32[]{:S(2)}, u32[]{:S(2)}) async-start(bf16[256,4,512]{2,0,1:T(8,128)(2,1)} %bitcast.131), calls=%async_computation | async-start | bytes 2097152 | tf_op jit(solution)/shard_map/all_to_all | solution.py:509
  197.6 33.4 %collective-permute-start.20 = (bf16[4736,128]{1,0:T(8,128)(2,1)}, bf16[4736,128]{1,0:T(8,128)(2,1)}, u32[]{:S(2)}, u32[]{:S(2)}) collective-permute-start(bf16[4736,128]{1,0:T(8,128)(2,1)} %get-tuple-element.82.refs_0_), channel_id=1, source_target_pairs={{0,8},{4,12},{8,0},{12,4},{16,24},{20,28},{24,16},{28,20},{1,9},{5... | collective-permute-start | bytes 3637256 | tf_op jit(solution)/shard_map/ppermute | solution.py:426
  199.0 32.0 %collective-permute-start.19 = (bf16[4736,128]{1,0:T(8,128)(2,1)S(1)}, bf16[4736,128]{1,0:T(8,128)(2,1)S(1)}, u32[]{:S(2)}, u32[]{:S(2)}) collective-permute-start(bf16[4736,128]{1,0:T(8,128)(2,1)S(1)} %get-tuple-element.81.refs_1_), channel_id=1, source_target_pairs={{0,4},{4,0},{8,12},{12,8},{16,20},{20,16},{24,28},{28,24},{1,5},{5... | collective-permute-start | bytes 3637256 | tf_op jit(solution)/shard_map/ppermute | solution.py:424
  204.3 77.7 %collective-permute-start.21 = (bf16[4736,128]{1,0:T(8,128)(2,1)S(1)}, bf16[4736,128]{1,0:T(8,128)(2,1)}, u32[]{:S(2)}, u32[]{:S(2)}) collective-permute-start(bf16[4736,128]{1,0:T(8,128)(2,1)S(1)} %get-tuple-element.81.refs_1_), channel_id=1, source_target_pairs={{0,8},{4,12},{8,0},{12,4},{16,24},{20,28},{24,16},{28,20},{1,9},{5... | collective-permute-start | bytes 3637256 | tf_op jit(solution)/shard_map/ppermute | solution.py:427
  218.8 29.6 %collective-permute-start.25 = (bf16[4736,128]{1,0:T(8,128)(2,1)S(1)}, bf16[4736,128]{1,0:T(8,128)(2,1)}, u32[]{:S(2)}, u32[]{:S(2)}) collective-permute-start(bf16[4736,128]{1,0:T(8,128)(2,1)S(1)} %get-tuple-element.81.refs_1_), channel_id=1, source_target_pairs={{0,16},{4,20},{8,24},{12,28},{16,0},{20,4},{24,8},{28,12},{1,17},{... | collective-permute-start | bytes 3637256 | tf_op jit(solution)/shard_map/ppermute | solution.py:426
  230.5 51.6 %collective-permute-start.24 = (bf16[4736,128]{1,0:T(8,128)(2,1)}, bf16[4736,128]{1,0:T(8,128)(2,1)}, u32[]{:S(2)}, u32[]{:S(2)}) collective-permute-start(bf16[4736,128]{1,0:T(8,128)(2,1)} %get-tuple-element.82.refs_0_), channel_id=1, source_target_pairs={{0,16},{4,20},{8,24},{12,28},{16,0},{20,4},{24,8},{28,12},{1,17},{... | collective-permute-start | bytes 3637256 | tf_op jit(solution)/shard_map/ppermute | solution.py:427
  231.1 51.6 %collective-permute-start.22 = (bf16[4736,128]{1,0:T(8,128)(2,1)}, bf16[4736,128]{1,0:T(8,128)(2,1)}, u32[]{:S(2)}, u32[]{:S(2)}) collective-permute-start(bf16[4736,128]{1,0:T(8,128)(2,1)} %collective-permute-done.20.refs_4_), channel_id=1, source_target_pairs={{0,4},{4,0},{8,12},{12,8},{16,20},{20,16},{24,28},{28,24},{1,5},{5... | collective-permute-start | bytes 3637256 | tf_op jit(solution)/shard_map/ppermute | solution.py:424
  231.1 68.4 %collective-permute-start.28 = (bf16[4736,128]{1,0:T(8,128)(2,1)}, bf16[4736,128]{1,0:T(8,128)(2,1)}, u32[]{:S(2)}, u32[]{:S(2)}) collective-permute-start(bf16[4736,128]{1,0:T(8,128)(2,1)} %collective-permute-done.20.refs_4_), channel_id=1, source_target_pairs={{0,16},{4,20},{8,24},{12,28},{16,0},{20,4},{24,8},{28,12},{1,17},{... | collective-permute-start | bytes 3637256 | tf_op jit(solution)/shard_map/ppermute | solution.py:428
  248.5 51.0 %collective-permute-start.29 = (bf16[4736,128]{1,0:T(8,128)(2,1)}, bf16[4736,128]{1,0:T(8,128)(2,1)}, u32[]{:S(2)}, u32[]{:S(2)}) collective-permute-start(bf16[4736,128]{1,0:T(8,128)(2,1)} %collective-permute-done.25.refs_9_), channel_id=1, source_target_pairs={{0,8},{4,12},{8,0},{12,4},{16,24},{20,28},{24,16},{28,20},{1,9},{5... | collective-permute-start | bytes 3637256 | tf_op jit(solution)/shard_map/ppermute | solution.py:428
  274.3 44.6 %all-to-all-start.1 = ((bf16[256,4,512]{2,0,1:T(8,128)(2,1)}), bf16[256,4,512]{2,0,1:T(8,128)(2,1)}, u32[]{:S(2)}, u32[]{:S(2)}) async-start(bf16[256,4,512]{2,0,1:T(8,128)(2,1)} %bitcast.132), calls=%async_computation.1 | async-start | bytes 2097152 | tf_op jit(solution)/shard_map/all_to_all | solution.py:509
  376.8 29.3 %all-to-all-start.2 = ((bf16[4,256,512]{2,1,0:T(8,128)(2,1)}), bf16[4,256,512]{2,1,0:T(8,128)(2,1)S(1)}, u32[]{:S(2)}, u32[]{:S(2)}) async-start(bf16[4,256,512]{2,1,0:T(8,128)(2,1)} %bitcast.28), calls=%async_computation.2 | async-start | bytes 2097152 | tf_op jit(solution)/shard_map/all_to_all | solution.py:536
  381.0 261.0 %reduce-scatter.2.cloned.1.call-start = ((), (), s32[]{:S(2)}) async-start(), calls=%async_computation.6 | async-start | bytes 19464192 | tf_op jit(solution)/shard_map/reduce_scatter | solution.py:359
  407.3 27.3 %all-to-all-start.3 = ((bf16[4,256,512]{2,1,0:T(8,128)(2,1)}), bf16[4,256,512]{2,1,0:T(8,128)(2,1)S(1)}, u32[]{:S(2)}, u32[]{:S(2)}) async-start(bf16[4,256,512]{2,1,0:T(8,128)(2,1)} %bitcast.31), calls=%async_computation.3 | async-start | bytes 2097152 | tf_op jit(solution)/shard_map/all_to_all | solution.py:536
  463.0 73.3 %collective-permute-start.41 = (bf16[512,1024]{1,0:T(8,128)(2,1)}, bf16[512,1024]{1,0:T(8,128)(2,1)}, u32[]{:S(2)}, u32[]{:S(2)}) collective-permute-start(bf16[512,1024]{1,0:T(8,128)(2,1)} %convolution_convert_fusion.2), channel_id=1, source_target_pairs={{3,2},{2,1},{7,6},{6,5},{11,10},{10,9},{15,14},{14,13},{19,18},{18... | collective-permute-start | bytes 3145736 | tf_op jit(solution)/shard_map/ppermute | solution.py:391
  465.5 85.7 %collective-permute-start.38 = (bf16[512,1024]{1,0:T(8,128)(2,1)}, bf16[512,1024]{1,0:T(8,128)(2,1)}, u32[]{:S(2)}, u32[]{:S(2)}) collective-permute-start(bf16[512,1024]{1,0:T(8,128)(2,1)} %convolution_convert_fusion.2), channel_id=1, source_target_pairs={{0,1},{1,2},{4,5},{5,6},{8,9},{9,10},{12,13},{13,14},{16,17},{17,1... | collective-permute-start | bytes 3145736 | tf_op jit(solution)/shard_map/ppermute | solution.py:390
  468.8 66.1 %collective-permute-start.42 = (bf16[512,1024]{1,0:T(8,128)(2,1)}, bf16[512,1024]{1,0:T(8,128)(2,1)}, u32[]{:S(2)}, u32[]{:S(2)}) collective-permute-start(bf16[512,1024]{1,0:T(8,128)(2,1)} %convolution_convert_fusion.4), channel_id=1, source_target_pairs={{3,1},{7,5},{11,9},{15,13},{19,17},{23,21},{27,25},{31,29}} | collective-permute-start | bytes 3145736 | tf_op jit(solution)/shard_map/ppermute | solution.py:393
  472.9 64.7 %collective-permute-start.39 = (bf16[512,1024]{1,0:T(8,128)(2,1)}, bf16[512,1024]{1,0:T(8,128)(2,1)}, u32[]{:S(2)}, u32[]{:S(2)}) collective-permute-start(bf16[512,1024]{1,0:T(8,128)(2,1)} %convolution_convert_fusion.3), channel_id=1, source_target_pairs={{0,2},{4,6},{8,10},{12,14},{16,18},{20,22},{24,26},{28,30}} | collective-permute-start | bytes 3145736 | tf_op jit(solution)/shard_map/ppermute | solution.py:392
  507.0 61.3 %collective-permute-start.35 = (bf16[512,1024]{1,0:T(8,128)(2,1)}, bf16[512,1024]{1,0:T(8,128)(2,1)}, u32[]{:S(2)}, u32[]{:S(2)}) collective-permute-start(bf16[512,1024]{1,0:T(8,128)(2,1)} %convolution_convert_fusion.6), channel_id=1, source_target_pairs={{3,2},{2,1},{7,6},{6,5},{11,10},{10,9},{15,14},{14,13},{19,18},{18... | collective-permute-start | bytes 3145736 | tf_op jit(solution)/shard_map/ppermute | solution.py:391
  535.0 40.1 %collective-permute-start.33 = (bf16[512,1024]{1,0:T(8,128)(2,1)}, bf16[512,1024]{1,0:T(8,128)(2,1)}, u32[]{:S(2)}, u32[]{:S(2)}) collective-permute-start(bf16[512,1024]{1,0:T(8,128)(2,1)} %convolution_convert_fusion.7), channel_id=1, source_target_pairs={{0,2},{4,6},{8,10},{12,14},{16,18},{20,22},{24,26},{28,30}} | collective-permute-start | bytes 3145736 | tf_op jit(solution)/shard_map/ppermute | solution.py:392
  536.3 50.2 %collective-permute-start.32 = (bf16[512,1024]{1,0:T(8,128)(2,1)}, bf16[512,1024]{1,0:T(8,128)(2,1)}, u32[]{:S(2)}, u32[]{:S(2)}) collective-permute-start(bf16[512,1024]{1,0:T(8,128)(2,1)} %convolution_convert_fusion.6), channel_id=1, source_target_pairs={{0,1},{1,2},{4,5},{5,6},{8,9},{9,10},{12,13},{13,14},{16,17},{17,1... | collective-permute-start | bytes 3145736 | tf_op jit(solution)/shard_map/ppermute | solution.py:390
  541.4 93.9 %all-to-all-start.4 = ((bf16[8,144,1792]{2,1,0:T(8,128)(2,1)}), bf16[8,144,1792]{2,1,0:T(8,128)(2,1)}, u32[]{:S(2)}, u32[]{:S(2)}) async-start(bf16[8,144,1792]{2,1,0:T(8,128)(2,1)} %fusion.14), calls=%async_computation.4 | async-start | bytes 8257536 | tf_op jit(solution)/shard_map/all_to_all | solution.py:581
  551.2 50.9 %collective-permute-start.43 = (bf16[512,1024]{1,0:T(8,128)(2,1)S(1)}, bf16[512,1024]{1,0:T(8,128)(2,1)S(1)}, u32[]{:S(2)}, u32[]{:S(2)}) collective-permute-start(bf16[512,1024]{1,0:T(8,128)(2,1)S(1)} %add_convert_fusion.2), channel_id=1, source_target_pairs={{1,0},{2,1},{3,2},{5,4},{6,5},{7,6},{9,8},{10,9},{11,10},{13,12},{... | collective-permute-start | bytes 3145736 | tf_op jit(solution)/shard_map/ppermute | solution.py:403
  557.8 51.0 %collective-permute-start.40 = (bf16[512,1024]{1,0:T(8,128)(2,1)S(1)}, bf16[512,1024]{1,0:T(8,128)(2,1)S(1)}, u32[]{:S(2)}, u32[]{:S(2)}) collective-permute-start(bf16[512,1024]{1,0:T(8,128)(2,1)S(1)} %add_convert_fusion.3), channel_id=1, source_target_pairs={{0,1},{1,2},{2,3},{4,5},{5,6},{6,7},{8,9},{9,10},{10,11},{12,13},{... | collective-permute-start | bytes 3145736 | tf_op jit(solution)/shard_map/ppermute | solution.py:400
  570.9 40.9 %collective-permute-start.37 = (bf16[512,1024]{1,0:T(8,128)(2,1)S(1)}, bf16[512,1024]{1,0:T(8,128)(2,1)S(1)}, u32[]{:S(2)}, u32[]{:S(2)}) collective-permute-start(bf16[512,1024]{1,0:T(8,128)(2,1)S(1)} %add_convert_fusion.4), channel_id=1, source_target_pairs={{1,0},{2,1},{3,2},{5,4},{6,5},{7,6},{9,8},{10,9},{11,10},{13,12},{... | collective-permute-start | bytes 3145736 | tf_op jit(solution)/shard_map/ppermute | solution.py:403
  589.0 42.3 %collective-permute-start.34 = (bf16[512,1024]{1,0:T(8,128)(2,1)S(1)}, bf16[512,1024]{1,0:T(8,128)(2,1)S(1)}, u32[]{:S(2)}, u32[]{:S(2)}) collective-permute-start(bf16[512,1024]{1,0:T(8,128)(2,1)S(1)} %add_convert_fusion.5), channel_id=1, source_target_pairs={{0,1},{1,2},{2,3},{4,5},{5,6},{6,7},{8,9},{9,10},{10,11},{12,13},{... | collective-permute-start | bytes 3145736 | tf_op jit(solution)/shard_map/ppermute | solution.py:400
  645.0 30.0 %collective-permute-start.47 = (bf16[2384,128]{1,0:T(8,128)(2,1)S(1)}, bf16[2384,128]{1,0:T(8,128)(2,1)S(1)}, u32[]{:S(2)}, u32[]{:S(2)}) collective-permute-start(bf16[2384,128]{1,0:T(8,128)(2,1)S(1)} %get-tuple-element.92), channel_id=1, source_target_pairs={{3,2},{2,1},{7,6},{6,5},{11,10},{10,9},{15,14},{14,13},{19,18},{18... | collective-permute-start | bytes 1830920 | tf_op jit(solution)/shard_map/ppermute | solution.py:391
  647.4 31.3 %collective-permute-start.44 = (bf16[2384,128]{1,0:T(8,128)(2,1)S(1)}, bf16[2384,128]{1,0:T(8,128)(2,1)S(1)}, u32[]{:S(2)}, u32[]{:S(2)}) collective-permute-start(bf16[2384,128]{1,0:T(8,128)(2,1)S(1)} %get-tuple-element.92), channel_id=1, source_target_pairs={{0,1},{1,2},{4,5},{5,6},{8,9},{9,10},{12,13},{13,14},{16,17},{17,1... | collective-permute-start | bytes 1830920 | tf_op jit(solution)/shard_map/ppermute | solution.py:390
  648.7 30.0 %collective-permute-start.45 = (bf16[2384,128]{1,0:T(8,128)(2,1)S(1)}, bf16[2384,128]{1,0:T(8,128)(2,1)S(1)}, u32[]{:S(2)}, u32[]{:S(2)}) collective-permute-start(bf16[2384,128]{1,0:T(8,128)(2,1)S(1)} %get-tuple-element.58), channel_id=1, source_target_pairs={{0,2},{4,6},{8,10},{12,14},{16,18},{20,22},{24,26},{28,30}} | collective-permute-start | bytes 1830920 | tf_op jit(solution)/shard_map/ppermute | solution.py:392
  (54 other events, 1102.4 us)
Sparse Core Ops, SparseCore 0:
  25.8 28.3 all-gather.2
  407.4 119.0 reduce-scatter.1

commit v7 on v6

--- a/solution.py
+++ b/solution.py
@@ -13,7 +13,7 @@
 BQ = 512
 BK = 256
 BK_FORWARD = 256
-HPS = 4
+HPS = 2
 
 
 def attn_fwd_kernel(lo_ref, q_ref, k_ref, v_ref, start_ref, o_ref, lse_ref, k_scr, *, bq, bk, heads):
@@ -305,6 +305,32 @@
         ),
         name="ffn_grad",
     )(x, c, hidden, dg, du)
+
+
+def spread_kernel(place_ref, back_ref, w_ref, out_ref):
+    out_ref[...] = dot_in(back_ref[...], w_ref[...], 0, 0).astype(jnp.bfloat16)
+
+
+def spread_block(back, w_turned, place, rows, tile=512):
+    depth, width = w_turned.shape
+    return pl.pallas_call(
+        spread_kernel,
+        out_shape=jax.ShapeDtypeStruct((rows, width), jnp.bfloat16),
+        grid_spec=pltpu.PrefetchScalarGridSpec(
+            num_scalar_prefetch=1,
+            grid=(width // tile,),
+            in_specs=[
+                pl.BlockSpec((depth, rows), lambda t, place: (0, place[0])),
+                pl.BlockSpec((depth, tile), lambda t, place: (0, t)),
+            ],
+            out_specs=pl.BlockSpec((rows, tile), lambda t, place: (0, t)),
+        ),
+        cost_estimate=pl.CostEstimate(
+            flops=2 * rows * width * depth, bytes_accessed=2 * (rows + width) * depth,
+            transcendentals=0,
+        ),
+        name="spread_block",
+    )(place.astype(jnp.int32)[None], back, w_turned)
 
 
 eps_norm = 1e-05
@@ -541,10 +567,16 @@
     grad_output = dot_dims(grad_branch, mixed_both, 0, 1).astype(low)
 
     grad_mixed_rows[0], every_grad = lax.optimization_barrier((grad_mixed_rows[0], every_grad))
+    own_out = lax.all_to_all(
+        grad_output.reshape(n_dp, depth, n_mp * cols), "dp", split_axis=0, concat_axis=0,
+        tiled=True,
+    )
+    own_out = jnp.sum(own_out.astype(jnp.float32), axis=0).astype(low)
     mine = scatter(every_grad, "dp", 0)
 
 
     grad_qkv, grad_normed = [], []
+    w_turned = w_qkv.T
     gain_attn_part = jnp.zeros((width,), jnp.float32)
     for m in range(batches):
         cos_table, sin_table = tables[m]
@@ -553,9 +585,7 @@
             sin_table,
         ).reshape(3 * cols, n_mp * tokens)
         grad_qkv.append(back)
-        spread = [
-            dot_dims(part, w_qkv, 0, 1).astype(low) for part in turned_blocks(back, "mp", 1)
-        ]
+        spread = [spread_block(back, w_turned, (lax.axis_index("mp") + place) % n_mp, tokens) for place in range(n_mp)]
         grad_normed.append(line_scatter(spread, "mp"))
         own_rows = turned_blocks(rows_all[m], "mp", 0)
         own_factors = turned_blocks(factors[m], "mp", 0)
@@ -569,25 +599,20 @@
 
     gain_parts = jnp.stack([gain_attn_part, gain_ffn_part]).astype(low)
     gain_parts = gain_parts.reshape(2, n_dp, depth).transpose(1, 0, 2).reshape(n_dp, 1, 2 * depth)
-    sums = jnp.concatenate(
-        [
-            grad_w.astype(low).reshape(n_dp, depth, 3 * cols),
-            grad_output.reshape(n_dp, depth, n_mp * cols),
-        ],
-        axis=2,
-    )
+    sums = grad_w.astype(low).reshape(n_dp, depth, 3 * cols)
+    assert 2 * depth <= 3 * cols
     gain_rows = jnp.pad(gain_parts, ((0, 0), (0, 15), (0, sums.shape[2] - 2 * depth)))
     sums = jnp.concatenate([sums, gain_rows], axis=1)
     sums = lax.all_to_all(sums, "dp", split_axis=0, concat_axis=0, tiled=True)
     sums = jnp.sum(sums.astype(jnp.float32), axis=0)
-    own_qkv, own_out = sums[:depth, : 3 * cols], sums[:depth, 3 * cols :]
+    own_qkv = sums[:depth]
     own_gain = sums[depth, : 2 * depth].reshape(2, n_mp, depth // n_mp).transpose(1, 0, 2)
     own_gain = own_gain.reshape(n_mp, 1, 2 * depth // n_mp)
     own_gain = jnp.pad(own_gain.astype(low), ((0, 0), (0, 15), (0, depth - own_gain.shape[2])))
     own_ffn = mine.reshape(3, n_mp, hidden_part, depth).transpose(1, 0, 2, 3)
     own_rest = jnp.concatenate(
         [
-            own_out.T.astype(low).reshape(n_mp, cols, depth),
+            own_out.T.reshape(n_mp, cols, depth),
             own_ffn.reshape(n_mp, -1, depth),
             own_gain,
         ],

time: 717 us -> 741 us (1.033)
  Pallas kernels: 163 us -> 196 us
  matrix products: 85.8 us -> 68.3 us
  other arithmetic: 41.9 us -> 57.8 us
    pallas_call x0 -> x8, Pallas kernels: none -> 27.9 us  [spread_block(): pl.pallas_call(spread_kernel, out_shape=jax.ShapeDtypeStruct((rows, width...]
    dot_general x18 -> x10, matrix products: 85.8 us -> 68.3 us  [dot_dims(): lax.dot_general(left, right, (((left_dim,), (right_dim,)), ((), ())), pre...]
    ppermute x3, waiting for transfers between devices: 23.2 us -> 7.81 us  [line_gather(): one_left = lax.ppermute(piece, axis, near_right)]
    ppermute x3, waiting for transfers between devices: 29.7 us -> 15.6 us  [line_scatter(): lax.ppermute(total(next_one, two_right, three_right).astype(jnp.bfloat16)...]
    ppermute x3, waiting for transfers between devices: 11.5 us -> 23.6 us  [line_scatter(): two_right = lax.ppermute(opposite, axis, [(0, 1), (1, 2)])]
    reduce_sum x0 -> x3, other arithmetic: none -> 10.8 us  [the longest x2 8.82 us: local(): jnp.sum(part.astype(jnp.float32) * rows.astype(jnp.float32) * factor, axi...]
    ppermute x3, starting transfers between devices: 15.1 us -> 6.04 us  [line_scatter(): lax.ppermute(total(next_one, two_right, three_right).astype(jnp.bfloat16)...]
    all_to_all x1, waiting for transfers between devices: 0.01 us -> 7.83 us  [local(): sums = lax.all_to_all(sums, 'dp', split_axis=0, concat_axis=0, tiled=True)]
  transfers between devices with their start and end apart: 57 -> 58, of which waited for: 18 -> 20; matrix products, arithmetic and copies ran while one was open for 18% -> 18% of each run, Pallas kernels for 19% -> 23%
where the time goes in v7:
time: 741 us; the launch traced here: 729 us
  waiting for transfers between devices  203 us (27%)
  Pallas kernels  196 us (26%)
  starting transfers between devices  131 us (18%)
  matrix products  68.3 us (9%)
  other arithmetic  57.8 us (8%)
  local copies, waits for them, and re-layouts  51.7 us (7%)
  between operations  21.1 us (3%)
    dot_general x10, matrix products, dot_dims(): lax.dot_general(left, right, (((left_dim,), (right_dim,)), ((), ())), pre...  68.3 us
    pallas_call x2, Pallas kernels, attn_bwd(): pl.pallas_call(functools.partial(attn_bwd_kernel, bq=bq, bk=bk, heads=hps...  54.7 us
    pallas_call x2, Pallas kernels, attn_fwd(): pl.pallas_call(functools.partial(attn_fwd_kernel, bq=bq, bk=bk, heads=hps...  48.3 us
    ppermute x3, waiting for transfers between devices, line_gather(): two_left = lax.ppermute(one_left, axis, [(1, 2), (2, 3)])  44.8 us
    ppermute x3, waiting for transfers between devices, line_scatter(): two_left = lax.ppermute(opposite, axis, [(3, 2), (2, 1)])  30.2 us
    pallas_call x8, Pallas kernels, spread_block(): pl.pallas_call(spread_kernel, out_shape=jax.ShapeDtypeStruct((rows, width...  27.9 us
    pallas_call x1, Pallas kernels, ffn_main(): pl.pallas_call(functools.partial(ffn_main_kernel, step=step), out_shape=[...  25.9 us
    pallas_call x1, Pallas kernels, ffn_grad(): pl.pallas_call(ffn_grad_kernel, out_shape=jax.ShapeDtypeStruct((chunks, 3...  24.9 us
  transfers between devices with their start and end apart: 58, of which 20 were waited for; matrix products, arithmetic and copies ran while one was open for 18% of the time, Pallas kernels for 23%

profile of v7, /device:TPU:20, one launch (start us, length us, event | category | flops | bytes accessed | tf_op | source)
XLA Modules:
  0.0 729.2 jit_solution(4704461671051579398)
XLA Ops:
  8.4 3.6 collective-permute-start.12
  17.1 3.6 collective-permute-start
  43.9 4.3 collective-permute-start.14
  51.8 5.0 collective-permute-start.16
  62.8 6.0 collective-permute-start.2
  68.8 26.2 %collective-permute-done.14 = bf16[2368,128]{1,0:T(8,128)(2,1)} collective-permute-done((bf16[2368,128]{1,0:T(8,128)(2,1)S(1)}, bf16[2368,128]{1,0:T(8,128)(2,1)}, u32[]{:S(2)}, u32[]{:S(2)}) %collective-permute-start.14) | collective-permute-done | bytes 606240 | tf_op jit(solution)/shard_map/ppermute | solution.py:400
  100.7 18.6 %collective-permute-done.2 = bf16[512,1024]{1,0:T(8,128)(2,1)S(1)} collective-permute-done((bf16[512,1024]{1,0:T(8,128)(2,1)}, bf16[512,1024]{1,0:T(8,128)(2,1)S(1)}, u32[]{:S(2)}, u32[]{:S(2)}) %collective-permute-start.2) | collective-permute-done | bytes 1048608 | tf_op jit(solution)/shard_map/ppermute | solution.py:400
  122.2 4.2 collective-permute-done.5
  128.9 3.9 collective-permute-start.9
  136.2 5.7 fusion.20
  143.7 5.0 collective-permute-done.6
  150.5 3.9 collective-permute-start.8
  156.5 6.3 collective-permute-start.10
  165.1 27.5 %attn_fwd.2 = (bf16[256,2048]{1,0:T(8,128)(2,1)}, f32[4,1,2048]{2,1,0:T(1,128)}) custom-call(s32[4]{0:T(128)} %get-tuple-element.139.lo_ref, bf16[768,2048]{1,0:T(8,128)(2,1)} %pad_maximum_fusion.1.q_ref.k_ref.v_ref, bf16[768,2048]{1,0:T(8,128)(2,1)} %pad_maximum_fusion.1.q_ref.k_ref.v_ref, bf16[768,2048]{1,0:T(8,128)(2,1)} %pad_maximum_fusion.1.q_ref.k_ref.v_ref, ...), custom_call_target="tpu_custom_call" | custom-call | flops 4294967296 | bytes 4194304 | tf_op jit(solution)/shard_map/attn_fwd/pallas_call | solution.py:132
  194.9 4.5 all-to-all-start
  209.4 10.0 %collective-permute-done.11 = bf16[512,1024]{1,0:T(8,128)(2,1)} collective-permute-done((bf16[512,1024]{1,0:T(8,128)(2,1)}, bf16[512,1024]{1,0:T(8,128)(2,1)}, u32[]{:S(2)}, u32[]{:S(2)}) %collective-permute-start.11) | collective-permute-done | bytes 1048608 | tf_op jit(solution)/shard_map/ppermute | solution.py:403
  223.3 3.9 fusion.25
  231.4 17.7 %collective-permute-done.25.refs_9_ = bf16[4736,128]{1,0:T(8,128)(2,1)} collective-permute-done((bf16[4736,128]{1,0:T(8,128)(2,1)S(1)}, bf16[4736,128]{1,0:T(8,128)(2,1)}, u32[]{:S(2)}, u32[]{:S(2)}) %collective-permute-start.25) | collective-permute-done | bytes 1212448 | tf_op jit(solution)/shard_map/ppermute | solution.py:452
  252.6 20.8 %attn_fwd.3 = (bf16[256,2048]{1,0:T(8,128)(2,1)}, f32[4,1,2048]{2,1,0:T(1,128)}) custom-call(s32[4]{0:T(128)} %get-tuple-element.138.lo_ref, bf16[768,2048]{1,0:T(8,128)(2,1)} %pad_maximum_fusion.2.q_ref.k_ref.v_ref, bf16[768,2048]{1,0:T(8,128)(2,1)} %pad_maximum_fusion.2.q_ref.k_ref.v_ref, bf16[768,2048]{1,0:T(8,128)(2,1)} %pad_maximum_fusion.2.q_ref.k_ref.v_ref, ...), custom_call_target="tpu_custom_call" | custom-call | flops 4294967296 | bytes 4194304 | tf_op jit(solution)/shard_map/attn_fwd/pallas_call | solution.py:132
  275.8 8.0 %all-to-all-start.1 = ((bf16[256,4,512]{2,0,1:T(8,128)(2,1)}), bf16[256,4,512]{2,0,1:T(8,128)(2,1)}, u32[]{:S(2)}, u32[]{:S(2)}) async-start(bf16[256,4,512]{2,0,1:T(8,128)(2,1)} %bitcast.149), calls=%async_computation.1 | async-start | bytes 2097152 | tf_op jit(solution)/shard_map/all_to_all | solution.py:535
  284.5 15.7 %collective-permute-done.28.refs_12_ = bf16[4736,128]{1,0:T(8,128)(2,1)} collective-permute-done((bf16[4736,128]{1,0:T(8,128)(2,1)}, bf16[4736,128]{1,0:T(8,128)(2,1)}, u32[]{:S(2)}, u32[]{:S(2)}) %collective-permute-start.28) | collective-permute-done | bytes 1212448 | tf_op jit(solution)/shard_map/ppermute | solution.py:454
  305.2 14.4 %assemble.1 = (bf16[1024,1024]{1,0:T(8,128)(2,1)}, bf16[2816,1024]{1,0:T(8,128)(2,1)}, bf16[2816,1024]{1,0:T(8,128)(2,1)}, bf16[2816,1024]{1,0:T(8,128)(2,1)}) custom-call(s32[8]{0:T(128)} %xor_multiply_fusion.lane_ref, bf16[4736,128]{1,0:T(8,128)(2,1)} %get-tuple-element.82.refs_0_, bf16[4736,128]{1,0:T(8,128)(2,1)} %copy-done.21, ...), custom_call_target="tpu_custom_call" | custom-call | bytes 38797312 | tf_op jit(solution)/shard_map/assemble/pallas_call | solution.py:221
  319.6 4.9 multiply_reduce_fusion.2
  328.1 25.9 %ffn_main.1 = (bf16[1024,2816]{1,0:T(8,128)(2,1)}, bf16[1024,2816]{1,0:T(8,128)(2,1)}, bf16[1024,2816]{1,0:T(8,128)(2,1)}) custom-call(bf16[1024,1024]{1,0:T(8,128)(2,1)} %multiply_convert_fusion.x_ref, bf16[1024,1024]{1,0:T(8,128)(2,1)} %bitcast.158, bf16[2816,1024]{1,0:T(8,128)(2,1)} %get-tuple-element.40.gate_ref, ...), custom_call_target="tpu_custom_call" | custom-call | flops 17716740096 | bytes 34603008 | tf_op jit(solution)/shard_map/ffn_main/pallas_call | solution.py:276
  354.0 9.9 %fusion.52 = f32[1024,1024]{1,0:T(8,128)S(1)} fusion(bf16[1024,2816]{1,0:T(8,128)(2,1)} %get-tuple-element.45.du_ref, bf16[2816,1024]{1,0:T(8,128)(2,1)} %get-tuple-element.41.up_ref), kind=kOutput, calls=%fused_computation.191 | convolution fusion | flops 5905580032 | bytes 15728640 | tf_op jit(solution)/shard_map/dot_general | solution.py:340
  364.0 9.0 %multiply_reduce_fusion = (bf16[1024]{0:T(1024)(128)(2,1)S(1)}, f32[1024]{0:T(1024)S(1)}, f32[1024,1024]{1,0:T(8,128)S(1)}) fusion(f32[1024,1024]{1,0:T(8,128)S(1)} %copy-done.11, f32[1024]{0:T(1024)S(1)} %get-tuple-element.128, f32[1024]{0:T(1024)S(1)} %bitcast.174, f32[1024,1024]{1,0:T(8,128)S(1)} %fusion.52, bf16[1024,2816]{1,0:T(8,128)(2,1)S(1)} %copy-done.42, ...), kind=kOutput, calls=%fused_computation.23 | convolution fusion | flops 5912918016 | bytes 24131584 | tf_op jit(solution)/shard_map/dot_general | solution.py:340
  378.6 4.2 all-to-all-start.2
  382.9 24.9 %ffn_grad.1 = bf16[8,3,2816,128]{3,2,1,0:T(8,128)(2,1)} custom-call(bf16[1024,1024]{1,0:T(8,128)(2,1)} %multiply_convert_fusion.x_ref, bf16[1024,1024]{1,0:T(8,128)(2,1)} %bitcast.159, bf16[1024,2816]{1,0:T(8,128)(2,1)} %get-tuple-element.43.h_ref, bf16[1024,2816]{1,0:T(8,128)(2,1)} %get-tuple-element.44.dg_ref, bf16[1024,2816]{1,0:T(8,128)(2,1)} %get-tuple-element.45.du_ref), custom_call_target="tpu_custom_call" | custom-call | flops 17716740096 | bytes 34603008 | tf_op jit(solution)/shard_map/ffn_grad/pallas_call | solution.py:296
  409.0 5.2 all-to-all-start.3
  416.0 7.2 convolution_convert_fusion
  423.2 13.3 %all-to-all-done.3 = bf16[4,256,512]{2,1,0:T(8,128)(2,1)S(1)} async-done(((bf16[4,256,512]{2,1,0:T(8,128)(2,1)}), bf16[4,256,512]{2,1,0:T(8,128)(2,1)S(1)}, u32[]{:S(2)}, u32[]{:S(2)}) %all-to-all-start.3) | async-done | bytes 1048608 | tf_op jit(solution)/shard_map/all_to_all | solution.py:562
  436.5 6.0 all-to-all-start.5
  443.5 24.0 %attn_bwd.3 = bf16[3,256,2048]{2,1,0:T(8,128)(2,1)} custom-call(s32[4]{0:T(128)} %get-tuple-element.138.lo_ref, bf16[768,2048]{1,0:T(8,128)(2,1)} %pad_maximum_fusion.2.q_ref.k_ref.v_ref, bf16[768,2048]{1,0:T(8,128)(2,1)} %pad_maximum_fusion.2.q_ref.k_ref.v_ref, bf16[768,2048]{1,0:T(8,128)(2,1)} %pad_maximum_fusion.2.q_ref.k_ref.v_ref, ...), custom_call_target="tpu_custom_call" | custom-call | flops 10737418240 | bytes 10485760 | tf_op jit(solution)/shard_map/attn_bwd/pallas_call | solution.py:152
  484.5 30.7 %attn_bwd.2 = bf16[3,256,2048]{2,1,0:T(8,128)(2,1)} custom-call(s32[4]{0:T(128)} %get-tuple-element.139.lo_ref, bf16[768,2048]{1,0:T(8,128)(2,1)} %pad_maximum_fusion.1.q_ref.k_ref.v_ref, bf16[768,2048]{1,0:T(8,128)(2,1)} %pad_maximum_fusion.1.q_ref.k_ref.v_ref, bf16[768,2048]{1,0:T(8,128)(2,1)} %pad_maximum_fusion.1.q_ref.k_ref.v_ref, ...), custom_call_target="tpu_custom_call" | custom-call | flops 10737418240 | bytes 10485760 | tf_op jit(solution)/shard_map/attn_bwd/pallas_call | solution.py:152
  524.0 3.6 spread_block.10
  527.6 6.5 fusion.18
  534.1 7.3 %add_convert_fusion.1 = bf16[1024,768]{1,0:T(8,128)(2,1)} fusion(f32[1024,768]{1,0:T(8,128)S(1)} %fusion.18, bf16[768,2048]{1,0:T(8,128)(2,1)S(1)} %bitcast.131, f32[2048]{0:T(1024)S(1)} %add_rsqrt_fusion, f32[1024]{0:T(1024)S(1)} %bitcast.181, bf16[3584,1024]{1,0:T(8,128)(2,1)} %copy-done.12, s32[]{:T(128)S(6)} %select_n.225), kind=kOutput, calls=%fused_computation.34 | convolution fusion | flops 3231186944 | bytes 12070916 | tf_op jit(solution)/shard_map/dot_general | solution.py:340
  552.0 5.4 multiply_reduce_fusion.6
  557.4 4.3 collective-permute-start.35
  568.8 4.8 collective-permute-start.43
  579.1 6.3 collective-permute-done.35
  590.1 22.8 %collective-permute-done.32 = bf16[512,1024]{1,0:T(8,128)(2,1)S(1)} collective-permute-done((bf16[512,1024]{1,0:T(8,128)(2,1)S(1)}, bf16[512,1024]{1,0:T(8,128)(2,1)S(1)}, u32[]{:S(2)}, u32[]{:S(2)}) %collective-permute-start.32) | collective-permute-done | bytes 1048608 | tf_op jit(solution)/shard_map/ppermute | solution.py:416
  620.0 11.4 %add_convert_fusion = bf16[1024,1024]{1,0:T(8,128)(2,1)} fusion(f32[1024,1024]{1,0:T(8,128)} %copy-done.10, bf16[1024,2816]{1,0:T(8,128)(2,1)} %get-tuple-element.43.h_ref, bf16[2816,1024]{1,0:T(8,128)(2,1)} %get-tuple-element.42.down_ref), kind=kOutput, calls=%fused_computation.26 | convolution fusion | flops 5907677184 | bytes 17825792 | tf_op jit(solution)/shard_map/dot_general | solution.py:340
  633.6 7.8 %all-to-all-done.4 = bf16[8,144,768]{2,1,0:T(8,128)(2,1)S(1)} async-done(((bf16[8,144,768]{2,1,0:T(8,128)(2,1)}), bf16[8,144,768]{2,1,0:T(8,128)(2,1)S(1)}, u32[]{:S(2)}, u32[]{:S(2)}) %all-to-all-start.4) | async-done | bytes 1769504 | tf_op jit(solution)/shard_map/all_to_all | solution.py:606
  646.9 11.1 %collective-permute-done.34 = bf16[512,1024]{1,0:T(8,128)(2,1)} collective-permute-done((bf16[512,1024]{1,0:T(8,128)(2,1)}, bf16[512,1024]{1,0:T(8,128)(2,1)}, u32[]{:S(2)}, u32[]{:S(2)}) %collective-permute-start.34) | collective-permute-done | bytes 1048608 | tf_op jit(solution)/shard_map/ppermute | solution.py:426
  673.1 24.0 %collective-permute-done.47 = bf16[2384,128]{1,0:T(8,128)(2,1)S(1)} collective-permute-done((bf16[2384,128]{1,0:T(8,128)(2,1)S(1)}, bf16[2384,128]{1,0:T(8,128)(2,1)S(1)}, u32[]{:S(2)}, u32[]{:S(2)}) %collective-permute-start.47) | collective-permute-done | bytes 610336 | tf_op jit(solution)/shard_map/ppermute | solution.py:417
  706.8 8.2 %collective-permute-done.49 = bf16[2384,128]{1,0:T(8,128)(2,1)S(1)} collective-permute-done((bf16[2384,128]{1,0:T(8,128)(2,1)S(1)}, bf16[2384,128]{1,0:T(8,128)(2,1)S(1)}, u32[]{:S(2)}, u32[]{:S(2)}) %collective-permute-start.49) | collective-permute-done | bytes 610336 | tf_op jit(solution)/shard_map/ppermute | solution.py:429
  715.0 4.5 collective-permute-done.46
  (296 shorter events, 196.0 us)
Async XLA Ops:
  7.2 126.5 %all-gather.3.cloned.1.call-start = ((), (), s32[]{:S(2)}) async-start(), calls=%async_computation.8 | async-start | bytes 1990656 | tf_op jit(solution)/shard_map/all_gather | solution.py:489
  8.4 34.0 %collective-permute-start.12 = (bf16[2368,128]{1,0:T(8,128)(2,1)S(1)}, bf16[2368,128]{1,0:T(8,128)(2,1)S(1)}, u32[]{:S(2)}, u32[]{:S(2)}) collective-permute-start(bf16[2368,128]{1,0:T(8,128)(2,1)S(1)} %pad_maximum_fusion.8), channel_id=1, source_target_pairs={{0,1},{1,2},{2,3},{4,5},{5,6},{6,7},{8,9},{9,10},{10,11},{12,13},{... | collective-permute-start | bytes 1818632 | tf_op jit(solution)/shard_map/ppermute | solution.py:398
  12.0 39.7 %collective-permute-start.15 = (bf16[2368,128]{1,0:T(8,128)(2,1)S(1)}, bf16[2368,128]{1,0:T(8,128)(2,1)S(1)}, u32[]{:S(2)}, u32[]{:S(2)}) collective-permute-start(bf16[2368,128]{1,0:T(8,128)(2,1)S(1)} %pad_maximum_fusion.8), channel_id=1, source_target_pairs={{1,0},{2,1},{3,2},{5,4},{6,5},{7,6},{9,8},{10,9},{11,10},{13,12},{... | collective-permute-start | bytes 1818632 | tf_op jit(solution)/shard_map/ppermute | solution.py:399
  17.1 42.5 %collective-permute-start = (bf16[512,1024]{1,0:T(8,128)(2,1)S(1)}, bf16[512,1024]{1,0:T(8,128)(2,1)}, u32[]{:S(2)}, u32[]{:S(2)}) collective-permute-start(bf16[512,1024]{1,0:T(8,128)(2,1)S(1)} %get-tuple-element.98), channel_id=1, source_target_pairs={{0,1},{1,2},{2,3},{4,5},{5,6},{6,7},{8,9},{9,10},{10,11},{12,13},{... | collective-permute-start | bytes 3145736 | tf_op jit(solution)/shard_map/ppermute | solution.py:398
  20.8 42.1 %collective-permute-start.3 = (bf16[512,1024]{1,0:T(8,128)(2,1)S(1)}, bf16[512,1024]{1,0:T(8,128)(2,1)}, u32[]{:S(2)}, u32[]{:S(2)}) collective-permute-start(bf16[512,1024]{1,0:T(8,128)(2,1)S(1)} %get-tuple-element.98), channel_id=1, source_target_pairs={{1,0},{2,1},{3,2},{5,4},{6,5},{7,6},{9,8},{10,9},{11,10},{13,12},{... | collective-permute-start | bytes 3145736 | tf_op jit(solution)/shard_map/ppermute | solution.py:399
  43.9 51.1 %collective-permute-start.14 = (bf16[2368,128]{1,0:T(8,128)(2,1)S(1)}, bf16[2368,128]{1,0:T(8,128)(2,1)}, u32[]{:S(2)}, u32[]{:S(2)}) collective-permute-start(bf16[2368,128]{1,0:T(8,128)(2,1)S(1)} %collective-permute-done.12), channel_id=1, source_target_pairs={{1,2},{2,3},{5,6},{6,7},{9,10},{10,11},{13,14},{14,15},{17,18},{18... | collective-permute-start | bytes 1818632 | tf_op jit(solution)/shard_map/ppermute | solution.py:400
  51.8 46.1 %collective-permute-start.16 = (bf16[2368,128]{1,0:T(8,128)(2,1)S(1)}, bf16[2368,128]{1,0:T(8,128)(2,1)S(1)}, u32[]{:S(2)}, u32[]{:S(2)}) collective-permute-start(bf16[2368,128]{1,0:T(8,128)(2,1)S(1)} %collective-permute-done.15), channel_id=1, source_target_pairs={{1,0},{2,1},{5,4},{6,5},{9,8},{10,9},{13,12},{14,13},{17,16},{18,1... | collective-permute-start | bytes 1818632 | tf_op jit(solution)/shard_map/ppermute | solution.py:401
  59.6 39.7 %collective-permute-start.17 = (bf16[2368,128]{1,0:T(8,128)(2,1)S(1)}, bf16[2368,128]{1,0:T(8,128)(2,1)S(1)}, u32[]{:S(2)}, u32[]{:S(2)}) collective-permute-start(bf16[2368,128]{1,0:T(8,128)(2,1)S(1)} %collective-permute-done.15), channel_id=1, source_target_pairs={{2,0},{6,4},{10,8},{14,12},{18,16},{22,20},{26,24},{30,28}} | collective-permute-start | bytes 1818632 | tf_op jit(solution)/shard_map/ppermute | solution.py:403
  60.9 39.7 %collective-permute-start.1 = (bf16[512,1024]{1,0:T(8,128)(2,1)}, bf16[512,1024]{1,0:T(8,128)(2,1)S(1)}, u32[]{:S(2)}, u32[]{:S(2)}) collective-permute-start(bf16[512,1024]{1,0:T(8,128)(2,1)} %collective-permute-done), channel_id=1, source_target_pairs={{1,3},{5,7},{9,11},{13,15},{17,19},{21,23},{25,27},{29,31}} | collective-permute-start | bytes 3145736 | tf_op jit(solution)/shard_map/ppermute | solution.py:402
  62.8 56.5 %collective-permute-start.2 = (bf16[512,1024]{1,0:T(8,128)(2,1)}, bf16[512,1024]{1,0:T(8,128)(2,1)S(1)}, u32[]{:S(2)}, u32[]{:S(2)}) collective-permute-start(bf16[512,1024]{1,0:T(8,128)(2,1)} %collective-permute-done), channel_id=1, source_target_pairs={{1,2},{2,3},{5,6},{6,7},{9,10},{10,11},{13,14},{14,15},{17,18},{18... | collective-permute-start | bytes 3145736 | tf_op jit(solution)/shard_map/ppermute | solution.py:400
  95.0 27.1 %collective-permute-start.4 = (bf16[512,1024]{1,0:T(8,128)(2,1)}, bf16[512,1024]{1,0:T(8,128)(2,1)S(1)}, u32[]{:S(2)}, u32[]{:S(2)}) collective-permute-start(bf16[512,1024]{1,0:T(8,128)(2,1)} %collective-permute-done.3), channel_id=1, source_target_pairs={{1,0},{2,1},{5,4},{6,5},{9,8},{10,9},{13,12},{14,13},{17,16},{18,1... | collective-permute-start | bytes 3145736 | tf_op jit(solution)/shard_map/ppermute | solution.py:401
  97.9 28.5 %collective-permute-start.5 = (bf16[512,1024]{1,0:T(8,128)(2,1)}, bf16[512,1024]{1,0:T(8,128)(2,1)S(1)}, u32[]{:S(2)}, u32[]{:S(2)}) collective-permute-start(bf16[512,1024]{1,0:T(8,128)(2,1)} %collective-permute-done.3), channel_id=1, source_target_pairs={{2,0},{6,4},{10,8},{14,12},{18,16},{22,20},{26,24},{30,28}} | collective-permute-start | bytes 3145736 | tf_op jit(solution)/shard_map/ppermute | solution.py:403
  100.6 128.6 %collective-permute-start.18 = (bf16[4736,128]{1,0:T(8,128)(2,1)}, bf16[4736,128]{1,0:T(8,128)(2,1)}, u32[]{:S(2)}, u32[]{:S(2)}) collective-permute-start(bf16[4736,128]{1,0:T(8,128)(2,1)} %get-tuple-element.82.refs_0_), channel_id=1, source_target_pairs={{0,4},{4,0},{8,12},{12,8},{16,20},{20,16},{24,28},{28,24},{1,5},{5... | collective-permute-start | bytes 3637256 | tf_op jit(solution)/shard_map/ppermute | solution.py:450
  128.9 27.7 %collective-permute-start.9 = (bf16[512,1024]{1,0:T(8,128)(2,1)}, bf16[512,1024]{1,0:T(8,128)(2,1)}, u32[]{:S(2)}, u32[]{:S(2)}) collective-permute-start(bf16[512,1024]{1,0:T(8,128)(2,1)} %get-tuple-element.37), channel_id=1, source_target_pairs={{1,0},{2,1},{3,2},{5,4},{6,5},{7,6},{9,8},{10,9},{11,10},{13,12},{... | collective-permute-start | bytes 3145736 | tf_op jit(solution)/shard_map/ppermute | solution.py:399
  148.7 50.7 %collective-permute-start.7 = (bf16[512,1024]{1,0:T(8,128)(2,1)}, bf16[512,1024]{1,0:T(8,128)(2,1)}, u32[]{:S(2)}, u32[]{:S(2)}) collective-permute-start(bf16[512,1024]{1,0:T(8,128)(2,1)} %collective-permute-done.6), channel_id=1, source_target_pairs={{1,3},{5,7},{9,11},{13,15},{17,19},{21,23},{25,27},{29,31}} | collective-permute-start | bytes 3145736 | tf_op jit(solution)/shard_map/ppermute | solution.py:402
  150.5 50.2 %collective-permute-start.8 = (bf16[512,1024]{1,0:T(8,128)(2,1)}, bf16[512,1024]{1,0:T(8,128)(2,1)}, u32[]{:S(2)}, u32[]{:S(2)}) collective-permute-start(bf16[512,1024]{1,0:T(8,128)(2,1)} %collective-permute-done.6), channel_id=1, source_target_pairs={{1,2},{2,3},{5,6},{6,7},{9,10},{10,11},{13,14},{14,15},{17,18},{18... | collective-permute-start | bytes 3145736 | tf_op jit(solution)/shard_map/ppermute | solution.py:400
  156.5 49.5 %collective-permute-start.10 = (bf16[512,1024]{1,0:T(8,128)(2,1)}, bf16[512,1024]{1,0:T(8,128)(2,1)}, u32[]{:S(2)}, u32[]{:S(2)}) collective-permute-start(bf16[512,1024]{1,0:T(8,128)(2,1)} %collective-permute-done.9), channel_id=1, source_target_pairs={{1,0},{2,1},{5,4},{6,5},{9,8},{10,9},{13,12},{14,13},{17,16},{18,1... | collective-permute-start | bytes 3145736 | tf_op jit(solution)/shard_map/ppermute | solution.py:401
  162.8 56.6 %collective-permute-start.11 = (bf16[512,1024]{1,0:T(8,128)(2,1)}, bf16[512,1024]{1,0:T(8,128)(2,1)}, u32[]{:S(2)}, u32[]{:S(2)}) collective-permute-start(bf16[512,1024]{1,0:T(8,128)(2,1)} %collective-permute-done.9), channel_id=1, source_target_pairs={{2,0},{6,4},{10,8},{14,12},{18,16},{22,20},{26,24},{30,28}} | collective-permute-start | bytes 3145736 | tf_op jit(solution)/shard_map/ppermute | solution.py:403
  194.9 80.9 %all-to-all-start = ((bf16[256,4,512]{2,0,1:T(8,128)(2,1)}), bf16[256,4,512]{2,0,1:T(8,128)(2,1)}, u32[]{:S(2)}, u32[]{:S(2)}) async-start(bf16[256,4,512]{2,0,1:T(8,128)(2,1)} %bitcast.148), calls=%async_computation | async-start | bytes 2097152 | tf_op jit(solution)/shard_map/all_to_all | solution.py:535
  199.4 30.3 %collective-permute-start.20 = (bf16[4736,128]{1,0:T(8,128)(2,1)}, bf16[4736,128]{1,0:T(8,128)(2,1)}, u32[]{:S(2)}, u32[]{:S(2)}) collective-permute-start(bf16[4736,128]{1,0:T(8,128)(2,1)} %get-tuple-element.82.refs_0_), channel_id=1, source_target_pairs={{0,8},{4,12},{8,0},{12,4},{16,24},{20,28},{24,16},{28,20},{1,9},{5... | collective-permute-start | bytes 3637256 | tf_op jit(solution)/shard_map/ppermute | solution.py:452
  200.8 28.9 %collective-permute-start.19 = (bf16[4736,128]{1,0:T(8,128)(2,1)S(1)}, bf16[4736,128]{1,0:T(8,128)(2,1)S(1)}, u32[]{:S(2)}, u32[]{:S(2)}) collective-permute-start(bf16[4736,128]{1,0:T(8,128)(2,1)S(1)} %get-tuple-element.81.refs_1_), channel_id=1, source_target_pairs={{0,4},{4,0},{8,12},{12,8},{16,20},{20,16},{24,28},{28,24},{1,5},{5... | collective-permute-start | bytes 3637256 | tf_op jit(solution)/shard_map/ppermute | solution.py:450
  206.1 77.7 %collective-permute-start.21 = (bf16[4736,128]{1,0:T(8,128)(2,1)S(1)}, bf16[4736,128]{1,0:T(8,128)(2,1)}, u32[]{:S(2)}, u32[]{:S(2)}) collective-permute-start(bf16[4736,128]{1,0:T(8,128)(2,1)S(1)} %get-tuple-element.81.refs_1_), channel_id=1, source_target_pairs={{0,8},{4,12},{8,0},{12,4},{16,24},{20,28},{24,16},{28,20},{1,9},{5... | collective-permute-start | bytes 3637256 | tf_op jit(solution)/shard_map/ppermute | solution.py:453
  219.5 29.6 %collective-permute-start.25 = (bf16[4736,128]{1,0:T(8,128)(2,1)S(1)}, bf16[4736,128]{1,0:T(8,128)(2,1)}, u32[]{:S(2)}, u32[]{:S(2)}) collective-permute-start(bf16[4736,128]{1,0:T(8,128)(2,1)S(1)} %get-tuple-element.81.refs_1_), channel_id=1, source_target_pairs={{0,16},{4,20},{8,24},{12,28},{16,0},{20,4},{24,8},{28,12},{1,17},{... | collective-permute-start | bytes 3637256 | tf_op jit(solution)/shard_map/ppermute | solution.py:452
  229.2 54.6 %collective-permute-start.24 = (bf16[4736,128]{1,0:T(8,128)(2,1)}, bf16[4736,128]{1,0:T(8,128)(2,1)}, u32[]{:S(2)}, u32[]{:S(2)}) collective-permute-start(bf16[4736,128]{1,0:T(8,128)(2,1)} %get-tuple-element.82.refs_0_), channel_id=1, source_target_pairs={{0,16},{4,20},{8,24},{12,28},{16,0},{20,4},{24,8},{28,12},{1,17},{... | collective-permute-start | bytes 3637256 | tf_op jit(solution)/shard_map/ppermute | solution.py:453
  229.7 54.7 %collective-permute-start.22 = (bf16[4736,128]{1,0:T(8,128)(2,1)}, bf16[4736,128]{1,0:T(8,128)(2,1)}, u32[]{:S(2)}, u32[]{:S(2)}) collective-permute-start(bf16[4736,128]{1,0:T(8,128)(2,1)} %collective-permute-done.20.refs_4_), channel_id=1, source_target_pairs={{0,4},{4,0},{8,12},{12,8},{16,20},{20,16},{24,28},{28,24},{1,5},{5... | collective-permute-start | bytes 3637256 | tf_op jit(solution)/shard_map/ppermute | solution.py:450
  229.7 70.5 %collective-permute-start.28 = (bf16[4736,128]{1,0:T(8,128)(2,1)}, bf16[4736,128]{1,0:T(8,128)(2,1)}, u32[]{:S(2)}, u32[]{:S(2)}) collective-permute-start(bf16[4736,128]{1,0:T(8,128)(2,1)} %collective-permute-done.20.refs_4_), channel_id=1, source_target_pairs={{0,16},{4,20},{8,24},{12,28},{16,0},{20,4},{24,8},{28,12},{1,17},{... | collective-permute-start | bytes 3637256 | tf_op jit(solution)/shard_map/ppermute | solution.py:454
  249.1 51.1 %collective-permute-start.29 = (bf16[4736,128]{1,0:T(8,128)(2,1)}, bf16[4736,128]{1,0:T(8,128)(2,1)}, u32[]{:S(2)}, u32[]{:S(2)}) collective-permute-start(bf16[4736,128]{1,0:T(8,128)(2,1)} %collective-permute-done.25.refs_9_), channel_id=1, source_target_pairs={{0,8},{4,12},{8,0},{12,4},{16,24},{20,28},{24,16},{28,20},{1,9},{5... | collective-permute-start | bytes 3637256 | tf_op jit(solution)/shard_map/ppermute | solution.py:454
  275.8 43.8 %all-to-all-start.1 = ((bf16[256,4,512]{2,0,1:T(8,128)(2,1)}), bf16[256,4,512]{2,0,1:T(8,128)(2,1)}, u32[]{:S(2)}, u32[]{:S(2)}) async-start(bf16[256,4,512]{2,0,1:T(8,128)(2,1)} %bitcast.149), calls=%async_computation.1 | async-start | bytes 2097152 | tf_op jit(solution)/shard_map/all_to_all | solution.py:535
  378.6 29.3 %all-to-all-start.2 = ((bf16[4,256,512]{2,1,0:T(8,128)(2,1)}), bf16[4,256,512]{2,1,0:T(8,128)(2,1)S(1)}, u32[]{:S(2)}, u32[]{:S(2)}) async-start(bf16[4,256,512]{2,1,0:T(8,128)(2,1)} %bitcast.28), calls=%async_computation.2 | async-start | bytes 2097152 | tf_op jit(solution)/shard_map/all_to_all | solution.py:562
  382.7 281.3 %reduce-scatter.2.cloned.1.call-start = ((), (), s32[]{:S(2)}) async-start(), calls=%async_computation.7 | async-start | bytes 19464192 | tf_op jit(solution)/shard_map/reduce_scatter | solution.py:385
  409.0 27.4 %all-to-all-start.3 = ((bf16[4,256,512]{2,1,0:T(8,128)(2,1)}), bf16[4,256,512]{2,1,0:T(8,128)(2,1)S(1)}, u32[]{:S(2)}, u32[]{:S(2)}) async-start(bf16[4,256,512]{2,1,0:T(8,128)(2,1)} %bitcast.153), calls=%async_computation.3 | async-start | bytes 2097152 | tf_op jit(solution)/shard_map/all_to_all | solution.py:562
  436.5 180.0 %all-to-all-start.5 = ((bf16[8,128,1024]{2,1,0:T(8,128)(2,1)}), bf16[8,128,1024]{2,1,0:T(8,128)(2,1)}, u32[]{:S(2)}, u32[]{:S(2)}) async-start(bf16[8,128,1024]{2,1,0:T(8,128)(2,1)} %bitcast.157), calls=%async_computation.5 | async-start | bytes 4194304 | tf_op jit(solution)/shard_map/all_to_all | solution.py:570
  471.0 90.8 %collective-permute-start.41 = (bf16[512,1024]{1,0:T(8,128)(2,1)}, bf16[512,1024]{1,0:T(8,128)(2,1)}, u32[]{:S(2)}, u32[]{:S(2)}) collective-permute-start(bf16[512,1024]{1,0:T(8,128)(2,1)} %spread_block.15), channel_id=1, source_target_pairs={{3,2},{2,1},{7,6},{6,5},{11,10},{10,9},{15,14},{14,13},{19,18},{18... | collective-permute-start | bytes 3145736 | tf_op jit(solution)/shard_map/ppermute | solution.py:417
  473.4 95.4 %collective-permute-start.38 = (bf16[512,1024]{1,0:T(8,128)(2,1)}, bf16[512,1024]{1,0:T(8,128)(2,1)}, u32[]{:S(2)}, u32[]{:S(2)}) collective-permute-start(bf16[512,1024]{1,0:T(8,128)(2,1)} %spread_block.15), channel_id=1, source_target_pairs={{0,1},{1,2},{4,5},{5,6},{8,9},{9,10},{12,13},{13,14},{16,17},{17,1... | collective-permute-start | bytes 3145736 | tf_op jit(solution)/shard_map/ppermute | solution.py:416
  478.2 79.2 %collective-permute-start.42 = (bf16[512,1024]{1,0:T(8,128)(2,1)}, bf16[512,1024]{1,0:T(8,128)(2,1)}, u32[]{:S(2)}, u32[]{:S(2)}) collective-permute-start(bf16[512,1024]{1,0:T(8,128)(2,1)} %spread_block.13), channel_id=1, source_target_pairs={{3,1},{7,5},{11,9},{15,13},{19,17},{23,21},{27,25},{31,29}} | collective-permute-start | bytes 3145736 | tf_op jit(solution)/shard_map/ppermute | solution.py:419
  483.3 79.8 %collective-permute-start.39 = (bf16[512,1024]{1,0:T(8,128)(2,1)}, bf16[512,1024]{1,0:T(8,128)(2,1)}, u32[]{:S(2)}, u32[]{:S(2)}) collective-permute-start(bf16[512,1024]{1,0:T(8,128)(2,1)} %spread_block.14), channel_id=1, source_target_pairs={{0,2},{4,6},{8,10},{12,14},{16,18},{20,22},{24,26},{28,30}} | collective-permute-start | bytes 3145736 | tf_op jit(solution)/shard_map/ppermute | solution.py:418
  518.7 58.1 %collective-permute-start.36 = (bf16[512,1024]{1,0:T(8,128)(2,1)}, bf16[512,1024]{1,0:T(8,128)(2,1)}, u32[]{:S(2)}, u32[]{:S(2)}) collective-permute-start(bf16[512,1024]{1,0:T(8,128)(2,1)} %spread_block.9), channel_id=1, source_target_pairs={{3,1},{7,5},{11,9},{15,13},{19,17},{23,21},{27,25},{31,29}} | collective-permute-start | bytes 3145736 | tf_op jit(solution)/shard_map/ppermute | solution.py:419
  557.4 27.9 %collective-permute-start.35 = (bf16[512,1024]{1,0:T(8,128)(2,1)S(1)}, bf16[512,1024]{1,0:T(8,128)(2,1)S(1)}, u32[]{:S(2)}, u32[]{:S(2)}) collective-permute-start(bf16[512,1024]{1,0:T(8,128)(2,1)S(1)} %copy-done.23), channel_id=1, source_target_pairs={{3,2},{2,1},{7,6},{6,5},{11,10},{10,9},{15,14},{14,13},{19,18},{18... | collective-permute-start | bytes 3145736 | tf_op jit(solution)/shard_map/ppermute | solution.py:417
  561.7 28.4 %collective-permute-start.33 = (bf16[512,1024]{1,0:T(8,128)(2,1)S(1)}, bf16[512,1024]{1,0:T(8,128)(2,1)S(1)}, u32[]{:S(2)}, u32[]{:S(2)}) collective-permute-start(bf16[512,1024]{1,0:T(8,128)(2,1)S(1)} %copy-done.16), channel_id=1, source_target_pairs={{0,2},{4,6},{8,10},{12,14},{16,18},{20,22},{24,26},{28,30}} | collective-permute-start | bytes 3145736 | tf_op jit(solution)/shard_map/ppermute | solution.py:418
  563.1 49.9 %collective-permute-start.32 = (bf16[512,1024]{1,0:T(8,128)(2,1)S(1)}, bf16[512,1024]{1,0:T(8,128)(2,1)S(1)}, u32[]{:S(2)}, u32[]{:S(2)}) collective-permute-start(bf16[512,1024]{1,0:T(8,128)(2,1)S(1)} %copy-done.23), channel_id=1, source_target_pairs={{0,1},{1,2},{4,5},{5,6},{8,9},{9,10},{12,13},{13,14},{16,17},{17,1... | collective-permute-start | bytes 3145736 | tf_op jit(solution)/shard_map/ppermute | solution.py:416
  568.8 75.6 %collective-permute-start.43 = (bf16[512,1024]{1,0:T(8,128)(2,1)}, bf16[512,1024]{1,0:T(8,128)(2,1)}, u32[]{:S(2)}, u32[]{:S(2)}) collective-permute-start(bf16[512,1024]{1,0:T(8,128)(2,1)} %add_convert_fusion.2), channel_id=1, source_target_pairs={{1,0},{2,1},{3,2},{5,4},{6,5},{7,6},{9,8},{10,9},{11,10},{13,12},{... | collective-permute-start | bytes 3145736 | tf_op jit(solution)/shard_map/ppermute | solution.py:429
  576.8 67.6 %collective-permute-start.40 = (bf16[512,1024]{1,0:T(8,128)(2,1)}, bf16[512,1024]{1,0:T(8,128)(2,1)}, u32[]{:S(2)}, u32[]{:S(2)}) collective-permute-start(bf16[512,1024]{1,0:T(8,128)(2,1)} %add_convert_fusion.3), channel_id=1, source_target_pairs={{0,1},{1,2},{2,3},{4,5},{5,6},{6,7},{8,9},{9,10},{10,11},{12,13},{... | collective-permute-start | bytes 3145736 | tf_op jit(solution)/shard_map/ppermute | solution.py:426
  588.2 58.7 %collective-permute-start.37 = (bf16[512,1024]{1,0:T(8,128)(2,1)}, bf16[512,1024]{1,0:T(8,128)(2,1)}, u32[]{:S(2)}, u32[]{:S(2)}) collective-permute-start(bf16[512,1024]{1,0:T(8,128)(2,1)} %add_convert_fusion.4), channel_id=1, source_target_pairs={{1,0},{2,1},{3,2},{5,4},{6,5},{7,6},{9,8},{10,9},{11,10},{13,12},{... | collective-permute-start | bytes 3145736 | tf_op jit(solution)/shard_map/ppermute | solution.py:429
  614.6 43.4 %collective-permute-start.34 = (bf16[512,1024]{1,0:T(8,128)(2,1)}, bf16[512,1024]{1,0:T(8,128)(2,1)}, u32[]{:S(2)}, u32[]{:S(2)}) collective-permute-start(bf16[512,1024]{1,0:T(8,128)(2,1)} %add_convert_fusion.5), channel_id=1, source_target_pairs={{0,1},{1,2},{2,3},{4,5},{5,6},{6,7},{8,9},{9,10},{10,11},{12,13},{... | collective-permute-start | bytes 3145736 | tf_op jit(solution)/shard_map/ppermute | solution.py:426
  616.5 25.0 %all-to-all-start.4 = ((bf16[8,144,768]{2,1,0:T(8,128)(2,1)}), bf16[8,144,768]{2,1,0:T(8,128)(2,1)S(1)}, u32[]{:S(2)}, u32[]{:S(2)}) async-start(bf16[8,144,768]{2,1,0:T(8,128)(2,1)} %fusion.17), calls=%async_computation.4 | async-start | bytes 3538944 | tf_op jit(solution)/shard_map/all_to_all | solution.py:606
  667.0 30.0 %collective-permute-start.47 = (bf16[2384,128]{1,0:T(8,128)(2,1)S(1)}, bf16[2384,128]{1,0:T(8,128)(2,1)S(1)}, u32[]{:S(2)}, u32[]{:S(2)}) collective-permute-start(bf16[2384,128]{1,0:T(8,128)(2,1)S(1)} %get-tuple-element.92), channel_id=1, source_target_pairs={{3,2},{2,1},{7,6},{6,5},{11,10},{10,9},{15,14},{14,13},{19,18},{18... | collective-permute-start | bytes 1830920 | tf_op jit(solution)/shard_map/ppermute | solution.py:417
  670.3 31.5 %collective-permute-start.44 = (bf16[2384,128]{1,0:T(8,128)(2,1)S(1)}, bf16[2384,128]{1,0:T(8,128)(2,1)S(1)}, u32[]{:S(2)}, u32[]{:S(2)}) collective-permute-start(bf16[2384,128]{1,0:T(8,128)(2,1)S(1)} %get-tuple-element.92), channel_id=1, source_target_pairs={{0,1},{1,2},{4,5},{5,6},{8,9},{9,10},{12,13},{13,14},{16,17},{17,1... | collective-permute-start | bytes 1830920 | tf_op jit(solution)/shard_map/ppermute | solution.py:416
  671.7 29.2 %collective-permute-start.45 = (bf16[2384,128]{1,0:T(8,128)(2,1)S(1)}, bf16[2384,128]{1,0:T(8,128)(2,1)S(1)}, u32[]{:S(2)}, u32[]{:S(2)}) collective-permute-start(bf16[2384,128]{1,0:T(8,128)(2,1)S(1)} %get-tuple-element.58), channel_id=1, source_target_pairs={{0,2},{4,6},{8,10},{12,14},{16,18},{20,22},{24,26},{28,30}} | collective-permute-start | bytes 1830920 | tf_op jit(solution)/shard_map/ppermute | solution.py:418
  (53 other events, 1062.1 us)
Sparse Core Ops, SparseCore 0:
  35.2 28.3 all-gather.2
  409.1 139.2 reduce-scatter.1
